TPU v7x, 256 devices: a whole 4x4x8 slice. The times are simulated.
256 devices in a mesh: pts: 4 (over x_hi, core), ctr: 64 (over z, x_lo, y).
Axes of the slice: x: 4 (x_hi: 2, x_lo: 2; x = x_hi * 2 + x_lo), y: 4, z: 8, core: 2. Of those that a mesh axis runs over, the one named last changes fastest.
Arguments:
- points: bfloat16 [32768, 128], P('pts'), may hold values from -16 to 16, as said below
- centers: bfloat16 [131072, 128], P('ctr'), may hold values from -16 to 16, as said below
- panel_inverse: bfloat16 [512, 512], P('pts'), as said below
- direction: float32 [32, 131072], P(None, 'ctr'), as said below
- residual: float32 [32, 131072], P(None, 'ctr'), as said below
Outputs:
- panel_rows: bfloat16 [131072, 512], P('ctr', 'pts')
- operator_image: float32 [32, 131072], P(None, 'ctr')
- new_residual: float32 [32, 131072], P(None, 'ctr')
Inputs may be any that keep to these rules, and one draw needn't show every extreme that they name: `points`: rows of 128 real features. `centers`: rows of 128 real features. panel_inverse is lower triangular with a positive diagonal. `direction`: finite real values. `residual`: finite real values.
All inputs are finite; a program needn't handle non-finite values.
Results may differ from a plain program's by a relative error of at most 0.001.
The roundings to bfloat16 on the way count: a program that leaves them out, or rounds other values in their place, can miss the bound.
Values may be sent and summed in bfloat16 or wider, within the bound.
No kernel may reach another device: no remote copies, remote signals or barrier semaphores. Data moves between devices by JAX's collectives and lax.ppermute only.
A program may use at most 128 MiB of HBM per device.

v0:
```python
import math

import jax
import jax.numpy as jnp
from jax import lax
from jax.sharding import Mesh
from jax.sharding import PartitionSpec as P

CTR = ("ctr_0", "ctr_1", "ctr_2")


RIDGE_TERM = 0.002


def sent_to_all(x, axis):
    copies = jnp.broadcast_to(x, (lax.axis_size(axis), *x.shape))
    return lax.all_to_all(copies, axis, split_axis=0, concat_axis=0, tiled=True)


def of_everyone(x, axis):
    return sent_to_all(x, axis).sum(axis=0)


def from_root(x, axes, root):
    x = jnp.where(lax.axis_index(axes) == root, x, jnp.zeros_like(x))
    for axis in axes:
        x = lax.psum(x, axis)
    return x


def in_one(arrays, axis):
    ends = [0]
    for a in arrays:
        ends.append(ends[-1] + a.size)
    subtotal = of_everyone(jnp.concatenate([a.ravel() for a in arrays]), axis)
    return tuple((subtotal[b:e].reshape(a.shape) for a, b, e in zip(arrays, ends, ends[1:])))


def cut_along(x, dim, length):
    shape = x.shape
    parts = x.reshape(*shape[:dim], length, shape[dim] // length, *shape[dim + 1 :])
    return jnp.moveaxis(parts, dim, 0)


def summed_on_arrival(x, axis, dim):
    length = lax.axis_size(axis)
    parts = lax.all_to_all(cut_along(x, dim, length), axis, 0, 0, tiled=True)
    return jnp.sum(parts, axis=0)


def laid_out(parts, dim):
    shape = list(parts.shape[1:])
    shape[dim] *= parts.shape[0]
    return jnp.moveaxis(parts, 0, dim).reshape(shape)


def gather_directly(x, axis, dim):
    return laid_out(sent_to_all(x, axis), dim)


def similarity(left, right):
    inner_terms = lax.dot_general(
        left, right, (((1,), (1,)), ((), ())), preferred_element_type=jnp.float32
    )
    left_sq = jnp.sum(jnp.square(left.astype(jnp.float32)), axis=1)
    right_sq = jnp.sum(jnp.square(right.astype(jnp.float32)), axis=1)
    feature_count = left.shape[1]
    return jnp.exp(
        -(left_sq[:, None] + right_sq[None, :] - 2.0 * inner_terms) / (2.0 * feature_count)
    )


def center_image(w_bf16, kernel_rows):
    return of_everyone(jnp.dot(w_bf16, kernel_rows, preferred_element_type=jnp.float32), "pts")


def shards(points, centers, panel_inverse, direction, residual):
    n_ctr = lax.axis_size(CTR)
    n_pts = lax.axis_size("pts")
    ctr_index = lax.axis_index(CTR)
    pts_index = lax.axis_index("pts")
    m_dev = centers.shape[0]
    npg = points.shape[0]
    panel_size = panel_inverse.shape[1]
    panel_share = panel_inverse.shape[0]
    outputs = direction.shape[0]
    contract_last = (((1,), (1,)), ((), ()))
    head_rows, head_vals = (
        from_root(centers[:panel_size], CTR, 0),
        from_root(direction[:, :panel_size].astype(jnp.bfloat16), CTR, 0),
    )
    z1_share = lax.dot_general(
        head_vals, panel_inverse, contract_last, preferred_element_type=jnp.float32
    ).astype(jnp.bfloat16)
    q_part = jnp.dot(z1_share, panel_inverse, preferred_element_type=jnp.float32)
    embedded = lax.dynamic_update_slice(
        jnp.zeros((outputs, panel_size), jnp.float32),
        z1_share.astype(jnp.float32),
        (jnp.int32(0), pts_index * panel_share),
    )
    q_sum, z1_full = in_one((q_part, embedded), "pts")
    q_bf16 = q_sum.astype(jnp.bfloat16)
    k_panel = similarity(centers, head_rows).astype(jnp.bfloat16)
    panel_rows = lax.dot_general(
        k_panel, panel_inverse, contract_last, preferred_element_type=jnp.float32
    ).astype(jnp.bfloat16)
    correction = lax.dot_general(q_bf16, k_panel, contract_last, preferred_element_type=jnp.float32)
    columns = ctr_index * m_dev + jnp.arange(m_dev, dtype=jnp.int32)
    padded = jnp.concatenate(
        [z1_full, jnp.zeros((outputs, m_dev - panel_size), jnp.float32)], axis=1
    )
    z_vector = jnp.where(columns[None, :] < panel_size, padded, direction - correction)
    z_bf16 = z_vector.astype(jnp.bfloat16)
    block_rows = min(512, npg)
    kernel_rows = lax.map(
        lambda point_rows: similarity(point_rows, centers).astype(jnp.bfloat16),
        points.reshape(npg // block_rows, block_rows, points.shape[1]),
    ).reshape(npg, m_dev)
    partial_value = lax.dot_general(
        z_bf16, kernel_rows, contract_last, preferred_element_type=jnp.float32
    )
    w_scale = 1.0 / (2.0 * math.sqrt(m_dev * n_ctr))
    image_scale = 1.0 / (2.0 * math.sqrt(npg * n_pts))
    owned_w = summed_on_arrival(partial_value, CTR, 1) * w_scale
    owned_bf16 = owned_w.astype(jnp.bfloat16)
    w_bf16 = gather_directly(owned_bf16, CTR, 1)
    center_terms = center_image(w_bf16, kernel_rows)
    operator_image = center_terms * image_scale + RIDGE_TERM * z_vector
    curvature, r_squares = in_one(
        (jnp.sum(z_vector * operator_image, axis=1), jnp.sum(residual * residual, axis=1)), CTR
    )
    new_residual = residual - (r_squares / curvature)[:, None] * operator_image
    return (panel_rows, operator_image, new_residual)


def solution(mesh):
    split = Mesh(
        mesh.devices.reshape(mesh.shape["pts"], 8, 2, 4), ("pts", "ctr_0", "ctr_1", "ctr_2")
    )
    placed = (P("pts", None), P(CTR, None), P("pts", None), P(None, CTR), P(None, CTR))
    return jax.shard_map(
        shards,
        mesh=split,
        in_specs=placed,
        out_specs=(P(CTR, "pts"), P(None, CTR), P(None, CTR)),
        check_vma=False,
    )
```

profile of v0, /device:TPU:1, one launch (start us, length us, event | category | flops | bytes accessed | tf_op | source)
XLA Modules:
  0.0 365.2 jit_solution(12828089693483969426)
XLA Ops:
  9.7 26.9 %psum.45 = bf16[32,512]{1,0:T(8,128)(2,1)S(1)} all-reduce(bf16[32,512]{1,0:T(8,128)(2,1)S(1)} %fusion.15), channel_id=1, replica_groups=mesh['pts'=4,'ctr_0'=8,'ctr_1'=2,'ctr_2'=4] {'ctr_0'}, use_global_device_ids=true, to_apply=%region_5.6 | all-reduce | flops 16384 | bytes 65536 | tf_op jit(solution)/shard_map/psum | solution.py:27
  36.6 6.7 %psum.46 = bf16[32,512]{1,0:T(8,128)(2,1)S(1)} all-reduce(bf16[32,512]{1,0:T(8,128)(2,1)S(1)} %psum.45), channel_id=1, replica_groups=mesh['pts'=4,'ctr_0'=8,'ctr_1'=2,'ctr_2'=4] {'ctr_1'}, use_global_device_ids=true, to_apply=%region_6.7 | all-reduce | flops 16384 | bytes 65536 | tf_op jit(solution)/shard_map/psum | solution.py:27
  43.3 13.5 %psum.47 = bf16[32,512]{1,0:T(8,128)(2,1)S(1)} all-reduce(bf16[32,512]{1,0:T(8,128)(2,1)S(1)} %psum.46), channel_id=1, replica_groups=mesh['pts'=4,'ctr_0'=8,'ctr_1'=2,'ctr_2'=4] {'ctr_2'}, use_global_device_ids=true, to_apply=%region_7.8 | all-reduce | flops 16384 | bytes 65536 | tf_op jit(solution)/shard_map/psum | solution.py:27
  58.3 16.8 %all-to-all-start = ((f32[4,1,32768]{2,1,0:T(1,128)}), f32[4,1,32768]{2,1,0:T(1,128)S(1)}, u32[]{:S(2)}, u32[]{:S(2)}) async-start(f32[4,1,32768]{2,1,0:T(1,128)} %broadcast_in_dim.47), calls=%async_computation | async-start | bytes 1048576 | tf_op jit(solution)/shard_map/all_to_all | solution.py:17
  75.1 7.1 %all-reduce.5.cloned.1.call-done = bf16[512,128]{1,0:T(8,128)(2,1)} async-done(((bf16[512,128]{1,0:T(8,128)(2,1)}), bf16[512,128]{1,0:T(8,128)(2,1)}) %all-reduce.5.cloned.1.call-update) | async-done | bytes 131088 | tf_op jit(solution)/shard_map/psum | solution.py:27
  82.2 96.1 %while.10 = (s32[]{:T(128)}, bf16[16,512,2048]{2,1,0:T(8,128)(2,1)}, bf16[16,512,128]{2,1,0:T(8,128)(2,1)}, bf16[2048,128]{1,0:T(8,128)(2,1)}, s32[]{:T(128)}) while((s32[]{:T(128)}, bf16[16,512,2048]{2,1,0:T(8,128)(2,1)}, bf16[16,512,128]{2,1,0:T(8,128)(2,1)}, bf16[2048,128]{1,0:T(8,128)(2,1)}, s32[]{:T(128)}) %tuple.34), condition=%wide.region_12.13_spmd, body=%wide.region_9.12_spmd.sunk | while | flops 275707392 | bytes 3429449 | solution.py:115
  84.7 3.6 fusion.35
  96.7 3.5 fusion.35
  102.7 3.6 fusion.35
  108.7 3.6 fusion.35
  120.7 3.6 fusion.35
  126.8 3.6 fusion.35
  132.8 3.6 fusion.35
  150.7 3.6 fusion.35
  156.7 3.6 fusion.35
  168.8 3.6 fusion.35
  179.8 46.7 %all-reduce.9.cloned.1.call-done = bf16[512,128]{1,0:T(8,128)(2,1)} async-done(((bf16[512,128]{1,0:T(8,128)(2,1)}), bf16[512,128]{1,0:T(8,128)(2,1)}) %all-reduce.9.cloned.1.call-update) | async-done | bytes 131088 | tf_op jit(solution)/shard_map/psum | solution.py:27
  230.9 15.4 %convolution_bitcast_fusion = f32[64,32,128]{2,1,0:T(8,128)S(1)} fusion(bf16[64,128,2048]{2,1,0:T(8,128)(2,1)} %bitcast.61, f32[32,2048]{1,0:T(8,128)S(1)} %fusion.9), kind=kOutput, calls=%fused_computation.16 | convolution fusion | flops 1073807360 | bytes 34865152 | tf_op jit(solution)/shard_map/dot_general | solution.py:119
  246.3 34.0 %all_to_all.27 = f32[64,32,128]{2,1,0:T(8,128)S(1)} all-to-all(f32[64,32,128]{2,1,0:T(8,128)S(1)} %convolution_bitcast_fusion), channel_id=1, replica_groups=mesh['pts'=4,'ctr_0'=8,'ctr_1'=2,'ctr_2'=4] {'ctr_0','ctr_1','ctr_2'}, dimensions={0} | all-to-all | bytes 2097152 | tf_op jit(solution)/shard_map/all_to_all | solution.py:47
  280.5 22.6 %all_to_all.28 = bf16[64,32,128]{2,1,0:T(8,128)(2,1)S(1)} all-to-all(bf16[64,32,128]{2,1,0:T(8,128)(2,1)S(1)} %broadcast_in_dim.49), channel_id=1, replica_groups=mesh['pts'=4,'ctr_0'=8,'ctr_1'=2,'ctr_2'=4] {'ctr_0','ctr_1','ctr_2'}, dimensions={0} | all-to-all | bytes 1048576 | tf_op jit(solution)/shard_map/all_to_all | solution.py:17
  303.1 13.5 %fusion.10 = f32[32,2048]{1,0:T(8,128)S(1)} fusion(bf16[8192,2048]{1,0:T(8,128)(2,1)} %bitcast.62, bf16[64,32,128]{2,1,0:T(8,128)(2,1)S(1)} %all_to_all.28), kind=kOutput, calls=%fused_computation.20 | convolution fusion | flops 1073741824 | bytes 34340864 | tf_op jit(solution)/shard_map/dot_general | solution.py:74
  316.7 24.0 %all_to_all.29 = f32[4,32,2048]{2,1,0:T(8,128)S(1)} all-to-all(f32[4,32,2048]{2,1,0:T(8,128)S(1)} %broadcast_in_dim.50), channel_id=1, replica_groups=mesh['pts'=4,'ctr_0'=8,'ctr_1'=2,'ctr_2'=4] {'pts'}, dimensions={0} | all-to-all | bytes 2097152 | tf_op jit(solution)/shard_map/all_to_all | solution.py:17
  343.4 5.1 %all-to-all-start.4 = ((f32[64,1,64]{2,1,0:T(1,128)}), f32[64,1,64]{2,1,0:T(1,128)S(1)}, u32[]{:S(2)}, u32[]{:S(2)}) async-start(f32[64,1,64]{2,1,0:T(1,128)} %broadcast_in_dim.51), calls=%async_computation.4 | async-start | bytes 65536 | tf_op jit(solution)/shard_map/all_to_all | solution.py:17
  350.0 7.7 %all-to-all-done.4 = f32[64,1,64]{2,1,0:T(1,128)S(1)} async-done(((f32[64,1,64]{2,1,0:T(1,128)}), f32[64,1,64]{2,1,0:T(1,128)S(1)}, u32[]{:S(2)}, u32[]{:S(2)}) %all-to-all-start.4) | async-done | bytes 16416 | tf_op jit(solution)/shard_map/all_to_all | solution.py:17
  (86 shorter events, 75.3 us)
Async XLA Ops:
  7.2 49.7 %copy-start = (bf16[128,512]{1,0:T(8,128)(2,1)S(1)}, bf16[128,512]{1,0:T(8,128)(2,1)}, u32[]{:S(2)}) copy-start(bf16[128,512]{1,0:T(8,128)(2,1)} %param.9) | copy-start | bytes 393220
  7.2 75.0 %all-reduce.5.cloned.1.call-start = ((), (), s32[]{:S(2)}) async-start(), calls=%async_computation.5 | async-start | bytes 262144 | tf_op jit(solution)/shard_map/psum | solution.py:27
  58.3 171.6 %all-to-all-start = ((f32[4,1,32768]{2,1,0:T(1,128)}), f32[4,1,32768]{2,1,0:T(1,128)S(1)}, u32[]{:S(2)}, u32[]{:S(2)}) async-start(f32[4,1,32768]{2,1,0:T(1,128)} %broadcast_in_dim.47), calls=%async_computation | async-start | bytes 1048576 | tf_op jit(solution)/shard_map/all_to_all | solution.py:17
  75.1 103.3 %all-reduce.7.cloned.1.call-start = ((), (), s32[]{:S(2)}) async-start(), calls=%async_computation.6 | async-start | bytes 262144 | tf_op jit(solution)/shard_map/psum | solution.py:27
  82.2 144.4 %all-reduce.9.cloned.1.call-start = ((), (), s32[]{:S(2)}) async-start(), calls=%async_computation.7 | async-start | bytes 262144 | tf_op jit(solution)/shard_map/psum | solution.py:27
  178.4 52.1 %copy-start.3 = (f32[32,2048]{1,0:T(8,128)S(1)}, f32[32,2048]{1,0:T(8,128)}, u32[]{:S(2)}) copy-start(f32[32,2048]{1,0:T(8,128)} %param.10) | copy-start | bytes 786436
  341.4 16.4 %copy-start.1 = (f32[32,2048]{1,0:T(8,128)S(1)}, f32[32,2048]{1,0:T(8,128)}, u32[]{:S(2)}) copy-start(f32[32,2048]{1,0:T(8,128)} %param.11) | copy-start | bytes 786436
  342.7 15.9 %copy-start.2 = (f32[32,2048]{1,0:T(8,128)}, f32[32,2048]{1,0:T(8,128)S(1)}, u32[]{:S(2)}) copy-start(f32[32,2048]{1,0:T(8,128)S(1)} %get-tuple-element.35) | copy-start | bytes 786436
  343.4 14.3 %all-to-all-start.4 = ((f32[64,1,64]{2,1,0:T(1,128)}), f32[64,1,64]{2,1,0:T(1,128)S(1)}, u32[]{:S(2)}, u32[]{:S(2)}) async-start(f32[64,1,64]{2,1,0:T(1,128)} %broadcast_in_dim.51), calls=%async_computation.4 | async-start | bytes 65536 | tf_op jit(solution)/shard_map/all_to_all | solution.py:17
Sparse Core Ops, SparseCore 0:
  10.9 71.2 all-reduce.4
  84.7 36.2 all-reduce.6
  178.5 48.0 all-reduce.8
where the time goes:
time: 367 us; the launch traced here: 365 us
  blocking collectives  128 us (35%)
  matrix products  90.3 us (25%)
  waiting for transfers between devices  61.6 us (17%)
  other arithmetic  47.4 us (13%)
  starting transfers between devices  21.9 us (6%)
  between operations  14 us (4%)
    dot_general x17, matrix products, similarity(): lax.dot_general(left, right, (((1,), (1,)), ((), ())), preferred_element_...  59.1 us
    psum x3, waiting for transfers between devices, from_root(): x = lax.psum(x, axis)  53.9 us
    psum x3, blocking collectives, from_root(): x = lax.psum(x, axis)  47.1 us
    all_to_all x2, blocking collectives, sent_to_all(): return lax.all_to_all(copies, axis, split_axis=0, concat_axis=0, tiled=True)  46.5 us
    all_to_all x1, blocking collectives, summed_on_arrival(): parts = lax.all_to_all(cut_along(x, dim, length), axis, 0, 0, tiled=True)  34 us
    reduce_sum x17, other arithmetic, similarity(): right_sq = jnp.sum(jnp.square(right.astype(jnp.float32)), axis=1)  23.2 us
    all_to_all x2, starting transfers between devices, sent_to_all(): return lax.all_to_all(copies, axis, split_axis=0, concat_axis=0, tiled=True)  21.9 us
    reduce_sum x17, other arithmetic, similarity(): left_sq = jnp.sum(jnp.square(left.astype(jnp.float32)), axis=1)  18.2 us
  transfers between devices with their start and end apart: 5, of which 3 were waited for; matrix products, arithmetic and copies ran while one was open for 29% of the time, Pallas kernels for 0%

commit v1 on v0

v1 whole, which is shorter than its diff:
```python
import functools
import math

import jax
import jax.numpy as jnp
from jax import lax
from jax.experimental import pallas as pl
from jax.experimental.pallas import tpu as pltpu
from jax.sharding import Mesh
from jax.sharding import PartitionSpec as P

CTR = ("ctr_0", "ctr_1", "ctr_2")
NEAR = ("ctr_1", "ctr_2")
FAR = "ctr_0"
RIDGE_TERM = 0.002

bf16, f32 = jnp.bfloat16, jnp.float32
LAST = (((1,), (1,)), ((), ()))
VMEM = pl.BlockSpec(memory_space=pltpu.VMEM)
SMEM = pl.BlockSpec(memory_space=pltpu.SMEM)
LIMIT = 12 << 20


def widened(x, side):
    xf = x.astype(f32)
    n = jnp.sum(xf * xf, axis=1, keepdims=True)
    high = n.astype(bf16).astype(f32)
    rest = n - high
    mid = rest.astype(bf16).astype(f32)
    low = rest - mid
    lane = lax.broadcasted_iota(jnp.int32, x.shape, 1)
    if side == 0:
        extra = jnp.where(lane < 6, 1.0, 0.0)
        extra = jnp.where(lane == 0, high, extra)
        extra = jnp.where(lane == 1, mid, extra)
        extra = jnp.where(lane == 2, low, extra)
        return jnp.concatenate([x, extra.astype(bf16)], axis=1)
    extra = jnp.where(lane < 3, -1.0, 0.0)
    extra = jnp.where(lane == 3, -high, extra)
    extra = jnp.where(lane == 4, -mid, extra)
    extra = jnp.where(lane == 5, -low, extra)
    return jnp.concatenate([(xf * 2.0).astype(bf16), extra.astype(bf16)], axis=1)


def similar(a, b, features):
    t = lax.dot_general(a, b, LAST, preferred_element_type=f32)
    return jnp.exp2(t * (math.log2(math.e) / (2 * features))).astype(bf16)


def block_kernel(tile, cols, left_ref, right_ref, out_ref, wide):
    features = left_ref.shape[1]
    wide[...] = widened(right_ref[...], 1)

    def step(i, carry):
        rows = pl.ds(pl.multiple_of(i * tile, tile), tile)
        left = widened(left_ref[rows], 0)
        for j in range(wide.shape[0] // cols):
            out_ref[rows, j * cols : (j + 1) * cols] = similar(
                left, wide[j * cols : (j + 1) * cols], features
            )
        return carry

    lax.fori_loop(0, left_ref.shape[0] // tile, step, 0)


def kernel_block(left, right, name, tile=1024, cols=256):
    rows, features = left.shape
    columns = right.shape[0]
    return pl.pallas_call(
        functools.partial(block_kernel, tile, cols),
        out_shape=jax.ShapeDtypeStruct((rows, columns), bf16),
        in_specs=[VMEM, VMEM],
        out_specs=VMEM,
        scratch_shapes=[pltpu.VMEM((columns, 2 * features), bf16)],
        compiler_params=pltpu.CompilerParams(vmem_limit_bytes=LIMIT),
        cost_estimate=pl.CostEstimate(
            flops=4 * rows * columns * features,
            bytes_accessed=2 * rows * columns,
            transcendentals=rows * columns,
        ),
        name=name,
    )(left, right)


def panel_kernel(flag_ref, centers_ref, head_ref, pinv_ref, dir_ref, z_ref, zz_ref, kp_ref):
    panel = pinv_ref.shape[0]
    outputs = dir_ref.shape[0]
    features = centers_ref.shape[1]
    vals = jnp.concatenate(
        [head_ref[pl.ds(panel + b * outputs, outputs)] for b in range(panel // features)], axis=1
    )
    z1 = lax.dot_general(vals, pinv_ref[...], LAST, preferred_element_type=f32).astype(bf16)
    q = jnp.dot(z1, pinv_ref[...], preferred_element_type=f32).astype(bf16)
    heads = widened(head_ref[:panel], 1)
    tile = panel
    for i in range(centers_ref.shape[0] // tile):
        rows = slice(i * tile, (i + 1) * tile)
        kp = similar(widened(centers_ref[rows], 0), heads, features)
        kp_ref[rows] = kp
        z = dir_ref[:, rows] - lax.dot_general(q, kp, LAST, preferred_element_type=f32)
        if i == 0:
            z = jnp.where(flag_ref[0] == 0, z1.astype(f32), z)
        z_ref[:, rows] = z
        high = z.astype(bf16)
        zz_ref[:outputs, rows] = high
        zz_ref[outputs:, rows] = (z - high.astype(f32)).astype(bf16)


def panel_step(flag, centers, head, pinv, direction):
    outputs, m_dev = direction.shape
    panel = pinv.shape[0]
    return pl.pallas_call(
        panel_kernel,
        out_shape=(
            jax.ShapeDtypeStruct((outputs, m_dev), f32),
            jax.ShapeDtypeStruct((2 * outputs, m_dev), bf16),
            jax.ShapeDtypeStruct((m_dev, panel), bf16),
        ),
        in_specs=[SMEM, VMEM, VMEM, VMEM, VMEM],
        out_specs=(VMEM, VMEM, VMEM),
        compiler_params=pltpu.CompilerParams(vmem_limit_bytes=LIMIT),
        cost_estimate=pl.CostEstimate(
            flops=6 * m_dev * panel * 128, bytes_accessed=4 << 20, transcendentals=m_dev * panel
        ),
        name="panel",
    )(flag, centers, head, pinv, direction)


def values_kernel(tile, zz_ref, *refs):
    blocks, (high_ref, both_ref) = refs[:-2], refs[-2:]
    outputs = high_ref.shape[1]
    done = 0
    for k_ref in blocks:
        for i in range(k_ref.shape[1] // tile):
            u = jnp.dot(zz_ref[...], k_ref[:, i * tile : (i + 1) * tile], preferred_element_type=f32)
            for b in range(tile // 128):
                part = u[:, b * 128 : (b + 1) * 128]
                high_ref[done] = part[:outputs]
                both_ref[done] = part[:outputs] + part[outputs:]
                done += 1


def values(zz, blocks, tile=512):
    outputs = zz.shape[0] // 2
    count = sum(k.shape[1] for k in blocks) // 128
    shape = jax.ShapeDtypeStruct((count, outputs, 128), f32)
    return pl.pallas_call(
        functools.partial(values_kernel, tile),
        out_shape=(shape, shape),
        in_specs=[VMEM] * (1 + len(blocks)),
        out_specs=(VMEM, VMEM),
        compiler_params=pltpu.CompilerParams(vmem_limit_bytes=LIMIT),
        cost_estimate=pl.CostEstimate(
            flops=2 * 256 * zz.shape[1] * count * 128,
            bytes_accessed=2 * zz.shape[1] * count * 128,
            transcendentals=0,
        ),
        name="values",
    )(zz, *blocks)


def image_kernel(tile, core_ref, w_ref, *refs):
    blocks, (keep_ref, send_ref, total) = refs[:-3], refs[-3:]
    per = tile // 128
    total[...] = jnp.zeros_like(total)
    done = 0
    for k_ref in blocks:

        def step(i, carry, k_ref=k_ref, done=done):
            w = jnp.concatenate([w_ref[done + i * per + b] for b in range(per)], axis=1)
            rows = pl.ds(pl.multiple_of(i * tile, tile), tile)
            total[...] += jnp.dot(w, k_ref[rows], preferred_element_type=f32)
            return carry

        lax.fori_loop(0, k_ref.shape[0] // tile, step, 0)
        done += k_ref.shape[0] // 128
    half = keep_ref.shape[0]
    mine = pl.multiple_of(core_ref[0] * half, half)
    keep_ref[...] = total[pl.ds(mine, half)]
    send_ref[...] = total[pl.ds(half - mine, half)]


def image(core, w, blocks, tile=1024):
    outputs = w.shape[1]
    m_dev = blocks[0].shape[1]
    points = sum(k.shape[0] for k in blocks)
    shape = jax.ShapeDtypeStruct((outputs // 2, m_dev), f32)
    return pl.pallas_call(
        functools.partial(image_kernel, tile),
        out_shape=(shape, shape),
        in_specs=[SMEM] + [VMEM] * (1 + len(blocks)),
        out_specs=(VMEM, VMEM),
        scratch_shapes=[pltpu.VMEM((outputs, m_dev), f32)],
        compiler_params=pltpu.CompilerParams(vmem_limit_bytes=LIMIT),
        cost_estimate=pl.CostEstimate(
            flops=2 * 256 * points * m_dev, bytes_accessed=2 * points * m_dev, transcendentals=0
        ),
        name="image",
    )(core, w, *blocks)


def exchange(x, axis):
    return lax.all_to_all(x, axis, 0, 0, tiled=True)


def copies(x, axis):
    n = lax.axis_size(axis)
    return exchange(jnp.broadcast_to(x[None], (n, *x.shape)), axis)


def swap(x, bit):
    n = lax.axis_size("pts")
    return lax.ppermute(x, "pts", [(i, i ^ bit) for i in range(n)])


def joined(first, mine, other):
    return jnp.where(
        first, jnp.concatenate([mine, other], axis=0), jnp.concatenate([other, mine], axis=0)
    )


def shards(points, centers, panel_inverse, direction, residual):
    n_ctr = lax.axis_size(CTR)
    n_near = lax.axis_size(NEAR)
    n_far = lax.axis_size(FAR)
    n_pts = lax.axis_size("pts")
    ctr_index = lax.axis_index(CTR)
    pts_index = lax.axis_index("pts")
    core = pts_index & 1
    m_dev, features = centers.shape
    npg = points.shape[0]
    panel = panel_inverse.shape[1]
    outputs = direction.shape[0]
    w_scale = 1.0 / (2.0 * math.sqrt(m_dev * n_ctr))
    image_scale = 1.0 / (2.0 * math.sqrt(npg * n_pts))

    vals = direction[:, :panel].astype(bf16)
    vals = jnp.moveaxis(vals.reshape(outputs, panel // features, features), 1, 0)
    head = jnp.concatenate([centers[:panel], vals.reshape(-1, features)], axis=0)
    piece = exchange(head.reshape(n_near, -1, features), NEAR)[0]
    piece = copies(piece, FAR)[0]
    head = copies(piece, NEAR).reshape(-1, features)

    pair = joined(core == 0, panel_inverse, swap(panel_inverse, 1))
    pinv = joined(pts_index < 2, pair, swap(pair, 2))

    halves = [points[: npg // 2], points[npg // 2 :]]
    by_center = [kernel_block(centers, h, f"by_center_{i}") for i, h in enumerate(halves)]

    z, zz, k_panel = panel_step(ctr_index.reshape(1), centers, head, pinv, direction)
    high, both = values(zz, by_center)

    parts = exchange(high.reshape(n_near, n_far * outputs, 128), NEAR)
    parts = jnp.sum(parts, axis=0)
    parts = exchange(parts.reshape(n_far, outputs, 128), FAR)
    owned = (jnp.sum(parts, axis=0) * w_scale).astype(bf16)
    w = copies(owned, FAR)
    w = copies(w.reshape(n_far * outputs, 128), NEAR).reshape(-1, outputs, 128)

    by_point = [kernel_block(h, centers, f"by_point_{i}") for i, h in enumerate(halves)]
    panel_rows = lax.dot_general(
        k_panel, panel_inverse, LAST, preferred_element_type=f32
    ).astype(bf16)

    mine = jnp.sum(w.astype(f32) * both, axis=(0, 2)) * image_scale
    mine = mine + (RIDGE_TERM / n_pts) * jnp.sum(z * z, axis=1)
    squares = jnp.sum(residual * residual, axis=1) * (1.0 / n_pts)
    scalars = jnp.concatenate([mine, squares])[None]
    scalars = scalars + swap(scalars, 1)
    scalars = scalars + swap(scalars, 2)
    scalars = jnp.sum(copies(scalars, CTR), axis=(0, 1))
    curvature, r_squares = scalars[:outputs], scalars[outputs:]

    keep, send = image(core.reshape(1), w, by_point)
    keep = keep + swap(send, 1)
    keep = keep + swap(keep, 2)
    total = joined(core == 0, keep, swap(keep, 1))
    operator_image = total * image_scale + RIDGE_TERM * z
    new_residual = residual - (r_squares / curvature)[:, None] * operator_image
    return (panel_rows, operator_image, new_residual)


def solution(mesh):
    split = Mesh(
        mesh.devices.reshape(mesh.shape["pts"], 8, 2, 4), ("pts", "ctr_0", "ctr_1", "ctr_2")
    )
    placed = (P("pts", None), P(CTR, None), P("pts", None), P(None, CTR), P(None, CTR))
    return jax.shard_map(
        shards,
        mesh=split,
        in_specs=placed,
        out_specs=(P(CTR, "pts"), P(None, CTR), P(None, CTR)),
        check_vma=False,
    )
```

time: 367 us -> 183 us (0.50)
  blocking collectives: 128 us -> 16.6 us
  matrix products: 90.3 us -> 1.5 us
  other arithmetic: 47.4 us -> 6.88 us
  waiting for transfers between devices: 61.6 us -> 22.8 us
  local copies, waits for them, and re-layouts: 2.03 us -> 40.6 us
  Pallas kernels: 0 us -> 38.1 us
  starting transfers between devices: 21.9 us -> 54.6 us
  between operations: 14 us -> 0.92 us
    dot_general x23 -> x1, matrix products: 90.3 us -> 1.5 us  [shards(): lax.dot_general(k_panel, panel_inverse, LAST, preferred_element_type=f32)]
    all_to_all x3 -> x1, blocking collectives: 80.5 us -> 16.6 us  [exchange(): return lax.all_to_all(x, axis, 0, 0, tiled=True)]
    psum x3 -> x0, waiting for transfers between devices: 53.9 us -> none  [from_root(): x = lax.psum(x, axis)]
    psum x3 -> x0, blocking collectives: 47.1 us -> none  [from_root(): x = lax.psum(x, axis)]
    reduce_sum x39 -> x6, other arithmetic: 44.1 us -> 3.7 us  [the longest x1 1.94 us: shards(): parts = jnp.sum(parts, axis=0)]
    pallas_call x0 -> x7, Pallas kernels: none -> 38.1 us  [the longest x4 23.6 us: kernel_block(): pl.pallas_call(functools.partial(block_kernel, tile, cols), out_shape=jax...]
    unnamed x10 -> x34, local copies, waits for them, and re-layouts: 0.09 us -> 33.6 us
    ppermute x0 -> x7, starting transfers between devices: none -> 17.7 us  [swap(): return lax.ppermute(x, 'pts', [(i, i ^ bit) for i in range(n)])]
  transfers between devices with their start and end apart: 5 -> 14, of which waited for: 3 -> 5; matrix products, arithmetic and copies ran while one was open for 29% -> 4% of each run, Pallas kernels for 0% -> 17%
where the time goes in v1:
time: 183 us; the launch traced here: 182 us
  starting transfers between devices  54.6 us (30%)
  local copies, waits for them, and re-layouts  40.6 us (22%)
  Pallas kernels  38.1 us (21%)
  waiting for transfers between devices  22.8 us (12%)
  blocking collectives  16.6 us (9%)
  other arithmetic  6.88 us (4%)
    all_to_all x7, starting transfers between devices, exchange(): return lax.all_to_all(x, axis, 0, 0, tiled=True)  36.9 us
    unnamed x34, local copies, waits for them, and re-layouts  33.6 us
    pallas_call x4, Pallas kernels, kernel_block(): pl.pallas_call(functools.partial(block_kernel, tile, cols), out_shape=jax...  23.6 us
    all_to_all x7, waiting for transfers between devices, exchange(): return lax.all_to_all(x, axis, 0, 0, tiled=True)  21.9 us
    ppermute x7, starting transfers between devices, swap(): return lax.ppermute(x, 'pts', [(i, i ^ bit) for i in range(n)])  17.7 us
    all_to_all x1, blocking collectives, exchange(): return lax.all_to_all(x, axis, 0, 0, tiled=True)  16.6 us
    pallas_call x1, Pallas kernels, image(): pl.pallas_call(functools.partial(image_kernel, tile), out_shape=(shape, s...  6.66 us
    pallas_call x1, Pallas kernels, values(): pl.pallas_call(functools.partial(values_kernel, tile), out_shape=(shape,...  5.95 us
  transfers between devices with their start and end apart: 14, of which 5 were waited for; matrix products, arithmetic and copies ran while one was open for 4% of the time, Pallas kernels for 17%

profile of v1, /device:TPU:1, one launch (start us, length us, event | category | flops | bytes accessed | tf_op | source)
XLA Modules:
  0.0 181.9 jit_solution(15861244791450038195)
XLA Ops:
  3.1 5.9 %all-to-all-start = ((bf16[8,80,128]{2,1,0:T(8,128)(2,1)}), bf16[8,80,128]{2,1,0:T(8,128)(2,1)S(1)}, u32[]{:S(2)}, u32[]{:S(2)}) async-start(bf16[8,80,128]{2,1,0:T(8,128)(2,1)} %bitcast.3), calls=%async_computation | async-start | bytes 327680 | tf_op jit(solution)/shard_map/all_to_all | solution.py:203
  15.4 8.2 %all-to-all-start.1 = ((bf16[8,80,128]{2,1,0:T(8,128)(2,1)}), bf16[8,80,128]{2,1,0:T(8,128)(2,1)S(1)}, u32[]{:S(2)}, u32[]{:S(2)}) async-start(bf16[8,80,128]{2,1,0:T(8,128)(2,1)} %broadcast_in_dim.40), calls=%async_computation.1 | async-start | bytes 327680 | tf_op jit(solution)/shard_map/all_to_all | solution.py:203
  23.6 5.9 %by_center_0.1.refs_0_ = bf16[2048,4096]{1,0:T(8,128)(2,1)S(1)} custom-call(bf16[2048,128]{1,0:T(8,128)(2,1)S(1)} %copy-done.6, bf16[4096,128]{1,0:T(8,128)(2,1)S(1)} %get-tuple-element.20.right_ref.left_ref), custom_call_target="tpu_custom_call" | custom-call | flops 4294967296 | bytes 16777216 | tf_op jit(solution)/shard_map/by_center_0/pallas_call | solution.py:69
  29.5 5.7 %copy-done = bf16[2048,4096]{1,0:T(8,128)(2,1)} copy-done((bf16[2048,4096]{1,0:T(8,128)(2,1)}, bf16[2048,4096]{1,0:T(8,128)(2,1)S(1)}, u32[]{:S(2)}) %copy-start) | copy-done | bytes 16777240
  38.6 3.6 %all-to-all-start.2 = ((bf16[8,80,128]{2,1,0:T(8,128)(2,1)}), bf16[8,80,128]{2,1,0:T(8,128)(2,1)S(1)}, u32[]{:S(2)}, u32[]{:S(2)}) async-start(bf16[8,80,128]{2,1,0:T(8,128)(2,1)} %broadcast_in_dim.42), calls=%async_computation.2 | async-start | bytes 327680 | tf_op jit(solution)/shard_map/all_to_all | solution.py:203
  42.1 5.9 %by_center_1.1.refs_1_ = bf16[2048,4096]{1,0:T(8,128)(2,1)S(1)} custom-call(bf16[2048,128]{1,0:T(8,128)(2,1)S(1)} %copy-done.6, bf16[4096,128]{1,0:T(8,128)(2,1)S(1)} %get-tuple-element.19.right_ref.left_ref), custom_call_target="tpu_custom_call" | custom-call | flops 4294967296 | bytes 16777216 | tf_op jit(solution)/shard_map/by_center_1/pallas_call | solution.py:69
  48.1 5.7 %copy-done.2 = bf16[2048,4096]{1,0:T(8,128)(2,1)} copy-done((bf16[2048,4096]{1,0:T(8,128)(2,1)}, bf16[2048,4096]{1,0:T(8,128)(2,1)S(1)}, u32[]{:S(2)}) %copy-start.2) | copy-done | bytes 16777240
  61.0 5.8 %copy-done.1 = bf16[2048,4096]{1,0:T(8,128)(2,1)S(1)} copy-done((bf16[2048,4096]{1,0:T(8,128)(2,1)S(1)}, bf16[2048,4096]{1,0:T(8,128)(2,1)}, u32[]{:S(2)}) %copy-start.1) | copy-done | bytes 16777240
  66.7 5.8 %copy-done.3 = bf16[2048,4096]{1,0:T(8,128)(2,1)S(1)} copy-done((bf16[2048,4096]{1,0:T(8,128)(2,1)S(1)}, bf16[2048,4096]{1,0:T(8,128)(2,1)}, u32[]{:S(2)}) %copy-start.3) | copy-done | bytes 16777240
  72.5 5.9 %values.1 = (f32[64,32,128]{2,1,0:T(8,128)S(1)}, f32[64,32,128]{2,1,0:T(8,128)S(1)}) custom-call(bf16[64,2048]{1,0:T(8,128)(2,1)S(1)} %get-tuple-element.11.zz_ref, bf16[2048,4096]{1,0:T(8,128)(2,1)S(1)} %copy-done.1, bf16[2048,4096]{1,0:T(8,128)(2,1)S(1)} %copy-done.3), custom_call_target="tpu_custom_call" | custom-call | flops 8589934592 | bytes 33554432 | tf_op jit(solution)/shard_map/values/pallas_call | solution.py:147
  79.4 16.6 %all_to_all.40 = f32[8,256,128]{2,1,0:T(8,128)} all-to-all(f32[8,256,128]{2,1,0:T(8,128)S(1)} %bitcast.25), channel_id=1, replica_groups=mesh['pts'=4,'ctr_0'=8,'ctr_1'=2,'ctr_2'=4] {'ctr_1','ctr_2'}, dimensions={0} | all-to-all | bytes 2097152 | tf_op jit(solution)/shard_map/all_to_all | solution.py:203
  97.9 6.6 %all-to-all-start.4 = ((f32[8,32,128]{2,1,0:T(8,128)}), f32[8,32,128]{2,1,0:T(8,128)S(1)}, u32[]{:S(2)}, u32[]{:S(2)}) async-start(f32[8,32,128]{2,1,0:T(8,128)} %bitcast.9), calls=%async_computation.4 | async-start | bytes 262144 | tf_op jit(solution)/shard_map/all_to_all | solution.py:203
  104.7 7.8 %all-to-all-done.4 = f32[8,32,128]{2,1,0:T(8,128)S(1)} async-done(((f32[8,32,128]{2,1,0:T(8,128)}), f32[8,32,128]{2,1,0:T(8,128)S(1)}, u32[]{:S(2)}, u32[]{:S(2)}) %all-to-all-start.4) | async-done | bytes 131104 | tf_op jit(solution)/shard_map/all_to_all | solution.py:203
  113.1 3.4 %all-to-all-start.5 = ((bf16[8,32,128]{2,1,0:T(8,128)(2,1)}), bf16[8,32,128]{2,1,0:T(8,128)(2,1)S(1)}, u32[]{:S(2)}, u32[]{:S(2)}) async-start(bf16[8,32,128]{2,1,0:T(8,128)(2,1)} %broadcast_in_dim.43), calls=%async_computation.5 | async-start | bytes 131072 | tf_op jit(solution)/shard_map/all_to_all | solution.py:203
  116.5 7.1 %all-to-all-done.5 = bf16[8,32,128]{2,1,0:T(8,128)(2,1)S(1)} async-done(((bf16[8,32,128]{2,1,0:T(8,128)(2,1)}), bf16[8,32,128]{2,1,0:T(8,128)(2,1)S(1)}, u32[]{:S(2)}, u32[]{:S(2)}) %all-to-all-start.5) | async-done | bytes 65568 | tf_op jit(solution)/shard_map/all_to_all | solution.py:203
  124.5 3.7 %all-to-all-start.6 = ((bf16[8,256,128]{2,1,0:T(8,128)(2,1)}), bf16[8,256,128]{2,1,0:T(8,128)(2,1)S(1)}, u32[]{:S(2)}, u32[]{:S(2)}) async-start(bf16[8,256,128]{2,1,0:T(8,128)(2,1)} %broadcast_in_dim.45), calls=%async_computation.6 | async-start | bytes 1048576 | tf_op jit(solution)/shard_map/all_to_all | solution.py:203
  128.2 5.9 %by_point_0.1.refs_0_ = bf16[4096,2048]{1,0:T(8,128)(2,1)S(1)} custom-call(bf16[4096,128]{1,0:T(8,128)(2,1)S(1)} %get-tuple-element.20.right_ref.left_ref, bf16[2048,128]{1,0:T(8,128)(2,1)S(1)} %copy-done.6), custom_call_target="tpu_custom_call" | custom-call | flops 4294967296 | bytes 16777216 | tf_op jit(solution)/shard_map/by_point_0/pallas_call | solution.py:69
  134.1 5.7 %copy-done.4 = bf16[4096,2048]{1,0:T(8,128)(2,1)} copy-done((bf16[4096,2048]{1,0:T(8,128)(2,1)}, bf16[4096,2048]{1,0:T(8,128)(2,1)S(1)}, u32[]{:S(2)}) %copy-start.4) | copy-done | bytes 16777240
  141.5 7.6 %collective-permute-start.5 = (f32[1,64]{1,0:T(1,128)S(1)}, f32[1,64]{1,0:T(1,128)S(1)}, u32[]{:S(2)}, u32[]{:S(2)}) collective-permute-start(f32[1,64]{1,0:T(1,128)S(1)} %maximum_bitcast_fusion), channel_id=1, source_target_pairs={{0,64},{64,0},{128,192},{192,128},{1,65},{65,1},{129,193},{193,129... | collective-permute-start | bytes 776 | tf_op jit(solution)/shard_map/ppermute | solution.py:213
  149.1 5.9 %by_point_1.1.refs_1_ = bf16[4096,2048]{1,0:T(8,128)(2,1)S(1)} custom-call(bf16[4096,128]{1,0:T(8,128)(2,1)S(1)} %get-tuple-element.19.right_ref.left_ref, bf16[2048,128]{1,0:T(8,128)(2,1)S(1)} %copy-done.6), custom_call_target="tpu_custom_call" | custom-call | flops 4294967296 | bytes 16777216 | tf_op jit(solution)/shard_map/by_point_1/pallas_call | solution.py:69
  155.7 6.7 %image.1 = (f32[16,2048]{1,0:T(8,128)S(1)}, f32[16,2048]{1,0:T(8,128)S(1)}) custom-call(s32[1]{0:T(128)} %bitcast.7.core_ref, bf16[64,32,128]{2,1,0:T(8,128)(2,1)S(1)} %bitcast.24, bf16[4096,2048]{1,0:T(8,128)(2,1)S(1)} %copy-done.5, bf16[4096,2048]{1,0:T(8,128)(2,1)S(1)} %by_point_1.1.refs_1_), custom_call_target="tpu_custom_call" | custom-call | flops 8589934592 | bytes 33554432 | tf_op jit(solution)/shard_map/image/pallas_call | solution.py:188
  163.4 5.5 %all-to-all-start.7 = ((f32[64,1,64]{2,1,0:T(1,128)}), f32[64,1,64]{2,1,0:T(1,128)S(1)}, u32[]{:S(2)}, u32[]{:S(2)}) async-start(f32[64,1,64]{2,1,0:T(1,128)} %broadcast_in_dim.48), calls=%async_computation.7 | async-start | bytes 65536 | tf_op jit(solution)/shard_map/all_to_all | solution.py:203
  169.0 3.7 %collective-permute-start.3 = (f32[16,2048]{1,0:T(8,128)S(1)}, f32[16,2048]{1,0:T(8,128)S(1)}, u32[]{:S(2)}, u32[]{:S(2)}) collective-permute-start(f32[16,2048]{1,0:T(8,128)S(1)} %add.26), channel_id=1, source_target_pairs={{0,128},{64,192},{128,0},{192,64},{1,129},{65,193},{129,1},{193,65... | collective-permute-start | bytes 393224 | tf_op jit(solution)/shard_map/ppermute | solution.py:213
  174.2 4.0 %all-to-all-done.7 = f32[64,1,64]{2,1,0:T(1,128)S(1)} async-done(((f32[64,1,64]{2,1,0:T(1,128)}), f32[64,1,64]{2,1,0:T(1,128)S(1)}, u32[]{:S(2)}, u32[]{:S(2)}) %all-to-all-start.7) | async-done | bytes 16416 | tf_op jit(solution)/shard_map/all_to_all | solution.py:203
  (78 shorter events, 32.4 us)
Async XLA Ops:
  3.1 11.6 %all-to-all-start = ((bf16[8,80,128]{2,1,0:T(8,128)(2,1)}), bf16[8,80,128]{2,1,0:T(8,128)(2,1)S(1)}, u32[]{:S(2)}, u32[]{:S(2)}) async-start(bf16[8,80,128]{2,1,0:T(8,128)(2,1)} %bitcast.3), calls=%async_computation | async-start | bytes 327680 | tf_op jit(solution)/shard_map/all_to_all | solution.py:203
  9.0 14.5 %copy-start.6 = (bf16[2048,128]{1,0:T(8,128)(2,1)S(1)}, bf16[2048,128]{1,0:T(8,128)(2,1)}, u32[]{:S(2)}) copy-start(bf16[2048,128]{1,0:T(8,128)(2,1)} %right_ref.3) | copy-start | bytes 1572868
  9.1 26.2 %collective-permute-start = (bf16[128,512]{1,0:T(8,128)(2,1)}, bf16[128,512]{1,0:T(8,128)(2,1)S(1)}, u32[]{:S(2)}, u32[]{:S(2)}) collective-permute-start(bf16[128,512]{1,0:T(8,128)(2,1)} %param.7), channel_id=1, source_target_pairs={{0,64},{64,0},{128,192},{192,128},{1,65},{65,1},{129,193},{193,129... | collective-permute-start | bytes 393224 | tf_op jit(solution)/shard_map/ppermute | solution.py:213
  15.4 22.5 %all-to-all-start.1 = ((bf16[8,80,128]{2,1,0:T(8,128)(2,1)}), bf16[8,80,128]{2,1,0:T(8,128)(2,1)S(1)}, u32[]{:S(2)}, u32[]{:S(2)}) async-start(bf16[8,80,128]{2,1,0:T(8,128)(2,1)} %broadcast_in_dim.40), calls=%async_computation.1 | async-start | bytes 327680 | tf_op jit(solution)/shard_map/all_to_all | solution.py:203
  23.6 11.7 %copy-start.16 = (bf16[128,512]{1,0:T(8,128)(2,1)S(1)}, bf16[128,512]{1,0:T(8,128)(2,1)}, u32[]{:S(2)}) copy-start(bf16[128,512]{1,0:T(8,128)(2,1)} %param.7) | copy-start | bytes 393220
  35.3 12.8 %copy-start.13 = (bf16[256,512]{1,0:T(8,128)(2,1)}, bf16[256,512]{1,0:T(8,128)(2,1)S(1)}, u32[]{:S(2)}) copy-start(bf16[256,512]{1,0:T(8,128)(2,1)S(1)} %maximum_select_fusion.1) | copy-start | bytes 786436
  35.3 18.5 %collective-permute-start.1 = (bf16[256,512]{1,0:T(8,128)(2,1)S(1)}, bf16[256,512]{1,0:T(8,128)(2,1)}, u32[]{:S(2)}, u32[]{:S(2)}) collective-permute-start(bf16[256,512]{1,0:T(8,128)(2,1)S(1)} %maximum_select_fusion.1), channel_id=1, source_target_pairs={{0,128},{64,192},{128,0},{192,64},{1,129},{65,193},{129,1},{193,65... | collective-permute-start | bytes 786440 | tf_op jit(solution)/shard_map/ppermute | solution.py:213
  38.6 16.6 %all-to-all-start.2 = ((bf16[8,80,128]{2,1,0:T(8,128)(2,1)}), bf16[8,80,128]{2,1,0:T(8,128)(2,1)S(1)}, u32[]{:S(2)}, u32[]{:S(2)}) async-start(bf16[8,80,128]{2,1,0:T(8,128)(2,1)} %broadcast_in_dim.42), calls=%async_computation.2 | async-start | bytes 327680 | tf_op jit(solution)/shard_map/all_to_all | solution.py:203
  48.1 5.7 %copy-start.2 = (bf16[2048,4096]{1,0:T(8,128)(2,1)}, bf16[2048,4096]{1,0:T(8,128)(2,1)S(1)}, u32[]{:S(2)}) copy-start(bf16[2048,4096]{1,0:T(8,128)(2,1)S(1)} %by_center_1.1.refs_1_) | copy-start | bytes 50331652
  60.9 5.8 %copy-start.1 = (bf16[2048,4096]{1,0:T(8,128)(2,1)S(1)}, bf16[2048,4096]{1,0:T(8,128)(2,1)}, u32[]{:S(2)}) copy-start(bf16[2048,4096]{1,0:T(8,128)(2,1)} %copy-done) | copy-start | bytes 50331652
  66.7 5.8 %copy-start.3 = (bf16[2048,4096]{1,0:T(8,128)(2,1)S(1)}, bf16[2048,4096]{1,0:T(8,128)(2,1)}, u32[]{:S(2)}) copy-start(bf16[2048,4096]{1,0:T(8,128)(2,1)} %copy-done.2) | copy-start | bytes 50331652
  79.4 25.1 %copy-start.14 = (f32[32,2048]{1,0:T(8,128)S(1)}, f32[32,2048]{1,0:T(8,128)}, u32[]{:S(2)}) copy-start(f32[32,2048]{1,0:T(8,128)} %param.9) | copy-start | bytes 786436
  97.9 14.5 %all-to-all-start.4 = ((f32[8,32,128]{2,1,0:T(8,128)}), f32[8,32,128]{2,1,0:T(8,128)S(1)}, u32[]{:S(2)}, u32[]{:S(2)}) async-start(f32[8,32,128]{2,1,0:T(8,128)} %bitcast.9), calls=%async_computation.4 | async-start | bytes 262144 | tf_op jit(solution)/shard_map/all_to_all | solution.py:203
  113.1 10.5 %all-to-all-start.5 = ((bf16[8,32,128]{2,1,0:T(8,128)(2,1)}), bf16[8,32,128]{2,1,0:T(8,128)(2,1)S(1)}, u32[]{:S(2)}, u32[]{:S(2)}) async-start(bf16[8,32,128]{2,1,0:T(8,128)(2,1)} %broadcast_in_dim.43), calls=%async_computation.5 | async-start | bytes 131072 | tf_op jit(solution)/shard_map/all_to_all | solution.py:203
  124.5 15.5 %all-to-all-start.6 = ((bf16[8,256,128]{2,1,0:T(8,128)(2,1)}), bf16[8,256,128]{2,1,0:T(8,128)(2,1)S(1)}, u32[]{:S(2)}, u32[]{:S(2)}) async-start(bf16[8,256,128]{2,1,0:T(8,128)(2,1)} %broadcast_in_dim.45), calls=%async_computation.6 | async-start | bytes 1048576 | tf_op jit(solution)/shard_map/all_to_all | solution.py:203
  141.5 13.5 %collective-permute-start.5 = (f32[1,64]{1,0:T(1,128)S(1)}, f32[1,64]{1,0:T(1,128)S(1)}, u32[]{:S(2)}, u32[]{:S(2)}) collective-permute-start(f32[1,64]{1,0:T(1,128)S(1)} %maximum_bitcast_fusion), channel_id=1, source_target_pairs={{0,64},{64,0},{128,192},{192,128},{1,65},{65,1},{129,193},{193,129... | collective-permute-start | bytes 776 | tf_op jit(solution)/shard_map/ppermute | solution.py:213
  149.1 6.6 %copy-start.5 = (bf16[4096,2048]{1,0:T(8,128)(2,1)S(1)}, bf16[4096,2048]{1,0:T(8,128)(2,1)}, u32[]{:S(2)}) copy-start(bf16[4096,2048]{1,0:T(8,128)(2,1)} %copy-done.4) | copy-start | bytes 50331652
  155.1 7.7 %collective-permute-start.6 = (f32[1,64]{1,0:T(1,128)S(1)}, f32[1,64]{1,0:T(1,128)S(1)}, u32[]{:S(2)}, u32[]{:S(2)}) collective-permute-start(f32[1,64]{1,0:T(1,128)S(1)} %fusion.6), channel_id=1, source_target_pairs={{0,128},{64,192},{128,0},{192,64},{1,129},{65,193},{129,1},{193,65... | collective-permute-start | bytes 776 | tf_op jit(solution)/shard_map/ppermute | solution.py:213
  155.7 17.0 %copy-start.8 = (bf16[2048,512]{1,0:T(8,128)(2,1)S(1)}, bf16[2048,512]{1,0:T(8,128)(2,1)}, u32[]{:S(2)}) copy-start(bf16[2048,512]{1,0:T(8,128)(2,1)} %copy-done.7) | copy-start | bytes 6291460
  162.4 18.7 %copy-start.15 = (f32[32,2048]{1,0:T(8,128)S(1)}, f32[32,2048]{1,0:T(8,128)}, u32[]{:S(2)}) copy-start(f32[32,2048]{1,0:T(8,128)} %param.9) | copy-start | bytes 786436
  162.4 6.6 %collective-permute-start.2 = (f32[16,2048]{1,0:T(8,128)S(1)}, f32[16,2048]{1,0:T(8,128)S(1)}, u32[]{:S(2)}, u32[]{:S(2)}) collective-permute-start(f32[16,2048]{1,0:T(8,128)S(1)} %get-tuple-element.14), channel_id=1, source_target_pairs={{0,64},{64,0},{128,192},{192,128},{1,65},{65,1},{129,193},{193,129... | collective-permute-start | bytes 393224 | tf_op jit(solution)/shard_map/ppermute | solution.py:213
  163.4 14.8 %all-to-all-start.7 = ((f32[64,1,64]{2,1,0:T(1,128)}), f32[64,1,64]{2,1,0:T(1,128)S(1)}, u32[]{:S(2)}, u32[]{:S(2)}) async-start(f32[64,1,64]{2,1,0:T(1,128)} %broadcast_in_dim.48), calls=%async_computation.7 | async-start | bytes 65536 | tf_op jit(solution)/shard_map/all_to_all | solution.py:203
  169.0 9.2 %collective-permute-start.3 = (f32[16,2048]{1,0:T(8,128)S(1)}, f32[16,2048]{1,0:T(8,128)S(1)}, u32[]{:S(2)}, u32[]{:S(2)}) collective-permute-start(f32[16,2048]{1,0:T(8,128)S(1)} %add.26), channel_id=1, source_target_pairs={{0,128},{64,192},{128,0},{192,64},{1,129},{65,193},{129,1},{193,65... | collective-permute-start | bytes 393224 | tf_op jit(solution)/shard_map/ppermute | solution.py:213
  178.3 2.8 %collective-permute-start.4 = (f32[16,2048]{1,0:T(8,128)S(1)}, f32[16,2048]{1,0:T(8,128)S(1)}, u32[]{:S(2)}, u32[]{:S(2)}) collective-permute-start(f32[16,2048]{1,0:T(8,128)S(1)} %add.27), channel_id=1, source_target_pairs={{0,64},{64,0},{128,192},{192,128},{1,65},{65,1},{129,193},{193,129... | collective-permute-start | bytes 393224 | tf_op jit(solution)/shard_map/ppermute | solution.py:213
  (7 other events, 16.3 us)

commit v2 on v1

v2 whole, which is shorter than its diff:
```python
import functools
import math

import jax
import jax.numpy as jnp
from jax import lax
from jax.experimental import pallas as pl
from jax.experimental.pallas import tpu as pltpu
from jax.sharding import Mesh
from jax.sharding import PartitionSpec as P

CTR = ("ctr_0", "ctr_1", "ctr_2")
NEAR = ("ctr_1", "ctr_2")
FAR = "ctr_0"
RIDGE_TERM = 0.002

bf16, f32 = jnp.bfloat16, jnp.float32
LAST = (((1,), (1,)), ((), ()))
VMEM = pl.BlockSpec(memory_space=pltpu.VMEM)
SMEM = pl.BlockSpec(memory_space=pltpu.SMEM)
ANY = pl.BlockSpec(memory_space=pl.ANY)
TOKEN = jax.ShapeDtypeStruct((8, 128), jnp.float32)
LIMIT = 12 << 20


def widened(x, side):
    xf = x.astype(f32)
    n = jnp.sum(xf * xf, axis=1, keepdims=True)
    high = n.astype(bf16).astype(f32)
    rest = n - high
    mid = rest.astype(bf16).astype(f32)
    low = rest - mid
    lane = lax.broadcasted_iota(jnp.int32, x.shape, 1)
    if side == 0:
        extra = jnp.where(lane < 6, 1.0, 0.0)
        extra = jnp.where(lane == 0, high, extra)
        extra = jnp.where(lane == 1, mid, extra)
        extra = jnp.where(lane == 2, low, extra)
        return jnp.concatenate([x, extra.astype(bf16)], axis=1)
    extra = jnp.where(lane < 3, -1.0, 0.0)
    extra = jnp.where(lane == 3, -high, extra)
    extra = jnp.where(lane == 4, -mid, extra)
    extra = jnp.where(lane == 5, -low, extra)
    return jnp.concatenate([(xf * 2.0).astype(bf16), extra.astype(bf16)], axis=1)


def similar(a, b, features):
    t = lax.dot_general(a, b, LAST, preferred_element_type=f32)
    return jnp.exp2(t * (math.log2(math.e) / (2 * features))).astype(bf16)


def by_center_kernel(cols, centers_ref, points_ref, out_ref, token_ref, wide):
    features = centers_ref.shape[1]

    @pl.when(pl.program_id(0) == 0)
    def _():
        wide[...] = widened(centers_ref[...], 0)
        token_ref[...] = jnp.zeros_like(token_ref)

    right = widened(points_ref[...], 1)
    for j in range(right.shape[0] // cols):
        cut = slice(j * cols, (j + 1) * cols)
        out_ref[0, :, cut] = similar(wide[...], right[cut], features)


def by_point_kernel(cols, tie_ref, points_ref, centers_ref, out_ref, token_ref, wide):
    features = centers_ref.shape[1]

    @pl.when(pl.program_id(0) == 0)
    def _():
        wide[...] = widened(centers_ref[...], 1)
        token_ref[...] = jnp.zeros_like(token_ref)

    left = widened(points_ref[...], 0)
    for j in range(wide.shape[0] // cols):
        cut = slice(j * cols, (j + 1) * cols)
        out_ref[0, :, cut] = similar(left, wide[cut], features)


def block_cost(rows, columns, features):
    return pl.CostEstimate(
        flops=4 * rows * columns * features,
        bytes_accessed=2 * rows * columns,
        transcendentals=rows * columns,
    )


def by_center_block(centers, points, part, parts, chunk=512, cols=256):
    m_dev, features = centers.shape
    count = points.shape[0] // parts // chunk
    return pl.pallas_call(
        functools.partial(by_center_kernel, cols),
        out_shape=(jax.ShapeDtypeStruct((count, m_dev, chunk), bf16), TOKEN),
        grid=(count,),
        in_specs=[
            pl.BlockSpec((m_dev, features), lambda i: (0, 0)),
            pl.BlockSpec((chunk, features), lambda i: (part * count + i, 0)),
        ],
        out_specs=(
            pl.BlockSpec((1, m_dev, chunk), lambda i: (i, 0, 0)),
            pl.BlockSpec(TOKEN.shape, lambda i: (0, 0)),
        ),
        scratch_shapes=[pltpu.VMEM((m_dev, 2 * features), bf16)],
        compiler_params=pltpu.CompilerParams(vmem_limit_bytes=60 << 20),
        cost_estimate=block_cost(m_dev, count * chunk, features),
        name=f"by_center_{part}",
    )(centers, points)


def by_point_block(tie, points, centers, part, parts, chunk=1024, cols=256):
    m_dev, features = centers.shape
    count = points.shape[0] // parts // chunk
    return pl.pallas_call(
        functools.partial(by_point_kernel, cols),
        out_shape=(jax.ShapeDtypeStruct((count, chunk, m_dev), bf16), TOKEN),
        grid=(count,),
        in_specs=[
            ANY,
            pl.BlockSpec((chunk, features), lambda i: (part * count + i, 0)),
            pl.BlockSpec((m_dev, features), lambda i: (0, 0)),
        ],
        out_specs=(
            pl.BlockSpec((1, chunk, m_dev), lambda i: (i, 0, 0)),
            pl.BlockSpec(TOKEN.shape, lambda i: (0, 0)),
        ),
        scratch_shapes=[pltpu.VMEM((m_dev, 2 * features), bf16)],
        compiler_params=pltpu.CompilerParams(vmem_limit_bytes=60 << 20),
        cost_estimate=block_cost(m_dev, count * chunk, features),
        name=f"by_point_{part}",
    )(tie, points, centers)


def head_kernel(flags_ref, centers_ref, dir_ref, out_ref, rows_ref, vals_ref, sems):
    panel, features = rows_ref.shape
    outputs = vals_ref.shape[0]
    first = pltpu.make_async_copy(centers_ref.at[pl.ds(0, panel)], rows_ref, sems.at[0])
    second = pltpu.make_async_copy(dir_ref.at[:, pl.ds(0, panel)], vals_ref, sems.at[1])
    first.start()
    second.start()
    first.wait()
    second.wait()
    per = out_ref.shape[1] // 16
    for g in range(out_ref.shape[0] * per):
        row = 16 * g
        if row < panel:
            x = rows_ref[row : row + 16]
        else:
            b, r = divmod(row - panel, outputs)
            x = vals_ref[r : r + 16, b * features : (b + 1) * features].astype(bf16)
        out_ref[g // per, (g % per) * 16 : (g % per + 1) * 16] = x


def head_payload(flags, centers, direction, panel, ways):
    outputs, features = direction.shape[0], centers.shape[1]
    rows = panel + outputs * panel // features
    return pl.pallas_call(
        head_kernel,
        out_shape=jax.ShapeDtypeStruct((ways, rows // ways, features), bf16),
        in_specs=[SMEM, ANY, ANY],
        out_specs=VMEM,
        scratch_shapes=[
            pltpu.VMEM((panel, features), bf16),
            pltpu.VMEM((outputs, panel), f32),
            pltpu.SemaphoreType.DMA((2,)),
        ],
        compiler_params=pltpu.CompilerParams(vmem_limit_bytes=60 << 20),
        name="head",
    )(flags, centers, direction)


def spread_kernel(x_ref, *refs):
    out_ref = refs[-1]
    x = x_ref[0] if len(x_ref.shape) == len(out_ref.shape) else x_ref[...]
    for i in range(out_ref.shape[0]):
        out_ref[i] = x


def spread(x, ways, ties=()):
    shape = x.shape[1:] if len(x.shape) == 3 else x.shape
    return pl.pallas_call(
        spread_kernel,
        out_shape=jax.ShapeDtypeStruct((ways, *shape), x.dtype),
        in_specs=[VMEM] + [ANY] * len(ties),
        out_specs=VMEM,
        compiler_params=pltpu.CompilerParams(vmem_limit_bytes=LIMIT),
        name="spread",
    )(x, *ties)


def sum_kernel(x_ref, out_ref):
    total = x_ref[0]
    for i in range(1, x_ref.shape[0]):
        total = total + x_ref[i]
    out_ref[...] = total


def summed(x):
    return pl.pallas_call(
        sum_kernel,
        out_shape=jax.ShapeDtypeStruct(x.shape[1:], x.dtype),
        in_specs=[VMEM],
        out_specs=VMEM,
        compiler_params=pltpu.CompilerParams(vmem_limit_bytes=LIMIT),
        name="summed",
    )(x)


def owned_kernel(scale, x_ref, *refs):
    out_ref = refs[-1]
    total = x_ref[0]
    for i in range(1, x_ref.shape[0]):
        total = total + x_ref[i]
    total = (total * scale).astype(bf16)
    for i in range(out_ref.shape[0]):
        out_ref[i] = total


def owned_copies(x, scale, ways, ties=()):
    return pl.pallas_call(
        functools.partial(owned_kernel, scale),
        out_shape=jax.ShapeDtypeStruct((ways, *x.shape[1:]), bf16),
        in_specs=[VMEM] + [ANY] * len(ties),
        out_specs=VMEM,
        compiler_params=pltpu.CompilerParams(vmem_limit_bytes=LIMIT),
        name="owned",
    )(x, *ties)


def chunk_copies(sources, buffer, sems):
    copies, at = [], 0
    for source in sources:
        for i in range(source.shape[0]):
            copies.append(pltpu.make_async_copy(source.at[i], buffer.at[at], sems.at[at]))
            at += 1
    return copies


def panel_kernel(
    parts, flags_ref, centers_ref, head_ref, mine_ref, other_ref, pair_ref, dir_ref, *refs
):
    sources, refs = refs[:parts], refs[parts:]
    z_out, kp_out, high_out, both_out, zsq_ref = refs[:5]
    blocks, pinv, zz, z_buf, kp_buf, high_buf, both_buf, sems, out_sems = refs[5:]
    copies = chunk_copies(sources, blocks, sems)
    for copy in copies:
        copy.start()
    share = mine_ref.shape[0]
    panel = pinv.shape[0]
    outputs = dir_ref.shape[0]
    features = centers_ref.shape[1]
    at = flags_ref[1]
    core = at % 2
    far = (2 - (at - core)) * share
    pinv[pl.ds(pl.multiple_of(at * share, share), share)] = mine_ref[...]
    pinv[pl.ds(pl.multiple_of((at + 1 - 2 * core) * share, share), share)] = other_ref[...]
    pinv[pl.ds(pl.multiple_of(far + core * share, share), share)] = pair_ref[:share]
    pinv[pl.ds(pl.multiple_of(far + (1 - core) * share, share), share)] = pair_ref[share:]
    head = jnp.concatenate([head_ref[i] for i in range(head_ref.shape[0])], axis=0)
    vals = jnp.concatenate(
        [head[panel + b * outputs : panel + (b + 1) * outputs] for b in range(panel // features)],
        axis=1,
    )
    z1 = lax.dot_general(vals, pinv[...], LAST, preferred_element_type=f32).astype(bf16)
    q = jnp.dot(z1, pinv[...], preferred_element_type=f32).astype(bf16)
    heads = widened(head[:panel], 1)
    tile = panel
    squares = jnp.zeros((outputs, 1), f32)
    for i in range(centers_ref.shape[0] // tile):
        rows = slice(i * tile, (i + 1) * tile)
        kp = similar(widened(centers_ref[rows], 0), heads, features)
        kp_buf[rows] = kp
        z = dir_ref[:, rows] - lax.dot_general(q, kp, LAST, preferred_element_type=f32)
        if i == 0:
            z = jnp.where(flags_ref[0] == 0, z1.astype(f32), z)
        z_buf[:, rows] = z
        squares = squares + jnp.sum(z * z, axis=1, keepdims=True)
        high = z.astype(bf16)
        zz[:outputs, rows] = high
        zz[outputs:, rows] = (z - high.astype(f32)).astype(bf16)
    zsq_ref[...] = squares
    puts = [
        pltpu.make_async_copy(z_buf, z_out, out_sems.at[0]),
        pltpu.make_async_copy(kp_buf, kp_out, out_sems.at[1]),
    ]
    for put in puts:
        put.start()
    per = blocks.shape[2] // 128
    for i, copy in enumerate(copies):
        copy.wait()
        u = jnp.dot(zz[...], blocks[i], preferred_element_type=f32)
        for b in range(per):
            part = u[:, b * 128 : (b + 1) * 128]
            high_buf[i * per + b] = part[:outputs]
            both_buf[i * per + b] = part[:outputs] + part[outputs:]
        span = pl.ds(i * per, per)
        for j, (buf, out) in enumerate(((high_buf, high_out), (both_buf, both_out))):
            puts.append(
                pltpu.make_async_copy(buf.at[span], out.at[span], out_sems.at[2 + 2 * i + j])
            )
            puts[-1].start()
    for put in puts:
        put.wait()


def panel_step(flags, centers, head, mine, other, pair, direction, blocks):
    outputs, m_dev = direction.shape
    panel = mine.shape[1]
    count, _, chunk = blocks[0].shape
    count = count * len(blocks)
    values = jax.ShapeDtypeStruct((count * chunk // 128, outputs, 128), f32)
    z = jax.ShapeDtypeStruct((outputs, m_dev), f32)
    k_panel = jax.ShapeDtypeStruct((m_dev, panel), bf16)
    return pl.pallas_call(
        functools.partial(panel_kernel, len(blocks)),
        out_shape=(z, k_panel, values, values, jax.ShapeDtypeStruct((outputs, 1), f32)),
        in_specs=[SMEM] + [VMEM] * 6 + [ANY] * len(blocks),
        out_specs=(ANY, ANY, ANY, ANY, VMEM),
        scratch_shapes=[
            pltpu.VMEM((count, m_dev, chunk), bf16),
            pltpu.VMEM((panel, panel), bf16),
            pltpu.VMEM((2 * outputs, m_dev), bf16),
            pltpu.VMEM(z.shape, f32),
            pltpu.VMEM(k_panel.shape, bf16),
            pltpu.VMEM(values.shape, f32),
            pltpu.VMEM(values.shape, f32),
            pltpu.SemaphoreType.DMA((count,)),
            pltpu.SemaphoreType.DMA((2 + 2 * count,)),
        ],
        compiler_params=pltpu.CompilerParams(vmem_limit_bytes=60 << 20),
        cost_estimate=pl.CostEstimate(
            flops=2 * 256 * m_dev * count * chunk,
            bytes_accessed=2 * m_dev * count * chunk,
            transcendentals=m_dev * panel,
        ),
        name="panel",
    )(flags, centers, head, mine, other, pair, direction, *blocks)


def image_kernel(parts, flags_ref, tie_ref, w_ref, *refs):
    sources = refs[:parts]
    keep_ref, send_ref, blocks, total, sems = refs[parts:]
    copies = chunk_copies(sources, blocks, sems)
    for copy in copies:
        copy.start()
    per = blocks.shape[1] // 128
    for i, copy in enumerate(copies):
        w = jnp.concatenate([w_ref[i * per + b] for b in range(per)], axis=1)
        copy.wait()
        part = jnp.dot(w, blocks[i], preferred_element_type=f32)
        total[...] = part if i == 0 else total[...] + part
    half = keep_ref.shape[0]
    mine = pl.multiple_of((flags_ref[1] % 2) * half, half)
    keep_ref[...] = total[pl.ds(mine, half)]
    send_ref[...] = total[pl.ds(half - mine, half)]


def image(flags, tie, w, blocks):
    outputs = w.shape[1]
    count, chunk, m_dev = blocks[0].shape
    count = count * len(blocks)
    shape = jax.ShapeDtypeStruct((outputs // 2, m_dev), f32)
    return pl.pallas_call(
        functools.partial(image_kernel, len(blocks)),
        out_shape=(shape, shape),
        in_specs=[SMEM, ANY, VMEM] + [ANY] * len(blocks),
        out_specs=(VMEM, VMEM),
        scratch_shapes=[
            pltpu.VMEM((count, chunk, m_dev), bf16),
            pltpu.VMEM((outputs, m_dev), f32),
            pltpu.SemaphoreType.DMA((count,)),
        ],
        compiler_params=pltpu.CompilerParams(vmem_limit_bytes=60 << 20),
        cost_estimate=pl.CostEstimate(
            flops=2 * 256 * count * chunk * m_dev,
            bytes_accessed=2 * count * chunk * m_dev,
            transcendentals=0,
        ),
        name="image",
    )(flags, tie, w, *blocks)


def exchange(x, axis):
    return lax.all_to_all(x, axis, 0, 0, tiled=True)


def products_kernel(scale, ridge, count, w_ref, both_ref, z_squares_ref, res_ref, out_ref):
    outputs = w_ref.shape[1]
    total = jnp.zeros(w_ref.shape[1:], f32)
    for i in range(w_ref.shape[0]):
        total = total + w_ref[i].astype(f32) * both_ref[i]
    mine = jnp.sum(total, axis=1, keepdims=True) * scale + ridge * z_squares_ref[...]
    squares = jnp.sum(res_ref[...] * res_ref[...], axis=1, keepdims=True) * (1.0 / count)
    lane = lax.broadcasted_iota(jnp.int32, total.shape, 1)
    row = lax.broadcasted_iota(jnp.int32, total.shape, 0)
    spread_out = jnp.where(lane == row, mine, jnp.where(lane == row + outputs, squares, 0.0))
    out_ref[...] = jnp.sum(spread_out, axis=0, keepdims=True)


def products(w, both, z_squares, residual, scale, count):
    return pl.pallas_call(
        functools.partial(products_kernel, scale, RIDGE_TERM / count, count),
        out_shape=jax.ShapeDtypeStruct((1, 128), f32),
        in_specs=[VMEM] * 4,
        out_specs=VMEM,
        compiler_params=pltpu.CompilerParams(vmem_limit_bytes=LIMIT),
        name="products",
    )(w, both, z_squares, residual)


def swap(x, bit):
    n = lax.axis_size("pts")
    return lax.ppermute(x, "pts", [(i, i ^ bit) for i in range(n)])


def rows_kernel(tie_ref, k_ref, pinv_ref, out_ref):
    out_ref[...] = lax.dot_general(
        k_ref[...], pinv_ref[...], LAST, preferred_element_type=f32
    ).astype(bf16)


def rows_step(tie, k_panel, share):
    return pl.pallas_call(
        rows_kernel,
        out_shape=jax.ShapeDtypeStruct((k_panel.shape[0], share.shape[0]), bf16),
        in_specs=[ANY, VMEM, VMEM],
        out_specs=VMEM,
        compiler_params=pltpu.CompilerParams(vmem_limit_bytes=LIMIT),
        cost_estimate=pl.CostEstimate(
            flops=2 * k_panel.size * share.shape[0],
            bytes_accessed=2 * k_panel.size,
            transcendentals=0,
        ),
        name="rows",
    )(tie, k_panel, share)


def final_kernel(scale, flags_ref, keep_ref, other_ref, z_ref, res_ref, sums_ref, op_ref, new_ref):
    outputs = z_ref.shape[0]
    half = keep_ref.shape[0]
    sums = jnp.sum(sums_ref[...], axis=0)
    lane = lax.broadcasted_iota(jnp.int32, (outputs, sums.shape[1]), 1)
    row = lax.broadcasted_iota(jnp.int32, (outputs, sums.shape[1]), 0)
    curvature = jnp.sum(jnp.where(lane == row, sums, 0.0), axis=1, keepdims=True)
    squares = jnp.sum(jnp.where(lane == row + outputs, sums, 0.0), axis=1, keepdims=True)
    op_ref[...] = RIDGE_TERM * z_ref[...]
    mine = pl.multiple_of((flags_ref[1] % 2) * half, half)
    op_ref[pl.ds(mine, half)] += keep_ref[...] * scale
    op_ref[pl.ds(half - mine, half)] += other_ref[...] * scale
    new_ref[...] = res_ref[...] - (squares / curvature) * op_ref[...]


def final_step(flags, keep, other, z, residual, sums, scale):
    shape = jax.ShapeDtypeStruct(z.shape, f32)
    return pl.pallas_call(
        functools.partial(final_kernel, scale),
        out_shape=(shape, shape),
        in_specs=[SMEM] + [VMEM] * 5,
        out_specs=(VMEM, VMEM),
        compiler_params=pltpu.CompilerParams(vmem_limit_bytes=LIMIT),
        name="final",
    )(flags, keep, other, z, residual, sums)


def shards(points, centers, panel_inverse, direction, residual):
    n_ctr = lax.axis_size(CTR)
    n_near = lax.axis_size(NEAR)
    n_far = lax.axis_size(FAR)
    n_pts = lax.axis_size("pts")
    flags = jnp.stack([lax.axis_index(CTR), lax.axis_index("pts")])
    m_dev, features = centers.shape
    npg = points.shape[0]
    panel = panel_inverse.shape[1]
    outputs = direction.shape[0]
    w_scale = 1.0 / (2.0 * math.sqrt(m_dev * n_ctr))
    image_scale = 1.0 / (2.0 * math.sqrt(npg * n_pts))

    head = exchange(head_payload(flags, centers, direction, panel, n_near), NEAR)
    by_center = [by_center_block(centers, points, i, 2) for i in range(2)]
    other = swap(panel_inverse, 1)
    pair = swap(jnp.concatenate([panel_inverse, other], axis=0), 2)
    head = exchange(spread(head, n_far), FAR)
    by_center, made = zip(*by_center)
    head = exchange(spread(head, n_near, (*made, pair)), NEAR)

    z, k_panel, high, both, z_squares = panel_step(
        flags, centers, head, panel_inverse, other, pair, direction, by_center
    )

    parts = exchange(high.reshape(n_near, n_far * outputs, 128), NEAR)
    by_point = [by_point_block(z_squares, points, centers, i, 2) for i in range(2)]
    by_point, made = zip(*by_point)
    parts = exchange(summed(parts).reshape(n_far, outputs, 128), FAR)
    w = exchange(owned_copies(parts, w_scale, n_far, made), FAR)
    w = exchange(spread(w.reshape(n_far * outputs, 128), n_near), NEAR)
    w = w.reshape(-1, outputs, 128)

    scalars = products(w, both, z_squares, residual, image_scale, n_pts)
    scalars = scalars + swap(scalars, 1)
    keep, send = image(flags, scalars, w, by_point)
    scalars = scalars + swap(scalars, 2)
    sums = exchange(jnp.broadcast_to(scalars[None], (n_ctr, *scalars.shape)), CTR)
    panel_rows = rows_step(keep, k_panel, panel_inverse)
    keep = keep + swap(send, 1)
    keep = keep + swap(keep, 2)
    operator_image, new_residual = final_step(
        flags, keep, swap(keep, 1), z, residual, sums, image_scale
    )
    return (panel_rows, operator_image, new_residual)


def solution(mesh):
    split = Mesh(
        mesh.devices.reshape(mesh.shape["pts"], 8, 2, 4), ("pts", "ctr_0", "ctr_1", "ctr_2")
    )
    placed = (P("pts", None), P(CTR, None), P("pts", None), P(None, CTR), P(None, CTR))
    return jax.shard_map(
        shards,
        mesh=split,
        in_specs=placed,
        out_specs=(P(CTR, "pts"), P(None, CTR), P(None, CTR)),
        check_vma=False,
    )
```

time: 183 us -> 178 us (0.973)
  Pallas kernels: 38.1 us -> 78.8 us
  local copies, waits for them, and re-layouts: 40.6 us -> 2.93 us
  blocking collectives: 16.6 us -> 38.3 us
  starting transfers between devices: 54.6 us -> 41 us
  waiting for transfers between devices: 22.8 us -> 13.6 us
  other arithmetic: 6.88 us -> 2.08 us
    pallas_call x7 -> x15, Pallas kernels: 38.1 us -> 78.8 us  [the longest x2 23.1 us: by_center_block(): pl.pallas_call(functools.partial(by_center_kernel, cols), out_shape=(jax....]
    unnamed x34, local copies, waits for them, and re-layouts: 33.6 us -> 2.31 us
    all_to_all x1 -> x3, blocking collectives: 16.6 us -> 38.3 us  [exchange(): return lax.all_to_all(x, axis, 0, 0, tiled=True)]
    all_to_all x7 -> x5, waiting for transfers between devices: 21.9 us -> 8.26 us  [exchange(): return lax.all_to_all(x, axis, 0, 0, tiled=True)]
    all_to_all x7 -> x5, starting transfers between devices: 36.9 us -> 26.1 us  [exchange(): return lax.all_to_all(x, axis, 0, 0, tiled=True)]
    ppermute x7, waiting for transfers between devices: 0.93 us -> 5.29 us  [swap(): return lax.ppermute(x, 'pts', [(i, i ^ bit) for i in range(n)])]
    reduce_sum x6 -> x0, other arithmetic: 3.7 us -> none  [the longest x1 1.94 us: shards(): parts = jnp.sum(parts, axis=0)]
    slice x3 -> x0, local copies, waits for them, and re-layouts: 3.44 us -> none  [the longest x1 1.68 us: shards(): halves = [points[:npg // 2], points[npg // 2:]]]
  transfers between devices with their start and end apart: 14 -> 12, of which waited for: 5 -> 5; matrix products, arithmetic and copies ran while one was open for 4% -> 1% of each run, Pallas kernels for 17% -> 27%
where the time goes in v2:
time: 178 us; the launch traced here: 177 us
  Pallas kernels  78.8 us (44%)
  starting transfers between devices  41 us (23%)
  blocking collectives  38.3 us (22%)
  waiting for transfers between devices  13.6 us (8%)
  local copies, waits for them, and re-layouts  2.93 us (2%)
  other arithmetic  2.08 us (1%)
    all_to_all x3, blocking collectives, exchange(): return lax.all_to_all(x, axis, 0, 0, tiled=True)  38.3 us
    all_to_all x5, starting transfers between devices, exchange(): return lax.all_to_all(x, axis, 0, 0, tiled=True)  26.1 us
    pallas_call x2, Pallas kernels, by_center_block(): pl.pallas_call(functools.partial(by_center_kernel, cols), out_shape=(jax....  23.1 us
    pallas_call x2, Pallas kernels, by_point_block(): pl.pallas_call(functools.partial(by_point_kernel, cols), out_shape=(jax.S...  19.5 us
    pallas_call x1, Pallas kernels, panel_step(): pl.pallas_call(functools.partial(panel_kernel, len(blocks)), out_shape=(z...  15.7 us
    ppermute x7, starting transfers between devices, swap(): return lax.ppermute(x, 'pts', [(i, i ^ bit) for i in range(n)])  14.8 us
    pallas_call x1, Pallas kernels, image(): pl.pallas_call(functools.partial(image_kernel, len(blocks)), out_shape=(s...  13.4 us
    all_to_all x5, waiting for transfers between devices, exchange(): return lax.all_to_all(x, axis, 0, 0, tiled=True)  8.26 us
  transfers between devices with their start and end apart: 12, of which 5 were waited for; matrix products, arithmetic and copies ran while one was open for 1% of the time, Pallas kernels for 27%

profile of v2, /device:TPU:1, one launch (start us, length us, event | category | flops | bytes accessed | tf_op | source)
XLA Modules:
  0.0 177.4 jit_solution(15340486117188305156)
XLA Ops:
  0.6 3.3 %collective-permute-start = (bf16[128,512]{1,0:T(8,128)(2,1)}, bf16[128,512]{1,0:T(8,128)(2,1)S(1)}, u32[]{:S(2)}, u32[]{:S(2)}) collective-permute-start(bf16[128,512]{1,0:T(8,128)(2,1)} %pinv_ref.1), channel_id=1, source_target_pairs={{0,64},{64,0},{128,192},{192,128},{1,65},{65,1},{129,193},{193,129... | collective-permute-start | bytes 393224 | tf_op jit(solution)/shard_map/ppermute | solution.py:412
  4.5 2.3 %head.1 = bf16[8,80,128]{2,1,0:T(8,128)(2,1)} custom-call(s32[2]{0:T(128)} %pad_add_fusion.flags_ref, bf16[2048,128]{1,0:T(8,128)(2,1)} %centers_ref.11, f32[32,2048]{1,0:T(8,128)} %dir_ref.3), custom_call_target="tpu_custom_call" | custom-call | tf_op jit(solution)/shard_map/head/pallas_call | solution.py:156
  6.8 3.4 %all-to-all-start = ((bf16[8,80,128]{2,1,0:T(8,128)(2,1)}), bf16[8,80,128]{2,1,0:T(8,128)(2,1)S(1)}, u32[]{:S(2)}, u32[]{:S(2)}) async-start(bf16[8,80,128]{2,1,0:T(8,128)(2,1)} %head.1), calls=%async_computation | async-start | bytes 327680 | tf_op jit(solution)/shard_map/all_to_all | solution.py:383
  10.2 11.6 %by_center_1.1 = (bf16[8,2048,512]{2,1,0:T(8,128)(2,1)}, f32[8,128]{1,0:T(8,128)}) custom-call(bf16[2048,128]{1,0:T(8,128)(2,1)} %centers_ref.11, bf16[8192,128]{1,0:T(8,128)(2,1)} %points_ref.7), custom_call_target="tpu_custom_call" | custom-call | flops 4294967296 | bytes 16777216 | tf_op jit(solution)/shard_map/by_center_1/pallas_call | solution.py:91
  21.8 2.5 %collective-permute-start.1 = (bf16[256,512]{1,0:T(8,128)(2,1)S(1)}, bf16[256,512]{1,0:T(8,128)(2,1)S(1)}, u32[]{:S(2)}, u32[]{:S(2)}) collective-permute-start(bf16[256,512]{1,0:T(8,128)(2,1)S(1)} %pad_maximum_fusion), channel_id=1, source_target_pairs={{0,128},{64,192},{128,0},{192,64},{1,129},{65,193},{129,1},{193,65... | collective-permute-start | bytes 786440 | tf_op jit(solution)/shard_map/ppermute | solution.py:412
  25.1 8.2 %all-to-all-start.1 = ((bf16[8,80,128]{2,1,0:T(8,128)(2,1)}), bf16[8,80,128]{2,1,0:T(8,128)(2,1)S(1)}, u32[]{:S(2)}, u32[]{:S(2)}) async-start(bf16[8,80,128]{2,1,0:T(8,128)(2,1)} %spread.3), calls=%async_computation.1 | async-start | bytes 327680 | tf_op jit(solution)/shard_map/all_to_all | solution.py:383
  33.3 11.6 %by_center_0.1 = (bf16[8,2048,512]{2,1,0:T(8,128)(2,1)}, f32[8,128]{1,0:T(8,128)}) custom-call(bf16[2048,128]{1,0:T(8,128)(2,1)} %centers_ref.11, bf16[8192,128]{1,0:T(8,128)(2,1)} %points_ref.7), custom_call_target="tpu_custom_call" | custom-call | flops 4294967296 | bytes 16777216 | tf_op jit(solution)/shard_map/by_center_0/pallas_call | solution.py:91
  45.5 10.0 %all_to_all.40.head_ref = bf16[8,80,128]{2,1,0:T(8,128)(2,1)} all-to-all(bf16[8,80,128]{2,1,0:T(8,128)(2,1)S(1)} %spread.4), channel_id=1, replica_groups=mesh['pts'=4,'ctr_0'=8,'ctr_1'=2,'ctr_2'=4] {'ctr_1','ctr_2'}, dimensions={0} | all-to-all | bytes 327680 | tf_op jit(solution)/shard_map/all_to_all | solution.py:383
  55.6 15.7 %panel.1 = (f32[32,2048]{1,0:T(8,128)}, bf16[2048,512]{1,0:T(8,128)(2,1)}, f32[64,32,128]{2,1,0:T(8,128)}, f32[64,32,128]{2,1,0:T(8,128)}, f32[32,1]{1,0:T(8,128)}) custom-call(s32[2]{0:T(128)} %pad_add_fusion.flags_ref, bf16[2048,128]{1,0:T(8,128)(2,1)} %centers_ref.11, bf16[8,80,128]{2,1,0:T(8,128)(2,1)} %all_to_all.40.head_ref, ...), custom_call_target="tpu_custom_call" | custom-call | flops 8589934592 | bytes 33554432 | tf_op jit(solution)/shard_map/panel/pallas_call | solution.py:313
  71.2 3.6 %all-to-all-start.3 = ((f32[8,256,128]{2,1,0:T(8,128)}), f32[8,256,128]{2,1,0:T(8,128)S(1)}, u32[]{:S(2)}, u32[]{:S(2)}) async-start(f32[8,256,128]{2,1,0:T(8,128)} %bitcast.11), calls=%async_computation.3 | async-start | bytes 2097152 | tf_op jit(solution)/shard_map/all_to_all | solution.py:383
  74.8 9.8 %by_point_1.1 = (bf16[4,1024,2048]{2,1,0:T(8,128)(2,1)}, f32[8,128]{1,0:T(8,128)}) custom-call(f32[32,1]{1,0:T(8,128)} %get-tuple-element.25.tie_ref.z_squares_ref, bf16[8192,128]{1,0:T(8,128)(2,1)} %points_ref.7, bf16[2048,128]{1,0:T(8,128)(2,1)} %centers_ref.11), custom_call_target="tpu_custom_call" | custom-call | flops 4294967296 | bytes 16777216 | tf_op jit(solution)/shard_map/by_point_1/pallas_call | solution.py:113
  84.6 1.4 all-to-all-done.3.x_ref
  86.7 6.4 %all-to-all-start.4 = ((f32[8,32,128]{2,1,0:T(8,128)}), f32[8,32,128]{2,1,0:T(8,128)S(1)}, u32[]{:S(2)}, u32[]{:S(2)}) async-start(f32[8,32,128]{2,1,0:T(8,128)} %bitcast.3), calls=%async_computation.4 | async-start | bytes 262144 | tf_op jit(solution)/shard_map/all_to_all | solution.py:383
  93.1 9.7 %by_point_0.1 = (bf16[4,1024,2048]{2,1,0:T(8,128)(2,1)}, f32[8,128]{1,0:T(8,128)}) custom-call(f32[32,1]{1,0:T(8,128)} %get-tuple-element.25.tie_ref.z_squares_ref, bf16[8192,128]{1,0:T(8,128)(2,1)} %points_ref.7, bf16[2048,128]{1,0:T(8,128)(2,1)} %centers_ref.11), custom_call_target="tpu_custom_call" | custom-call | flops 4294967296 | bytes 16777216 | tf_op jit(solution)/shard_map/by_point_0/pallas_call | solution.py:113
  103.5 13.7 %all_to_all.41 = bf16[8,32,128]{2,1,0:T(8,128)(2,1)S(1)} all-to-all(bf16[8,32,128]{2,1,0:T(8,128)(2,1)S(1)} %owned.1), channel_id=1, replica_groups=mesh['pts'=4,'ctr_0'=8,'ctr_1'=2,'ctr_2'=4] {'ctr_0'}, dimensions={0} | all-to-all | bytes 131072 | tf_op jit(solution)/shard_map/all_to_all | solution.py:383
  117.3 14.6 %all_to_all.42 = bf16[8,256,128]{2,1,0:T(8,128)(2,1)S(1)} all-to-all(bf16[8,256,128]{2,1,0:T(8,128)(2,1)S(1)} %spread.5), channel_id=1, replica_groups=mesh['pts'=4,'ctr_0'=8,'ctr_1'=2,'ctr_2'=4] {'ctr_1','ctr_2'}, dimensions={0} | all-to-all | bytes 1048576 | tf_op jit(solution)/shard_map/all_to_all | solution.py:383
  132.2 4.2 %collective-permute-start.2 = (f32[1,128]{1,0:T(1,128)S(1)}, f32[1,128]{1,0:T(1,128)S(1)}, u32[]{:S(2)}, u32[]{:S(2)}) collective-permute-start(f32[1,128]{1,0:T(1,128)S(1)} %products.1), channel_id=1, source_target_pairs={{0,64},{64,0},{128,192},{192,128},{1,65},{65,1},{129,193},{193,129... | collective-permute-start | bytes 1544 | tf_op jit(solution)/shard_map/ppermute | solution.py:412
  137.8 13.4 %image.1 = (f32[16,2048]{1,0:T(8,128)}, f32[16,2048]{1,0:T(8,128)}) custom-call(s32[2]{0:T(128)} %pad_add_fusion.flags_ref, f32[1,128]{1,0:T(1,128)} %add.20.tie_ref, bf16[64,32,128]{2,1,0:T(8,128)(2,1)} %bitcast.9, bf16[4,1024,2048]{2,1,0:T(8,128)(2,1)} %get-tuple-element.29.refs_0_, bf16[4,1024,2048]{2,1,0:T(8,128)(2,1)} %get-tuple-element.30.refs_1_), custom_call_target="tpu_custom_call" | custom-call | flops 8589934592 | bytes 33554432 | tf_op jit(solution)/shard_map/image/pallas_call | solution.py:362
  153.8 1.8 %collective-permute-start.4 = (f32[16,2048]{1,0:T(8,128)S(1)}, f32[16,2048]{1,0:T(8,128)S(1)}, u32[]{:S(2)}, u32[]{:S(2)}) collective-permute-start(f32[16,2048]{1,0:T(8,128)S(1)} %add.21), channel_id=1, source_target_pairs={{0,128},{64,192},{128,0},{192,64},{1,129},{65,193},{129,1},{193,65... | collective-permute-start | bytes 393224 | tf_op jit(solution)/shard_map/ppermute | solution.py:412
  156.9 3.2 %collective-permute-done.4 = f32[16,2048]{1,0:T(8,128)S(1)} collective-permute-done((f32[16,2048]{1,0:T(8,128)S(1)}, f32[16,2048]{1,0:T(8,128)S(1)}, u32[]{:S(2)}, u32[]{:S(2)}) %collective-permute-start.4) | collective-permute-done | bytes 131104 | tf_op jit(solution)/shard_map/ppermute | solution.py:412
  162.0 4.6 %all-to-all-start.7 = ((f32[64,1,128]{2,1,0:T(1,128)}), f32[64,1,128]{2,1,0:T(1,128)S(1)}, u32[]{:S(2)}, u32[]{:S(2)}) async-start(f32[64,1,128]{2,1,0:T(1,128)} %broadcast_in_dim.9), calls=%async_computation.7 | async-start | bytes 65536 | tf_op jit(solution)/shard_map/all_to_all | solution.py:383
  167.6 1.5 rows.1
  169.1 6.9 %all-to-all-done.7.sums_ref = f32[64,1,128]{2,1,0:T(1,128)S(1)} async-done(((f32[64,1,128]{2,1,0:T(1,128)}), f32[64,1,128]{2,1,0:T(1,128)S(1)}, u32[]{:S(2)}, u32[]{:S(2)}) %all-to-all-start.7) | async-done | bytes 32800 | tf_op jit(solution)/shard_map/all_to_all | solution.py:383
  176.0 1.5 final.1
  (59 shorter events, 11.8 us)
Async XLA Ops:
  0.6 21.2 %copy-start.2 = (bf16[128,512]{1,0:T(8,128)(2,1)S(1)}, bf16[128,512]{1,0:T(8,128)(2,1)}, u32[]{:S(2)}) copy-start(bf16[128,512]{1,0:T(8,128)(2,1)} %pinv_ref.1) | copy-start | bytes 393220
  0.6 21.2 %collective-permute-start = (bf16[128,512]{1,0:T(8,128)(2,1)}, bf16[128,512]{1,0:T(8,128)(2,1)S(1)}, u32[]{:S(2)}, u32[]{:S(2)}) collective-permute-start(bf16[128,512]{1,0:T(8,128)(2,1)} %pinv_ref.1), channel_id=1, source_target_pairs={{0,64},{64,0},{128,192},{192,128},{1,65},{65,1},{129,193},{193,129... | collective-permute-start | bytes 393224 | tf_op jit(solution)/shard_map/ppermute | solution.py:412
  6.8 17.6 %all-to-all-start = ((bf16[8,80,128]{2,1,0:T(8,128)(2,1)}), bf16[8,80,128]{2,1,0:T(8,128)(2,1)S(1)}, u32[]{:S(2)}, u32[]{:S(2)}) async-start(bf16[8,80,128]{2,1,0:T(8,128)(2,1)} %head.1), calls=%async_computation | async-start | bytes 327680 | tf_op jit(solution)/shard_map/all_to_all | solution.py:383
  21.8 23.0 %copy-start.11 = (f32[8,128]{1,0:T(8,128)S(1)}, f32[8,128]{1,0:T(8,128)}, u32[]{:S(2)}) copy-start(f32[8,128]{1,0:T(8,128)} %get-tuple-element.21.refs_1_) | copy-start | bytes 12292
  21.8 33.8 %copy-start.15 = (bf16[128,512]{1,0:T(8,128)(2,1)}, bf16[128,512]{1,0:T(8,128)(2,1)S(1)}, u32[]{:S(2)}) copy-start(bf16[128,512]{1,0:T(8,128)(2,1)S(1)} %collective-permute-done.other_ref) | copy-start | bytes 393220
  21.8 23.0 %collective-permute-start.1 = (bf16[256,512]{1,0:T(8,128)(2,1)S(1)}, bf16[256,512]{1,0:T(8,128)(2,1)S(1)}, u32[]{:S(2)}, u32[]{:S(2)}) collective-permute-start(bf16[256,512]{1,0:T(8,128)(2,1)S(1)} %pad_maximum_fusion), channel_id=1, source_target_pairs={{0,128},{64,192},{128,0},{192,64},{1,129},{65,193},{129,1},{193,65... | collective-permute-start | bytes 786440 | tf_op jit(solution)/shard_map/ppermute | solution.py:412
  25.1 19.8 %all-to-all-start.1 = ((bf16[8,80,128]{2,1,0:T(8,128)(2,1)}), bf16[8,80,128]{2,1,0:T(8,128)(2,1)S(1)}, u32[]{:S(2)}, u32[]{:S(2)}) async-start(bf16[8,80,128]{2,1,0:T(8,128)(2,1)} %spread.3), calls=%async_computation.1 | async-start | bytes 327680 | tf_op jit(solution)/shard_map/all_to_all | solution.py:383
  71.2 14.8 %all-to-all-start.3 = ((f32[8,256,128]{2,1,0:T(8,128)}), f32[8,256,128]{2,1,0:T(8,128)S(1)}, u32[]{:S(2)}, u32[]{:S(2)}) async-start(f32[8,256,128]{2,1,0:T(8,128)} %bitcast.11), calls=%async_computation.3 | async-start | bytes 2097152 | tf_op jit(solution)/shard_map/all_to_all | solution.py:383
  74.8 57.0 %copy-start.5 = (f32[64,32,128]{2,1,0:T(8,128)S(1)}, f32[64,32,128]{2,1,0:T(8,128)}, u32[]{:S(2)}) copy-start(f32[64,32,128]{2,1,0:T(8,128)} %get-tuple-element.28.both_ref) | copy-start | bytes 3145732
  74.8 57.0 %copy-start.6 = (f32[32,2048]{1,0:T(8,128)S(1)}, f32[32,2048]{1,0:T(8,128)}, u32[]{:S(2)}) copy-start(f32[32,2048]{1,0:T(8,128)} %res_ref.3) | copy-start | bytes 786436
  74.8 57.0 %copy-start.9 = (f32[32,1]{1,0:T(8,128)S(1)}, f32[32,1]{1,0:T(8,128)}, u32[]{:S(2)}) copy-start(f32[32,1]{1,0:T(8,128)} %get-tuple-element.25.tie_ref.z_squares_ref) | copy-start | bytes 388
  84.6 18.2 %copy-start.13 = (f32[8,128]{1,0:T(8,128)S(1)}, f32[8,128]{1,0:T(8,128)}, u32[]{:S(2)}) copy-start(f32[8,128]{1,0:T(8,128)} %get-tuple-element.27.refs_1_) | copy-start | bytes 12292
  86.7 16.1 %all-to-all-start.4 = ((f32[8,32,128]{2,1,0:T(8,128)}), f32[8,32,128]{2,1,0:T(8,128)S(1)}, u32[]{:S(2)}, u32[]{:S(2)}) async-start(f32[8,32,128]{2,1,0:T(8,128)} %bitcast.3), calls=%async_computation.4 | async-start | bytes 262144 | tf_op jit(solution)/shard_map/all_to_all | solution.py:383
  132.2 5.1 %collective-permute-start.2 = (f32[1,128]{1,0:T(1,128)S(1)}, f32[1,128]{1,0:T(1,128)S(1)}, u32[]{:S(2)}, u32[]{:S(2)}) collective-permute-start(f32[1,128]{1,0:T(1,128)S(1)} %products.1), channel_id=1, source_target_pairs={{0,64},{64,0},{128,192},{192,128},{1,65},{65,1},{129,193},{193,129... | collective-permute-start | bytes 1544 | tf_op jit(solution)/shard_map/ppermute | solution.py:412
  137.8 17.9 %copy-start.16 = (f32[1,128]{1,0:T(1,128)S(1)}, f32[1,128]{1,0:T(1,128)}, u32[]{:S(2)}) copy-start(f32[1,128]{1,0:T(1,128)} %add.20.tie_ref) | copy-start | bytes 1540
  137.8 28.9 %copy-start.1 = (bf16[2048,512]{1,0:T(8,128)(2,1)S(1)}, bf16[2048,512]{1,0:T(8,128)(2,1)}, u32[]{:S(2)}) copy-start(bf16[2048,512]{1,0:T(8,128)(2,1)} %get-tuple-element.32.k_ref) | copy-start | bytes 6291460
  137.8 28.9 %copy-start.3 = (bf16[128,512]{1,0:T(8,128)(2,1)S(1)}, bf16[128,512]{1,0:T(8,128)(2,1)}, u32[]{:S(2)}) copy-start(bf16[128,512]{1,0:T(8,128)(2,1)} %pinv_ref.1) | copy-start | bytes 393220
  137.8 38.2 %copy-start.8 = (f32[32,2048]{1,0:T(8,128)S(1)}, f32[32,2048]{1,0:T(8,128)}, u32[]{:S(2)}) copy-start(f32[32,2048]{1,0:T(8,128)} %get-tuple-element.34.z_ref) | copy-start | bytes 786436
  137.8 38.2 %copy-start.10 = (s32[2]{0:T(128)S(1)}, s32[2]{0:T(128)}, u32[]{:S(2)}) copy-start(s32[2]{0:T(128)} %pad_add_fusion.flags_ref) | copy-start | bytes 28
  151.2 1.6 collective-permute-start.3
  153.8 6.3 %collective-permute-start.4 = (f32[16,2048]{1,0:T(8,128)S(1)}, f32[16,2048]{1,0:T(8,128)S(1)}, u32[]{:S(2)}, u32[]{:S(2)}) collective-permute-start(f32[16,2048]{1,0:T(8,128)S(1)} %add.21), channel_id=1, source_target_pairs={{0,128},{64,192},{128,0},{192,64},{1,129},{65,193},{129,1},{193,65... | collective-permute-start | bytes 393224 | tf_op jit(solution)/shard_map/ppermute | solution.py:412
  155.6 5.8 %collective-permute-start.6 = (f32[1,128]{1,0:T(1,128)S(1)}, f32[1,128]{1,0:T(1,128)S(1)}, u32[]{:S(2)}, u32[]{:S(2)}) collective-permute-start(f32[1,128]{1,0:T(1,128)S(1)} %copy-done.16), channel_id=1, source_target_pairs={{0,128},{64,192},{128,0},{192,64},{1,129},{65,193},{129,1},{193,65... | collective-permute-start | bytes 1544 | tf_op jit(solution)/shard_map/ppermute | solution.py:412
  160.1 15.8 %collective-permute-start.5 = (f32[16,2048]{1,0:T(8,128)S(1)}, f32[16,2048]{1,0:T(8,128)S(1)}, u32[]{:S(2)}, u32[]{:S(2)}) collective-permute-start(f32[16,2048]{1,0:T(8,128)S(1)} %add.22.keep_ref), channel_id=1, source_target_pairs={{0,64},{64,0},{128,192},{192,128},{1,65},{65,1},{129,193},{193,129... | collective-permute-start | bytes 393224 | tf_op jit(solution)/shard_map/ppermute | solution.py:412
  162.0 13.9 %all-to-all-start.7 = ((f32[64,1,128]{2,1,0:T(1,128)}), f32[64,1,128]{2,1,0:T(1,128)S(1)}, u32[]{:S(2)}, u32[]{:S(2)}) async-start(f32[64,1,128]{2,1,0:T(1,128)} %broadcast_in_dim.9), calls=%async_computation.7 | async-start | bytes 65536 | tf_op jit(solution)/shard_map/all_to_all | solution.py:383
  (5 other events, 18.9 us)

commit v3 on v2

v3 whole, which is shorter than its diff:
```python
import functools
import math

import jax
import jax.numpy as jnp
from jax import lax
from jax.experimental import pallas as pl
from jax.experimental.pallas import tpu as pltpu
from jax.sharding import Mesh
from jax.sharding import PartitionSpec as P


CTR = ("ctr_0", "ctr_1", "ctr_2")
NEAR = ("ctr_1", "ctr_2")
FAR = "ctr_0"
RIDGE_TERM = 0.002

bf16, f32 = jnp.bfloat16, jnp.float32
LAST = (((1,), (1,)), ((), ()))
VMEM = pl.BlockSpec(memory_space=pltpu.VMEM)
SMEM = pl.BlockSpec(memory_space=pltpu.SMEM)
ANY = pl.BlockSpec(memory_space=pl.ANY)
LIMIT = 12 << 20


def widened(x, side):
    xf = x.astype(f32)
    n = jnp.sum(xf * xf, axis=1, keepdims=True)
    high = n.astype(bf16).astype(f32)
    rest = n - high
    mid = rest.astype(bf16).astype(f32)
    low = rest - mid
    lane = lax.broadcasted_iota(jnp.int32, x.shape, 1)
    if side == 0:
        extra = jnp.where(lane < 6, 1.0, 0.0)
        extra = jnp.where(lane == 0, high, extra)
        extra = jnp.where(lane == 1, mid, extra)
        extra = jnp.where(lane == 2, low, extra)
        return jnp.concatenate([x, extra.astype(bf16)], axis=1)
    extra = jnp.where(lane < 3, -1.0, 0.0)
    extra = jnp.where(lane == 3, -high, extra)
    extra = jnp.where(lane == 4, -mid, extra)
    extra = jnp.where(lane == 5, -low, extra)
    return jnp.concatenate([(xf * 2.0).astype(bf16), extra.astype(bf16)], axis=1)


def similar(a, b, features):
    t = lax.dot_general(a, b, LAST, preferred_element_type=f32)
    return jnp.exp2(t * (math.log2(math.e) / (2 * features))).astype(bf16)


def chunk_loop(first, count, make, out_ref, buffers, sems):
    def put(i):
        slot = lax.rem(i, 2)
        return pltpu.make_async_copy(buffers.at[slot], out_ref.at[first + i], sems.at[slot])

    def step(i, carry):
        @pl.when(i >= 2)
        def _():
            put(i - 2).wait()

        make(first + i, buffers.at[lax.rem(i, 2)])
        put(i).start()
        return carry

    lax.fori_loop(0, count, step, 0)
    for i in range(max(count - 2, 0), count):
        put(jnp.int32(i)).wait()


def centers_major(cols, wide, points, out):
    right = widened(points, 1)
    for j in range(right.shape[0] // cols):
        cut = slice(j * cols, (j + 1) * cols)
        out[:, cut] = similar(wide[...], right[cut], points.shape[1])


def points_major(cols, wide, points, out):
    left = widened(points, 0)
    for j in range(wide.shape[0] // cols):
        cut = slice(j * cols, (j + 1) * cols)
        out[:, cut] = similar(left, wide[cut], points.shape[1])


def block_kernel(side, first, count, chunk, cols, *refs):
    points_ref, centers_ref = refs[-6:-4]
    out_ref, wide, buffers, sems = refs[-4:]
    wide[...] = widened(centers_ref[...], side)
    fill = points_major if side else centers_major

    def make(i, out):
        rows = pl.ds(pl.multiple_of(i * chunk, chunk), chunk)
        fill(cols, wide, points_ref[rows], out)

    chunk_loop(first, count, make, out_ref, buffers, sems)


def block_part(side, shape, first, count, points, centers, made=None, tie=None, cols=256):
    m_dev, features = centers.shape
    chunk = shape[2] if side == 0 else shape[1]
    extra = [x for x in (made, tie) if x is not None]
    return pl.pallas_call(
        functools.partial(block_kernel, side, first, count, chunk, cols),
        out_shape=jax.ShapeDtypeStruct(shape, bf16),
        in_specs=[ANY] * len(extra) + [VMEM, VMEM],
        out_specs=ANY,
        scratch_shapes=[
            pltpu.VMEM((m_dev, 2 * features), bf16),
            pltpu.VMEM((2, *shape[1:]), bf16),
            pltpu.SemaphoreType.DMA((2,)),
        ],
        input_output_aliases={} if made is None else {0: 0},
        compiler_params=pltpu.CompilerParams(vmem_limit_bytes=44 << 20),
        cost_estimate=pl.CostEstimate(
            flops=4 * m_dev * count * chunk * features,
            bytes_accessed=2 * m_dev * count * chunk,
            transcendentals=m_dev * count * chunk,
        ),
    )(*extra, points, centers)


def head_kernel(centers_ref, dir_ref, out_ref, rows_ref, vals_ref, sems):
    panel, features = rows_ref.shape
    outputs = vals_ref.shape[0]
    first = pltpu.make_async_copy(centers_ref.at[pl.ds(0, panel)], rows_ref, sems.at[0])
    second = pltpu.make_async_copy(dir_ref.at[:, pl.ds(0, panel)], vals_ref, sems.at[1])
    first.start()
    second.start()
    first.wait()
    second.wait()
    per = out_ref.shape[1] // 16
    for g in range(out_ref.shape[0] * per):
        row = 16 * g
        if row < panel:
            x = rows_ref[row : row + 16]
        else:
            b, r = divmod(row - panel, outputs)
            x = vals_ref[r : r + 16, b * features : (b + 1) * features].astype(bf16)
        out_ref[g // per, (g % per) * 16 : (g % per + 1) * 16] = x


def head_payload(centers, direction, panel, ways):
    outputs, features = direction.shape[0], centers.shape[1]
    rows = panel + outputs * panel // features
    return pl.pallas_call(
        head_kernel,
        out_shape=jax.ShapeDtypeStruct((ways, rows // ways, features), bf16),
        in_specs=[ANY, ANY],
        out_specs=VMEM,
        scratch_shapes=[
            pltpu.VMEM((panel, features), bf16),
            pltpu.VMEM((outputs, panel), f32),
            pltpu.SemaphoreType.DMA((2,)),
        ],
        compiler_params=pltpu.CompilerParams(vmem_limit_bytes=60 << 20),
        name="head",
    )(centers, direction)


def spread_kernel(x_ref, *refs):
    out_ref = refs[-1]
    x = x_ref[0] if len(x_ref.shape) == len(out_ref.shape) else x_ref[...]
    for i in range(out_ref.shape[0]):
        out_ref[i] = x


def spread(x, ways):
    shape = x.shape[1:] if len(x.shape) == 3 else x.shape
    return pl.pallas_call(
        spread_kernel,
        out_shape=jax.ShapeDtypeStruct((ways, *shape), x.dtype),
        in_specs=[VMEM],
        out_specs=VMEM,
        compiler_params=pltpu.CompilerParams(vmem_limit_bytes=LIMIT),
        name="spread",
    )(x)


def sum_kernel(x_ref, out_ref):
    total = x_ref[0]
    for i in range(1, x_ref.shape[0]):
        total = total + x_ref[i]
    out_ref[...] = total


def summed(x):
    return pl.pallas_call(
        sum_kernel,
        out_shape=jax.ShapeDtypeStruct(x.shape[1:], x.dtype),
        in_specs=[VMEM],
        out_specs=VMEM,
        compiler_params=pltpu.CompilerParams(vmem_limit_bytes=LIMIT),
        name="summed",
    )(x)


def owned_kernel(scale, x_ref, *refs):
    out_ref = refs[-1]
    total = x_ref[0]
    for i in range(1, x_ref.shape[0]):
        total = total + x_ref[i]
    total = (total * scale).astype(bf16)
    for i in range(out_ref.shape[0]):
        out_ref[i] = total


def owned_copies(x, scale, ways):
    return pl.pallas_call(
        functools.partial(owned_kernel, scale),
        out_shape=jax.ShapeDtypeStruct((ways, *x.shape[1:]), bf16),
        in_specs=[VMEM],
        out_specs=VMEM,
        compiler_params=pltpu.CompilerParams(vmem_limit_bytes=LIMIT),
        name="owned",
    )(x)


def chunk_copies(source, buffer, sems):
    return [
        pltpu.make_async_copy(source.at[i], buffer.at[i], sems.at[i])
        for i in range(buffer.shape[0])
    ]


def panel_kernel(
    cols, flags_ref, centers_ref, head_ref, mine_ref, other_ref, pair_ref, dir_ref, points_ref,
    source_ref, z_ref, rows_ref, high_ref, both_ref, zsq_ref, blocks, made, wide, pinv, zz, sems,
):
    copies = chunk_copies(source_ref, blocks, sems)
    for copy in copies:
        copy.start()
    share = mine_ref.shape[0]
    panel = pinv.shape[0]
    outputs = dir_ref.shape[0]
    features = centers_ref.shape[1]
    at = flags_ref[1]
    core = at % 2
    far = (2 - (at - core)) * share
    pinv[pl.ds(pl.multiple_of(at * share, share), share)] = mine_ref[...]
    pinv[pl.ds(pl.multiple_of((at + 1 - 2 * core) * share, share), share)] = other_ref[...]
    pinv[pl.ds(pl.multiple_of(far + core * share, share), share)] = pair_ref[:share]
    pinv[pl.ds(pl.multiple_of(far + (1 - core) * share, share), share)] = pair_ref[share:]
    head = jnp.concatenate([head_ref[i] for i in range(head_ref.shape[0])], axis=0)
    vals = jnp.concatenate(
        [head[panel + b * outputs : panel + (b + 1) * outputs] for b in range(panel // features)],
        axis=1,
    )
    z1 = lax.dot_general(vals, pinv[...], LAST, preferred_element_type=f32).astype(bf16)
    q = jnp.dot(z1, pinv[...], preferred_element_type=f32).astype(bf16)
    heads = widened(head[:panel], 1)
    tile = panel
    squares = jnp.zeros((outputs, 1), f32)
    for i in range(centers_ref.shape[0] // tile):
        rows = slice(i * tile, (i + 1) * tile)
        wide[rows] = widened(centers_ref[rows], 0)
        kp = similar(wide[rows], heads, features)
        rows_ref[rows] = lax.dot_general(
            kp, mine_ref[...], LAST, preferred_element_type=f32
        ).astype(bf16)
        z = dir_ref[:, rows] - lax.dot_general(q, kp, LAST, preferred_element_type=f32)
        if i == 0:
            z = jnp.where(flags_ref[0] == 0, z1.astype(f32), z)
        z_ref[:, rows] = z
        squares = squares + jnp.sum(z * z, axis=1, keepdims=True)
        high = z.astype(bf16)
        zz[:outputs, rows] = high
        zz[outputs:, rows] = (z - high.astype(f32)).astype(bf16)
    zsq_ref[...] = squares
    chunk = blocks.shape[2]
    per = chunk // 128
    stored = len(copies)
    total = points_ref.shape[0] // chunk
    for i in [*range(stored, total), *range(stored)]:
        if i >= stored:
            centers_major(cols, wide, points_ref[i * chunk : (i + 1) * chunk], made)
            u = jnp.dot(zz[...], made[...], preferred_element_type=f32)
        else:
            copies[i].wait()
            u = jnp.dot(zz[...], blocks[i], preferred_element_type=f32)
        for b in range(per):
            part = u[:, b * 128 : (b + 1) * 128]
            high_ref[i * per + b] = part[:outputs]
            both_ref[i * per + b] = part[:outputs] + part[outputs:]


def panel_step(flags, centers, head, mine, other, pair, direction, points, block, cols=256):
    outputs, m_dev = direction.shape
    share, panel = mine.shape
    count, _, chunk = block.shape
    values = jax.ShapeDtypeStruct((points.shape[0] // 128, outputs, 128), f32)
    return pl.pallas_call(
        functools.partial(panel_kernel, cols),
        out_shape=(
            jax.ShapeDtypeStruct((outputs, m_dev), f32),
            jax.ShapeDtypeStruct((m_dev, share), bf16),
            values,
            values,
            jax.ShapeDtypeStruct((outputs, 1), f32),
        ),
        in_specs=[SMEM] + [VMEM] * 7 + [ANY],
        out_specs=(VMEM,) * 5,
        scratch_shapes=[
            pltpu.VMEM((count, m_dev, chunk), bf16),
            pltpu.VMEM((m_dev, chunk), bf16),
            pltpu.VMEM((m_dev, 2 * centers.shape[1]), bf16),
            pltpu.VMEM((panel, panel), bf16),
            pltpu.VMEM((2 * outputs, m_dev), bf16),
            pltpu.SemaphoreType.DMA((count,)),
        ],
        compiler_params=pltpu.CompilerParams(vmem_limit_bytes=44 << 20),
        cost_estimate=pl.CostEstimate(
            flops=2 * 256 * m_dev * points.shape[0],
            bytes_accessed=2 * m_dev * points.shape[0],
            transcendentals=m_dev * panel,
        ),
        name="panel",
    )(flags, centers, head, mine, other, pair, direction, points, block)


def image_kernel(
    cols, flags_ref, tie_ref, w_ref, centers_ref, points_ref, source_ref, keep_ref, send_ref,
    blocks, made, wide, total, sems,
):
    copies = chunk_copies(source_ref, blocks, sems)
    for copy in copies:
        copy.start()
    wide[...] = widened(centers_ref[...], 1)
    chunk = blocks.shape[1]
    per = chunk // 128
    stored = len(copies)
    count = points_ref.shape[0] // chunk
    total[...] = jnp.zeros_like(total)
    for i in [*range(stored, count), *range(stored)]:
        w = jnp.concatenate([w_ref[i * per + b] for b in range(per)], axis=1)
        if i >= stored:
            points_major(cols, wide, points_ref[i * chunk : (i + 1) * chunk], made)
            total[...] += jnp.dot(w, made[...], preferred_element_type=f32)
        else:
            copies[i].wait()
            total[...] += jnp.dot(w, blocks[i], preferred_element_type=f32)
    half = keep_ref.shape[0]
    mine = pl.multiple_of((flags_ref[1] % 2) * half, half)
    keep_ref[...] = total[pl.ds(mine, half)]
    send_ref[...] = total[pl.ds(half - mine, half)]


def image(flags, tie, w, centers, points, block, cols=256):
    outputs = w.shape[1]
    count, chunk, m_dev = block.shape
    shape = jax.ShapeDtypeStruct((outputs // 2, m_dev), f32)
    return pl.pallas_call(
        functools.partial(image_kernel, cols),
        out_shape=(shape, shape),
        in_specs=[SMEM, VMEM, VMEM, VMEM, VMEM, ANY],
        out_specs=(VMEM, VMEM),
        scratch_shapes=[
            pltpu.VMEM((count, chunk, m_dev), bf16),
            pltpu.VMEM((chunk, m_dev), bf16),
            pltpu.VMEM((m_dev, 2 * centers.shape[1]), bf16),
            pltpu.VMEM((outputs, m_dev), f32),
            pltpu.SemaphoreType.DMA((count,)),
        ],
        compiler_params=pltpu.CompilerParams(vmem_limit_bytes=44 << 20),
        cost_estimate=pl.CostEstimate(
            flops=2 * 256 * points.shape[0] * m_dev,
            bytes_accessed=2 * points.shape[0] * m_dev,
            transcendentals=0,
        ),
        name="image",
    )(flags, tie, w, centers, points, block)


def exchange(x, axis):
    return lax.all_to_all(x, axis, 0, 0, tiled=True)


def products_kernel(scale, ridge, count, w_ref, both_ref, z_squares_ref, res_ref, out_ref):
    outputs = w_ref.shape[1]
    total = jnp.zeros(w_ref.shape[1:], f32)
    for i in range(w_ref.shape[0]):
        total = total + w_ref[i].astype(f32) * both_ref[i]
    mine = jnp.sum(total, axis=1, keepdims=True) * scale + ridge * z_squares_ref[...]
    squares = jnp.sum(res_ref[...] * res_ref[...], axis=1, keepdims=True) * (1.0 / count)
    lane = lax.broadcasted_iota(jnp.int32, total.shape, 1)
    row = lax.broadcasted_iota(jnp.int32, total.shape, 0)
    spread_out = jnp.where(lane == row, mine, jnp.where(lane == row + outputs, squares, 0.0))
    out_ref[...] = jnp.sum(spread_out, axis=0, keepdims=True)


def products(w, both, z_squares, residual, scale, count):
    return pl.pallas_call(
        functools.partial(products_kernel, scale, RIDGE_TERM / count, count),
        out_shape=jax.ShapeDtypeStruct((1, 128), f32),
        in_specs=[VMEM] * 4,
        out_specs=VMEM,
        compiler_params=pltpu.CompilerParams(vmem_limit_bytes=LIMIT),
        name="products",
    )(w, both, z_squares, residual)


def swap(x, bit):
    n = lax.axis_size("pts")
    return lax.ppermute(x, "pts", [(i, i ^ bit) for i in range(n)])


def final_kernel(scale, flags_ref, keep_ref, other_ref, z_ref, res_ref, sums_ref, op_ref, new_ref):
    outputs = z_ref.shape[0]
    half = keep_ref.shape[0]
    sums = jnp.sum(sums_ref[...], axis=0)
    lane = lax.broadcasted_iota(jnp.int32, (outputs, sums.shape[1]), 1)
    row = lax.broadcasted_iota(jnp.int32, (outputs, sums.shape[1]), 0)
    curvature = jnp.sum(jnp.where(lane == row, sums, 0.0), axis=1, keepdims=True)
    squares = jnp.sum(jnp.where(lane == row + outputs, sums, 0.0), axis=1, keepdims=True)
    op_ref[...] = RIDGE_TERM * z_ref[...]
    mine = pl.multiple_of((flags_ref[1] % 2) * half, half)
    op_ref[pl.ds(mine, half)] += keep_ref[...] * scale
    op_ref[pl.ds(half - mine, half)] += other_ref[...] * scale
    new_ref[...] = res_ref[...] - (squares / curvature) * op_ref[...]


def final_step(flags, keep, other, z, residual, sums, scale):
    shape = jax.ShapeDtypeStruct(z.shape, f32)
    return pl.pallas_call(
        functools.partial(final_kernel, scale),
        out_shape=(shape, shape),
        in_specs=[SMEM] + [VMEM] * 5,
        out_specs=(VMEM, VMEM),
        compiler_params=pltpu.CompilerParams(vmem_limit_bytes=LIMIT),
        name="final",
    )(flags, keep, other, z, residual, sums)


def step(points, centers, panel_inverse, direction, residual):
    n_ctr = lax.axis_size(CTR)
    n_near = lax.axis_size(NEAR)
    n_far = lax.axis_size(FAR)
    n_pts = lax.axis_size("pts")
    flags = jnp.stack([lax.axis_index(CTR), lax.axis_index("pts")])
    m_dev, _ = centers.shape
    npg = points.shape[0]
    panel = panel_inverse.shape[1]
    outputs = direction.shape[0]
    w_scale = 1.0 / (2.0 * math.sqrt(m_dev * n_ctr))
    image_scale = 1.0 / (2.0 * math.sqrt(npg * n_pts))

    head = exchange(head_payload(centers, direction, panel, n_near), NEAR)
    shape = (13, m_dev, 512)
    block = None
    for first, count in ((0, 4), (4, 5), (9, 4)):
        block = block_part(0, shape, first, count, points, centers, block)
    other = swap(panel_inverse, 1)
    pair = swap(jnp.concatenate([panel_inverse, other], axis=0), 2)
    head = exchange(spread(head, n_far), FAR)
    head = exchange(spread(head, n_near), NEAR)

    z, panel_rows, high, both, z_squares = panel_step(
        flags, centers, head, panel_inverse, other, pair, direction, points, block
    )

    parts = exchange(high.reshape(n_near, n_far * outputs, 128), NEAR)
    parts = summed(parts).reshape(n_far, outputs, 128)
    parts = exchange(parts, FAR)
    shape = (6, 1024, m_dev)
    block = None
    for first, count in ((0, 4), (4, 2)):
        block = block_part(1, shape, first, count, points, centers, block, z_squares)
    w = exchange(owned_copies(parts, w_scale, n_far), FAR)
    w = exchange(spread(w.reshape(n_far * outputs, 128), n_near), NEAR)
    w = w.reshape(-1, outputs, 128)

    scalars = products(w, both, z_squares, residual, image_scale, n_pts)
    scalars = scalars + swap(scalars, 1)
    keep, send = image(flags, scalars, w, centers, points, block)
    scalars = scalars + swap(scalars, 2)
    sums = jnp.broadcast_to(scalars[None], (n_ctr, *scalars.shape))
    sums = exchange(sums, CTR)
    keep = keep + swap(send, 1)
    keep = keep + swap(keep, 2)
    operator_image, new_residual = final_step(
        flags, keep, swap(keep, 1), z, residual, sums, image_scale
    )
    return (panel_rows, operator_image, new_residual)


def solution(mesh):
    split = Mesh(
        mesh.devices.reshape(mesh.shape["pts"], 8, 2, 4), ("pts", "ctr_0", "ctr_1", "ctr_2")
    )
    placed = (P("pts", None), P(CTR, None), P("pts", None), P(None, CTR), P(None, CTR))
    return jax.shard_map(
        step,
        mesh=split,
        in_specs=placed,
        out_specs=(P(CTR, "pts"), P(None, CTR), P(None, CTR)),
        check_vma=False,
    )
```

time: 178 us -> 167 us (0.938)
  blocking collectives: 38.3 us -> 57.3 us
  Pallas kernels: 78.8 us -> 61.1 us
  waiting for transfers between devices: 13.6 us -> 4.78 us
  starting transfers between devices: 41 us -> 36.3 us
  local copies, waits for them, and re-layouts: 2.93 us -> 4.86 us
    all_to_all x3 -> x4, blocking collectives: 38.3 us -> 57.3 us  [exchange(): return lax.all_to_all(x, axis, 0, 0, tiled=True)]
    pallas_call x7, Pallas kernels: 73.2 us -> 55.4 us  [the longest x5 32.5 us: block_part(): pl.pallas_call(functools.partial(block_kernel, side, first, count, chunk,...]
    all_to_all x5 -> x4, waiting for transfers between devices: 8.26 us -> 0.01 us  [exchange(): return lax.all_to_all(x, axis, 0, 0, tiled=True)]
    all_to_all x5 -> x4, starting transfers between devices: 26.1 us -> 19.6 us  [exchange(): return lax.all_to_all(x, axis, 0, 0, tiled=True)]
    unnamed x34 -> x30, local copies, waits for them, and re-layouts: 2.31 us -> 4.84 us
    ppermute x7, starting transfers between devices: 14.8 us -> 16.7 us  [swap(): return lax.ppermute(x, 'pts', [(i, i ^ bit) for i in range(n)])]
  transfers between devices with their start and end apart: 12 -> 11, of which waited for: 5 -> 2; matrix products, arithmetic and copies ran while one was open for 1% -> 1% of each run, Pallas kernels for 27% -> 21%
where the time goes in v3:
time: 167 us; the launch traced here: 166 us
  Pallas kernels  61.1 us (37%)
  blocking collectives  57.3 us (34%)
  starting transfers between devices  36.3 us (22%)
  local copies, waits for them, and re-layouts  4.86 us (3%)
  waiting for transfers between devices  4.78 us (3%)
    all_to_all x4, blocking collectives, exchange(): return lax.all_to_all(x, axis, 0, 0, tiled=True)  57.3 us
    pallas_call x5, Pallas kernels, block_part(): pl.pallas_call(functools.partial(block_kernel, side, first, count, chunk,...  32.5 us
    all_to_all x4, starting transfers between devices, exchange(): return lax.all_to_all(x, axis, 0, 0, tiled=True)  19.6 us
    ppermute x7, starting transfers between devices, swap(): return lax.ppermute(x, 'pts', [(i, i ^ bit) for i in range(n)])  16.7 us
    pallas_call x1, Pallas kernels, panel_step(): pl.pallas_call(functools.partial(panel_kernel, cols), out_shape=(jax.Shap...  13 us
    pallas_call x1, Pallas kernels, image(): pl.pallas_call(functools.partial(image_kernel, cols), out_shape=(shape, s...  9.9 us
    unnamed x30, local copies, waits for them, and re-layouts  4.84 us
    ppermute x7, waiting for transfers between devices, swap(): return lax.ppermute(x, 'pts', [(i, i ^ bit) for i in range(n)])  4.77 us
  transfers between devices with their start and end apart: 11, of which 2 were waited for; matrix products, arithmetic and copies ran while one was open for 1% of the time, Pallas kernels for 21%

profile of v3, /device:TPU:1, one launch (start us, length us, event | category | flops | bytes accessed | tf_op | source)
XLA Modules:
  0.0 166.1 jit_solution(17413378798116486139)
XLA Ops:
  0.6 3.3 %collective-permute-start = (bf16[128,512]{1,0:T(8,128)(2,1)}, bf16[128,512]{1,0:T(8,128)(2,1)S(1)}, u32[]{:S(2)}, u32[]{:S(2)}) collective-permute-start(bf16[128,512]{1,0:T(8,128)(2,1)} %mine_ref.1), channel_id=1, source_target_pairs={{0,64},{64,0},{128,192},{192,128},{1,65},{65,1},{129,193},{193,129... | collective-permute-start | bytes 393224 | tf_op jit(solution)/shard_map/ppermute | solution.py:403
  3.9 1.6 head.1
  5.5 3.4 %all-to-all-start = ((bf16[8,80,128]{2,1,0:T(8,128)(2,1)}), bf16[8,80,128]{2,1,0:T(8,128)(2,1)S(1)}, u32[]{:S(2)}, u32[]{:S(2)}) async-start(bf16[8,80,128]{2,1,0:T(8,128)(2,1)} %head.1), calls=%async_computation | async-start | bytes 327680 | tf_op jit(solution)/shard_map/all_to_all | solution.py:374
  9.0 1.6 copy-done
  11.6 5.8 %shard_map.76.refs_0_ = bf16[13,2048,512]{2,1,0:T(8,128)(2,1)} custom-call(bf16[8192,128]{1,0:T(8,128)(2,1)S(1)} %copy-done, bf16[2048,128]{1,0:T(8,128)(2,1)S(1)} %copy-done.2), custom_call_target="tpu_custom_call" | custom-call | flops 2147483648 | bytes 8388608 | tf_op jit(solution)/shard_map/pallas_call | solution.py:102
  18.1 8.2 %all-to-all-start.1 = ((bf16[8,80,128]{2,1,0:T(8,128)(2,1)}), bf16[8,80,128]{2,1,0:T(8,128)(2,1)S(1)}, u32[]{:S(2)}, u32[]{:S(2)}) async-start(bf16[8,80,128]{2,1,0:T(8,128)(2,1)} %spread.3), calls=%async_computation.1 | async-start | bytes 327680 | tf_op jit(solution)/shard_map/all_to_all | solution.py:374
  26.3 7.1 %shard_map.77.refs_0_ = bf16[13,2048,512]{2,1,0:T(8,128)(2,1)} custom-call(bf16[13,2048,512]{2,1,0:T(8,128)(2,1)} %shard_map.76.refs_0_, bf16[8192,128]{1,0:T(8,128)(2,1)S(1)} %copy-done.1, bf16[2048,128]{1,0:T(8,128)(2,1)S(1)} %copy-done.3), custom_call_target="tpu_custom_call", output_to_operand_aliasing={{}: (0, {})} | custom-call | flops 2684354560 | bytes 10485760 | tf_op jit(solution)/shard_map/pallas_call | solution.py:102
  34.2 2.5 %collective-permute-start.1 = (bf16[256,512]{1,0:T(8,128)(2,1)}, bf16[256,512]{1,0:T(8,128)(2,1)}, u32[]{:S(2)}, u32[]{:S(2)}) collective-permute-start(bf16[256,512]{1,0:T(8,128)(2,1)} %pad_maximum_fusion), channel_id=1, source_target_pairs={{0,128},{64,192},{128,0},{192,64},{1,129},{65,193},{129,1},{193,65... | collective-permute-start | bytes 786440 | tf_op jit(solution)/shard_map/ppermute | solution.py:403
  37.4 4.5 %all-to-all-start.2 = ((bf16[8,80,128]{2,1,0:T(8,128)(2,1)}), bf16[8,80,128]{2,1,0:T(8,128)(2,1)S(1)}, u32[]{:S(2)}, u32[]{:S(2)}) async-start(bf16[8,80,128]{2,1,0:T(8,128)(2,1)} %spread.4), calls=%async_computation.2 | async-start | bytes 327680 | tf_op jit(solution)/shard_map/all_to_all | solution.py:374
  41.9 5.8 %shard_map.78.source_ref = bf16[13,2048,512]{2,1,0:T(8,128)(2,1)} custom-call(bf16[13,2048,512]{2,1,0:T(8,128)(2,1)} %shard_map.77.refs_0_, bf16[8192,128]{1,0:T(8,128)(2,1)S(1)} %copy-done.1, bf16[2048,128]{1,0:T(8,128)(2,1)S(1)} %copy-done.3), custom_call_target="tpu_custom_call", output_to_operand_aliasing={{}: (0, {})} | custom-call | flops 2147483648 | bytes 8388608 | tf_op jit(solution)/shard_map/pallas_call | solution.py:102
  48.8 13.0 %panel.1 = (f32[32,2048]{1,0:T(8,128)S(1)}, bf16[2048,128]{1,0:T(8,128)(2,1)}, f32[64,32,128]{2,1,0:T(8,128)S(1)}, f32[64,32,128]{2,1,0:T(8,128)S(1)}, f32[32,1]{1,0:T(8,128)S(1)}) custom-call(s32[2]{0:T(128)S(1)} %pad_add_fusion.flags_ref, bf16[2048,128]{1,0:T(8,128)(2,1)S(1)} %copy-done.3, bf16[8,80,128]{2,1,0:T(8,128)(2,1)S(1)} %all-to-all-done.2.head_ref, ...), custom_call_target="tpu_custom_call" | custom-call | flops 8589934592 | bytes 33554432 | tf_op jit(solution)/shard_map/panel/pallas_call | solution.py:291
  61.8 17.9 %all_to_all.40.x_ref = f32[8,256,128]{2,1,0:T(8,128)S(1)} all-to-all(f32[8,256,128]{2,1,0:T(8,128)S(1)} %bitcast.10), channel_id=1, replica_groups=mesh['pts'=4,'ctr_0'=8,'ctr_1'=2,'ctr_2'=4] {'ctr_1','ctr_2'}, dimensions={0} | all-to-all | bytes 2097152 | tf_op jit(solution)/shard_map/all_to_all | solution.py:374
  79.8 14.3 %all_to_all.41.x_ref = f32[8,32,128]{2,1,0:T(8,128)S(1)} all-to-all(f32[8,32,128]{2,1,0:T(8,128)S(1)} %bitcast.11), channel_id=1, replica_groups=mesh['pts'=4,'ctr_0'=8,'ctr_1'=2,'ctr_2'=4] {'ctr_0'}, dimensions={0} | all-to-all | bytes 262144 | tf_op jit(solution)/shard_map/all_to_all | solution.py:374
  94.1 9.6 %all_to_all.42 = bf16[8,32,128]{2,1,0:T(8,128)(2,1)S(1)} all-to-all(bf16[8,32,128]{2,1,0:T(8,128)(2,1)S(1)} %owned.1), channel_id=1, replica_groups=mesh['pts'=4,'ctr_0'=8,'ctr_1'=2,'ctr_2'=4] {'ctr_0'}, dimensions={0} | all-to-all | bytes 131072 | tf_op jit(solution)/shard_map/all_to_all | solution.py:374
  104.5 3.5 %all-to-all-start.6 = ((bf16[8,256,128]{2,1,0:T(8,128)(2,1)}), bf16[8,256,128]{2,1,0:T(8,128)(2,1)S(1)}, u32[]{:S(2)}, u32[]{:S(2)}) async-start(bf16[8,256,128]{2,1,0:T(8,128)(2,1)} %spread.5), calls=%async_computation.6 | async-start | bytes 1048576 | tf_op jit(solution)/shard_map/all_to_all | solution.py:374
  108.0 8.5 %shard_map.79.refs_0_ = bf16[6,1024,2048]{2,1,0:T(8,128)(2,1)} custom-call(f32[32,1]{1,0:T(8,128)S(1)} %get-tuple-element.15.z_squares_ref.refs_0_.refs_1_, bf16[8192,128]{1,0:T(8,128)(2,1)S(1)} %copy-done.1, bf16[2048,128]{1,0:T(8,128)(2,1)S(1)} %copy-done.3), custom_call_target="tpu_custom_call" | custom-call | flops 4294967296 | bytes 16777216 | tf_op jit(solution)/shard_map/pallas_call | solution.py:102
  118.1 6.7 %collective-permute-start.2 = (f32[1,128]{1,0:T(1,128)S(1)}, f32[1,128]{1,0:T(1,128)S(1)}, u32[]{:S(2)}, u32[]{:S(2)}) collective-permute-start(f32[1,128]{1,0:T(1,128)S(1)} %products.1), channel_id=1, source_target_pairs={{0,64},{64,0},{128,192},{192,128},{1,65},{65,1},{129,193},{193,129... | collective-permute-start | bytes 1544 | tf_op jit(solution)/shard_map/ppermute | solution.py:403
  124.8 5.3 %shard_map.80.source_ref = bf16[6,1024,2048]{2,1,0:T(8,128)(2,1)} custom-call(bf16[6,1024,2048]{2,1,0:T(8,128)(2,1)} %shard_map.79.refs_0_, f32[32,1]{1,0:T(8,128)S(1)} %get-tuple-element.15.z_squares_ref.refs_0_.refs_1_, bf16[8192,128]{1,0:T(8,128)(2,1)S(1)} %copy-done.1, bf16[2048,128]{1,0:T(8,128)(2,1)S(1)} %copy-done.3), custom_call_target="tpu_custom_call", output_to_operand_aliasing={{}: (0, {})} | custom-call | flops 2147483648 | bytes 8388608 | tf_op jit(solution)/shard_map/pallas_call | solution.py:102
  130.1 9.9 %image.1 = (f32[16,2048]{1,0:T(8,128)S(1)}, f32[16,2048]{1,0:T(8,128)S(1)}) custom-call(s32[2]{0:T(128)S(1)} %copy-done.14, f32[1,128]{1,0:T(1,128)S(1)} %add.20.tie_ref, bf16[64,32,128]{2,1,0:T(8,128)(2,1)S(1)} %bitcast.9, bf16[2048,128]{1,0:T(8,128)(2,1)S(1)} %copy-done.3, bf16[8192,128]{1,0:T(8,128)(2,1)S(1)} %copy-done.1, ...), custom_call_target="tpu_custom_call" | custom-call | flops 8589934592 | bytes 33554432 | tf_op jit(solution)/shard_map/image/pallas_call | solution.py:351
  140.1 1.3 collective-permute-done.3
  141.5 1.8 %collective-permute-start.4 = (f32[16,2048]{1,0:T(8,128)S(1)}, f32[16,2048]{1,0:T(8,128)S(1)}, u32[]{:S(2)}, u32[]{:S(2)}) collective-permute-start(f32[16,2048]{1,0:T(8,128)S(1)} %add.21), channel_id=1, source_target_pairs={{0,128},{64,192},{128,0},{192,64},{1,129},{65,193},{129,1},{193,65... | collective-permute-start | bytes 393224 | tf_op jit(solution)/shard_map/ppermute | solution.py:403
  144.5 3.4 %collective-permute-done.4 = f32[16,2048]{1,0:T(8,128)S(1)} collective-permute-done((f32[16,2048]{1,0:T(8,128)S(1)}, f32[16,2048]{1,0:T(8,128)S(1)}, u32[]{:S(2)}, u32[]{:S(2)}) %collective-permute-start.4) | collective-permute-done | bytes 131104 | tf_op jit(solution)/shard_map/ppermute | solution.py:403
  149.1 15.5 %all_to_all.43.sums_ref = f32[64,1,128]{2,1,0:T(1,128)S(1)} all-to-all(f32[64,1,128]{2,1,0:T(1,128)S(1)} %broadcast_in_dim.9), channel_id=1, replica_groups=mesh['pts'=4,'ctr_0'=8,'ctr_1'=2,'ctr_2'=4] {'ctr_0','ctr_1','ctr_2'}, dimensions={0} | all-to-all | bytes 65536 | tf_op jit(solution)/shard_map/all_to_all | solution.py:374
  164.6 1.5 final.1
  (54 shorter events, 9.2 us)
Async XLA Ops:
  0.6 25.7 %copy-start.3 = (bf16[2048,128]{1,0:T(8,128)(2,1)S(1)}, bf16[2048,128]{1,0:T(8,128)(2,1)}, u32[]{:S(2)}) copy-start(bf16[2048,128]{1,0:T(8,128)(2,1)} %centers_ref.5) | copy-start | bytes 1572868
  0.6 32.8 %collective-permute-start = (bf16[128,512]{1,0:T(8,128)(2,1)}, bf16[128,512]{1,0:T(8,128)(2,1)S(1)}, u32[]{:S(2)}, u32[]{:S(2)}) collective-permute-start(bf16[128,512]{1,0:T(8,128)(2,1)} %mine_ref.1), channel_id=1, source_target_pairs={{0,64},{64,0},{128,192},{192,128},{1,65},{65,1},{129,193},{193,129... | collective-permute-start | bytes 393224 | tf_op jit(solution)/shard_map/ppermute | solution.py:403
  5.5 11.9 %all-to-all-start = ((bf16[8,80,128]{2,1,0:T(8,128)(2,1)}), bf16[8,80,128]{2,1,0:T(8,128)(2,1)S(1)}, u32[]{:S(2)}, u32[]{:S(2)}) async-start(bf16[8,80,128]{2,1,0:T(8,128)(2,1)} %head.1), calls=%async_computation | async-start | bytes 327680 | tf_op jit(solution)/shard_map/all_to_all | solution.py:374
  9.0 1.6 copy-start
  11.6 14.7 %copy-start.1 = (bf16[8192,128]{1,0:T(8,128)(2,1)S(1)}, bf16[8192,128]{1,0:T(8,128)(2,1)}, u32[]{:S(2)}) copy-start(bf16[8192,128]{1,0:T(8,128)(2,1)} %points_ref.3) | copy-start | bytes 6291460
  18.1 18.5 %all-to-all-start.1 = ((bf16[8,80,128]{2,1,0:T(8,128)(2,1)}), bf16[8,80,128]{2,1,0:T(8,128)(2,1)S(1)}, u32[]{:S(2)}, u32[]{:S(2)}) async-start(bf16[8,80,128]{2,1,0:T(8,128)(2,1)} %spread.3), calls=%async_computation.1 | async-start | bytes 327680 | tf_op jit(solution)/shard_map/all_to_all | solution.py:374
  26.3 7.1 %copy-start.10 = (bf16[128,512]{1,0:T(8,128)(2,1)S(1)}, bf16[128,512]{1,0:T(8,128)(2,1)}, u32[]{:S(2)}) copy-start(bf16[128,512]{1,0:T(8,128)(2,1)} %mine_ref.1) | copy-start | bytes 393220
  33.5 3.9 %copy-start.11 = (bf16[128,512]{1,0:T(8,128)(2,1)}, bf16[128,512]{1,0:T(8,128)(2,1)S(1)}, u32[]{:S(2)}) copy-start(bf16[128,512]{1,0:T(8,128)(2,1)S(1)} %collective-permute-done.other_ref) | copy-start | bytes 393220
  34.2 13.6 %collective-permute-start.1 = (bf16[256,512]{1,0:T(8,128)(2,1)}, bf16[256,512]{1,0:T(8,128)(2,1)}, u32[]{:S(2)}, u32[]{:S(2)}) collective-permute-start(bf16[256,512]{1,0:T(8,128)(2,1)} %pad_maximum_fusion), channel_id=1, source_target_pairs={{0,128},{64,192},{128,0},{192,64},{1,129},{65,193},{129,1},{193,65... | collective-permute-start | bytes 786440 | tf_op jit(solution)/shard_map/ppermute | solution.py:403
  37.4 10.5 %all-to-all-start.2 = ((bf16[8,80,128]{2,1,0:T(8,128)(2,1)}), bf16[8,80,128]{2,1,0:T(8,128)(2,1)S(1)}, u32[]{:S(2)}, u32[]{:S(2)}) async-start(bf16[8,80,128]{2,1,0:T(8,128)(2,1)} %spread.4), calls=%async_computation.2 | async-start | bytes 327680 | tf_op jit(solution)/shard_map/all_to_all | solution.py:374
  41.9 5.9 %copy-start.7 = (f32[32,2048]{1,0:T(8,128)S(1)}, f32[32,2048]{1,0:T(8,128)}, u32[]{:S(2)}) copy-start(f32[32,2048]{1,0:T(8,128)} %dir_ref.3) | copy-start | bytes 786436
  47.8 56.7 %copy-start.13 = (s32[2]{0:T(128)}, s32[2]{0:T(128)S(1)}, u32[]{:S(2)}) copy-start(s32[2]{0:T(128)S(1)} %pad_add_fusion.flags_ref) | copy-start | bytes 28
  47.8 68.7 %copy-start.6 = (f32[32,2048]{1,0:T(8,128)S(1)}, f32[32,2048]{1,0:T(8,128)}, u32[]{:S(2)}) copy-start(f32[32,2048]{1,0:T(8,128)} %res_ref.3) | copy-start | bytes 786436
  61.8 18.0 %copy-start.4 = (f32[64,32,128]{2,1,0:T(8,128)}, f32[64,32,128]{2,1,0:T(8,128)S(1)}, u32[]{:S(2)}) copy-start(f32[64,32,128]{2,1,0:T(8,128)S(1)} %get-tuple-element.14.both_ref) | copy-start | bytes 3145732
  61.8 41.9 %copy-start.8 = (f32[32,2048]{1,0:T(8,128)}, f32[32,2048]{1,0:T(8,128)S(1)}, u32[]{:S(2)}) copy-start(f32[32,2048]{1,0:T(8,128)S(1)} %get-tuple-element.18.z_ref) | copy-start | bytes 786436
  104.5 12.0 %all-to-all-start.6 = ((bf16[8,256,128]{2,1,0:T(8,128)(2,1)}), bf16[8,256,128]{2,1,0:T(8,128)(2,1)S(1)}, u32[]{:S(2)}, u32[]{:S(2)}) async-start(bf16[8,256,128]{2,1,0:T(8,128)(2,1)} %spread.5), calls=%async_computation.6 | async-start | bytes 1048576 | tf_op jit(solution)/shard_map/all_to_all | solution.py:374
  116.6 1.2 copy-start.5
  117.8 12.3 %copy-start.14 = (s32[2]{0:T(128)S(1)}, s32[2]{0:T(128)}, u32[]{:S(2)}) copy-start(s32[2]{0:T(128)} %copy-done.13) | copy-start | bytes 28
  118.1 11.9 %collective-permute-start.2 = (f32[1,128]{1,0:T(1,128)S(1)}, f32[1,128]{1,0:T(1,128)S(1)}, u32[]{:S(2)}, u32[]{:S(2)}) collective-permute-start(f32[1,128]{1,0:T(1,128)S(1)} %products.1), channel_id=1, source_target_pairs={{0,64},{64,0},{128,192},{192,128},{1,65},{65,1},{129,193},{193,129... | collective-permute-start | bytes 1544 | tf_op jit(solution)/shard_map/ppermute | solution.py:403
  130.1 34.5 %copy-start.9 = (f32[32,2048]{1,0:T(8,128)S(1)}, f32[32,2048]{1,0:T(8,128)}, u32[]{:S(2)}) copy-start(f32[32,2048]{1,0:T(8,128)} %copy-done.8) | copy-start | bytes 786436
  140.0 1.4 collective-permute-start.3
  141.5 6.5 %collective-permute-start.4 = (f32[16,2048]{1,0:T(8,128)S(1)}, f32[16,2048]{1,0:T(8,128)S(1)}, u32[]{:S(2)}, u32[]{:S(2)}) collective-permute-start(f32[16,2048]{1,0:T(8,128)S(1)} %add.21), channel_id=1, source_target_pairs={{0,128},{64,192},{128,0},{192,64},{1,129},{65,193},{129,1},{193,65... | collective-permute-start | bytes 393224 | tf_op jit(solution)/shard_map/ppermute | solution.py:403
  143.3 5.8 %collective-permute-start.6 = (f32[1,128]{1,0:T(1,128)S(1)}, f32[1,128]{1,0:T(1,128)S(1)}, u32[]{:S(2)}, u32[]{:S(2)}) collective-permute-start(f32[1,128]{1,0:T(1,128)S(1)} %add.20.tie_ref), channel_id=1, source_target_pairs={{0,128},{64,192},{128,0},{192,64},{1,129},{65,193},{129,1},{193,65... | collective-permute-start | bytes 1544 | tf_op jit(solution)/shard_map/ppermute | solution.py:403
  148.0 16.6 %collective-permute-start.5 = (f32[16,2048]{1,0:T(8,128)S(1)}, f32[16,2048]{1,0:T(8,128)S(1)}, u32[]{:S(2)}, u32[]{:S(2)}) collective-permute-start(f32[16,2048]{1,0:T(8,128)S(1)} %add.22.keep_ref), channel_id=1, source_target_pairs={{0,64},{64,0},{128,192},{192,128},{1,65},{65,1},{129,193},{193,129... | collective-permute-start | bytes 393224 | tf_op jit(solution)/shard_map/ppermute | solution.py:403
  (2 other events, 2.0 us)

commit v4 on v3

--- a/solution.py
+++ b/solution.py
@@ -21,6 +21,8 @@
 SMEM = pl.BlockSpec(memory_space=pltpu.SMEM)
 ANY = pl.BlockSpec(memory_space=pl.ANY)
 LIMIT = 12 << 20
+CHUNK = 1024
+WIDTH = 256
 
 
 def widened(x, side):
@@ -49,72 +51,80 @@
     return jnp.exp2(t * (math.log2(math.e) / (2 * features))).astype(bf16)
 
 
-def chunk_loop(first, count, make, out_ref, buffers, sems):
-    def put(i):
+def tiles(side, wide, points):
+    features = points.shape[1]
+    extended = widened(points, 1 - side)
+    columns = extended if side == 0 else wide
+    for j in range(columns.shape[0] // WIDTH):
+        cut = columns[j * WIDTH : (j + 1) * WIDTH]
+        yield similar(wide[...], cut, features) if side == 0 else similar(extended, cut, features)
+
+
+def block_kernel(side, first, count, *refs):
+    points_ref, centers_ref = refs[-9:-7]
+    out_ref, points_buf, centers_buf, wide, buffers, sems, in_sems = refs[-7:]
+    per = buffers.shape[1]
+    load = points_buf.shape[0]
+    loads = [
+        pltpu.make_async_copy(centers_ref, centers_buf, in_sems.at[0]),
+        pltpu.make_async_copy(
+            points_ref.at[pl.ds(first * CHUNK, load)], points_buf, in_sems.at[1]
+        ),
+    ]
+    for copy in loads:
+        copy.start()
+    loads[0].wait()
+    wide[...] = widened(centers_buf[...], side)
+    loads[1].wait()
+
+    def put(i, j):
         slot = lax.rem(i, 2)
-        return pltpu.make_async_copy(buffers.at[slot], out_ref.at[first + i], sems.at[slot])
+        return pltpu.make_async_copy(
+            buffers.at[slot, j], out_ref.at[(first + i) * per + j], sems.at[slot, j]
+        )
 
     def step(i, carry):
-        @pl.when(i >= 2)
-        def _():
-            put(i - 2).wait()
-
-        make(first + i, buffers.at[lax.rem(i, 2)])
-        put(i).start()
+        rows = pl.ds(pl.multiple_of(i * CHUNK, CHUNK), CHUNK)
+        for j, tile in enumerate(tiles(side, wide, points_buf[rows])):
+            if count > 2:
+
+                @pl.when(i >= 2)
+                def _(j=j):
+                    put(i - 2, j).wait()
+
+            buffers[lax.rem(i, 2), j] = tile
+            put(i, j).start()
         return carry
 
     lax.fori_loop(0, count, step, 0)
     for i in range(max(count - 2, 0), count):
-        put(jnp.int32(i)).wait()
-
-
-def centers_major(cols, wide, points, out):
-    right = widened(points, 1)
-    for j in range(right.shape[0] // cols):
-        cut = slice(j * cols, (j + 1) * cols)
-        out[:, cut] = similar(wide[...], right[cut], points.shape[1])
-
-
-def points_major(cols, wide, points, out):
-    left = widened(points, 0)
-    for j in range(wide.shape[0] // cols):
-        cut = slice(j * cols, (j + 1) * cols)
-        out[:, cut] = similar(left, wide[cut], points.shape[1])
-
-
-def block_kernel(side, first, count, chunk, cols, *refs):
-    points_ref, centers_ref = refs[-6:-4]
-    out_ref, wide, buffers, sems = refs[-4:]
-    wide[...] = widened(centers_ref[...], side)
-    fill = points_major if side else centers_major
-
-    def make(i, out):
-        rows = pl.ds(pl.multiple_of(i * chunk, chunk), chunk)
-        fill(cols, wide, points_ref[rows], out)
-
-    chunk_loop(first, count, make, out_ref, buffers, sems)
-
-
-def block_part(side, shape, first, count, points, centers, made=None, tie=None, cols=256):
+        for j in range(per):
+            put(jnp.int32(i), j).wait()
+
+
+def block_part(side, chunks, first, count, points, centers, made=None, tie=None):
     m_dev, features = centers.shape
-    chunk = shape[2] if side == 0 else shape[1]
+    per, rows = (CHUNK // WIDTH, m_dev) if side == 0 else (m_dev // WIDTH, CHUNK)
     extra = [x for x in (made, tie) if x is not None]
     return pl.pallas_call(
-        functools.partial(block_kernel, side, first, count, chunk, cols),
-        out_shape=jax.ShapeDtypeStruct(shape, bf16),
-        in_specs=[ANY] * len(extra) + [VMEM, VMEM],
+        functools.partial(block_kernel, side, first, count),
+        out_shape=jax.ShapeDtypeStruct((chunks * per, rows, WIDTH), bf16),
+        in_specs=[ANY] * (len(extra) + 2),
         out_specs=ANY,
         scratch_shapes=[
+            pltpu.VMEM((count * CHUNK, features), bf16),
+            pltpu.VMEM((m_dev, features), bf16),
             pltpu.VMEM((m_dev, 2 * features), bf16),
-            pltpu.VMEM((2, *shape[1:]), bf16),
+            pltpu.VMEM((2, per, rows, WIDTH), bf16),
+            pltpu.SemaphoreType.DMA((2, per)),
             pltpu.SemaphoreType.DMA((2,)),
         ],
         input_output_aliases={} if made is None else {0: 0},
-        compiler_params=pltpu.CompilerParams(vmem_limit_bytes=44 << 20),
+        compiler_params=pltpu.CompilerParams(vmem_limit_bytes=60 << 20),
         cost_estimate=pl.CostEstimate(
-            flops=4 * m_dev * count * chunk * features,
-            bytes_accessed=2 * m_dev * count * chunk,
-            transcendentals=m_dev * count * chunk,
+            flops=4 * m_dev * count * CHUNK * features,
+            bytes_accessed=2 * m_dev * count * CHUNK,
+            transcendentals=m_dev * count * CHUNK,
         ),
     )(*extra, points, centers)
 
@@ -183,12 +193,15 @@
     out_ref[...] = total
 
 
-def summed(x):
+def summed(x, steps=4):
+    ways, rows, lanes = x.shape
+    block = rows // steps
     return pl.pallas_call(
         sum_kernel,
-        out_shape=jax.ShapeDtypeStruct(x.shape[1:], x.dtype),
-        in_specs=[VMEM],
-        out_specs=VMEM,
+        out_shape=jax.ShapeDtypeStruct((rows, lanes), x.dtype),
+        grid=(steps,),
+        in_specs=[pl.BlockSpec((ways, block, lanes), lambda i: (0, i, 0))],
+        out_specs=pl.BlockSpec((block, lanes), lambda i: (i, 0)),
         compiler_params=pltpu.CompilerParams(vmem_limit_bytes=LIMIT),
         name="summed",
     )(x)
@@ -215,20 +228,24 @@
     )(x)
 
 
-def chunk_copies(source, buffer, sems):
-    return [
-        pltpu.make_async_copy(source.at[i], buffer.at[i], sems.at[i])
-        for i in range(buffer.shape[0])
-    ]
+def chunk_copy(source, buffer, sems, i):
+    per = buffer.shape[0] // sems.shape[0]
+    span = pl.ds(i * per, per)
+    return pltpu.make_async_copy(source.at[span], buffer.at[span], sems.at[i])
 
 
 def panel_kernel(
-    cols, flags_ref, centers_ref, head_ref, mine_ref, other_ref, pair_ref, dir_ref, points_ref,
-    source_ref, z_ref, rows_ref, high_ref, both_ref, zsq_ref, blocks, made, wide, pinv, zz, sems,
+    flags_ref, centers_ref, head_ref, mine_ref, other_ref, pair_ref, dir_ref, points_ref,
+    source_ref, z_ref, rows_ref, high_out, both_out, zsq_ref, blocks, made, wide, pinv, zz,
+    points_buf, high_ref, both_ref, sems, points_sem, out_sems,
 ):
-    copies = chunk_copies(source_ref, blocks, sems)
-    for copy in copies:
-        copy.start()
+    stored = sems.shape[0]
+    local = pltpu.make_async_copy(
+        points_ref.at[pl.ds(stored * CHUNK, points_buf.shape[0])], points_buf, points_sem
+    )
+    local.start()
+    for i in range(stored):
+        chunk_copy(source_ref, blocks, sems, i).start()
     share = mine_ref.shape[0]
     panel = pinv.shape[0]
     outputs = dir_ref.shape[0]
@@ -266,30 +283,57 @@
         zz[:outputs, rows] = high
         zz[outputs:, rows] = (z - high.astype(f32)).astype(bf16)
     zsq_ref[...] = squares
-    chunk = blocks.shape[2]
-    per = chunk // 128
-    stored = len(copies)
-    total = points_ref.shape[0] // chunk
-    for i in [*range(stored, total), *range(stored)]:
-        if i >= stored:
-            centers_major(cols, wide, points_ref[i * chunk : (i + 1) * chunk], made)
-            u = jnp.dot(zz[...], made[...], preferred_element_type=f32)
-        else:
-            copies[i].wait()
-            u = jnp.dot(zz[...], blocks[i], preferred_element_type=f32)
-        for b in range(per):
-            part = u[:, b * 128 : (b + 1) * 128]
-            high_ref[i * per + b] = part[:outputs]
-            both_ref[i * per + b] = part[:outputs] + part[outputs:]
-
-
-def panel_step(flags, centers, head, mine, other, pair, direction, points, block, cols=256):
+    local.wait()
+    total = points_ref.shape[0] // CHUNK
+    width = WIDTH // 128
+    per = CHUNK // WIDTH
+
+    def puts(i):
+        span = pl.ds(i * per * width, per * width)
+        return [
+            pltpu.make_async_copy(buf.at[span], out.at[span], out_sems.at[i, k])
+            for k, (buf, out) in enumerate(((high_ref, high_out), (both_ref, both_out)))
+        ]
+
+    def use(i, source, at):
+        for j in range(per):
+            u = jnp.dot(zz[...], source[at + j], preferred_element_type=f32)
+            for b in range(width):
+                part = u[:, b * 128 : (b + 1) * 128]
+                row = (i * per + j) * width + b
+                high_ref[row] = part[:outputs]
+                both_ref[row] = part[:outputs] + part[outputs:]
+        for put in puts(i):
+            put.start()
+
+    def local_step(i, carry):
+        rows = pl.ds(pl.multiple_of((i - stored) * CHUNK, CHUNK), CHUNK)
+        for j, tile in enumerate(tiles(0, wide, points_buf[rows])):
+            made[j] = tile
+        use(i, made, 0)
+        return carry
+
+    def stored_step(i, carry):
+        chunk_copy(source_ref, blocks, sems, i).wait()
+        use(i, blocks, i * per)
+        return carry
+
+    lax.fori_loop(stored, total, local_step, 0)
+    lax.fori_loop(0, stored, stored_step, 0)
+    for i in range(total):
+        for put in puts(i):
+            put.wait()
+
+
+def panel_step(flags, centers, head, mine, other, pair, direction, points, block):
     outputs, m_dev = direction.shape
     share, panel = mine.shape
-    count, _, chunk = block.shape
+    features = centers.shape[1]
+    count = points.shape[0] // CHUNK
+    stored = block.shape[0] * WIDTH // CHUNK
     values = jax.ShapeDtypeStruct((points.shape[0] // 128, outputs, 128), f32)
     return pl.pallas_call(
-        functools.partial(panel_kernel, cols),
+        panel_kernel,
         out_shape=(
             jax.ShapeDtypeStruct((outputs, m_dev), f32),
             jax.ShapeDtypeStruct((m_dev, share), bf16),
@@ -297,17 +341,22 @@
             values,
             jax.ShapeDtypeStruct((outputs, 1), f32),
         ),
-        in_specs=[SMEM] + [VMEM] * 7 + [ANY],
-        out_specs=(VMEM,) * 5,
+        in_specs=[SMEM] + [VMEM] * 6 + [ANY, ANY],
+        out_specs=(VMEM, VMEM, ANY, ANY, VMEM),
         scratch_shapes=[
-            pltpu.VMEM((count, m_dev, chunk), bf16),
-            pltpu.VMEM((m_dev, chunk), bf16),
-            pltpu.VMEM((m_dev, 2 * centers.shape[1]), bf16),
+            pltpu.VMEM(block.shape, bf16),
+            pltpu.VMEM((CHUNK // WIDTH, m_dev, WIDTH), bf16),
+            pltpu.VMEM((m_dev, 2 * features), bf16),
             pltpu.VMEM((panel, panel), bf16),
             pltpu.VMEM((2 * outputs, m_dev), bf16),
-            pltpu.SemaphoreType.DMA((count,)),
+            pltpu.VMEM(((count - stored) * CHUNK, features), bf16),
+            pltpu.VMEM(values.shape, f32),
+            pltpu.VMEM(values.shape, f32),
+            pltpu.SemaphoreType.DMA((stored,)),
+            pltpu.SemaphoreType.DMA,
+            pltpu.SemaphoreType.DMA((count, 2)),
         ],
-        compiler_params=pltpu.CompilerParams(vmem_limit_bytes=44 << 20),
+        compiler_params=pltpu.CompilerParams(vmem_limit_bytes=60 << 20),
         cost_estimate=pl.CostEstimate(
             flops=2 * 256 * m_dev * points.shape[0],
             bytes_accessed=2 * m_dev * points.shape[0],
@@ -318,47 +367,65 @@
 
 
 def image_kernel(
-    cols, flags_ref, tie_ref, w_ref, centers_ref, points_ref, source_ref, keep_ref, send_ref,
-    blocks, made, wide, total, sems,
+    flags_ref, tie_ref, w_ref, centers_ref, points_ref, source_ref, keep_ref, send_ref,
+    blocks, wide, total, points_buf, sems, points_sem,
 ):
-    copies = chunk_copies(source_ref, blocks, sems)
-    for copy in copies:
-        copy.start()
+    stored = sems.shape[0]
+    local = pltpu.make_async_copy(
+        points_ref.at[pl.ds(stored * CHUNK, points_buf.shape[0])], points_buf, points_sem
+    )
+    local.start()
+    for i in range(stored):
+        chunk_copy(source_ref, blocks, sems, i).start()
     wide[...] = widened(centers_ref[...], 1)
-    chunk = blocks.shape[1]
-    per = chunk // 128
-    stored = len(copies)
-    count = points_ref.shape[0] // chunk
     total[...] = jnp.zeros_like(total)
-    for i in [*range(stored, count), *range(stored)]:
-        w = jnp.concatenate([w_ref[i * per + b] for b in range(per)], axis=1)
-        if i >= stored:
-            points_major(cols, wide, points_ref[i * chunk : (i + 1) * chunk], made)
-            total[...] += jnp.dot(w, made[...], preferred_element_type=f32)
-        else:
-            copies[i].wait()
-            total[...] += jnp.dot(w, blocks[i], preferred_element_type=f32)
+    local.wait()
+    count = points_ref.shape[0] // CHUNK
+    width = CHUNK // 128
+    per = wide.shape[0] // WIDTH
+
+    def use(i, made):
+        w = jnp.concatenate([w_ref[i * width + b] for b in range(width)], axis=1)
+        for j, tile in enumerate(made):
+            cut = slice(j * WIDTH, (j + 1) * WIDTH)
+            total[:, cut] += jnp.dot(w, tile, preferred_element_type=f32)
+
+    def local_step(i, carry):
+        rows = pl.ds(pl.multiple_of((i - stored) * CHUNK, CHUNK), CHUNK)
+        use(i, tiles(1, wide, points_buf[rows]))
+        return carry
+
+    def stored_step(i, carry):
+        chunk_copy(source_ref, blocks, sems, i).wait()
+        use(i, (blocks[i * per + j] for j in range(per)))
+        return carry
+
+    lax.fori_loop(stored, count, local_step, 0)
+    lax.fori_loop(0, stored, stored_step, 0)
     half = keep_ref.shape[0]
     mine = pl.multiple_of((flags_ref[1] % 2) * half, half)
     keep_ref[...] = total[pl.ds(mine, half)]
     send_ref[...] = total[pl.ds(half - mine, half)]
 
 
-def image(flags, tie, w, centers, points, block, cols=256):
+def image(flags, tie, w, centers, points, block):
     outputs = w.shape[1]
-    count, chunk, m_dev = block.shape
+    m_dev, features = centers.shape
+    count = points.shape[0] // CHUNK
+    stored = block.shape[0] * WIDTH // m_dev
     shape = jax.ShapeDtypeStruct((outputs // 2, m_dev), f32)
     return pl.pallas_call(
-        functools.partial(image_kernel, cols),
+        image_kernel,
         out_shape=(shape, shape),
-        in_specs=[SMEM, VMEM, VMEM, VMEM, VMEM, ANY],
+        in_specs=[SMEM, VMEM, VMEM, VMEM, ANY, ANY],
         out_specs=(VMEM, VMEM),
         scratch_shapes=[
-            pltpu.VMEM((count, chunk, m_dev), bf16),
-            pltpu.VMEM((chunk, m_dev), bf16),
-            pltpu.VMEM((m_dev, 2 * centers.shape[1]), bf16),
+            pltpu.VMEM(block.shape, bf16),
+            pltpu.VMEM((m_dev, 2 * features), bf16),
             pltpu.VMEM((outputs, m_dev), f32),
-            pltpu.SemaphoreType.DMA((count,)),
+            pltpu.VMEM(((count - stored) * CHUNK, features), bf16),
+            pltpu.SemaphoreType.DMA((stored,)),
+            pltpu.SemaphoreType.DMA,
         ],
         compiler_params=pltpu.CompilerParams(vmem_limit_bytes=44 << 20),
         cost_estimate=pl.CostEstimate(
@@ -444,10 +511,9 @@
     image_scale = 1.0 / (2.0 * math.sqrt(npg * n_pts))
 
     head = exchange(head_payload(centers, direction, panel, n_near), NEAR)
-    shape = (13, m_dev, 512)
     block = None
-    for first, count in ((0, 4), (4, 5), (9, 4)):
-        block = block_part(0, shape, first, count, points, centers, block)
+    for i in range(3):
+        block = block_part(0, 6, 2 * i, 2, points, centers, block)
     other = swap(panel_inverse, 1)
     pair = swap(jnp.concatenate([panel_inverse, other], axis=0), 2)
     head = exchange(spread(head, n_far), FAR)
@@ -460,10 +526,9 @@
     parts = exchange(high.reshape(n_near, n_far * outputs, 128), NEAR)
     parts = summed(parts).reshape(n_far, outputs, 128)
     parts = exchange(parts, FAR)
-    shape = (6, 1024, m_dev)
     block = None
     for first, count in ((0, 4), (4, 2)):
-        block = block_part(1, shape, first, count, points, centers, block, z_squares)
+        block = block_part(1, 6, first, count, points, centers, block, z_squares)
     w = exchange(owned_copies(parts, w_scale, n_far), FAR)
     w = exchange(spread(w.reshape(n_far * outputs, 128), n_near), NEAR)
     w = w.reshape(-1, outputs, 128)

time: 167 us -> 181 us (1.084)
  Pallas kernels: 61.1 us -> 78.2 us
  local copies, waits for them, and re-layouts: 4.86 us -> 1.42 us
    pallas_call x8, Pallas kernels: 55.4 us -> 72.5 us  [the longest x5 42.3 us: block_part(): pl.pallas_call(functools.partial(block_kernel, side, first, count), out_s...]
    all_to_all x4, starting transfers between devices: 19.6 us -> 24 us  [exchange(): return lax.all_to_all(x, axis, 0, 0, tiled=True)]
    unnamed x30 -> x22, local copies, waits for them, and re-layouts: 4.84 us -> 1.4 us
    ppermute x7, starting transfers between devices: 16.7 us -> 13.7 us  [swap(): return lax.ppermute(x, 'pts', [(i, i ^ bit) for i in range(n)])]
  transfers between devices with their start and end apart: 11 -> 11, of which waited for: 2 -> 2; matrix products, arithmetic and copies ran while one was open for 1% -> 0% of each run, Pallas kernels for 21% -> 24%
where the time goes in v4:
time: 181 us; the launch traced here: 180 us
  Pallas kernels  78.2 us (43%)
  blocking collectives  57.1 us (32%)
  starting transfers between devices  37.7 us (21%)
  waiting for transfers between devices  4.52 us (2%)
    all_to_all x4, blocking collectives, exchange(): return lax.all_to_all(x, axis, 0, 0, tiled=True)  57.1 us
    pallas_call x5, Pallas kernels, block_part(): pl.pallas_call(functools.partial(block_kernel, side, first, count), out_s...  42.3 us
    all_to_all x4, starting transfers between devices, exchange(): return lax.all_to_all(x, axis, 0, 0, tiled=True)  24 us
    pallas_call x1, Pallas kernels, panel_step(): pl.pallas_call(panel_kernel, out_shape=(jax.ShapeDtypeStruct((outputs, m_...  17.3 us
    ppermute x7, starting transfers between devices, swap(): return lax.ppermute(x, 'pts', [(i, i ^ bit) for i in range(n)])  13.7 us
    pallas_call x1, Pallas kernels, image(): pl.pallas_call(image_kernel, out_shape=(shape, shape), in_specs=[SMEM, VM...  12.7 us
    ppermute x7, waiting for transfers between devices, swap(): return lax.ppermute(x, 'pts', [(i, i ^ bit) for i in range(n)])  4.51 us
  transfers between devices with their start and end apart: 11, of which 2 were waited for; matrix products, arithmetic and copies ran while one was open for 0% of the time, Pallas kernels for 24%

profile of v4, /device:TPU:1, one launch (start us, length us, event | category | flops | bytes accessed | tf_op | source)
XLA Modules:
  0.0 180.4 jit_solution(4605916015166551032)
XLA Ops:
  0.6 1.6 head.1
  2.2 5.9 %all-to-all-start = ((bf16[8,80,128]{2,1,0:T(8,128)(2,1)}), bf16[8,80,128]{2,1,0:T(8,128)(2,1)S(1)}, u32[]{:S(2)}, u32[]{:S(2)}) async-start(bf16[8,80,128]{2,1,0:T(8,128)(2,1)} %head.1), calls=%async_computation | async-start | bytes 327680 | tf_op jit(solution)/shard_map/all_to_all | solution.py:441
  9.1 6.2 %shard_map.76.refs_0_ = bf16[24,2048,256]{2,1,0:T(8,128)(2,1)} custom-call(bf16[8192,128]{1,0:T(8,128)(2,1)} %points_ref.3, bf16[2048,128]{1,0:T(8,128)(2,1)} %centers_ref.5), custom_call_target="tpu_custom_call" | custom-call | flops 2147483648 | bytes 8388608 | tf_op jit(solution)/shard_map/pallas_call | solution.py:109
  16.0 8.2 %all-to-all-start.1 = ((bf16[8,80,128]{2,1,0:T(8,128)(2,1)}), bf16[8,80,128]{2,1,0:T(8,128)(2,1)S(1)}, u32[]{:S(2)}, u32[]{:S(2)}) async-start(bf16[8,80,128]{2,1,0:T(8,128)(2,1)} %spread.3), calls=%async_computation.1 | async-start | bytes 327680 | tf_op jit(solution)/shard_map/all_to_all | solution.py:441
  24.2 6.1 %shard_map.77.refs_0_ = bf16[24,2048,256]{2,1,0:T(8,128)(2,1)} custom-call(bf16[24,2048,256]{2,1,0:T(8,128)(2,1)} %shard_map.76.refs_0_, bf16[8192,128]{1,0:T(8,128)(2,1)} %points_ref.3, bf16[2048,128]{1,0:T(8,128)(2,1)} %centers_ref.5), custom_call_target="tpu_custom_call", output_to_operand_aliasing={{}: (0, {})} | custom-call | flops 2147483648 | bytes 8388608 | tf_op jit(solution)/shard_map/pallas_call | solution.py:109
  30.4 2.5 %collective-permute-start.1 = (bf16[256,512]{1,0:T(8,128)(2,1)S(1)}, bf16[256,512]{1,0:T(8,128)(2,1)S(1)}, u32[]{:S(2)}, u32[]{:S(2)}) collective-permute-start(bf16[256,512]{1,0:T(8,128)(2,1)S(1)} %pad_maximum_fusion), channel_id=1, source_target_pairs={{0,128},{64,192},{128,0},{192,64},{1,129},{65,193},{129,1},{193,65... | collective-permute-start | bytes 786440 | tf_op jit(solution)/shard_map/ppermute | solution.py:470
  33.6 5.9 %all-to-all-start.2 = ((bf16[8,80,128]{2,1,0:T(8,128)(2,1)}), bf16[8,80,128]{2,1,0:T(8,128)(2,1)S(1)}, u32[]{:S(2)}, u32[]{:S(2)}) async-start(bf16[8,80,128]{2,1,0:T(8,128)(2,1)} %spread.4), calls=%async_computation.2 | async-start | bytes 327680 | tf_op jit(solution)/shard_map/all_to_all | solution.py:441
  39.6 6.2 %shard_map.78.source_ref = bf16[24,2048,256]{2,1,0:T(8,128)(2,1)} custom-call(bf16[24,2048,256]{2,1,0:T(8,128)(2,1)} %shard_map.77.refs_0_, bf16[8192,128]{1,0:T(8,128)(2,1)} %points_ref.3, bf16[2048,128]{1,0:T(8,128)(2,1)} %centers_ref.5), custom_call_target="tpu_custom_call", output_to_operand_aliasing={{}: (0, {})} | custom-call | flops 2147483648 | bytes 8388608 | tf_op jit(solution)/shard_map/pallas_call | solution.py:109
  47.8 17.3 %panel.1 = (f32[32,2048]{1,0:T(8,128)}, bf16[2048,128]{1,0:T(8,128)(2,1)}, f32[64,32,128]{2,1,0:T(8,128)}, f32[64,32,128]{2,1,0:T(8,128)}, f32[32,1]{1,0:T(8,128)}) custom-call(s32[2]{0:T(128)} %pad_add_fusion.flags_ref, bf16[2048,128]{1,0:T(8,128)(2,1)} %centers_ref.5, bf16[8,80,128]{2,1,0:T(8,128)(2,1)} %copy-done.7, bf16[128,512]{1,0:T(8,128)(2,1)} %mine_ref.1, ...), custom_call_target="tpu_custom_call" | custom-call | flops 8589934592 | bytes 33554432 | tf_op jit(solution)/shard_map/panel/pallas_call | solution.py:335
  65.1 18.2 %all_to_all.40.x_ref = f32[8,256,128]{2,1,0:T(8,128)S(1)} all-to-all(f32[8,256,128]{2,1,0:T(8,128)} %bitcast.12), channel_id=1, replica_groups=mesh['pts'=4,'ctr_0'=8,'ctr_1'=2,'ctr_2'=4] {'ctr_1','ctr_2'}, dimensions={0} | all-to-all | bytes 2097152 | tf_op jit(solution)/shard_map/all_to_all | solution.py:441
  83.5 13.8 %all_to_all.41.x_ref = f32[8,32,128]{2,1,0:T(8,128)S(1)} all-to-all(f32[8,32,128]{2,1,0:T(8,128)S(1)} %bitcast.10), channel_id=1, replica_groups=mesh['pts'=4,'ctr_0'=8,'ctr_1'=2,'ctr_2'=4] {'ctr_0'}, dimensions={0} | all-to-all | bytes 262144 | tf_op jit(solution)/shard_map/all_to_all | solution.py:441
  97.3 9.6 %all_to_all.42 = bf16[8,32,128]{2,1,0:T(8,128)(2,1)S(1)} all-to-all(bf16[8,32,128]{2,1,0:T(8,128)(2,1)S(1)} %owned.1), channel_id=1, replica_groups=mesh['pts'=4,'ctr_0'=8,'ctr_1'=2,'ctr_2'=4] {'ctr_0'}, dimensions={0} | all-to-all | bytes 131072 | tf_op jit(solution)/shard_map/all_to_all | solution.py:441
  107.8 3.9 %all-to-all-start.6 = ((bf16[8,256,128]{2,1,0:T(8,128)(2,1)}), bf16[8,256,128]{2,1,0:T(8,128)(2,1)S(1)}, u32[]{:S(2)}, u32[]{:S(2)}) async-start(bf16[8,256,128]{2,1,0:T(8,128)(2,1)} %spread.5), calls=%async_computation.6 | async-start | bytes 1048576 | tf_op jit(solution)/shard_map/all_to_all | solution.py:441
  111.7 17.7 %shard_map.79.refs_0_ = bf16[48,1024,256]{2,1,0:T(8,128)(2,1)} custom-call(f32[32,1]{1,0:T(8,128)} %get-tuple-element.15.z_squares_ref.refs_0_.refs_1_, bf16[8192,128]{1,0:T(8,128)(2,1)} %points_ref.3, bf16[2048,128]{1,0:T(8,128)(2,1)} %centers_ref.5), custom_call_target="tpu_custom_call" | custom-call | flops 4294967296 | bytes 16777216 | tf_op jit(solution)/shard_map/pallas_call | solution.py:109
  129.8 5.7 %collective-permute-start.2 = (f32[1,128]{1,0:T(1,128)S(1)}, f32[1,128]{1,0:T(1,128)S(1)}, u32[]{:S(2)}, u32[]{:S(2)}) collective-permute-start(f32[1,128]{1,0:T(1,128)S(1)} %products.1), channel_id=1, source_target_pairs={{0,64},{64,0},{128,192},{192,128},{1,65},{65,1},{129,193},{193,129... | collective-permute-start | bytes 1544 | tf_op jit(solution)/shard_map/ppermute | solution.py:470
  135.5 6.0 %shard_map.80.source_ref = bf16[48,1024,256]{2,1,0:T(8,128)(2,1)} custom-call(bf16[48,1024,256]{2,1,0:T(8,128)(2,1)} %shard_map.79.refs_0_, f32[32,1]{1,0:T(8,128)} %get-tuple-element.15.z_squares_ref.refs_0_.refs_1_, bf16[8192,128]{1,0:T(8,128)(2,1)} %points_ref.3, bf16[2048,128]{1,0:T(8,128)(2,1)} %centers_ref.5), custom_call_target="tpu_custom_call", output_to_operand_aliasing={{}: (0, {})} | custom-call | flops 2147483648 | bytes 8388608 | tf_op jit(solution)/shard_map/pallas_call | solution.py:109
  141.6 12.7 %image.1 = (f32[16,2048]{1,0:T(8,128)S(1)}, f32[16,2048]{1,0:T(8,128)S(1)}) custom-call(s32[2]{0:T(128)S(1)} %copy-done.6, f32[1,128]{1,0:T(1,128)S(1)} %add.20.tie_ref, bf16[64,32,128]{2,1,0:T(8,128)(2,1)S(1)} %bitcast.9, bf16[2048,128]{1,0:T(8,128)(2,1)S(1)} %copy-done.1, bf16[8192,128]{1,0:T(8,128)(2,1)S(1)} %copy-done, ...), custom_call_target="tpu_custom_call" | custom-call | flops 8589934592 | bytes 33554432 | tf_op jit(solution)/shard_map/image/pallas_call | solution.py:417
  154.7 1.1 collective-permute-done.3
  155.8 1.8 %collective-permute-start.4 = (f32[16,2048]{1,0:T(8,128)S(1)}, f32[16,2048]{1,0:T(8,128)S(1)}, u32[]{:S(2)}, u32[]{:S(2)}) collective-permute-start(f32[16,2048]{1,0:T(8,128)S(1)} %add.21), channel_id=1, source_target_pairs={{0,128},{64,192},{128,0},{192,64},{1,129},{65,193},{129,1},{193,65... | collective-permute-start | bytes 393224 | tf_op jit(solution)/shard_map/ppermute | solution.py:470
  157.6 1.2 collective-permute-start.6
  158.9 3.4 %collective-permute-done.4 = f32[16,2048]{1,0:T(8,128)S(1)} collective-permute-done((f32[16,2048]{1,0:T(8,128)S(1)}, f32[16,2048]{1,0:T(8,128)S(1)}, u32[]{:S(2)}, u32[]{:S(2)}) %collective-permute-start.4) | collective-permute-done | bytes 131104 | tf_op jit(solution)/shard_map/ppermute | solution.py:470
  162.3 1.2 collective-permute-start.5
  163.5 15.5 %all_to_all.43.sums_ref = f32[64,1,128]{2,1,0:T(1,128)S(1)} all-to-all(f32[64,1,128]{2,1,0:T(1,128)S(1)} %broadcast_in_dim.9), channel_id=1, replica_groups=mesh['pts'=4,'ctr_0'=8,'ctr_1'=2,'ctr_2'=4] {'ctr_0','ctr_1','ctr_2'}, dimensions={0} | all-to-all | bytes 65536 | tf_op jit(solution)/shard_map/all_to_all | solution.py:441
  179.0 1.5 final.1
  (46 shorter events, 6.2 us)
Async XLA Ops:
  2.2 13.1 %all-to-all-start = ((bf16[8,80,128]{2,1,0:T(8,128)(2,1)}), bf16[8,80,128]{2,1,0:T(8,128)(2,1)S(1)}, u32[]{:S(2)}, u32[]{:S(2)}) async-start(bf16[8,80,128]{2,1,0:T(8,128)(2,1)} %head.1), calls=%async_computation | async-start | bytes 327680 | tf_op jit(solution)/shard_map/all_to_all | solution.py:441
  8.2 22.2 %collective-permute-start = (bf16[128,512]{1,0:T(8,128)(2,1)}, bf16[128,512]{1,0:T(8,128)(2,1)S(1)}, u32[]{:S(2)}, u32[]{:S(2)}) collective-permute-start(bf16[128,512]{1,0:T(8,128)(2,1)} %mine_ref.1), channel_id=1, source_target_pairs={{0,64},{64,0},{128,192},{192,128},{1,65},{65,1},{129,193},{193,129... | collective-permute-start | bytes 393224 | tf_op jit(solution)/shard_map/ppermute | solution.py:470
  16.0 16.9 %all-to-all-start.1 = ((bf16[8,80,128]{2,1,0:T(8,128)(2,1)}), bf16[8,80,128]{2,1,0:T(8,128)(2,1)S(1)}, u32[]{:S(2)}, u32[]{:S(2)}) async-start(bf16[8,80,128]{2,1,0:T(8,128)(2,1)} %spread.3), calls=%async_computation.1 | async-start | bytes 327680 | tf_op jit(solution)/shard_map/all_to_all | solution.py:441
  24.2 6.2 %copy-start.8 = (bf16[128,512]{1,0:T(8,128)(2,1)S(1)}, bf16[128,512]{1,0:T(8,128)(2,1)}, u32[]{:S(2)}) copy-start(bf16[128,512]{1,0:T(8,128)(2,1)} %mine_ref.1) | copy-start | bytes 393220
  30.4 15.4 %copy-start.9 = (bf16[128,512]{1,0:T(8,128)(2,1)}, bf16[128,512]{1,0:T(8,128)(2,1)S(1)}, u32[]{:S(2)}) copy-start(bf16[128,512]{1,0:T(8,128)(2,1)S(1)} %collective-permute-done.other_ref) | copy-start | bytes 393220
  30.4 16.0 %collective-permute-start.1 = (bf16[256,512]{1,0:T(8,128)(2,1)S(1)}, bf16[256,512]{1,0:T(8,128)(2,1)S(1)}, u32[]{:S(2)}, u32[]{:S(2)}) collective-permute-start(bf16[256,512]{1,0:T(8,128)(2,1)S(1)} %pad_maximum_fusion), channel_id=1, source_target_pairs={{0,128},{64,192},{128,0},{192,64},{1,129},{65,193},{129,1},{193,65... | collective-permute-start | bytes 786440 | tf_op jit(solution)/shard_map/ppermute | solution.py:470
  33.6 12.8 %all-to-all-start.2 = ((bf16[8,80,128]{2,1,0:T(8,128)(2,1)}), bf16[8,80,128]{2,1,0:T(8,128)(2,1)S(1)}, u32[]{:S(2)}, u32[]{:S(2)}) async-start(bf16[8,80,128]{2,1,0:T(8,128)(2,1)} %spread.4), calls=%async_computation.2 | async-start | bytes 327680 | tf_op jit(solution)/shard_map/all_to_all | solution.py:441
  46.4 83.0 %copy-start.3 = (f32[32,2048]{1,0:T(8,128)S(1)}, f32[32,2048]{1,0:T(8,128)}, u32[]{:S(2)}) copy-start(f32[32,2048]{1,0:T(8,128)} %res_ref.3) | copy-start | bytes 786436
  46.4 0.7 copy-start.10
  47.2 0.7 copy-start.7
  65.1 64.4 %copy-start.2 = (f32[64,32,128]{2,1,0:T(8,128)S(1)}, f32[64,32,128]{2,1,0:T(8,128)}, u32[]{:S(2)}) copy-start(f32[64,32,128]{2,1,0:T(8,128)} %get-tuple-element.14.both_ref) | copy-start | bytes 3145732
  65.1 64.4 %copy-start.5 = (f32[32,1]{1,0:T(8,128)S(1)}, f32[32,1]{1,0:T(8,128)}, u32[]{:S(2)}) copy-start(f32[32,1]{1,0:T(8,128)} %get-tuple-element.15.z_squares_ref.refs_0_.refs_1_) | copy-start | bytes 388
  107.8 21.6 %all-to-all-start.6 = ((bf16[8,256,128]{2,1,0:T(8,128)(2,1)}), bf16[8,256,128]{2,1,0:T(8,128)(2,1)S(1)}, u32[]{:S(2)}, u32[]{:S(2)}) async-start(bf16[8,256,128]{2,1,0:T(8,128)(2,1)} %spread.5), calls=%async_computation.6 | async-start | bytes 1048576 | tf_op jit(solution)/shard_map/all_to_all | solution.py:441
  129.8 11.8 %copy-start = (bf16[8192,128]{1,0:T(8,128)(2,1)S(1)}, bf16[8192,128]{1,0:T(8,128)(2,1)}, u32[]{:S(2)}) copy-start(bf16[8192,128]{1,0:T(8,128)(2,1)} %points_ref.3) | copy-start | bytes 6291460
  129.8 11.8 %copy-start.1 = (bf16[2048,128]{1,0:T(8,128)(2,1)S(1)}, bf16[2048,128]{1,0:T(8,128)(2,1)}, u32[]{:S(2)}) copy-start(bf16[2048,128]{1,0:T(8,128)(2,1)} %centers_ref.5) | copy-start | bytes 1572868
  129.8 11.8 %copy-start.6 = (s32[2]{0:T(128)S(1)}, s32[2]{0:T(128)}, u32[]{:S(2)}) copy-start(s32[2]{0:T(128)} %pad_add_fusion.flags_ref) | copy-start | bytes 28
  129.8 11.7 %collective-permute-start.2 = (f32[1,128]{1,0:T(1,128)S(1)}, f32[1,128]{1,0:T(1,128)S(1)}, u32[]{:S(2)}, u32[]{:S(2)}) collective-permute-start(f32[1,128]{1,0:T(1,128)S(1)} %products.1), channel_id=1, source_target_pairs={{0,64},{64,0},{128,192},{192,128},{1,65},{65,1},{129,193},{193,129... | collective-permute-start | bytes 1544 | tf_op jit(solution)/shard_map/ppermute | solution.py:470
  141.5 37.4 %copy-start.4 = (f32[32,2048]{1,0:T(8,128)S(1)}, f32[32,2048]{1,0:T(8,128)}, u32[]{:S(2)}) copy-start(f32[32,2048]{1,0:T(8,128)} %get-tuple-element.18.z_ref) | copy-start | bytes 786436
  154.4 1.4 collective-permute-start.3
  155.8 6.4 %collective-permute-start.4 = (f32[16,2048]{1,0:T(8,128)S(1)}, f32[16,2048]{1,0:T(8,128)S(1)}, u32[]{:S(2)}, u32[]{:S(2)}) collective-permute-start(f32[16,2048]{1,0:T(8,128)S(1)} %add.21), channel_id=1, source_target_pairs={{0,128},{64,192},{128,0},{192,64},{1,129},{65,193},{129,1},{193,65... | collective-permute-start | bytes 393224 | tf_op jit(solution)/shard_map/ppermute | solution.py:470
  157.6 5.8 %collective-permute-start.6 = (f32[1,128]{1,0:T(1,128)S(1)}, f32[1,128]{1,0:T(1,128)S(1)}, u32[]{:S(2)}, u32[]{:S(2)}) collective-permute-start(f32[1,128]{1,0:T(1,128)S(1)} %add.20.tie_ref), channel_id=1, source_target_pairs={{0,128},{64,192},{128,0},{192,64},{1,129},{65,193},{129,1},{193,65... | collective-permute-start | bytes 1544 | tf_op jit(solution)/shard_map/ppermute | solution.py:470
  162.3 16.7 %collective-permute-start.5 = (f32[16,2048]{1,0:T(8,128)S(1)}, f32[16,2048]{1,0:T(8,128)S(1)}, u32[]{:S(2)}, u32[]{:S(2)}) collective-permute-start(f32[16,2048]{1,0:T(8,128)S(1)} %add.22.keep_ref), channel_id=1, source_target_pairs={{0,64},{64,0},{128,192},{192,128},{1,65},{65,1},{129,193},{193,129... | collective-permute-start | bytes 393224 | tf_op jit(solution)/shard_map/ppermute | solution.py:470

commit v5 on v4

--- a/solution.py
+++ b/solution.py
@@ -22,6 +22,7 @@
 ANY = pl.BlockSpec(memory_space=pl.ANY)
 LIMIT = 12 << 20
 CHUNK = 1024
+HALF = 512
 WIDTH = 256
 
 
@@ -51,24 +52,24 @@
     return jnp.exp2(t * (math.log2(math.e) / (2 * features))).astype(bf16)
 
 
-def tiles(side, wide, points):
+def fill(side, wide, points, out):
     features = points.shape[1]
     extended = widened(points, 1 - side)
     columns = extended if side == 0 else wide
     for j in range(columns.shape[0] // WIDTH):
-        cut = columns[j * WIDTH : (j + 1) * WIDTH]
-        yield similar(wide[...], cut, features) if side == 0 else similar(extended, cut, features)
-
-
-def block_kernel(side, first, count, *refs):
+        cut = slice(j * WIDTH, (j + 1) * WIDTH)
+        rows = wide[...] if side == 0 else extended
+        out[:, cut] = similar(rows, columns[cut], features)
+
+
+def block_kernel(side, size, first, count, *refs):
     points_ref, centers_ref = refs[-9:-7]
     out_ref, points_buf, centers_buf, wide, buffers, sems, in_sems = refs[-7:]
-    per = buffers.shape[1]
-    load = points_buf.shape[0]
+    slots = buffers.shape[0]
     loads = [
         pltpu.make_async_copy(centers_ref, centers_buf, in_sems.at[0]),
         pltpu.make_async_copy(
-            points_ref.at[pl.ds(first * CHUNK, load)], points_buf, in_sems.at[1]
+            points_ref.at[pl.ds(first * size, count * size)], points_buf, in_sems.at[1]
         ),
     ]
     for copy in loads:
@@ -77,54 +78,51 @@
     wide[...] = widened(centers_buf[...], side)
     loads[1].wait()
 
-    def put(i, j):
-        slot = lax.rem(i, 2)
-        return pltpu.make_async_copy(
-            buffers.at[slot, j], out_ref.at[(first + i) * per + j], sems.at[slot, j]
-        )
+    def put(i):
+        slot = lax.rem(i, slots)
+        return pltpu.make_async_copy(buffers.at[slot], out_ref.at[first + i], sems.at[slot])
 
     def step(i, carry):
-        rows = pl.ds(pl.multiple_of(i * CHUNK, CHUNK), CHUNK)
-        for j, tile in enumerate(tiles(side, wide, points_buf[rows])):
-            if count > 2:
-
-                @pl.when(i >= 2)
-                def _(j=j):
-                    put(i - 2, j).wait()
-
-            buffers[lax.rem(i, 2), j] = tile
-            put(i, j).start()
+        if count > slots:
+
+            @pl.when(i >= slots)
+            def _():
+                put(i - slots).wait()
+
+        rows = pl.ds(pl.multiple_of(i * size, size), size)
+        fill(side, wide, points_buf[rows], buffers.at[lax.rem(i, slots)])
+        put(i).start()
         return carry
 
     lax.fori_loop(0, count, step, 0)
-    for i in range(max(count - 2, 0), count):
-        for j in range(per):
-            put(jnp.int32(i), j).wait()
-
-
-def block_part(side, chunks, first, count, points, centers, made=None, tie=None):
+    for i in range(max(count - slots, 0), count):
+        put(jnp.int32(i)).wait()
+
+
+def block_part(side, size, chunks, first, count, points, centers, made=None, tie=None):
     m_dev, features = centers.shape
-    per, rows = (CHUNK // WIDTH, m_dev) if side == 0 else (m_dev // WIDTH, CHUNK)
+    rows, columns = (m_dev, size) if side == 0 else (size, m_dev)
+    slots = min(count, 2)
     extra = [x for x in (made, tie) if x is not None]
     return pl.pallas_call(
-        functools.partial(block_kernel, side, first, count),
-        out_shape=jax.ShapeDtypeStruct((chunks * per, rows, WIDTH), bf16),
+        functools.partial(block_kernel, side, size, first, count),
+        out_shape=jax.ShapeDtypeStruct((chunks, rows, columns), bf16),
         in_specs=[ANY] * (len(extra) + 2),
         out_specs=ANY,
         scratch_shapes=[
-            pltpu.VMEM((count * CHUNK, features), bf16),
+            pltpu.VMEM((count * size, features), bf16),
             pltpu.VMEM((m_dev, features), bf16),
             pltpu.VMEM((m_dev, 2 * features), bf16),
-            pltpu.VMEM((2, per, rows, WIDTH), bf16),
-            pltpu.SemaphoreType.DMA((2, per)),
+            pltpu.VMEM((slots, rows, columns), bf16),
+            pltpu.SemaphoreType.DMA((slots,)),
             pltpu.SemaphoreType.DMA((2,)),
         ],
         input_output_aliases={} if made is None else {0: 0},
         compiler_params=pltpu.CompilerParams(vmem_limit_bytes=60 << 20),
         cost_estimate=pl.CostEstimate(
-            flops=4 * m_dev * count * CHUNK * features,
-            bytes_accessed=2 * m_dev * count * CHUNK,
-            transcendentals=m_dev * count * CHUNK,
+            flops=4 * m_dev * count * size * features,
+            bytes_accessed=2 * m_dev * count * size,
+            transcendentals=m_dev * count * size,
         ),
     )(*extra, points, centers)
 
@@ -229,9 +227,7 @@
 
 
 def chunk_copy(source, buffer, sems, i):
-    per = buffer.shape[0] // sems.shape[0]
-    span = pl.ds(i * per, per)
-    return pltpu.make_async_copy(source.at[span], buffer.at[span], sems.at[i])
+    return pltpu.make_async_copy(source.at[i], buffer.at[i], sems.at[i])
 
 
 def panel_kernel(
@@ -241,7 +237,7 @@
 ):
     stored = sems.shape[0]
     local = pltpu.make_async_copy(
-        points_ref.at[pl.ds(stored * CHUNK, points_buf.shape[0])], points_buf, points_sem
+        points_ref.at[pl.ds(stored * HALF, points_buf.shape[0])], points_buf, points_sem
     )
     local.start()
     for i in range(stored):
@@ -284,41 +280,39 @@
         zz[outputs:, rows] = (z - high.astype(f32)).astype(bf16)
     zsq_ref[...] = squares
     local.wait()
-    total = points_ref.shape[0] // CHUNK
-    width = WIDTH // 128
-    per = CHUNK // WIDTH
+    total = points_ref.shape[0] // HALF
+    per = HALF // 128
+    pair = made.shape[1] // HALF
 
     def puts(i):
-        span = pl.ds(i * per * width, per * width)
+        span = pl.ds(i * per, per)
         return [
             pltpu.make_async_copy(buf.at[span], out.at[span], out_sems.at[i, k])
             for k, (buf, out) in enumerate(((high_ref, high_out), (both_ref, both_out)))
         ]
 
-    def use(i, source, at):
-        for j in range(per):
-            u = jnp.dot(zz[...], source[at + j], preferred_element_type=f32)
-            for b in range(width):
-                part = u[:, b * 128 : (b + 1) * 128]
-                row = (i * per + j) * width + b
-                high_ref[row] = part[:outputs]
-                both_ref[row] = part[:outputs] + part[outputs:]
-        for put in puts(i):
-            put.start()
+    def use(i, block):
+        u = jnp.dot(zz[...], block, preferred_element_type=f32)
+        for b in range(block.shape[1] // 128):
+            part = u[:, b * 128 : (b + 1) * 128]
+            high_ref[i * per + b] = part[:outputs]
+            both_ref[i * per + b] = part[:outputs] + part[outputs:]
+        for k in range(block.shape[1] // HALF):
+            for put in puts(i + k):
+                put.start()
 
     def local_step(i, carry):
-        rows = pl.ds(pl.multiple_of((i - stored) * CHUNK, CHUNK), CHUNK)
-        for j, tile in enumerate(tiles(0, wide, points_buf[rows])):
-            made[j] = tile
-        use(i, made, 0)
+        rows = pl.ds(pl.multiple_of(i * pair * HALF, pair * HALF), pair * HALF)
+        fill(0, wide, points_buf[rows], made)
+        use(stored + pair * i, made[...])
         return carry
 
     def stored_step(i, carry):
         chunk_copy(source_ref, blocks, sems, i).wait()
-        use(i, blocks, i * per)
+        use(i, blocks[i])
         return carry
 
-    lax.fori_loop(stored, total, local_step, 0)
+    lax.fori_loop(0, (total - stored) // pair, local_step, 0)
     lax.fori_loop(0, stored, stored_step, 0)
     for i in range(total):
         for put in puts(i):
@@ -329,8 +323,8 @@
     outputs, m_dev = direction.shape
     share, panel = mine.shape
     features = centers.shape[1]
-    count = points.shape[0] // CHUNK
-    stored = block.shape[0] * WIDTH // CHUNK
+    count = points.shape[0] // HALF
+    stored = block.shape[0]
     values = jax.ShapeDtypeStruct((points.shape[0] // 128, outputs, 128), f32)
     return pl.pallas_call(
         panel_kernel,
@@ -345,11 +339,11 @@
         out_specs=(VMEM, VMEM, ANY, ANY, VMEM),
         scratch_shapes=[
             pltpu.VMEM(block.shape, bf16),
-            pltpu.VMEM((CHUNK // WIDTH, m_dev, WIDTH), bf16),
+            pltpu.VMEM((m_dev, CHUNK), bf16),
             pltpu.VMEM((m_dev, 2 * features), bf16),
             pltpu.VMEM((panel, panel), bf16),
             pltpu.VMEM((2 * outputs, m_dev), bf16),
-            pltpu.VMEM(((count - stored) * CHUNK, features), bf16),
+            pltpu.VMEM(((count - stored) * HALF, features), bf16),
             pltpu.VMEM(values.shape, f32),
             pltpu.VMEM(values.shape, f32),
             pltpu.SemaphoreType.DMA((stored,)),
@@ -368,7 +362,7 @@
 
 def image_kernel(
     flags_ref, tie_ref, w_ref, centers_ref, points_ref, source_ref, keep_ref, send_ref,
-    blocks, wide, total, points_buf, sems, points_sem,
+    blocks, made, wide, total, points_buf, sems, points_sem,
 ):
     stored = sems.shape[0]
     local = pltpu.make_async_copy(
@@ -382,22 +376,20 @@
     local.wait()
     count = points_ref.shape[0] // CHUNK
     width = CHUNK // 128
-    per = wide.shape[0] // WIDTH
-
-    def use(i, made):
+
+    def use(i, block):
         w = jnp.concatenate([w_ref[i * width + b] for b in range(width)], axis=1)
-        for j, tile in enumerate(made):
-            cut = slice(j * WIDTH, (j + 1) * WIDTH)
-            total[:, cut] += jnp.dot(w, tile, preferred_element_type=f32)
+        total[...] += jnp.dot(w, block, preferred_element_type=f32)
 
     def local_step(i, carry):
         rows = pl.ds(pl.multiple_of((i - stored) * CHUNK, CHUNK), CHUNK)
-        use(i, tiles(1, wide, points_buf[rows]))
+        fill(1, wide, points_buf[rows], made)
+        use(i, made[...])
         return carry
 
     def stored_step(i, carry):
         chunk_copy(source_ref, blocks, sems, i).wait()
-        use(i, (blocks[i * per + j] for j in range(per)))
+        use(i, blocks[i])
         return carry
 
     lax.fori_loop(stored, count, local_step, 0)
@@ -412,7 +404,7 @@
     outputs = w.shape[1]
     m_dev, features = centers.shape
     count = points.shape[0] // CHUNK
-    stored = block.shape[0] * WIDTH // m_dev
+    stored = block.shape[0]
     shape = jax.ShapeDtypeStruct((outputs // 2, m_dev), f32)
     return pl.pallas_call(
         image_kernel,
@@ -421,6 +413,7 @@
         out_specs=(VMEM, VMEM),
         scratch_shapes=[
             pltpu.VMEM(block.shape, bf16),
+            pltpu.VMEM((CHUNK, m_dev), bf16),
             pltpu.VMEM((m_dev, 2 * features), bf16),
             pltpu.VMEM((outputs, m_dev), f32),
             pltpu.VMEM(((count - stored) * CHUNK, features), bf16),
@@ -513,7 +506,7 @@
     head = exchange(head_payload(centers, direction, panel, n_near), NEAR)
     block = None
     for i in range(3):
-        block = block_part(0, 6, 2 * i, 2, points, centers, block)
+        block = block_part(0, HALF, 6, 2 * i, 2, points, centers, block)
     other = swap(panel_inverse, 1)
     pair = swap(jnp.concatenate([panel_inverse, other], axis=0), 2)
     head = exchange(spread(head, n_far), FAR)
@@ -527,8 +520,8 @@
     parts = summed(parts).reshape(n_far, outputs, 128)
     parts = exchange(parts, FAR)
     block = None
-    for first, count in ((0, 4), (4, 2)):
-        block = block_part(1, 6, first, count, points, centers, block, z_squares)
+    for first, count in ((0, 4), (4, 1), (5, 1)):
+        block = block_part(1, CHUNK, 6, first, count, points, centers, block, z_squares)
     w = exchange(owned_copies(parts, w_scale, n_far), FAR)
     w = exchange(spread(w.reshape(n_far * outputs, 128), n_near), NEAR)
     w = w.reshape(-1, outputs, 128)

time: 181 us -> 176 us (0.972)
  Pallas kernels: 78.2 us -> 69.8 us
  waiting for transfers between devices: 4.52 us -> 9.57 us
    pallas_call x5 -> x6, Pallas kernels: 42.3 us -> 33.4 us  [block_part(): pl.pallas_call(functools.partial(block_kernel, side, size, first, count),...]
    all_to_all x4, waiting for transfers between devices: 0.01 us -> 4.95 us  [exchange(): return lax.all_to_all(x, axis, 0, 0, tiled=True)]
    pallas_call x1, Pallas kernels: 17.3 us -> 20.3 us  [panel_step(): pl.pallas_call(panel_kernel, out_shape=(jax.ShapeDtypeStruct((outputs, m_...]
    all_to_all x4, starting transfers between devices: 24 us -> 21.2 us  [exchange(): return lax.all_to_all(x, axis, 0, 0, tiled=True)]
    pallas_call x1, Pallas kernels: 12.7 us -> 10.2 us  [image(): pl.pallas_call(image_kernel, out_shape=(shape, shape), in_specs=[SMEM, VM...]
    ppermute x7, starting transfers between devices: 13.7 us -> 15.5 us  [swap(): return lax.ppermute(x, 'pts', [(i, i ^ bit) for i in range(n)])]
  transfers between devices with their start and end apart: 11 -> 11, of which waited for: 2 -> 4; matrix products, arithmetic and copies ran while one was open for 0% -> 0% of each run, Pallas kernels for 24% -> 20%
where the time goes in v5:
time: 176 us; the launch traced here: 175 us
  Pallas kernels  69.8 us (40%)
  blocking collectives  56 us (32%)
  starting transfers between devices  36.7 us (21%)
  waiting for transfers between devices  9.57 us (5%)
    all_to_all x4, blocking collectives, exchange(): return lax.all_to_all(x, axis, 0, 0, tiled=True)  56 us
    pallas_call x6, Pallas kernels, block_part(): pl.pallas_call(functools.partial(block_kernel, side, size, first, count),...  33.4 us
    all_to_all x4, starting transfers between devices, exchange(): return lax.all_to_all(x, axis, 0, 0, tiled=True)  21.2 us
    pallas_call x1, Pallas kernels, panel_step(): pl.pallas_call(panel_kernel, out_shape=(jax.ShapeDtypeStruct((outputs, m_...  20.3 us
    ppermute x7, starting transfers between devices, swap(): return lax.ppermute(x, 'pts', [(i, i ^ bit) for i in range(n)])  15.5 us
    pallas_call x1, Pallas kernels, image(): pl.pallas_call(image_kernel, out_shape=(shape, shape), in_specs=[SMEM, VM...  10.2 us
    all_to_all x4, waiting for transfers between devices, exchange(): return lax.all_to_all(x, axis, 0, 0, tiled=True)  4.95 us
    ppermute x7, waiting for transfers between devices, swap(): return lax.ppermute(x, 'pts', [(i, i ^ bit) for i in range(n)])  4.61 us
  transfers between devices with their start and end apart: 11, of which 4 were waited for; matrix products, arithmetic and copies ran while one was open for 0% of the time, Pallas kernels for 20%

profile of v5, /device:TPU:1, one launch (start us, length us, event | category | flops | bytes accessed | tf_op | source)
XLA Modules:
  0.0 174.9 jit_solution(13411107554999418930)
XLA Ops:
  0.6 1.6 head.1
  2.3 5.9 %all-to-all-start = ((bf16[8,80,128]{2,1,0:T(8,128)(2,1)}), bf16[8,80,128]{2,1,0:T(8,128)(2,1)S(1)}, u32[]{:S(2)}, u32[]{:S(2)}) async-start(bf16[8,80,128]{2,1,0:T(8,128)(2,1)} %head.1), calls=%async_computation | async-start | bytes 327680 | tf_op jit(solution)/shard_map/all_to_all | solution.py:434
  9.2 4.7 %all-to-all-done.x_ref = bf16[8,80,128]{2,1,0:T(8,128)(2,1)S(1)} async-done(((bf16[8,80,128]{2,1,0:T(8,128)(2,1)}), bf16[8,80,128]{2,1,0:T(8,128)(2,1)S(1)}, u32[]{:S(2)}, u32[]{:S(2)}) %all-to-all-start) | async-done | bytes 163872 | tf_op jit(solution)/shard_map/all_to_all | solution.py:434
  14.6 8.2 %all-to-all-start.1 = ((bf16[8,80,128]{2,1,0:T(8,128)(2,1)}), bf16[8,80,128]{2,1,0:T(8,128)(2,1)S(1)}, u32[]{:S(2)}, u32[]{:S(2)}) async-start(bf16[8,80,128]{2,1,0:T(8,128)(2,1)} %spread.3), calls=%async_computation.1 | async-start | bytes 327680 | tf_op jit(solution)/shard_map/all_to_all | solution.py:434
  22.8 4.6 %shard_map.76.refs_0_ = bf16[6,2048,512]{2,1,0:T(8,128)(2,1)} custom-call(bf16[8192,128]{1,0:T(8,128)(2,1)} %points_ref.3, bf16[2048,128]{1,0:T(8,128)(2,1)} %centers_ref.5), custom_call_target="tpu_custom_call" | custom-call | flops 1073741824 | bytes 4194304 | tf_op jit(solution)/shard_map/pallas_call | solution.py:107
  27.4 2.5 %collective-permute-start.1 = (bf16[256,512]{1,0:T(8,128)(2,1)S(1)}, bf16[256,512]{1,0:T(8,128)(2,1)S(1)}, u32[]{:S(2)}, u32[]{:S(2)}) collective-permute-start(bf16[256,512]{1,0:T(8,128)(2,1)S(1)} %pad_maximum_fusion), channel_id=1, source_target_pairs={{0,128},{64,192},{128,0},{192,64},{1,129},{65,193},{129,1},{193,65... | collective-permute-start | bytes 786440 | tf_op jit(solution)/shard_map/ppermute | solution.py:463
  29.9 4.7 %shard_map.77.refs_0_ = bf16[6,2048,512]{2,1,0:T(8,128)(2,1)} custom-call(bf16[6,2048,512]{2,1,0:T(8,128)(2,1)} %shard_map.76.refs_0_, bf16[8192,128]{1,0:T(8,128)(2,1)} %points_ref.3, bf16[2048,128]{1,0:T(8,128)(2,1)} %centers_ref.5), custom_call_target="tpu_custom_call", output_to_operand_aliasing={{}: (0, {})} | custom-call | flops 1073741824 | bytes 4194304 | tf_op jit(solution)/shard_map/pallas_call | solution.py:107
  35.3 3.4 %all-to-all-start.2 = ((bf16[8,80,128]{2,1,0:T(8,128)(2,1)}), bf16[8,80,128]{2,1,0:T(8,128)(2,1)S(1)}, u32[]{:S(2)}, u32[]{:S(2)}) async-start(bf16[8,80,128]{2,1,0:T(8,128)(2,1)} %spread.4), calls=%async_computation.2 | async-start | bytes 327680 | tf_op jit(solution)/shard_map/all_to_all | solution.py:434
  38.7 4.6 %shard_map.78.source_ref = bf16[6,2048,512]{2,1,0:T(8,128)(2,1)} custom-call(bf16[6,2048,512]{2,1,0:T(8,128)(2,1)} %shard_map.77.refs_0_, bf16[8192,128]{1,0:T(8,128)(2,1)} %points_ref.3, bf16[2048,128]{1,0:T(8,128)(2,1)} %centers_ref.5), custom_call_target="tpu_custom_call", output_to_operand_aliasing={{}: (0, {})} | custom-call | flops 1073741824 | bytes 4194304 | tf_op jit(solution)/shard_map/pallas_call | solution.py:107
  45.4 20.3 %panel.1 = (f32[32,2048]{1,0:T(8,128)}, bf16[2048,128]{1,0:T(8,128)(2,1)}, f32[64,32,128]{2,1,0:T(8,128)}, f32[64,32,128]{2,1,0:T(8,128)}, f32[32,1]{1,0:T(8,128)}) custom-call(s32[2]{0:T(128)} %pad_add_fusion.flags_ref, bf16[2048,128]{1,0:T(8,128)(2,1)} %centers_ref.5, bf16[8,80,128]{2,1,0:T(8,128)(2,1)} %copy-done.7, bf16[128,512]{1,0:T(8,128)(2,1)} %mine_ref.1, ...), custom_call_target="tpu_custom_call" | custom-call | flops 8589934592 | bytes 33554432 | tf_op jit(solution)/shard_map/panel/pallas_call | solution.py:329
  65.7 16.7 %all_to_all.40.x_ref = f32[8,256,128]{2,1,0:T(8,128)S(1)} all-to-all(f32[8,256,128]{2,1,0:T(8,128)} %bitcast.12), channel_id=1, replica_groups=mesh['pts'=4,'ctr_0'=8,'ctr_1'=2,'ctr_2'=4] {'ctr_1','ctr_2'}, dimensions={0} | all-to-all | bytes 2097152 | tf_op jit(solution)/shard_map/all_to_all | solution.py:434
  82.5 14.4 %all_to_all.41.x_ref = f32[8,32,128]{2,1,0:T(8,128)S(1)} all-to-all(f32[8,32,128]{2,1,0:T(8,128)S(1)} %bitcast.10), channel_id=1, replica_groups=mesh['pts'=4,'ctr_0'=8,'ctr_1'=2,'ctr_2'=4] {'ctr_0'}, dimensions={0} | all-to-all | bytes 262144 | tf_op jit(solution)/shard_map/all_to_all | solution.py:434
  97.0 9.6 %all_to_all.42 = bf16[8,32,128]{2,1,0:T(8,128)(2,1)S(1)} all-to-all(bf16[8,32,128]{2,1,0:T(8,128)(2,1)S(1)} %owned.1), channel_id=1, replica_groups=mesh['pts'=4,'ctr_0'=8,'ctr_1'=2,'ctr_2'=4] {'ctr_0'}, dimensions={0} | all-to-all | bytes 131072 | tf_op jit(solution)/shard_map/all_to_all | solution.py:434
  107.4 3.7 %all-to-all-start.6 = ((bf16[8,256,128]{2,1,0:T(8,128)(2,1)}), bf16[8,256,128]{2,1,0:T(8,128)(2,1)S(1)}, u32[]{:S(2)}, u32[]{:S(2)}) async-start(bf16[8,256,128]{2,1,0:T(8,128)(2,1)} %spread.5), calls=%async_computation.6 | async-start | bytes 1048576 | tf_op jit(solution)/shard_map/all_to_all | solution.py:434
  111.1 9.6 %shard_map.79.refs_0_ = bf16[6,1024,2048]{2,1,0:T(8,128)(2,1)} custom-call(f32[32,1]{1,0:T(8,128)} %get-tuple-element.15.z_squares_ref.refs_0_.refs_1_, bf16[8192,128]{1,0:T(8,128)(2,1)} %points_ref.3, bf16[2048,128]{1,0:T(8,128)(2,1)} %centers_ref.5), custom_call_target="tpu_custom_call" | custom-call | flops 4294967296 | bytes 16777216 | tf_op jit(solution)/shard_map/pallas_call | solution.py:107
  120.8 5.0 %shard_map.80.refs_0_ = bf16[6,1024,2048]{2,1,0:T(8,128)(2,1)} custom-call(bf16[6,1024,2048]{2,1,0:T(8,128)(2,1)} %shard_map.79.refs_0_, f32[32,1]{1,0:T(8,128)} %get-tuple-element.15.z_squares_ref.refs_0_.refs_1_, bf16[8192,128]{1,0:T(8,128)(2,1)} %points_ref.3, bf16[2048,128]{1,0:T(8,128)(2,1)} %centers_ref.5), custom_call_target="tpu_custom_call", output_to_operand_aliasing={{}: (0, {})} | custom-call | flops 1073741824 | bytes 4194304 | tf_op jit(solution)/shard_map/pallas_call | solution.py:107
  126.1 7.6 %collective-permute-start.2 = (f32[1,128]{1,0:T(1,128)S(1)}, f32[1,128]{1,0:T(1,128)S(1)}, u32[]{:S(2)}, u32[]{:S(2)}) collective-permute-start(f32[1,128]{1,0:T(1,128)S(1)} %products.1), channel_id=1, source_target_pairs={{0,64},{64,0},{128,192},{192,128},{1,65},{65,1},{129,193},{193,129... | collective-permute-start | bytes 1544 | tf_op jit(solution)/shard_map/ppermute | solution.py:463
  133.8 4.9 %shard_map.81.source_ref = bf16[6,1024,2048]{2,1,0:T(8,128)(2,1)} custom-call(bf16[6,1024,2048]{2,1,0:T(8,128)(2,1)} %shard_map.80.refs_0_, f32[32,1]{1,0:T(8,128)} %get-tuple-element.15.z_squares_ref.refs_0_.refs_1_, bf16[8192,128]{1,0:T(8,128)(2,1)} %points_ref.3, bf16[2048,128]{1,0:T(8,128)(2,1)} %centers_ref.5), custom_call_target="tpu_custom_call", output_to_operand_aliasing={{}: (0, {})} | custom-call | flops 1073741824 | bytes 4194304 | tf_op jit(solution)/shard_map/pallas_call | solution.py:107
  138.8 10.2 %image.1 = (f32[16,2048]{1,0:T(8,128)S(1)}, f32[16,2048]{1,0:T(8,128)S(1)}) custom-call(s32[2]{0:T(128)S(1)} %copy-done.6, f32[1,128]{1,0:T(1,128)S(1)} %add.20.tie_ref, bf16[64,32,128]{2,1,0:T(8,128)(2,1)S(1)} %bitcast.9, bf16[2048,128]{1,0:T(8,128)(2,1)S(1)} %copy-done.1, bf16[8192,128]{1,0:T(8,128)(2,1)S(1)} %copy-done, ...), custom_call_target="tpu_custom_call" | custom-call | flops 8589934592 | bytes 33554432 | tf_op jit(solution)/shard_map/image/pallas_call | solution.py:409
  149.3 1.2 collective-permute-done.3
  151.1 2.5 %collective-permute-start.6 = (f32[1,128]{1,0:T(1,128)S(1)}, f32[1,128]{1,0:T(1,128)S(1)}, u32[]{:S(2)}, u32[]{:S(2)}) collective-permute-start(f32[1,128]{1,0:T(1,128)S(1)} %add.20.tie_ref), channel_id=1, source_target_pairs={{0,128},{64,192},{128,0},{192,64},{1,129},{65,193},{129,1},{193,65... | collective-permute-start | bytes 1544 | tf_op jit(solution)/shard_map/ppermute | solution.py:463
  153.5 3.4 %collective-permute-done.4 = f32[16,2048]{1,0:T(8,128)S(1)} collective-permute-done((f32[16,2048]{1,0:T(8,128)S(1)}, f32[16,2048]{1,0:T(8,128)S(1)}, u32[]{:S(2)}, u32[]{:S(2)}) %collective-permute-start.4) | collective-permute-done | bytes 131104 | tf_op jit(solution)/shard_map/ppermute | solution.py:463
  158.1 15.3 %all_to_all.43.sums_ref = f32[64,1,128]{2,1,0:T(1,128)S(1)} all-to-all(f32[64,1,128]{2,1,0:T(1,128)S(1)} %broadcast_in_dim.9), channel_id=1, replica_groups=mesh['pts'=4,'ctr_0'=8,'ctr_1'=2,'ctr_2'=4] {'ctr_0','ctr_1','ctr_2'}, dimensions={0} | all-to-all | bytes 65536 | tf_op jit(solution)/shard_map/all_to_all | solution.py:434
  173.4 1.5 final.1
  (47 shorter events, 7.9 us)
Async XLA Ops:
  0.6 26.7 %copy-start.8 = (bf16[128,512]{1,0:T(8,128)(2,1)S(1)}, bf16[128,512]{1,0:T(8,128)(2,1)}, u32[]{:S(2)}) copy-start(bf16[128,512]{1,0:T(8,128)(2,1)} %mine_ref.1) | copy-start | bytes 393220
  2.3 11.6 %all-to-all-start = ((bf16[8,80,128]{2,1,0:T(8,128)(2,1)}), bf16[8,80,128]{2,1,0:T(8,128)(2,1)S(1)}, u32[]{:S(2)}, u32[]{:S(2)}) async-start(bf16[8,80,128]{2,1,0:T(8,128)(2,1)} %head.1), calls=%async_computation | async-start | bytes 327680 | tf_op jit(solution)/shard_map/all_to_all | solution.py:434
  8.2 19.1 %collective-permute-start = (bf16[128,512]{1,0:T(8,128)(2,1)}, bf16[128,512]{1,0:T(8,128)(2,1)S(1)}, u32[]{:S(2)}, u32[]{:S(2)}) collective-permute-start(bf16[128,512]{1,0:T(8,128)(2,1)} %mine_ref.1), channel_id=1, source_target_pairs={{0,64},{64,0},{128,192},{192,128},{1,65},{65,1},{129,193},{193,129... | collective-permute-start | bytes 393224 | tf_op jit(solution)/shard_map/ppermute | solution.py:463
  14.6 20.0 %all-to-all-start.1 = ((bf16[8,80,128]{2,1,0:T(8,128)(2,1)}), bf16[8,80,128]{2,1,0:T(8,128)(2,1)S(1)}, u32[]{:S(2)}, u32[]{:S(2)}) async-start(bf16[8,80,128]{2,1,0:T(8,128)(2,1)} %spread.3), calls=%async_computation.1 | async-start | bytes 327680 | tf_op jit(solution)/shard_map/all_to_all | solution.py:434
  27.4 7.2 %copy-start.9 = (bf16[128,512]{1,0:T(8,128)(2,1)}, bf16[128,512]{1,0:T(8,128)(2,1)S(1)}, u32[]{:S(2)}) copy-start(bf16[128,512]{1,0:T(8,128)(2,1)S(1)} %collective-permute-done.other_ref) | copy-start | bytes 393220
  27.4 16.6 %collective-permute-start.1 = (bf16[256,512]{1,0:T(8,128)(2,1)S(1)}, bf16[256,512]{1,0:T(8,128)(2,1)S(1)}, u32[]{:S(2)}, u32[]{:S(2)}) collective-permute-start(bf16[256,512]{1,0:T(8,128)(2,1)S(1)} %pad_maximum_fusion), channel_id=1, source_target_pairs={{0,128},{64,192},{128,0},{192,64},{1,129},{65,193},{129,1},{193,65... | collective-permute-start | bytes 786440 | tf_op jit(solution)/shard_map/ppermute | solution.py:463
  35.3 8.9 %all-to-all-start.2 = ((bf16[8,80,128]{2,1,0:T(8,128)(2,1)}), bf16[8,80,128]{2,1,0:T(8,128)(2,1)S(1)}, u32[]{:S(2)}, u32[]{:S(2)}) async-start(bf16[8,80,128]{2,1,0:T(8,128)(2,1)} %spread.4), calls=%async_computation.2 | async-start | bytes 327680 | tf_op jit(solution)/shard_map/all_to_all | solution.py:434
  44.0 0.7 copy-start.10
  44.7 0.7 copy-start.7
  107.4 18.3 %all-to-all-start.6 = ((bf16[8,256,128]{2,1,0:T(8,128)(2,1)}), bf16[8,256,128]{2,1,0:T(8,128)(2,1)S(1)}, u32[]{:S(2)}, u32[]{:S(2)}) async-start(bf16[8,256,128]{2,1,0:T(8,128)(2,1)} %spread.5), calls=%async_computation.6 | async-start | bytes 1048576 | tf_op jit(solution)/shard_map/all_to_all | solution.py:434
  120.8 5.0 %copy-start.2 = (f32[64,32,128]{2,1,0:T(8,128)S(1)}, f32[64,32,128]{2,1,0:T(8,128)}, u32[]{:S(2)}) copy-start(f32[64,32,128]{2,1,0:T(8,128)} %get-tuple-element.14.both_ref) | copy-start | bytes 3145732
  120.8 5.0 %copy-start.3 = (f32[32,2048]{1,0:T(8,128)S(1)}, f32[32,2048]{1,0:T(8,128)}, u32[]{:S(2)}) copy-start(f32[32,2048]{1,0:T(8,128)} %res_ref.3) | copy-start | bytes 786436
  120.8 5.0 %copy-start.4 = (f32[32,1]{1,0:T(8,128)S(1)}, f32[32,1]{1,0:T(8,128)}, u32[]{:S(2)}) copy-start(f32[32,1]{1,0:T(8,128)} %get-tuple-element.15.z_squares_ref.refs_0_.refs_1_) | copy-start | bytes 388
  126.1 12.6 %copy-start = (bf16[8192,128]{1,0:T(8,128)(2,1)S(1)}, bf16[8192,128]{1,0:T(8,128)(2,1)}, u32[]{:S(2)}) copy-start(bf16[8192,128]{1,0:T(8,128)(2,1)} %points_ref.3) | copy-start | bytes 6291460
  126.1 12.6 %copy-start.1 = (bf16[2048,128]{1,0:T(8,128)(2,1)S(1)}, bf16[2048,128]{1,0:T(8,128)(2,1)}, u32[]{:S(2)}) copy-start(bf16[2048,128]{1,0:T(8,128)(2,1)} %centers_ref.5) | copy-start | bytes 1572868
  126.1 12.6 %copy-start.6 = (s32[2]{0:T(128)S(1)}, s32[2]{0:T(128)}, u32[]{:S(2)}) copy-start(s32[2]{0:T(128)} %pad_add_fusion.flags_ref) | copy-start | bytes 28
  126.1 12.6 %collective-permute-start.2 = (f32[1,128]{1,0:T(1,128)S(1)}, f32[1,128]{1,0:T(1,128)S(1)}, u32[]{:S(2)}, u32[]{:S(2)}) collective-permute-start(f32[1,128]{1,0:T(1,128)S(1)} %products.1), channel_id=1, source_target_pairs={{0,64},{64,0},{128,192},{192,128},{1,65},{65,1},{129,193},{193,129... | collective-permute-start | bytes 1544 | tf_op jit(solution)/shard_map/ppermute | solution.py:463
  138.8 34.7 %copy-start.5 = (f32[32,2048]{1,0:T(8,128)S(1)}, f32[32,2048]{1,0:T(8,128)}, u32[]{:S(2)}) copy-start(f32[32,2048]{1,0:T(8,128)} %get-tuple-element.18.z_ref) | copy-start | bytes 786436
  149.0 1.4 collective-permute-start.3
  150.5 6.5 %collective-permute-start.4 = (f32[16,2048]{1,0:T(8,128)S(1)}, f32[16,2048]{1,0:T(8,128)S(1)}, u32[]{:S(2)}, u32[]{:S(2)}) collective-permute-start(f32[16,2048]{1,0:T(8,128)S(1)} %add.21), channel_id=1, source_target_pairs={{0,128},{64,192},{128,0},{192,64},{1,129},{65,193},{129,1},{193,65... | collective-permute-start | bytes 393224 | tf_op jit(solution)/shard_map/ppermute | solution.py:463
  151.1 7.0 %collective-permute-start.6 = (f32[1,128]{1,0:T(1,128)S(1)}, f32[1,128]{1,0:T(1,128)S(1)}, u32[]{:S(2)}, u32[]{:S(2)}) collective-permute-start(f32[1,128]{1,0:T(1,128)S(1)} %add.20.tie_ref), channel_id=1, source_target_pairs={{0,128},{64,192},{128,0},{192,64},{1,129},{65,193},{129,1},{193,65... | collective-permute-start | bytes 1544 | tf_op jit(solution)/shard_map/ppermute | solution.py:463
  157.0 16.5 %collective-permute-start.5 = (f32[16,2048]{1,0:T(8,128)S(1)}, f32[16,2048]{1,0:T(8,128)S(1)}, u32[]{:S(2)}, u32[]{:S(2)}) collective-permute-start(f32[16,2048]{1,0:T(8,128)S(1)} %add.22.keep_ref), channel_id=1, source_target_pairs={{0,64},{64,0},{128,192},{192,128},{1,65},{65,1},{129,193},{193,129... | collective-permute-start | bytes 393224 | tf_op jit(solution)/shard_map/ppermute | solution.py:463

commit v6 on v5

--- a/solution.py
+++ b/solution.py
@@ -22,7 +22,6 @@
 ANY = pl.BlockSpec(memory_space=pl.ANY)
 LIMIT = 12 << 20
 CHUNK = 1024
-HALF = 512
 WIDTH = 256
 
 
@@ -127,7 +126,48 @@
     )(*extra, points, centers)
 
 
-def head_kernel(centers_ref, dir_ref, out_ref, rows_ref, vals_ref, sems):
+def resident_kernel(points_ref, centers_ref, out_ref, points_buf, centers_buf, wide, sems):
+    loads = [
+        pltpu.make_async_copy(centers_ref, centers_buf, sems.at[0]),
+        pltpu.make_async_copy(points_ref, points_buf, sems.at[1]),
+    ]
+    for copy in loads:
+        copy.start()
+    for copy in loads:
+        copy.wait()
+    wide[...] = widened(centers_buf[...], 0)
+    for i in range(points_buf.shape[0] // CHUNK):
+        rows = slice(i * CHUNK, (i + 1) * CHUNK)
+        fill(0, wide, points_buf[rows], out_ref.at[:, rows])
+
+
+def resident_part(first, count, points, centers, limit):
+    m_dev, features = centers.shape
+
+    def kernel(points_ref, *refs):
+        resident_kernel(points_ref.at[pl.ds(first * CHUNK, count * CHUNK)], *refs)
+
+    return pl.pallas_call(
+        kernel,
+        out_shape=jax.ShapeDtypeStruct((m_dev, count * CHUNK), bf16),
+        in_specs=[ANY, ANY],
+        out_specs=VMEM,
+        scratch_shapes=[
+            pltpu.VMEM((count * CHUNK, features), bf16),
+            pltpu.VMEM((m_dev, features), bf16),
+            pltpu.VMEM((m_dev, 2 * features), bf16),
+            pltpu.SemaphoreType.DMA((2,)),
+        ],
+        compiler_params=pltpu.CompilerParams(vmem_limit_bytes=limit << 20),
+        cost_estimate=pl.CostEstimate(
+            flops=4 * m_dev * count * CHUNK * features,
+            bytes_accessed=2 * m_dev * count * CHUNK,
+            transcendentals=m_dev * count * CHUNK,
+        ),
+    )(points, centers)
+
+
+def head_kernel(flags_ref, centers_ref, dir_ref, out_ref, rows_ref, vals_ref, sems):
     panel, features = rows_ref.shape
     outputs = vals_ref.shape[0]
     first = pltpu.make_async_copy(centers_ref.at[pl.ds(0, panel)], rows_ref, sems.at[0])
@@ -136,24 +176,28 @@
     second.start()
     first.wait()
     second.wait()
-    per = out_ref.shape[1] // 16
-    for g in range(out_ref.shape[0] * per):
-        row = 16 * g
+    root = flags_ref[0] == 0
+    core = flags_ref[1] % 2
+    half = out_ref.shape[0]
+
+    def piece(row):
         if row < panel:
-            x = rows_ref[row : row + 16]
-        else:
-            b, r = divmod(row - panel, outputs)
-            x = vals_ref[r : r + 16, b * features : (b + 1) * features].astype(bf16)
-        out_ref[g // per, (g % per) * 16 : (g % per + 1) * 16] = x
-
-
-def head_payload(centers, direction, panel, ways):
+            return rows_ref[row : row + 16]
+        b, r = divmod(row - panel, outputs)
+        return vals_ref[r : r + 16, b * features : (b + 1) * features].astype(bf16)
+
+    for row in range(0, half, 16):
+        x = jnp.where(core == 0, piece(row).astype(f32), piece(row + half).astype(f32))
+        out_ref[row : row + 16] = jnp.where(root, x, 0.0).astype(bf16)
+
+
+def head_payload(flags, centers, direction, panel):
     outputs, features = direction.shape[0], centers.shape[1]
     rows = panel + outputs * panel // features
     return pl.pallas_call(
         head_kernel,
-        out_shape=jax.ShapeDtypeStruct((ways, rows // ways, features), bf16),
-        in_specs=[ANY, ANY],
+        out_shape=jax.ShapeDtypeStruct((rows // 2, features), bf16),
+        in_specs=[SMEM, ANY, ANY],
         out_specs=VMEM,
         scratch_shapes=[
             pltpu.VMEM((panel, features), bf16),
@@ -162,7 +206,7 @@
         ],
         compiler_params=pltpu.CompilerParams(vmem_limit_bytes=60 << 20),
         name="head",
-    )(centers, direction)
+    )(flags, centers, direction)
 
 
 def spread_kernel(x_ref, *refs):
@@ -231,17 +275,12 @@
 
 
 def panel_kernel(
-    flags_ref, centers_ref, head_ref, mine_ref, other_ref, pair_ref, dir_ref, points_ref,
-    source_ref, z_ref, rows_ref, high_out, both_out, zsq_ref, blocks, made, wide, pinv, zz,
-    points_buf, high_ref, both_ref, sems, points_sem, out_sems,
+    parts, flags_ref, centers_ref, head_ref, head_other_ref, mine_ref, other_ref, pair_ref, dir_ref,
+    *refs
 ):
-    stored = sems.shape[0]
-    local = pltpu.make_async_copy(
-        points_ref.at[pl.ds(stored * HALF, points_buf.shape[0])], points_buf, points_sem
-    )
-    local.start()
-    for i in range(stored):
-        chunk_copy(source_ref, blocks, sems, i).start()
+    blocks, refs = refs[:parts], refs[parts:]
+    z_ref, rows_ref, high_out, both_out, zsq_ref = refs[:5]
+    head, pinv, zz, high_ref, both_ref, out_sems = refs[5:]
     share = mine_ref.shape[0]
     panel = pinv.shape[0]
     outputs = dir_ref.shape[0]
@@ -253,7 +292,9 @@
     pinv[pl.ds(pl.multiple_of((at + 1 - 2 * core) * share, share), share)] = other_ref[...]
     pinv[pl.ds(pl.multiple_of(far + core * share, share), share)] = pair_ref[:share]
     pinv[pl.ds(pl.multiple_of(far + (1 - core) * share, share), share)] = pair_ref[share:]
-    head = jnp.concatenate([head_ref[i] for i in range(head_ref.shape[0])], axis=0)
+    half = head_other_ref.shape[0]
+    head[pl.ds(pl.multiple_of(core * half, half), half)] = head_ref[...]
+    head[pl.ds(pl.multiple_of(half - core * half, half), half)] = head_other_ref[...]
     vals = jnp.concatenate(
         [head[panel + b * outputs : panel + (b + 1) * outputs] for b in range(panel // features)],
         axis=1,
@@ -265,8 +306,7 @@
     squares = jnp.zeros((outputs, 1), f32)
     for i in range(centers_ref.shape[0] // tile):
         rows = slice(i * tile, (i + 1) * tile)
-        wide[rows] = widened(centers_ref[rows], 0)
-        kp = similar(wide[rows], heads, features)
+        kp = similar(widened(centers_ref[rows], 0), heads, features)
         rows_ref[rows] = lax.dot_general(
             kp, mine_ref[...], LAST, preferred_element_type=f32
         ).astype(bf16)
@@ -279,55 +319,35 @@
         zz[:outputs, rows] = high
         zz[outputs:, rows] = (z - high.astype(f32)).astype(bf16)
     zsq_ref[...] = squares
-    local.wait()
-    total = points_ref.shape[0] // HALF
-    per = HALF // 128
-    pair = made.shape[1] // HALF
-
-    def puts(i):
-        span = pl.ds(i * per, per)
-        return [
-            pltpu.make_async_copy(buf.at[span], out.at[span], out_sems.at[i, k])
-            for k, (buf, out) in enumerate(((high_ref, high_out), (both_ref, both_out)))
-        ]
-
-    def use(i, block):
-        u = jnp.dot(zz[...], block, preferred_element_type=f32)
-        for b in range(block.shape[1] // 128):
-            part = u[:, b * 128 : (b + 1) * 128]
-            high_ref[i * per + b] = part[:outputs]
-            both_ref[i * per + b] = part[:outputs] + part[outputs:]
-        for k in range(block.shape[1] // HALF):
-            for put in puts(i + k):
-                put.start()
-
-    def local_step(i, carry):
-        rows = pl.ds(pl.multiple_of(i * pair * HALF, pair * HALF), pair * HALF)
-        fill(0, wide, points_buf[rows], made)
-        use(stored + pair * i, made[...])
-        return carry
-
-    def stored_step(i, carry):
-        chunk_copy(source_ref, blocks, sems, i).wait()
-        use(i, blocks[i])
-        return carry
-
-    lax.fori_loop(0, (total - stored) // pair, local_step, 0)
-    lax.fori_loop(0, stored, stored_step, 0)
-    for i in range(total):
-        for put in puts(i):
-            put.wait()
-
-
-def panel_step(flags, centers, head, mine, other, pair, direction, points, block):
+    puts = []
+    done = 0
+    for block in blocks:
+        for i in range(block.shape[1] // CHUNK):
+            chunk = block[:, i * CHUNK : (i + 1) * CHUNK]
+            u = jnp.dot(zz[...], chunk, preferred_element_type=f32)
+            for b in range(CHUNK // 128):
+                part = u[:, b * 128 : (b + 1) * 128]
+                high_ref[done + b] = part[:outputs]
+                both_ref[done + b] = part[:outputs] + part[outputs:]
+            span = pl.ds(done, CHUNK // 128)
+            for buf, out in ((high_ref, high_out), (both_ref, both_out)):
+                puts.append(
+                    pltpu.make_async_copy(buf.at[span], out.at[span], out_sems.at[len(puts)])
+                )
+                puts[-1].start()
+            done += CHUNK // 128
+    for put in puts:
+        put.wait()
+
+
+def panel_step(flags, centers, head, head_other, mine, other, pair, direction, blocks):
     outputs, m_dev = direction.shape
     share, panel = mine.shape
     features = centers.shape[1]
-    count = points.shape[0] // HALF
-    stored = block.shape[0]
-    values = jax.ShapeDtypeStruct((points.shape[0] // 128, outputs, 128), f32)
-    return pl.pallas_call(
-        panel_kernel,
+    count = sum(block.shape[1] for block in blocks)
+    values = jax.ShapeDtypeStruct((count // 128, outputs, 128), f32)
+    return pl.pallas_call(
+        functools.partial(panel_kernel, len(blocks)),
         out_shape=(
             jax.ShapeDtypeStruct((outputs, m_dev), f32),
             jax.ShapeDtypeStruct((m_dev, share), bf16),
@@ -335,29 +355,24 @@
             values,
             jax.ShapeDtypeStruct((outputs, 1), f32),
         ),
-        in_specs=[SMEM] + [VMEM] * 6 + [ANY, ANY],
+        in_specs=[SMEM] + [VMEM] * (7 + len(blocks)),
         out_specs=(VMEM, VMEM, ANY, ANY, VMEM),
         scratch_shapes=[
-            pltpu.VMEM(block.shape, bf16),
-            pltpu.VMEM((m_dev, CHUNK), bf16),
-            pltpu.VMEM((m_dev, 2 * features), bf16),
+            pltpu.VMEM((2 * head_other.shape[0], features), bf16),
             pltpu.VMEM((panel, panel), bf16),
             pltpu.VMEM((2 * outputs, m_dev), bf16),
-            pltpu.VMEM(((count - stored) * HALF, features), bf16),
             pltpu.VMEM(values.shape, f32),
             pltpu.VMEM(values.shape, f32),
-            pltpu.SemaphoreType.DMA((stored,)),
-            pltpu.SemaphoreType.DMA,
-            pltpu.SemaphoreType.DMA((count, 2)),
+            pltpu.SemaphoreType.DMA((2 * count // CHUNK,)),
         ],
-        compiler_params=pltpu.CompilerParams(vmem_limit_bytes=60 << 20),
+        compiler_params=pltpu.CompilerParams(vmem_limit_bytes=16 << 20),
         cost_estimate=pl.CostEstimate(
-            flops=2 * 256 * m_dev * points.shape[0],
-            bytes_accessed=2 * m_dev * points.shape[0],
+            flops=2 * 256 * m_dev * count,
+            bytes_accessed=2 * m_dev * count,
             transcendentals=m_dev * panel,
         ),
         name="panel",
-    )(flags, centers, head, mine, other, pair, direction, points, block)
+    )(flags, centers, head, head_other, mine, other, pair, direction, *blocks)
 
 
 def image_kernel(
@@ -458,6 +473,11 @@
     )(w, both, z_squares, residual)
 
 
+def tree_stage(x, axis, stride):
+    pairs = [(i, i + stride) for i in range(0, lax.axis_size(axis), 2 * stride)]
+    return x + lax.ppermute(x, axis, pairs)
+
+
 def swap(x, bit):
     n = lax.axis_size("pts")
     return lax.ppermute(x, "pts", [(i, i ^ bit) for i in range(n)])
@@ -503,24 +523,28 @@
     w_scale = 1.0 / (2.0 * math.sqrt(m_dev * n_ctr))
     image_scale = 1.0 / (2.0 * math.sqrt(npg * n_pts))
 
-    head = exchange(head_payload(centers, direction, panel, n_near), NEAR)
-    block = None
-    for i in range(3):
-        block = block_part(0, HALF, 6, 2 * i, 2, points, centers, block)
+    head = head_payload(flags, centers, direction, panel)
+    by_center = []
+    first = 0
+    stages = n_far.bit_length() - 1
+    for count, limit in ((3, 12), (3, 12), (2, 12)):
+        by_center.append(resident_part(first, count, points, centers, limit))
+        first += count
+    for i in range(stages):
+        head = tree_stage(head, FAR, n_far >> (i + 1))
     other = swap(panel_inverse, 1)
     pair = swap(jnp.concatenate([panel_inverse, other], axis=0), 2)
-    head = exchange(spread(head, n_far), FAR)
-    head = exchange(spread(head, n_near), NEAR)
-
+    head = exchange(spread(head, n_near), NEAR)[0]
     z, panel_rows, high, both, z_squares = panel_step(
-        flags, centers, head, panel_inverse, other, pair, direction, points, block
+        flags, centers, head, swap(head, 1),
+        panel_inverse, other, pair, direction, by_center,
     )
 
     parts = exchange(high.reshape(n_near, n_far * outputs, 128), NEAR)
     parts = summed(parts).reshape(n_far, outputs, 128)
     parts = exchange(parts, FAR)
     block = None
-    for first, count in ((0, 4), (4, 1), (5, 1)):
+    for first, count in ((0, 5), (5, 1)):
         block = block_part(1, CHUNK, 6, first, count, points, centers, block, z_squares)
     w = exchange(owned_copies(parts, w_scale, n_far), FAR)
     w = exchange(spread(w.reshape(n_far * outputs, 128), n_near), NEAR)

time: 176 us -> 189 us (1.074)
  local copies, waits for them, and re-layouts: 1.18 us -> 21.8 us
  Pallas kernels: 69.8 us -> 57.5 us
  blocking collectives: 56 us -> 59.2 us
  starting transfers between devices: 36.7 us -> 39 us
    unnamed x22 -> x36, local copies, waits for them, and re-layouts: 1.16 us -> 20.8 us
    pallas_call x6 -> x2, Pallas kernels: 33.4 us -> 16.6 us  [block_part(): pl.pallas_call(functools.partial(block_kernel, side, size, first, count),...]
    all_to_all x4 -> x2, starting transfers between devices: 21.2 us -> 8.83 us  [exchange(): return lax.all_to_all(x, axis, 0, 0, tiled=True)]
    ppermute x0 -> x3, starting transfers between devices: none -> 12.2 us  [tree_stage(): return x + lax.ppermute(x, axis, pairs)]
    all_to_all x4 -> x2, waiting for transfers between devices: 4.95 us -> 0.01 us  [exchange(): return lax.all_to_all(x, axis, 0, 0, tiled=True)]
    pallas_call x2 -> x5, Pallas kernels: 21.9 us -> 26.8 us  [the longest x1 12.9 us: panel_step(): pl.pallas_call(functools.partial(panel_kernel, len(blocks)), out_shape=(j...]
    all_to_all x4, blocking collectives: 56 us -> 59.2 us  [exchange(): return lax.all_to_all(x, axis, 0, 0, tiled=True)]
    ppermute x0 -> x3, waiting for transfers between devices: none -> 3.25 us  [tree_stage(): return x + lax.ppermute(x, axis, pairs)]
  transfers between devices with their start and end apart: 11 -> 13, of which waited for: 4 -> 4; matrix products, arithmetic and copies ran while one was open for 0% -> 1% of each run, Pallas kernels for 20% -> 15%
where the time goes in v6:
time: 189 us
  blocking collectives  59.2 us (31%)
  Pallas kernels  57.5 us (30%)
  starting transfers between devices  39 us (21%)
  local copies, waits for them, and re-layouts  21.8 us (12%)
  waiting for transfers between devices  7.87 us (4%)
  other arithmetic  2.31 us (1%)
    all_to_all x4, blocking collectives, exchange(): return lax.all_to_all(x, axis, 0, 0, tiled=True)  59.2 us
    unnamed x36, local copies, waits for them, and re-layouts  20.8 us
    ppermute x8, starting transfers between devices, swap(): return lax.ppermute(x, 'pts', [(i, i ^ bit) for i in range(n)])  18 us
    pallas_call x2, Pallas kernels, block_part(): pl.pallas_call(functools.partial(block_kernel, side, size, first, count),...  16.6 us
    pallas_call x1, Pallas kernels, panel_step(): pl.pallas_call(functools.partial(panel_kernel, len(blocks)), out_shape=(j...  12.9 us
    ppermute x3, starting transfers between devices, tree_stage(): return x + lax.ppermute(x, axis, pairs)  12.2 us
    pallas_call x3, Pallas kernels, resident_part(): pl.pallas_call(kernel, out_shape=jax.ShapeDtypeStruct((m_dev, count * CHU...  11.6 us
    pallas_call x1, Pallas kernels, image(): pl.pallas_call(image_kernel, out_shape=(shape, shape), in_specs=[SMEM, VM...  10.2 us
  transfers between devices with their start and end apart: 13, of which 4 were waited for; matrix products, arithmetic and copies ran while one was open for 1% of the time, Pallas kernels for 15%

profile of v6, /device:TPU:1, one launch (start us, length us, event | category | flops | bytes accessed | tf_op | source)
XLA Modules:
  0.0 188.7 jit_solution(4872168627241854725)
XLA Ops:
  1.2 2.2 %head.1 = bf16[320,128]{1,0:T(8,128)(2,1)} custom-call(s32[2]{0:T(128)} %pad_add_fusion.flags_ref, bf16[2048,128]{1,0:T(8,128)(2,1)} %centers_ref.5, f32[32,2048]{1,0:T(8,128)} %dir_ref.3), custom_call_target="tpu_custom_call" | custom-call | tf_op jit(solution)/shard_map/head/pallas_call | solution.py:197
  3.5 9.6 %collective-permute-start = (bf16[320,128]{1,0:T(8,128)(2,1)}, bf16[320,128]{1,0:T(8,128)(2,1)S(1)}, u32[]{:S(2)}, u32[]{:S(2)}) collective-permute-start(bf16[320,128]{1,0:T(8,128)(2,1)} %head.1), channel_id=1, source_target_pairs={{0,32},{1,33},{2,34},{3,35},{4,36},{5,37},{6,38},{7,39},{64,96},{6... | collective-permute-start | bytes 245768 | tf_op jit(solution)/shard_map/ppermute | solution.py:478
  19.9 2.2 %collective-permute-start.4 = (bf16[128,512]{1,0:T(8,128)(2,1)}, bf16[128,512]{1,0:T(8,128)(2,1)S(1)}, u32[]{:S(2)}, u32[]{:S(2)}) collective-permute-start(bf16[128,512]{1,0:T(8,128)(2,1)} %mine_ref.1), channel_id=1, source_target_pairs={{0,64},{64,0},{128,192},{192,128},{1,65},{65,1},{129,193},{193,129... | collective-permute-start | bytes 393224 | tf_op jit(solution)/shard_map/ppermute | solution.py:483
  23.1 5.1 %all-to-all-start = ((bf16[8,320,128]{2,1,0:T(8,128)(2,1)}), bf16[8,320,128]{2,1,0:T(8,128)(2,1)}, u32[]{:S(2)}, u32[]{:S(2)}) async-start(bf16[8,320,128]{2,1,0:T(8,128)(2,1)} %spread.2), calls=%async_computation | async-start | bytes 1310720 | tf_op jit(solution)/shard_map/all_to_all | solution.py:449
  30.8 4.3 %shard_map.76.refs_0_ = bf16[2048,3072]{1,0:T(8,128)(2,1)S(1)} custom-call(bf16[8192,128]{1,0:T(8,128)(2,1)S(1)} %copy-done, bf16[2048,128]{1,0:T(8,128)(2,1)S(1)} %copy-done.7), custom_call_target="tpu_custom_call" | custom-call | flops 3221225472 | bytes 12582912 | tf_op jit(solution)/shard_map/pallas_call | solution.py:150
  35.1 4.5 %copy-done.3 = bf16[2048,3072]{1,0:T(8,128)(2,1)} copy-done((bf16[2048,3072]{1,0:T(8,128)(2,1)}, bf16[2048,3072]{1,0:T(8,128)(2,1)S(1)}, u32[]{:S(2)}) %copy-start.3) | copy-done | bytes 12582936
  39.6 4.3 %shard_map.77.refs_1_ = bf16[2048,3072]{1,0:T(8,128)(2,1)S(1)} custom-call(bf16[8192,128]{1,0:T(8,128)(2,1)S(1)} %copy-done, bf16[2048,128]{1,0:T(8,128)(2,1)S(1)} %copy-done.7), custom_call_target="tpu_custom_call" | custom-call | flops 3221225472 | bytes 12582912 | tf_op jit(solution)/shard_map/pallas_call | solution.py:150
  43.9 4.5 %copy-done.5 = bf16[2048,3072]{1,0:T(8,128)(2,1)} copy-done((bf16[2048,3072]{1,0:T(8,128)(2,1)}, bf16[2048,3072]{1,0:T(8,128)(2,1)S(1)}, u32[]{:S(2)}) %copy-start.5) | copy-done | bytes 12582936
  49.2 2.4 %collective-permute-start.5 = (bf16[256,512]{1,0:T(8,128)(2,1)}, bf16[256,512]{1,0:T(8,128)(2,1)S(1)}, u32[]{:S(2)}, u32[]{:S(2)}) collective-permute-start(bf16[256,512]{1,0:T(8,128)(2,1)} %pad_maximum_fusion), channel_id=1, source_target_pairs={{0,128},{64,192},{128,0},{192,64},{1,129},{65,193},{129,1},{193,65... | collective-permute-start | bytes 786440 | tf_op jit(solution)/shard_map/ppermute | solution.py:483
  52.5 2.5 %collective-permute-start.3 = (bf16[320,128]{1,0:T(8,128)(2,1)S(1)}, bf16[320,128]{1,0:T(8,128)(2,1)S(1)}, u32[]{:S(2)}, u32[]{:S(2)}) collective-permute-start(bf16[320,128]{1,0:T(8,128)(2,1)S(1)} %slice_bitcast_fusion.head_ref), channel_id=1, source_target_pairs={{0,64},{64,0},{128,192},{192,128},{1,65},{65,1},{129,193},{193,129... | collective-permute-start | bytes 245768 | tf_op jit(solution)/shard_map/ppermute | solution.py:483
  55.0 3.1 %shard_map.78.refs_2_ = bf16[2048,2048]{1,0:T(8,128)(2,1)S(1)} custom-call(bf16[8192,128]{1,0:T(8,128)(2,1)S(1)} %copy-done.1, bf16[2048,128]{1,0:T(8,128)(2,1)S(1)} %copy-done.8), custom_call_target="tpu_custom_call" | custom-call | flops 2147483648 | bytes 8388608 | tf_op jit(solution)/shard_map/pallas_call | solution.py:150
  58.1 4.6 %copy-done.4 = bf16[2048,3072]{1,0:T(8,128)(2,1)S(1)} copy-done((bf16[2048,3072]{1,0:T(8,128)(2,1)S(1)}, bf16[2048,3072]{1,0:T(8,128)(2,1)}, u32[]{:S(2)}) %copy-start.4) | copy-done | bytes 12582936
  62.7 4.6 %copy-done.6 = bf16[2048,3072]{1,0:T(8,128)(2,1)S(1)} copy-done((bf16[2048,3072]{1,0:T(8,128)(2,1)S(1)}, bf16[2048,3072]{1,0:T(8,128)(2,1)}, u32[]{:S(2)}) %copy-start.6) | copy-done | bytes 12582936
  67.3 12.9 %panel.1 = (f32[32,2048]{1,0:T(8,128)S(1)}, bf16[2048,128]{1,0:T(8,128)(2,1)}, f32[64,32,128]{2,1,0:T(8,128)S(1)}, f32[64,32,128]{2,1,0:T(8,128)S(1)}, f32[32,1]{1,0:T(8,128)S(1)}) custom-call(s32[2]{0:T(128)S(1)} %copy-done.17, bf16[2048,128]{1,0:T(8,128)(2,1)S(1)} %copy-done.8, bf16[320,128]{1,0:T(8,128)(2,1)S(1)} %slice_bitcast_fusion.head_ref, ...), custom_call_target="tpu_custom_call" | custom-call | flops 8589934592 | bytes 33554432 | tf_op jit(solution)/shard_map/panel/pallas_call | solution.py:349
  80.3 17.6 %all_to_all.30.x_ref = f32[8,256,128]{2,1,0:T(8,128)S(1)} all-to-all(f32[8,256,128]{2,1,0:T(8,128)S(1)} %bitcast.12), channel_id=1, replica_groups=mesh['pts'=4,'ctr_0'=8,'ctr_1'=2,'ctr_2'=4] {'ctr_1','ctr_2'}, dimensions={0} | all-to-all | bytes 2097152 | tf_op jit(solution)/shard_map/all_to_all | solution.py:449
  98.0 16.8 %all_to_all.31.x_ref = f32[8,32,128]{2,1,0:T(8,128)S(1)} all-to-all(f32[8,32,128]{2,1,0:T(8,128)S(1)} %bitcast.13), channel_id=1, replica_groups=mesh['pts'=4,'ctr_0'=8,'ctr_1'=2,'ctr_2'=4] {'ctr_0'}, dimensions={0} | all-to-all | bytes 262144 | tf_op jit(solution)/shard_map/all_to_all | solution.py:449
  114.9 9.6 %all_to_all.32 = bf16[8,32,128]{2,1,0:T(8,128)(2,1)S(1)} all-to-all(bf16[8,32,128]{2,1,0:T(8,128)(2,1)S(1)} %owned.1), channel_id=1, replica_groups=mesh['pts'=4,'ctr_0'=8,'ctr_1'=2,'ctr_2'=4] {'ctr_0'}, dimensions={0} | all-to-all | bytes 131072 | tf_op jit(solution)/shard_map/all_to_all | solution.py:449
  125.4 3.7 %all-to-all-start.4 = ((bf16[8,256,128]{2,1,0:T(8,128)(2,1)}), bf16[8,256,128]{2,1,0:T(8,128)(2,1)S(1)}, u32[]{:S(2)}, u32[]{:S(2)}) async-start(bf16[8,256,128]{2,1,0:T(8,128)(2,1)} %spread.3), calls=%async_computation.4 | async-start | bytes 1048576 | tf_op jit(solution)/shard_map/all_to_all | solution.py:449
  129.2 11.6 %shard_map.79.refs_0_ = bf16[6,1024,2048]{2,1,0:T(8,128)(2,1)} custom-call(f32[32,1]{1,0:T(8,128)} %copy-done.15, bf16[8192,128]{1,0:T(8,128)(2,1)} %points_ref.7, bf16[2048,128]{1,0:T(8,128)(2,1)} %centers_ref.5), custom_call_target="tpu_custom_call" | custom-call | flops 5368709120 | bytes 20971520 | tf_op jit(solution)/shard_map/pallas_call | solution.py:106
  141.2 6.4 %collective-permute-start.6 = (f32[1,128]{1,0:T(1,128)S(1)}, f32[1,128]{1,0:T(1,128)S(1)}, u32[]{:S(2)}, u32[]{:S(2)}) collective-permute-start(f32[1,128]{1,0:T(1,128)S(1)} %products.1), channel_id=1, source_target_pairs={{0,64},{64,0},{128,192},{192,128},{1,65},{65,1},{129,193},{193,129... | collective-permute-start | bytes 1544 | tf_op jit(solution)/shard_map/ppermute | solution.py:483
  147.6 4.9 %shard_map.80.source_ref = bf16[6,1024,2048]{2,1,0:T(8,128)(2,1)} custom-call(bf16[6,1024,2048]{2,1,0:T(8,128)(2,1)} %shard_map.79.refs_0_, f32[32,1]{1,0:T(8,128)} %copy-done.15, bf16[8192,128]{1,0:T(8,128)(2,1)} %points_ref.7, bf16[2048,128]{1,0:T(8,128)(2,1)} %centers_ref.5), custom_call_target="tpu_custom_call", output_to_operand_aliasing={{}: (0, {})} | custom-call | flops 1073741824 | bytes 4194304 | tf_op jit(solution)/shard_map/pallas_call | solution.py:106
  152.6 10.2 %image.1 = (f32[16,2048]{1,0:T(8,128)S(1)}, f32[16,2048]{1,0:T(8,128)S(1)}) custom-call(s32[2]{0:T(128)S(1)} %copy-done.17, f32[1,128]{1,0:T(1,128)S(1)} %add.32.tie_ref, bf16[64,32,128]{2,1,0:T(8,128)(2,1)S(1)} %bitcast.11, bf16[2048,128]{1,0:T(8,128)(2,1)S(1)} %copy-done.9, bf16[8192,128]{1,0:T(8,128)(2,1)S(1)} %copy-done.2, ...), custom_call_target="tpu_custom_call" | custom-call | flops 8589934592 | bytes 33554432 | tf_op jit(solution)/shard_map/image/pallas_call | solution.py:424
  167.3 3.4 %collective-permute-done.8 = f32[16,2048]{1,0:T(8,128)S(1)} collective-permute-done((f32[16,2048]{1,0:T(8,128)S(1)}, f32[16,2048]{1,0:T(8,128)S(1)}, u32[]{:S(2)}, u32[]{:S(2)}) %collective-permute-start.8) | collective-permute-done | bytes 131104 | tf_op jit(solution)/shard_map/ppermute | solution.py:483
  171.9 15.3 %all_to_all.33.sums_ref = f32[64,1,128]{2,1,0:T(1,128)S(1)} all-to-all(f32[64,1,128]{2,1,0:T(1,128)S(1)} %broadcast_in_dim.9), channel_id=1, replica_groups=mesh['pts'=4,'ctr_0'=8,'ctr_1'=2,'ctr_2'=4] {'ctr_0','ctr_1','ctr_2'}, dimensions={0} | all-to-all | bytes 65536 | tf_op jit(solution)/shard_map/all_to_all | solution.py:449
  (67 shorter events, 21.2 us)
Async XLA Ops:
  3.5 11.4 %collective-permute-start = (bf16[320,128]{1,0:T(8,128)(2,1)}, bf16[320,128]{1,0:T(8,128)(2,1)S(1)}, u32[]{:S(2)}, u32[]{:S(2)}) collective-permute-start(bf16[320,128]{1,0:T(8,128)(2,1)} %head.1), channel_id=1, source_target_pairs={{0,32},{1,33},{2,34},{3,35},{4,36},{5,37},{6,38},{7,39},{64,96},{6... | collective-permute-start | bytes 245768 | tf_op jit(solution)/shard_map/ppermute | solution.py:478
  15.8 2.8 %collective-permute-start.1 = (bf16[320,128]{1,0:T(8,128)(2,1)S(1)}, bf16[320,128]{1,0:T(8,128)(2,1)S(1)}, u32[]{:S(2)}, u32[]{:S(2)}) collective-permute-start(bf16[320,128]{1,0:T(8,128)(2,1)S(1)} %add.29), channel_id=1, source_target_pairs={{0,16},{32,48},{1,17},{33,49},{2,18},{34,50},{3,19},{35,51},{4,20}... | collective-permute-start | bytes 245768 | tf_op jit(solution)/shard_map/ppermute | solution.py:478
  18.6 3.5 %collective-permute-start.2 = (bf16[320,128]{1,0:T(8,128)(2,1)S(1)}, bf16[320,128]{1,0:T(8,128)(2,1)S(1)}, u32[]{:S(2)}, u32[]{:S(2)}) collective-permute-start(bf16[320,128]{1,0:T(8,128)(2,1)S(1)} %add.30), channel_id=1, source_target_pairs={{0,8},{16,24},{32,40},{48,56},{1,9},{17,25},{33,41},{49,57},{2,10}... | collective-permute-start | bytes 245768 | tf_op jit(solution)/shard_map/ppermute | solution.py:478
  19.9 28.5 %collective-permute-start.4 = (bf16[128,512]{1,0:T(8,128)(2,1)}, bf16[128,512]{1,0:T(8,128)(2,1)S(1)}, u32[]{:S(2)}, u32[]{:S(2)}) collective-permute-start(bf16[128,512]{1,0:T(8,128)(2,1)} %mine_ref.1), channel_id=1, source_target_pairs={{0,64},{64,0},{128,192},{192,128},{1,65},{65,1},{129,193},{193,129... | collective-permute-start | bytes 393224 | tf_op jit(solution)/shard_map/ppermute | solution.py:483
  23.1 28.5 %all-to-all-start = ((bf16[8,320,128]{2,1,0:T(8,128)(2,1)}), bf16[8,320,128]{2,1,0:T(8,128)(2,1)}, u32[]{:S(2)}, u32[]{:S(2)}) async-start(bf16[8,320,128]{2,1,0:T(8,128)(2,1)} %spread.2), calls=%async_computation | async-start | bytes 1310720 | tf_op jit(solution)/shard_map/all_to_all | solution.py:449
  30.8 17.6 %copy-start.12 = (bf16[128,512]{1,0:T(8,128)(2,1)S(1)}, bf16[128,512]{1,0:T(8,128)(2,1)}, u32[]{:S(2)}) copy-start(bf16[128,512]{1,0:T(8,128)(2,1)} %mine_ref.1) | copy-start | bytes 393220
  30.8 24.2 %copy-start.1 = (bf16[8192,128]{1,0:T(8,128)(2,1)S(1)}, bf16[8192,128]{1,0:T(8,128)(2,1)}, u32[]{:S(2)}) copy-start(bf16[8192,128]{1,0:T(8,128)(2,1)} %points_ref.7) | copy-start | bytes 6291460
  30.8 24.2 %copy-start.8 = (bf16[2048,128]{1,0:T(8,128)(2,1)S(1)}, bf16[2048,128]{1,0:T(8,128)(2,1)}, u32[]{:S(2)}) copy-start(bf16[2048,128]{1,0:T(8,128)(2,1)} %centers_ref.5) | copy-start | bytes 1572868
  39.6 18.5 %copy-start.10 = (f32[32,2048]{1,0:T(8,128)S(1)}, f32[32,2048]{1,0:T(8,128)}, u32[]{:S(2)}) copy-start(f32[32,2048]{1,0:T(8,128)} %dir_ref.3) | copy-start | bytes 786436
  39.6 18.5 %copy-start.17 = (s32[2]{0:T(128)S(1)}, s32[2]{0:T(128)}, u32[]{:S(2)}) copy-start(s32[2]{0:T(128)} %pad_add_fusion.flags_ref) | copy-start | bytes 28
  49.2 8.9 %collective-permute-start.5 = (bf16[256,512]{1,0:T(8,128)(2,1)}, bf16[256,512]{1,0:T(8,128)(2,1)S(1)}, u32[]{:S(2)}, u32[]{:S(2)}) collective-permute-start(bf16[256,512]{1,0:T(8,128)(2,1)} %pad_maximum_fusion), channel_id=1, source_target_pairs={{0,128},{64,192},{128,0},{192,64},{1,129},{65,193},{129,1},{193,65... | collective-permute-start | bytes 786440 | tf_op jit(solution)/shard_map/ppermute | solution.py:483
  52.5 5.6 %collective-permute-start.3 = (bf16[320,128]{1,0:T(8,128)(2,1)S(1)}, bf16[320,128]{1,0:T(8,128)(2,1)S(1)}, u32[]{:S(2)}, u32[]{:S(2)}) collective-permute-start(bf16[320,128]{1,0:T(8,128)(2,1)S(1)} %slice_bitcast_fusion.head_ref), channel_id=1, source_target_pairs={{0,64},{64,0},{128,192},{192,128},{1,65},{65,1},{129,193},{193,129... | collective-permute-start | bytes 245768 | tf_op jit(solution)/shard_map/ppermute | solution.py:483
  80.2 44.3 %copy-start.13 = (f32[32,2048]{1,0:T(8,128)}, f32[32,2048]{1,0:T(8,128)S(1)}, u32[]{:S(2)}) copy-start(f32[32,2048]{1,0:T(8,128)S(1)} %get-tuple-element.18.z_ref) | copy-start | bytes 786436
  80.3 44.3 %copy-start.15 = (f32[32,1]{1,0:T(8,128)}, f32[32,1]{1,0:T(8,128)S(1)}, u32[]{:S(2)}) copy-start(f32[32,1]{1,0:T(8,128)S(1)} %get-tuple-element.15.z_squares_ref.refs_0_.refs_1_) | copy-start | bytes 388
  125.4 15.4 %all-to-all-start.4 = ((bf16[8,256,128]{2,1,0:T(8,128)(2,1)}), bf16[8,256,128]{2,1,0:T(8,128)(2,1)S(1)}, u32[]{:S(2)}, u32[]{:S(2)}) async-start(bf16[8,256,128]{2,1,0:T(8,128)(2,1)} %spread.3), calls=%async_computation.4 | async-start | bytes 1048576 | tf_op jit(solution)/shard_map/all_to_all | solution.py:449
  129.1 11.7 %copy-start.11 = (f32[32,2048]{1,0:T(8,128)S(1)}, f32[32,2048]{1,0:T(8,128)}, u32[]{:S(2)}) copy-start(f32[32,2048]{1,0:T(8,128)} %res_ref.3) | copy-start | bytes 786436
  129.2 11.7 %copy-start.16 = (f32[32,1]{1,0:T(8,128)S(1)}, f32[32,1]{1,0:T(8,128)}, u32[]{:S(2)}) copy-start(f32[32,1]{1,0:T(8,128)} %copy-done.15) | copy-start | bytes 388
  141.2 11.4 %copy-start.9 = (bf16[2048,128]{1,0:T(8,128)(2,1)S(1)}, bf16[2048,128]{1,0:T(8,128)(2,1)}, u32[]{:S(2)}) copy-start(bf16[2048,128]{1,0:T(8,128)(2,1)} %centers_ref.5) | copy-start | bytes 1572868
  141.2 11.3 %collective-permute-start.6 = (f32[1,128]{1,0:T(1,128)S(1)}, f32[1,128]{1,0:T(1,128)S(1)}, u32[]{:S(2)}, u32[]{:S(2)}) collective-permute-start(f32[1,128]{1,0:T(1,128)S(1)} %products.1), channel_id=1, source_target_pairs={{0,64},{64,0},{128,192},{192,128},{1,65},{65,1},{129,193},{193,129... | collective-permute-start | bytes 1544 | tf_op jit(solution)/shard_map/ppermute | solution.py:483
  152.6 34.6 %copy-start.14 = (f32[32,2048]{1,0:T(8,128)S(1)}, f32[32,2048]{1,0:T(8,128)}, u32[]{:S(2)}) copy-start(f32[32,2048]{1,0:T(8,128)} %copy-done.13) | copy-start | bytes 786436
  162.8 1.4 collective-permute-start.7
  164.3 6.5 %collective-permute-start.8 = (f32[16,2048]{1,0:T(8,128)S(1)}, f32[16,2048]{1,0:T(8,128)S(1)}, u32[]{:S(2)}, u32[]{:S(2)}) collective-permute-start(f32[16,2048]{1,0:T(8,128)S(1)} %add.33), channel_id=1, source_target_pairs={{0,128},{64,192},{128,0},{192,64},{1,129},{65,193},{129,1},{193,65... | collective-permute-start | bytes 393224 | tf_op jit(solution)/shard_map/ppermute | solution.py:483
  166.0 5.9 %collective-permute-start.10 = (f32[1,128]{1,0:T(1,128)S(1)}, f32[1,128]{1,0:T(1,128)S(1)}, u32[]{:S(2)}, u32[]{:S(2)}) collective-permute-start(f32[1,128]{1,0:T(1,128)S(1)} %add.32.tie_ref), channel_id=1, source_target_pairs={{0,128},{64,192},{128,0},{192,64},{1,129},{65,193},{129,1},{193,65... | collective-permute-start | bytes 1544 | tf_op jit(solution)/shard_map/ppermute | solution.py:483
  170.8 16.4 %collective-permute-start.9 = (f32[16,2048]{1,0:T(8,128)S(1)}, f32[16,2048]{1,0:T(8,128)S(1)}, u32[]{:S(2)}, u32[]{:S(2)}) collective-permute-start(f32[16,2048]{1,0:T(8,128)S(1)} %add.34.keep_ref), channel_id=1, source_target_pairs={{0,64},{64,0},{128,192},{192,128},{1,65},{65,1},{129,193},{193,129... | collective-permute-start | bytes 393224 | tf_op jit(solution)/shard_map/ppermute | solution.py:483
  (7 other events, 32.2 us)

commit v7 on v6

--- a/solution.py
+++ b/solution.py
@@ -473,9 +473,23 @@
     )(w, both, z_squares, residual)
 
 
-def tree_stage(x, axis, stride):
-    pairs = [(i, i + stride) for i in range(0, lax.axis_size(axis), 2 * stride)]
-    return x + lax.ppermute(x, axis, pairs)
+def tree_pairs(sizes):
+    n_far, n_near = sizes
+    stages, holders, stride = [], [0], n_near
+    while stride > 1:
+        stride //= 2
+        stages.append([(i, i + stride) for i in holders])
+        holders = holders + [i + stride for i in holders]
+    stride = n_far
+    while stride > 1:
+        stride //= 2
+        stages.append([(i, i + stride * n_near) for i in holders])
+        holders = holders + [i + stride * n_near for i in holders]
+    return stages
+
+
+def tree_stage(x, pairs):
+    return x + lax.ppermute(x, CTR, pairs)
 
 
 def swap(x, bit):
@@ -526,15 +540,13 @@
     head = head_payload(flags, centers, direction, panel)
     by_center = []
     first = 0
-    stages = n_far.bit_length() - 1
     for count, limit in ((3, 12), (3, 12), (2, 12)):
         by_center.append(resident_part(first, count, points, centers, limit))
         first += count
-    for i in range(stages):
-        head = tree_stage(head, FAR, n_far >> (i + 1))
+    for links in tree_pairs((n_far, n_near)):
+        head = tree_stage(head, links)
     other = swap(panel_inverse, 1)
     pair = swap(jnp.concatenate([panel_inverse, other], axis=0), 2)
-    head = exchange(spread(head, n_near), NEAR)[0]
     z, panel_rows, high, both, z_squares = panel_step(
         flags, centers, head, swap(head, 1),
         panel_inverse, other, pair, direction, by_center,

time: 189 us -> 160 us (0.85)
  local copies, waits for them, and re-layouts: 21.8 us -> 2.72 us
  starting transfers between devices: 39 us -> 30.6 us
    unnamed x36 -> x30, local copies, waits for them, and re-layouts: 20.8 us -> 2.7 us
    all_to_all x2 -> x1, starting transfers between devices: 8.83 us -> 3.88 us  [exchange(): return lax.all_to_all(x, axis, 0, 0, tiled=True)]
    ppermute x8, starting transfers between devices: 18 us -> 16 us  [swap(): return lax.ppermute(x, 'pts', [(i, i ^ bit) for i in range(n)])]
    ppermute x3 -> x6, starting transfers between devices: 12.2 us -> 10.7 us  [tree_stage(): return x + lax.ppermute(x, CTR, pairs)]
  transfers between devices with their start and end apart: 13 -> 15, of which waited for: 4 -> 4; matrix products, arithmetic and copies ran while one was open for 1% -> 0% of each run, Pallas kernels for 15% -> 18%
where the time goes in v7:
time: 160 us; the launch traced here: 159 us
  blocking collectives  58.5 us (37%)
  Pallas kernels  56.6 us (35%)
  starting transfers between devices  30.6 us (19%)
  waiting for transfers between devices  7.87 us (5%)
  local copies, waits for them, and re-layouts  2.72 us (2%)
  other arithmetic  1.69 us (1%)
    all_to_all x4, blocking collectives, exchange(): return lax.all_to_all(x, axis, 0, 0, tiled=True)  58.5 us
    pallas_call x2, Pallas kernels, block_part(): pl.pallas_call(functools.partial(block_kernel, side, size, first, count),...  16.6 us
    ppermute x8, starting transfers between devices, swap(): return lax.ppermute(x, 'pts', [(i, i ^ bit) for i in range(n)])  16 us
    pallas_call x1, Pallas kernels, panel_step(): pl.pallas_call(functools.partial(panel_kernel, len(blocks)), out_shape=(j...  13 us
    pallas_call x3, Pallas kernels, resident_part(): pl.pallas_call(kernel, out_shape=jax.ShapeDtypeStruct((m_dev, count * CHU...  11.6 us
    ppermute x6, starting transfers between devices, tree_stage(): return x + lax.ppermute(x, CTR, pairs)  10.7 us
    pallas_call x1, Pallas kernels, image(): pl.pallas_call(image_kernel, out_shape=(shape, shape), in_specs=[SMEM, VM...  10.3 us
    ppermute x8, waiting for transfers between devices, swap(): return lax.ppermute(x, 'pts', [(i, i ^ bit) for i in range(n)])  4.62 us
  transfers between devices with their start and end apart: 15, of which 4 were waited for; matrix products, arithmetic and copies ran while one was open for 0% of the time, Pallas kernels for 18%

profile of v7, /device:TPU:1, one launch (start us, length us, event | category | flops | bytes accessed | tf_op | source)
XLA Modules:
  0.0 159.1 jit_solution(16370065107274477925)
XLA Ops:
  1.2 2.2 %head.1 = bf16[320,128]{1,0:T(8,128)(2,1)} custom-call(s32[2]{0:T(128)} %pad_add_fusion.flags_ref, bf16[2048,128]{1,0:T(8,128)(2,1)} %centers_ref.5, f32[32,2048]{1,0:T(8,128)} %dir_ref.3), custom_call_target="tpu_custom_call" | custom-call | tf_op jit(solution)/shard_map/head/pallas_call | solution.py:197
  3.5 4.1 %collective-permute-start = (bf16[320,128]{1,0:T(8,128)(2,1)}, bf16[320,128]{1,0:T(8,128)(2,1)S(1)}, u32[]{:S(2)}, u32[]{:S(2)}) collective-permute-start(bf16[320,128]{1,0:T(8,128)(2,1)} %head.1), channel_id=1, source_target_pairs={{0,4},{64,68},{128,132},{192,196}} | collective-permute-start | bytes 245768 | tf_op jit(solution)/shard_map/ppermute | solution.py:492
  7.6 1.8 %collective-permute-done = bf16[320,128]{1,0:T(8,128)(2,1)S(1)} collective-permute-done((bf16[320,128]{1,0:T(8,128)(2,1)}, bf16[320,128]{1,0:T(8,128)(2,1)S(1)}, u32[]{:S(2)}, u32[]{:S(2)}) %collective-permute-start) | collective-permute-done | bytes 81952 | tf_op jit(solution)/shard_map/ppermute | solution.py:492
  11.6 1.5 collective-permute-done.1
  14.4 2.2 %collective-permute-start.7 = (bf16[128,512]{1,0:T(8,128)(2,1)}, bf16[128,512]{1,0:T(8,128)(2,1)S(1)}, u32[]{:S(2)}, u32[]{:S(2)}) collective-permute-start(bf16[128,512]{1,0:T(8,128)(2,1)} %mine_ref.1), channel_id=1, source_target_pairs={{0,64},{64,0},{128,192},{192,128},{1,65},{65,1},{129,193},{193,129... | collective-permute-start | bytes 393224 | tf_op jit(solution)/shard_map/ppermute | solution.py:497
  17.9 1.6 copy-done
  20.5 4.3 %shard_map.76.refs_0_ = bf16[2048,3072]{1,0:T(8,128)(2,1)S(1)} custom-call(bf16[8192,128]{1,0:T(8,128)(2,1)S(1)} %copy-done, bf16[2048,128]{1,0:T(8,128)(2,1)S(1)} %copy-done.2), custom_call_target="tpu_custom_call" | custom-call | flops 3221225472 | bytes 12582912 | tf_op jit(solution)/shard_map/pallas_call | solution.py:150
  26.2 2.5 %collective-permute-start.8 = (bf16[256,512]{1,0:T(8,128)(2,1)S(1)}, bf16[256,512]{1,0:T(8,128)(2,1)S(1)}, u32[]{:S(2)}, u32[]{:S(2)}) collective-permute-start(bf16[256,512]{1,0:T(8,128)(2,1)S(1)} %pad_maximum_fusion), channel_id=1, source_target_pairs={{0,128},{64,192},{128,0},{192,64},{1,129},{65,193},{129,1},{193,65... | collective-permute-start | bytes 786440 | tf_op jit(solution)/shard_map/ppermute | solution.py:497
  30.2 4.3 %shard_map.77.refs_1_ = bf16[2048,3072]{1,0:T(8,128)(2,1)S(1)} custom-call(bf16[8192,128]{1,0:T(8,128)(2,1)S(1)} %copy-done, bf16[2048,128]{1,0:T(8,128)(2,1)S(1)} %copy-done.3), custom_call_target="tpu_custom_call" | custom-call | flops 3221225472 | bytes 12582912 | tf_op jit(solution)/shard_map/pallas_call | solution.py:150
  34.6 2.5 %collective-permute-start.6 = (bf16[320,128]{1,0:T(8,128)(2,1)S(1)}, bf16[320,128]{1,0:T(8,128)(2,1)S(1)}, u32[]{:S(2)}, u32[]{:S(2)}) collective-permute-start(bf16[320,128]{1,0:T(8,128)(2,1)S(1)} %add.43.head_ref), channel_id=1, source_target_pairs={{0,64},{64,0},{128,192},{192,128},{1,65},{65,1},{129,193},{193,129... | collective-permute-start | bytes 245768 | tf_op jit(solution)/shard_map/ppermute | solution.py:497
  37.1 3.1 %shard_map.78.refs_2_ = bf16[2048,2048]{1,0:T(8,128)(2,1)S(1)} custom-call(bf16[8192,128]{1,0:T(8,128)(2,1)S(1)} %copy-done, bf16[2048,128]{1,0:T(8,128)(2,1)S(1)} %copy-done.3), custom_call_target="tpu_custom_call" | custom-call | flops 2147483648 | bytes 8388608 | tf_op jit(solution)/shard_map/pallas_call | solution.py:150
  40.2 13.0 %panel.1 = (f32[32,2048]{1,0:T(8,128)S(1)}, bf16[2048,128]{1,0:T(8,128)(2,1)}, f32[64,32,128]{2,1,0:T(8,128)S(1)}, f32[64,32,128]{2,1,0:T(8,128)S(1)}, f32[32,1]{1,0:T(8,128)S(1)}) custom-call(s32[2]{0:T(128)S(1)} %copy-done.14, bf16[2048,128]{1,0:T(8,128)(2,1)S(1)} %copy-done.3, bf16[320,128]{1,0:T(8,128)(2,1)S(1)} %add.43.head_ref, ...), custom_call_target="tpu_custom_call" | custom-call | flops 8589934592 | bytes 33554432 | tf_op jit(solution)/shard_map/panel/pallas_call | solution.py:349
  53.2 21.5 %all_to_all.25.x_ref = f32[8,256,128]{2,1,0:T(8,128)S(1)} all-to-all(f32[8,256,128]{2,1,0:T(8,128)S(1)} %bitcast.10), channel_id=1, replica_groups=mesh['pts'=4,'ctr_0'=8,'ctr_1'=2,'ctr_2'=4] {'ctr_1','ctr_2'}, dimensions={0} | all-to-all | bytes 2097152 | tf_op jit(solution)/shard_map/all_to_all | solution.py:449
  74.9 12.2 %all_to_all.26.x_ref = f32[8,32,128]{2,1,0:T(8,128)S(1)} all-to-all(f32[8,32,128]{2,1,0:T(8,128)S(1)} %bitcast.11), channel_id=1, replica_groups=mesh['pts'=4,'ctr_0'=8,'ctr_1'=2,'ctr_2'=4] {'ctr_0'}, dimensions={0} | all-to-all | bytes 262144 | tf_op jit(solution)/shard_map/all_to_all | solution.py:449
  87.2 9.6 %all_to_all.27 = bf16[8,32,128]{2,1,0:T(8,128)(2,1)S(1)} all-to-all(bf16[8,32,128]{2,1,0:T(8,128)(2,1)S(1)} %owned.1), channel_id=1, replica_groups=mesh['pts'=4,'ctr_0'=8,'ctr_1'=2,'ctr_2'=4] {'ctr_0'}, dimensions={0} | all-to-all | bytes 131072 | tf_op jit(solution)/shard_map/all_to_all | solution.py:449
  97.6 3.9 %all-to-all-start.3 = ((bf16[8,256,128]{2,1,0:T(8,128)(2,1)}), bf16[8,256,128]{2,1,0:T(8,128)(2,1)S(1)}, u32[]{:S(2)}, u32[]{:S(2)}) async-start(bf16[8,256,128]{2,1,0:T(8,128)(2,1)} %spread.1), calls=%async_computation.3 | async-start | bytes 1048576 | tf_op jit(solution)/shard_map/all_to_all | solution.py:449
  101.5 11.7 %shard_map.79.refs_0_ = bf16[6,1024,2048]{2,1,0:T(8,128)(2,1)} custom-call(f32[32,1]{1,0:T(8,128)} %copy-done.12, bf16[8192,128]{1,0:T(8,128)(2,1)} %points_ref.7, bf16[2048,128]{1,0:T(8,128)(2,1)} %centers_ref.5), custom_call_target="tpu_custom_call" | custom-call | flops 5368709120 | bytes 20971520 | tf_op jit(solution)/shard_map/pallas_call | solution.py:106
  113.6 4.4 %collective-permute-start.9 = (f32[1,128]{1,0:T(1,128)S(1)}, f32[1,128]{1,0:T(1,128)S(1)}, u32[]{:S(2)}, u32[]{:S(2)}) collective-permute-start(f32[1,128]{1,0:T(1,128)S(1)} %products.1), channel_id=1, source_target_pairs={{0,64},{64,0},{128,192},{192,128},{1,65},{65,1},{129,193},{193,129... | collective-permute-start | bytes 1544 | tf_op jit(solution)/shard_map/ppermute | solution.py:497
  118.0 4.9 %shard_map.80.source_ref = bf16[6,1024,2048]{2,1,0:T(8,128)(2,1)} custom-call(bf16[6,1024,2048]{2,1,0:T(8,128)(2,1)} %shard_map.79.refs_0_, f32[32,1]{1,0:T(8,128)} %copy-done.12, bf16[8192,128]{1,0:T(8,128)(2,1)} %points_ref.7, bf16[2048,128]{1,0:T(8,128)(2,1)} %centers_ref.5), custom_call_target="tpu_custom_call", output_to_operand_aliasing={{}: (0, {})} | custom-call | flops 1073741824 | bytes 4194304 | tf_op jit(solution)/shard_map/pallas_call | solution.py:106
  123.0 10.3 %image.1 = (f32[16,2048]{1,0:T(8,128)S(1)}, f32[16,2048]{1,0:T(8,128)S(1)}) custom-call(s32[2]{0:T(128)S(1)} %copy-done.14, f32[1,128]{1,0:T(1,128)S(1)} %add.44.tie_ref, bf16[64,32,128]{2,1,0:T(8,128)(2,1)S(1)} %bitcast.9, bf16[2048,128]{1,0:T(8,128)(2,1)S(1)} %copy-done.4, bf16[8192,128]{1,0:T(8,128)(2,1)S(1)} %copy-done.1, ...), custom_call_target="tpu_custom_call" | custom-call | flops 8589934592 | bytes 33554432 | tf_op jit(solution)/shard_map/image/pallas_call | solution.py:424
  134.7 2.0 %collective-permute-start.11 = (f32[16,2048]{1,0:T(8,128)S(1)}, f32[16,2048]{1,0:T(8,128)S(1)}, u32[]{:S(2)}, u32[]{:S(2)}) collective-permute-start(f32[16,2048]{1,0:T(8,128)S(1)} %add.45), channel_id=1, source_target_pairs={{0,128},{64,192},{128,0},{192,64},{1,129},{65,193},{129,1},{193,65... | collective-permute-start | bytes 393224 | tf_op jit(solution)/shard_map/ppermute | solution.py:497
  137.8 3.4 %collective-permute-done.11 = f32[16,2048]{1,0:T(8,128)S(1)} collective-permute-done((f32[16,2048]{1,0:T(8,128)S(1)}, f32[16,2048]{1,0:T(8,128)S(1)}, u32[]{:S(2)}, u32[]{:S(2)}) %collective-permute-start.11) | collective-permute-done | bytes 131104 | tf_op jit(solution)/shard_map/ppermute | solution.py:497
  142.4 15.2 %all_to_all.28.sums_ref = f32[64,1,128]{2,1,0:T(1,128)S(1)} all-to-all(f32[64,1,128]{2,1,0:T(1,128)S(1)} %broadcast_in_dim.9), channel_id=1, replica_groups=mesh['pts'=4,'ctr_0'=8,'ctr_1'=2,'ctr_2'=4] {'ctr_0','ctr_1','ctr_2'}, dimensions={0} | all-to-all | bytes 65536 | tf_op jit(solution)/shard_map/all_to_all | solution.py:449
  157.6 1.5 final.1
  (66 shorter events, 14.5 us)
Async XLA Ops:
  0.6 25.6 %copy-start.9 = (bf16[128,512]{1,0:T(8,128)(2,1)S(1)}, bf16[128,512]{1,0:T(8,128)(2,1)}, u32[]{:S(2)}) copy-start(bf16[128,512]{1,0:T(8,128)(2,1)} %mine_ref.1) | copy-start | bytes 393220
  3.5 26.7 %copy-start.3 = (bf16[2048,128]{1,0:T(8,128)(2,1)S(1)}, bf16[2048,128]{1,0:T(8,128)(2,1)}, u32[]{:S(2)}) copy-start(bf16[2048,128]{1,0:T(8,128)(2,1)} %centers_ref.5) | copy-start | bytes 1572868
  3.5 5.9 %collective-permute-start = (bf16[320,128]{1,0:T(8,128)(2,1)}, bf16[320,128]{1,0:T(8,128)(2,1)S(1)}, u32[]{:S(2)}, u32[]{:S(2)}) collective-permute-start(bf16[320,128]{1,0:T(8,128)(2,1)} %head.1), channel_id=1, source_target_pairs={{0,4},{64,68},{128,132},{192,196}} | collective-permute-start | bytes 245768 | tf_op jit(solution)/shard_map/ppermute | solution.py:492
  10.3 2.8 %collective-permute-start.1 = (bf16[320,128]{1,0:T(8,128)(2,1)S(1)}, bf16[320,128]{1,0:T(8,128)(2,1)S(1)}, u32[]{:S(2)}, u32[]{:S(2)}) collective-permute-start(bf16[320,128]{1,0:T(8,128)(2,1)S(1)} %add.38), channel_id=1, source_target_pairs={{0,2},{4,6},{64,66},{68,70},{128,130},{132,134},{192,194},{196,198}} | collective-permute-start | bytes 245768 | tf_op jit(solution)/shard_map/ppermute | solution.py:492
  13.1 3.5 %collective-permute-start.2 = (bf16[320,128]{1,0:T(8,128)(2,1)S(1)}, bf16[320,128]{1,0:T(8,128)(2,1)S(1)}, u32[]{:S(2)}, u32[]{:S(2)}) collective-permute-start(bf16[320,128]{1,0:T(8,128)(2,1)S(1)} %add.39), channel_id=1, source_target_pairs={{0,1},{4,5},{2,3},{6,7},{64,65},{68,69},{66,67},{70,71},{128,129},... | collective-permute-start | bytes 245768 | tf_op jit(solution)/shard_map/ppermute | solution.py:492
  14.4 11.8 %collective-permute-start.7 = (bf16[128,512]{1,0:T(8,128)(2,1)}, bf16[128,512]{1,0:T(8,128)(2,1)S(1)}, u32[]{:S(2)}, u32[]{:S(2)}) collective-permute-start(bf16[128,512]{1,0:T(8,128)(2,1)} %mine_ref.1), channel_id=1, source_target_pairs={{0,64},{64,0},{128,192},{192,128},{1,65},{65,1},{129,193},{193,129... | collective-permute-start | bytes 393224 | tf_op jit(solution)/shard_map/ppermute | solution.py:497
  16.6 8.2 %collective-permute-start.3 = (bf16[320,128]{1,0:T(8,128)(2,1)S(1)}, bf16[320,128]{1,0:T(8,128)(2,1)S(1)}, u32[]{:S(2)}, u32[]{:S(2)}) collective-permute-start(bf16[320,128]{1,0:T(8,128)(2,1)S(1)} %add.40), channel_id=1, source_target_pairs={{0,32},{4,36},{2,34},{6,38},{1,33},{5,37},{3,35},{7,39},{64,96},{6... | collective-permute-start | bytes 245768 | tf_op jit(solution)/shard_map/ppermute | solution.py:492
  24.9 3.9 %collective-permute-start.4 = (bf16[320,128]{1,0:T(8,128)(2,1)S(1)}, bf16[320,128]{1,0:T(8,128)(2,1)S(1)}, u32[]{:S(2)}, u32[]{:S(2)}) collective-permute-start(bf16[320,128]{1,0:T(8,128)(2,1)S(1)} %add.41), channel_id=1, source_target_pairs={{0,16},{4,20},{2,18},{6,22},{1,17},{5,21},{3,19},{7,23},{32,48},{3... | collective-permute-start | bytes 245768 | tf_op jit(solution)/shard_map/ppermute | solution.py:492
  26.2 13.9 %collective-permute-start.8 = (bf16[256,512]{1,0:T(8,128)(2,1)S(1)}, bf16[256,512]{1,0:T(8,128)(2,1)S(1)}, u32[]{:S(2)}, u32[]{:S(2)}) collective-permute-start(bf16[256,512]{1,0:T(8,128)(2,1)S(1)} %pad_maximum_fusion), channel_id=1, source_target_pairs={{0,128},{64,192},{128,0},{192,64},{1,129},{65,193},{129,1},{193,65... | collective-permute-start | bytes 786440 | tf_op jit(solution)/shard_map/ppermute | solution.py:497
  28.8 5.7 %collective-permute-start.5 = (bf16[320,128]{1,0:T(8,128)(2,1)S(1)}, bf16[320,128]{1,0:T(8,128)(2,1)S(1)}, u32[]{:S(2)}, u32[]{:S(2)}) collective-permute-start(bf16[320,128]{1,0:T(8,128)(2,1)S(1)} %add.42), channel_id=1, source_target_pairs={{0,8},{4,12},{2,10},{6,14},{1,9},{5,13},{3,11},{7,15},{32,40},{36,... | collective-permute-start | bytes 245768 | tf_op jit(solution)/shard_map/ppermute | solution.py:492
  34.6 5.6 %collective-permute-start.6 = (bf16[320,128]{1,0:T(8,128)(2,1)S(1)}, bf16[320,128]{1,0:T(8,128)(2,1)S(1)}, u32[]{:S(2)}, u32[]{:S(2)}) collective-permute-start(bf16[320,128]{1,0:T(8,128)(2,1)S(1)} %add.43.head_ref), channel_id=1, source_target_pairs={{0,64},{64,0},{128,192},{192,128},{1,65},{65,1},{129,193},{193,129... | collective-permute-start | bytes 245768 | tf_op jit(solution)/shard_map/ppermute | solution.py:497
  53.2 21.7 %copy-start.6 = (f32[64,32,128]{2,1,0:T(8,128)}, f32[64,32,128]{2,1,0:T(8,128)S(1)}, u32[]{:S(2)}) copy-start(f32[64,32,128]{2,1,0:T(8,128)S(1)} %get-tuple-element.14.both_ref) | copy-start | bytes 3145732
  53.2 43.6 %copy-start.10 = (f32[32,2048]{1,0:T(8,128)}, f32[32,2048]{1,0:T(8,128)S(1)}, u32[]{:S(2)}) copy-start(f32[32,2048]{1,0:T(8,128)S(1)} %get-tuple-element.18.z_ref) | copy-start | bytes 786436
  53.2 43.6 %copy-start.12 = (f32[32,1]{1,0:T(8,128)}, f32[32,1]{1,0:T(8,128)S(1)}, u32[]{:S(2)}) copy-start(f32[32,1]{1,0:T(8,128)S(1)} %get-tuple-element.15.z_squares_ref.refs_0_.refs_1_) | copy-start | bytes 388
  97.6 15.6 %all-to-all-start.3 = ((bf16[8,256,128]{2,1,0:T(8,128)(2,1)}), bf16[8,256,128]{2,1,0:T(8,128)(2,1)S(1)}, u32[]{:S(2)}, u32[]{:S(2)}) async-start(bf16[8,256,128]{2,1,0:T(8,128)(2,1)} %spread.1), calls=%async_computation.3 | async-start | bytes 1048576 | tf_op jit(solution)/shard_map/all_to_all | solution.py:449
  101.5 11.7 %copy-start.7 = (f32[64,32,128]{2,1,0:T(8,128)S(1)}, f32[64,32,128]{2,1,0:T(8,128)}, u32[]{:S(2)}) copy-start(f32[64,32,128]{2,1,0:T(8,128)} %copy-done.6) | copy-start | bytes 3145732
  101.5 11.7 %copy-start.8 = (f32[32,2048]{1,0:T(8,128)S(1)}, f32[32,2048]{1,0:T(8,128)}, u32[]{:S(2)}) copy-start(f32[32,2048]{1,0:T(8,128)} %res_ref.3) | copy-start | bytes 786436
  101.5 11.7 %copy-start.13 = (f32[32,1]{1,0:T(8,128)S(1)}, f32[32,1]{1,0:T(8,128)}, u32[]{:S(2)}) copy-start(f32[32,1]{1,0:T(8,128)} %copy-done.12) | copy-start | bytes 388
  113.6 9.3 %collective-permute-start.9 = (f32[1,128]{1,0:T(1,128)S(1)}, f32[1,128]{1,0:T(1,128)S(1)}, u32[]{:S(2)}, u32[]{:S(2)}) collective-permute-start(f32[1,128]{1,0:T(1,128)S(1)} %products.1), channel_id=1, source_target_pairs={{0,64},{64,0},{128,192},{192,128},{1,65},{65,1},{129,193},{193,129... | collective-permute-start | bytes 1544 | tf_op jit(solution)/shard_map/ppermute | solution.py:497
  123.0 34.6 %copy-start.11 = (f32[32,2048]{1,0:T(8,128)S(1)}, f32[32,2048]{1,0:T(8,128)}, u32[]{:S(2)}) copy-start(f32[32,2048]{1,0:T(8,128)} %copy-done.10) | copy-start | bytes 786436
  133.3 1.4 collective-permute-start.10
  134.7 6.5 %collective-permute-start.11 = (f32[16,2048]{1,0:T(8,128)S(1)}, f32[16,2048]{1,0:T(8,128)S(1)}, u32[]{:S(2)}, u32[]{:S(2)}) collective-permute-start(f32[16,2048]{1,0:T(8,128)S(1)} %add.45), channel_id=1, source_target_pairs={{0,128},{64,192},{128,0},{192,64},{1,129},{65,193},{129,1},{193,65... | collective-permute-start | bytes 393224 | tf_op jit(solution)/shard_map/ppermute | solution.py:497
  136.7 5.6 %collective-permute-start.13 = (f32[1,128]{1,0:T(1,128)S(1)}, f32[1,128]{1,0:T(1,128)S(1)}, u32[]{:S(2)}, u32[]{:S(2)}) collective-permute-start(f32[1,128]{1,0:T(1,128)S(1)} %add.44.tie_ref), channel_id=1, source_target_pairs={{0,128},{64,192},{128,0},{192,64},{1,129},{65,193},{129,1},{193,65... | collective-permute-start | bytes 1544 | tf_op jit(solution)/shard_map/ppermute | solution.py:497
  141.2 16.4 %collective-permute-start.12 = (f32[16,2048]{1,0:T(8,128)S(1)}, f32[16,2048]{1,0:T(8,128)S(1)}, u32[]{:S(2)}, u32[]{:S(2)}) collective-permute-start(f32[16,2048]{1,0:T(8,128)S(1)} %add.46.keep_ref), channel_id=1, source_target_pairs={{0,64},{64,0},{128,192},{192,128},{1,65},{65,1},{129,193},{193,129... | collective-permute-start | bytes 393224 | tf_op jit(solution)/shard_map/ppermute | solution.py:497
  (6 other events, 44.2 us)

commit v8 on v7

--- a/solution.py
+++ b/solution.py
@@ -23,6 +23,7 @@
 LIMIT = 12 << 20
 CHUNK = 1024
 WIDTH = 256
+EXTRA = 16
 
 
 def widened(x, side):
@@ -209,64 +210,106 @@
     )(flags, centers, direction)
 
 
-def spread_kernel(x_ref, *refs):
-    out_ref = refs[-1]
-    x = x_ref[0] if len(x_ref.shape) == len(out_ref.shape) else x_ref[...]
+def pieces(x, count):
+    parts = []
+    for i in range(count):
+        part = x.astype(bf16)
+        parts.append(part)
+        if i + 1 < count:
+            x = x - part.astype(f32)
+    return parts
+
+
+def partial_sums(ref, outputs, rows=slice(None)):
+    totals = None
+    for i in range(ref.shape[0]):
+        x = ref[i, rows].astype(f32)
+        x = (x[:outputs] + x[outputs : 2 * outputs], x[2 * outputs :])
+        totals = x if totals is None else (totals[0] + x[0], totals[1] + x[1])
+    return totals
+
+
+def sum_kernel(x_ref, out_ref):
+    rows = out_ref.shape[1]
+    outputs = rows // 3
+    for k in range(out_ref.shape[0]):
+        high, low = partial_sums(x_ref, outputs, slice(k * rows, (k + 1) * rows))
+        out_ref[k] = jnp.concatenate([*pieces(high, 2), low.astype(bf16)], axis=0)
+
+
+def summed(x, rows, per=2):
+    ways, lanes = x.shape[0], x.shape[2]
+    count = x.shape[1] // rows
+    return pl.pallas_call(
+        sum_kernel,
+        out_shape=jax.ShapeDtypeStruct((count, rows, lanes), bf16),
+        grid=(count // per,),
+        in_specs=[pl.BlockSpec((ways, per * rows, lanes), lambda i: (0, i, 0))],
+        out_specs=pl.BlockSpec((per, rows, lanes), lambda i: (i, 0, 0)),
+        compiler_params=pltpu.CompilerParams(vmem_limit_bytes=LIMIT),
+        name="summed",
+    )(x)
+
+
+def scalar_rows(x):
+    rows = jnp.concatenate([p.astype(f32) for p in pieces(x, 3)], axis=0)
+    return jnp.concatenate([rows, jnp.zeros((EXTRA - 3, x.shape[1]), f32)], axis=0).astype(bf16)
+
+
+def owned_kernel(scale, image_scale, count, x_ref, z_squares_ref, res_ref, out_ref):
+    outputs = z_squares_ref.shape[0]
+    high, low = partial_sums(x_ref, outputs)
+    w = (high * scale).astype(bf16)
+    mine = jnp.sum(w.astype(f32) * (high + low), axis=1, keepdims=True) * image_scale
+    mine = mine + (RIDGE_TERM / count) * z_squares_ref[...]
+    squares = jnp.sum(res_ref[...] * res_ref[...], axis=1, keepdims=True) * (1.0 / count)
+    lane = lax.broadcasted_iota(jnp.int32, w.shape, 1)
+    row = lax.broadcasted_iota(jnp.int32, w.shape, 0)
+    scalars = jnp.where(lane == row, mine, jnp.where(lane == row + outputs, squares, 0.0))
+    scalars = scalar_rows(jnp.sum(scalars, axis=0, keepdims=True))
     for i in range(out_ref.shape[0]):
-        out_ref[i] = x
-
-
-def spread(x, ways):
-    shape = x.shape[1:] if len(x.shape) == 3 else x.shape
-    return pl.pallas_call(
-        spread_kernel,
-        out_shape=jax.ShapeDtypeStruct((ways, *shape), x.dtype),
+        out_ref[i, :outputs] = w
+        out_ref[i, outputs:] = scalars
+
+
+def owned_copies(x, z_squares, residual, scale, image_scale, count, ways):
+    outputs, lanes = z_squares.shape[0], x.shape[2]
+    return pl.pallas_call(
+        functools.partial(owned_kernel, scale, image_scale, count),
+        out_shape=jax.ShapeDtypeStruct((ways, outputs + EXTRA, lanes), bf16),
+        in_specs=[VMEM] * 3,
+        out_specs=VMEM,
+        compiler_params=pltpu.CompilerParams(vmem_limit_bytes=LIMIT),
+        name="owned",
+    )(x, z_squares, residual)
+
+
+def scalar_sum(ref, first):
+    total = ref[0, first : first + EXTRA].astype(f32)
+    for i in range(1, ref.shape[0]):
+        total = total + ref[i, first : first + EXTRA].astype(f32)
+    return jnp.sum(total, axis=0, keepdims=True)
+
+
+def relay_kernel(x_ref, out_ref):
+    ways, rows, _ = x_ref.shape
+    outputs = rows - EXTRA
+    scalars = scalar_rows(scalar_sum(x_ref, outputs))
+    for i in range(out_ref.shape[0]):
+        for k in range(ways):
+            out_ref[i, k * outputs : (k + 1) * outputs] = x_ref[k, :outputs]
+        out_ref[i, ways * outputs :] = scalars
+
+
+def relay_copies(x, ways):
+    count, rows, lanes = x.shape
+    return pl.pallas_call(
+        relay_kernel,
+        out_shape=jax.ShapeDtypeStruct((ways, count * (rows - EXTRA) + EXTRA, lanes), bf16),
         in_specs=[VMEM],
         out_specs=VMEM,
         compiler_params=pltpu.CompilerParams(vmem_limit_bytes=LIMIT),
-        name="spread",
-    )(x)
-
-
-def sum_kernel(x_ref, out_ref):
-    total = x_ref[0]
-    for i in range(1, x_ref.shape[0]):
-        total = total + x_ref[i]
-    out_ref[...] = total
-
-
-def summed(x, steps=4):
-    ways, rows, lanes = x.shape
-    block = rows // steps
-    return pl.pallas_call(
-        sum_kernel,
-        out_shape=jax.ShapeDtypeStruct((rows, lanes), x.dtype),
-        grid=(steps,),
-        in_specs=[pl.BlockSpec((ways, block, lanes), lambda i: (0, i, 0))],
-        out_specs=pl.BlockSpec((block, lanes), lambda i: (i, 0)),
-        compiler_params=pltpu.CompilerParams(vmem_limit_bytes=LIMIT),
-        name="summed",
-    )(x)
-
-
-def owned_kernel(scale, x_ref, *refs):
-    out_ref = refs[-1]
-    total = x_ref[0]
-    for i in range(1, x_ref.shape[0]):
-        total = total + x_ref[i]
-    total = (total * scale).astype(bf16)
-    for i in range(out_ref.shape[0]):
-        out_ref[i] = total
-
-
-def owned_copies(x, scale, ways):
-    return pl.pallas_call(
-        functools.partial(owned_kernel, scale),
-        out_shape=jax.ShapeDtypeStruct((ways, *x.shape[1:]), bf16),
-        in_specs=[VMEM],
-        out_specs=VMEM,
-        compiler_params=pltpu.CompilerParams(vmem_limit_bytes=LIMIT),
-        name="owned",
+        name="relay",
     )(x)
 
 
@@ -279,8 +322,8 @@
     *refs
 ):
     blocks, refs = refs[:parts], refs[parts:]
-    z_ref, rows_ref, high_out, both_out, zsq_ref = refs[:5]
-    head, pinv, zz, high_ref, both_ref, out_sems = refs[5:]
+    z_ref, rows_ref, parts_out, zsq_ref = refs[:4]
+    head, pinv, zz, parts_buf, out_sems = refs[4:]
     share = mine_ref.shape[0]
     panel = pinv.shape[0]
     outputs = dir_ref.shape[0]
@@ -327,14 +370,16 @@
             u = jnp.dot(zz[...], chunk, preferred_element_type=f32)
             for b in range(CHUNK // 128):
                 part = u[:, b * 128 : (b + 1) * 128]
-                high_ref[done + b] = part[:outputs]
-                both_ref[done + b] = part[:outputs] + part[outputs:]
+                parts_buf[done + b] = jnp.concatenate(
+                    [*pieces(part[:outputs], 2), part[outputs:].astype(bf16)], axis=0
+                )
             span = pl.ds(done, CHUNK // 128)
-            for buf, out in ((high_ref, high_out), (both_ref, both_out)):
-                puts.append(
-                    pltpu.make_async_copy(buf.at[span], out.at[span], out_sems.at[len(puts)])
+            puts.append(
+                pltpu.make_async_copy(
+                    parts_buf.at[span], parts_out.at[span], out_sems.at[len(puts)]
                 )
-                puts[-1].start()
+            )
+            puts[-1].start()
             done += CHUNK // 128
     for put in puts:
         put.wait()
@@ -345,25 +390,23 @@
     share, panel = mine.shape
     features = centers.shape[1]
     count = sum(block.shape[1] for block in blocks)
-    values = jax.ShapeDtypeStruct((count // 128, outputs, 128), f32)
+    values = jax.ShapeDtypeStruct((count // 128, 3 * outputs, 128), bf16)
     return pl.pallas_call(
         functools.partial(panel_kernel, len(blocks)),
         out_shape=(
             jax.ShapeDtypeStruct((outputs, m_dev), f32),
             jax.ShapeDtypeStruct((m_dev, share), bf16),
             values,
-            values,
             jax.ShapeDtypeStruct((outputs, 1), f32),
         ),
         in_specs=[SMEM] + [VMEM] * (7 + len(blocks)),
-        out_specs=(VMEM, VMEM, ANY, ANY, VMEM),
+        out_specs=(VMEM, VMEM, ANY, VMEM),
         scratch_shapes=[
             pltpu.VMEM((2 * head_other.shape[0], features), bf16),
             pltpu.VMEM((panel, panel), bf16),
             pltpu.VMEM((2 * outputs, m_dev), bf16),
-            pltpu.VMEM(values.shape, f32),
-            pltpu.VMEM(values.shape, f32),
-            pltpu.SemaphoreType.DMA((2 * count // CHUNK,)),
+            pltpu.VMEM(values.shape, bf16),
+            pltpu.SemaphoreType.DMA((count // CHUNK,)),
         ],
         compiler_params=pltpu.CompilerParams(vmem_limit_bytes=16 << 20),
         cost_estimate=pl.CostEstimate(
@@ -376,7 +419,7 @@
 
 
 def image_kernel(
-    flags_ref, tie_ref, w_ref, centers_ref, points_ref, source_ref, keep_ref, send_ref,
+    flags_ref, w_ref, centers_ref, points_ref, source_ref, keep_ref, send_ref,
     blocks, made, wide, total, points_buf, sems, points_sem,
 ):
     stored = sems.shape[0]
@@ -391,9 +434,12 @@
     local.wait()
     count = points_ref.shape[0] // CHUNK
     width = CHUNK // 128
+    outputs, m_dev = total.shape
 
     def use(i, block):
-        w = jnp.concatenate([w_ref[i * width + b] for b in range(width)], axis=1)
+        w = jnp.concatenate(
+            [w_ref[i, b * outputs : (b + 1) * outputs] for b in range(width)], axis=1
+        )
         total[...] += jnp.dot(w, block, preferred_element_type=f32)
 
     def local_step(i, carry):
@@ -411,20 +457,22 @@
     lax.fori_loop(0, stored, stored_step, 0)
     half = keep_ref.shape[0]
     mine = pl.multiple_of((flags_ref[1] % 2) * half, half)
-    keep_ref[...] = total[pl.ds(mine, half)]
-    send_ref[...] = total[pl.ds(half - mine, half)]
-
-
-def image(flags, tie, w, centers, points, block):
-    outputs = w.shape[1]
+    keep_ref[:, :m_dev] = total[pl.ds(mine, half)]
+    send_ref[:, :m_dev] = total[pl.ds(half - mine, half)]
+    scalars = jnp.broadcast_to(scalar_sum(w_ref, width * outputs), (half, 128))
+    keep_ref[:, m_dev:] = scalars
+    send_ref[:, m_dev:] = scalars
+
+
+def image(flags, outputs, w, centers, points, block):
     m_dev, features = centers.shape
     count = points.shape[0] // CHUNK
     stored = block.shape[0]
-    shape = jax.ShapeDtypeStruct((outputs // 2, m_dev), f32)
+    shape = jax.ShapeDtypeStruct((outputs // 2, m_dev + 128), f32)
     return pl.pallas_call(
         image_kernel,
         out_shape=(shape, shape),
-        in_specs=[SMEM, VMEM, VMEM, VMEM, ANY, ANY],
+        in_specs=[SMEM, VMEM, VMEM, ANY, ANY],
         out_specs=(VMEM, VMEM),
         scratch_shapes=[
             pltpu.VMEM(block.shape, bf16),
@@ -442,35 +490,11 @@
             transcendentals=0,
         ),
         name="image",
-    )(flags, tie, w, centers, points, block)
+    )(flags, w, centers, points, block)
 
 
 def exchange(x, axis):
     return lax.all_to_all(x, axis, 0, 0, tiled=True)
-
-
-def products_kernel(scale, ridge, count, w_ref, both_ref, z_squares_ref, res_ref, out_ref):
-    outputs = w_ref.shape[1]
-    total = jnp.zeros(w_ref.shape[1:], f32)
-    for i in range(w_ref.shape[0]):
-        total = total + w_ref[i].astype(f32) * both_ref[i]
-    mine = jnp.sum(total, axis=1, keepdims=True) * scale + ridge * z_squares_ref[...]
-    squares = jnp.sum(res_ref[...] * res_ref[...], axis=1, keepdims=True) * (1.0 / count)
-    lane = lax.broadcasted_iota(jnp.int32, total.shape, 1)
-    row = lax.broadcasted_iota(jnp.int32, total.shape, 0)
-    spread_out = jnp.where(lane == row, mine, jnp.where(lane == row + outputs, squares, 0.0))
-    out_ref[...] = jnp.sum(spread_out, axis=0, keepdims=True)
-
-
-def products(w, both, z_squares, residual, scale, count):
-    return pl.pallas_call(
-        functools.partial(products_kernel, scale, RIDGE_TERM / count, count),
-        out_shape=jax.ShapeDtypeStruct((1, 128), f32),
-        in_specs=[VMEM] * 4,
-        out_specs=VMEM,
-        compiler_params=pltpu.CompilerParams(vmem_limit_bytes=LIMIT),
-        name="products",
-    )(w, both, z_squares, residual)
 
 
 def tree_pairs(sizes):
@@ -497,31 +521,31 @@
     return lax.ppermute(x, "pts", [(i, i ^ bit) for i in range(n)])
 
 
-def final_kernel(scale, flags_ref, keep_ref, other_ref, z_ref, res_ref, sums_ref, op_ref, new_ref):
-    outputs = z_ref.shape[0]
+def final_kernel(scale, flags_ref, keep_ref, other_ref, z_ref, res_ref, op_ref, new_ref):
+    outputs, m_dev = z_ref.shape
     half = keep_ref.shape[0]
-    sums = jnp.sum(sums_ref[...], axis=0)
+    sums = keep_ref[0:1, m_dev:]
     lane = lax.broadcasted_iota(jnp.int32, (outputs, sums.shape[1]), 1)
     row = lax.broadcasted_iota(jnp.int32, (outputs, sums.shape[1]), 0)
     curvature = jnp.sum(jnp.where(lane == row, sums, 0.0), axis=1, keepdims=True)
     squares = jnp.sum(jnp.where(lane == row + outputs, sums, 0.0), axis=1, keepdims=True)
     op_ref[...] = RIDGE_TERM * z_ref[...]
     mine = pl.multiple_of((flags_ref[1] % 2) * half, half)
-    op_ref[pl.ds(mine, half)] += keep_ref[...] * scale
-    op_ref[pl.ds(half - mine, half)] += other_ref[...] * scale
+    op_ref[pl.ds(mine, half)] += keep_ref[:, :m_dev] * scale
+    op_ref[pl.ds(half - mine, half)] += other_ref[:, :m_dev] * scale
     new_ref[...] = res_ref[...] - (squares / curvature) * op_ref[...]
 
 
-def final_step(flags, keep, other, z, residual, sums, scale):
+def final_step(flags, keep, other, z, residual, scale):
     shape = jax.ShapeDtypeStruct(z.shape, f32)
     return pl.pallas_call(
         functools.partial(final_kernel, scale),
         out_shape=(shape, shape),
-        in_specs=[SMEM] + [VMEM] * 5,
+        in_specs=[SMEM] + [VMEM] * 4,
         out_specs=(VMEM, VMEM),
         compiler_params=pltpu.CompilerParams(vmem_limit_bytes=LIMIT),
         name="final",
-    )(flags, keep, other, z, residual, sums)
+    )(flags, keep, other, z, residual)
 
 
 def step(points, centers, panel_inverse, direction, residual):
@@ -547,32 +571,25 @@
         head = tree_stage(head, links)
     other = swap(panel_inverse, 1)
     pair = swap(jnp.concatenate([panel_inverse, other], axis=0), 2)
-    z, panel_rows, high, both, z_squares = panel_step(
+    z, panel_rows, parts, z_squares = panel_step(
         flags, centers, head, swap(head, 1),
         panel_inverse, other, pair, direction, by_center,
     )
 
-    parts = exchange(high.reshape(n_near, n_far * outputs, 128), NEAR)
-    parts = summed(parts).reshape(n_far, outputs, 128)
-    parts = exchange(parts, FAR)
+    rows = 3 * outputs
+    parts = exchange(parts.reshape(n_near, n_far * rows, 128), NEAR)
+    parts = exchange(summed(parts, rows), FAR)
     block = None
     for first, count in ((0, 5), (5, 1)):
         block = block_part(1, CHUNK, 6, first, count, points, centers, block, z_squares)
-    w = exchange(owned_copies(parts, w_scale, n_far), FAR)
-    w = exchange(spread(w.reshape(n_far * outputs, 128), n_near), NEAR)
-    w = w.reshape(-1, outputs, 128)
-
-    scalars = products(w, both, z_squares, residual, image_scale, n_pts)
-    scalars = scalars + swap(scalars, 1)
-    keep, send = image(flags, scalars, w, centers, points, block)
-    scalars = scalars + swap(scalars, 2)
-    sums = jnp.broadcast_to(scalars[None], (n_ctr, *scalars.shape))
-    sums = exchange(sums, CTR)
+    w = owned_copies(parts, z_squares, residual, w_scale, image_scale, n_pts, n_far)
+    w = exchange(w, FAR)
+    w = exchange(relay_copies(w, n_near), NEAR)
+
+    keep, send = image(flags, outputs, w, centers, points, block)
     keep = keep + swap(send, 1)
     keep = keep + swap(keep, 2)
-    operator_image, new_residual = final_step(
-        flags, keep, swap(keep, 1), z, residual, sums, image_scale
-    )
+    operator_image, new_residual = final_step(flags, keep, swap(keep, 1), z, residual, image_scale)
     return (panel_rows, operator_image, new_residual)
 
 

time: 160 us -> 151 us (0.944)
  blocking collectives: 58.5 us -> 50 us
  waiting for transfers between devices: 7.87 us -> 9.7 us
    all_to_all x4 -> x3, blocking collectives: 58.5 us -> 50 us  [exchange(): return lax.all_to_all(x, axis, 0, 0, tiled=True)]
    ppermute x8 -> x6, starting transfers between devices: 16 us -> 13.9 us  [swap(): return lax.ppermute(x, 'pts', [(i, i ^ bit) for i in range(n)])]
    ppermute x8 -> x6, waiting for transfers between devices: 4.62 us -> 6.44 us  [swap(): return lax.ppermute(x, 'pts', [(i, i ^ bit) for i in range(n)])]
  transfers between devices with their start and end apart: 15 -> 13, of which waited for: 4 -> 5; matrix products, arithmetic and copies ran while one was open for 0% -> 0% of each run, Pallas kernels for 18% -> 19%
where the time goes in v8:
time: 151 us; the launch traced here: 150 us
  Pallas kernels  56 us (37%)
  blocking collectives  50 us (33%)
  starting transfers between devices  29.4 us (19%)
  waiting for transfers between devices  9.7 us (6%)
  local copies, waits for them, and re-layouts  2.7 us (2%)
  other arithmetic  1.68 us (1%)
    all_to_all x3, blocking collectives, exchange(): return lax.all_to_all(x, axis, 0, 0, tiled=True)  50 us
    pallas_call x2, Pallas kernels, block_part(): pl.pallas_call(functools.partial(block_kernel, side, size, first, count),...  16.6 us
    ppermute x6, starting transfers between devices, swap(): return lax.ppermute(x, 'pts', [(i, i ^ bit) for i in range(n)])  13.9 us
    pallas_call x1, Pallas kernels, panel_step(): pl.pallas_call(functools.partial(panel_kernel, len(blocks)), out_shape=(j...  12.2 us
    pallas_call x3, Pallas kernels, resident_part(): pl.pallas_call(kernel, out_shape=jax.ShapeDtypeStruct((m_dev, count * CHU...  11.6 us
    ppermute x6, starting transfers between devices, tree_stage(): return x + lax.ppermute(x, CTR, pairs)  10.5 us
    pallas_call x1, Pallas kernels, image(): pl.pallas_call(image_kernel, out_shape=(shape, shape), in_specs=[SMEM, VM...  10.3 us
    ppermute x6, waiting for transfers between devices, swap(): return lax.ppermute(x, 'pts', [(i, i ^ bit) for i in range(n)])  6.44 us
  transfers between devices with their start and end apart: 13, of which 5 were waited for; matrix products, arithmetic and copies ran while one was open for 0% of the time, Pallas kernels for 19%

profile of v8, /device:TPU:1, one launch (start us, length us, event | category | flops | bytes accessed | tf_op | source)
XLA Modules:
  0.0 150.5 jit_solution(4915072652304286680)
XLA Ops:
  1.2 2.2 %head.1 = bf16[320,128]{1,0:T(8,128)(2,1)} custom-call(s32[2]{0:T(128)} %pad_add_fusion.flags_ref, bf16[2048,128]{1,0:T(8,128)(2,1)} %centers_ref.5, f32[32,2048]{1,0:T(8,128)} %dir_ref.3), custom_call_target="tpu_custom_call" | custom-call | tf_op jit(solution)/shard_map/head/pallas_call | solution.py:198
  3.5 3.9 %collective-permute-start = (bf16[320,128]{1,0:T(8,128)(2,1)}, bf16[320,128]{1,0:T(8,128)(2,1)S(1)}, u32[]{:S(2)}, u32[]{:S(2)}) collective-permute-start(bf16[320,128]{1,0:T(8,128)(2,1)} %head.1), channel_id=1, source_target_pairs={{0,4},{64,68},{128,132},{192,196}} | collective-permute-start | bytes 245768 | tf_op jit(solution)/shard_map/ppermute | solution.py:516
  7.4 1.8 %collective-permute-done = bf16[320,128]{1,0:T(8,128)(2,1)S(1)} collective-permute-done((bf16[320,128]{1,0:T(8,128)(2,1)}, bf16[320,128]{1,0:T(8,128)(2,1)S(1)}, u32[]{:S(2)}, u32[]{:S(2)}) %collective-permute-start) | collective-permute-done | bytes 81952 | tf_op jit(solution)/shard_map/ppermute | solution.py:516
  11.4 1.5 collective-permute-done.1
  14.2 2.2 %collective-permute-start.7 = (bf16[128,512]{1,0:T(8,128)(2,1)}, bf16[128,512]{1,0:T(8,128)(2,1)S(1)}, u32[]{:S(2)}, u32[]{:S(2)}) collective-permute-start(bf16[128,512]{1,0:T(8,128)(2,1)} %mine_ref.1), channel_id=1, source_target_pairs={{0,64},{64,0},{128,192},{192,128},{1,65},{65,1},{129,193},{193,129... | collective-permute-start | bytes 393224 | tf_op jit(solution)/shard_map/ppermute | solution.py:521
  17.8 1.6 %copy-done = bf16[8192,128]{1,0:T(8,128)(2,1)S(1)} copy-done((bf16[8192,128]{1,0:T(8,128)(2,1)S(1)}, bf16[8192,128]{1,0:T(8,128)(2,1)}, u32[]{:S(2)}) %copy-start) | copy-done | bytes 2097176
  20.4 4.3 %shard_map.77.refs_1_ = bf16[2048,3072]{1,0:T(8,128)(2,1)S(1)} custom-call(bf16[8192,128]{1,0:T(8,128)(2,1)S(1)} %copy-done, bf16[2048,128]{1,0:T(8,128)(2,1)S(1)} %copy-done.2), custom_call_target="tpu_custom_call" | custom-call | flops 3221225472 | bytes 12582912 | tf_op jit(solution)/shard_map/pallas_call | solution.py:151
  26.1 2.5 %collective-permute-start.8 = (bf16[256,512]{1,0:T(8,128)(2,1)S(1)}, bf16[256,512]{1,0:T(8,128)(2,1)S(1)}, u32[]{:S(2)}, u32[]{:S(2)}) collective-permute-start(bf16[256,512]{1,0:T(8,128)(2,1)S(1)} %pad_maximum_fusion), channel_id=1, source_target_pairs={{0,128},{64,192},{128,0},{192,64},{1,129},{65,193},{129,1},{193,65... | collective-permute-start | bytes 786440 | tf_op jit(solution)/shard_map/ppermute | solution.py:521
  28.7 1.4 collective-permute-start.5
  30.1 4.3 %shard_map.76.refs_0_ = bf16[2048,3072]{1,0:T(8,128)(2,1)S(1)} custom-call(bf16[8192,128]{1,0:T(8,128)(2,1)S(1)} %copy-done, bf16[2048,128]{1,0:T(8,128)(2,1)S(1)} %copy-done.3), custom_call_target="tpu_custom_call" | custom-call | flops 3221225472 | bytes 12582912 | tf_op jit(solution)/shard_map/pallas_call | solution.py:151
  34.5 2.5 %collective-permute-start.6 = (bf16[320,128]{1,0:T(8,128)(2,1)S(1)}, bf16[320,128]{1,0:T(8,128)(2,1)S(1)}, u32[]{:S(2)}, u32[]{:S(2)}) collective-permute-start(bf16[320,128]{1,0:T(8,128)(2,1)S(1)} %add.37.head_ref), channel_id=1, source_target_pairs={{0,64},{64,0},{128,192},{192,128},{1,65},{65,1},{129,193},{193,129... | collective-permute-start | bytes 245768 | tf_op jit(solution)/shard_map/ppermute | solution.py:521
  37.0 3.1 %shard_map.78.refs_2_ = bf16[2048,2048]{1,0:T(8,128)(2,1)S(1)} custom-call(bf16[8192,128]{1,0:T(8,128)(2,1)S(1)} %copy-done, bf16[2048,128]{1,0:T(8,128)(2,1)S(1)} %copy-done.3), custom_call_target="tpu_custom_call" | custom-call | flops 2147483648 | bytes 8388608 | tf_op jit(solution)/shard_map/pallas_call | solution.py:151
  40.1 12.2 %panel.1 = (f32[32,2048]{1,0:T(8,128)S(1)}, bf16[2048,128]{1,0:T(8,128)(2,1)}, bf16[64,96,128]{2,1,0:T(8,128)(2,1)S(1)}, f32[32,1]{1,0:T(8,128)S(1)}) custom-call(s32[2]{0:T(128)S(1)} %copy-done.12, bf16[2048,128]{1,0:T(8,128)(2,1)S(1)} %copy-done.3, bf16[320,128]{1,0:T(8,128)(2,1)S(1)} %add.37.head_ref, ...), custom_call_target="tpu_custom_call" | custom-call | flops 8589934592 | bytes 33554432 | tf_op jit(solution)/shard_map/panel/pallas_call | solution.py:394
  52.3 27.1 %all_to_all.20.x_ref = bf16[8,768,128]{2,1,0:T(8,128)(2,1)S(1)} all-to-all(bf16[8,768,128]{2,1,0:T(8,128)(2,1)S(1)} %bitcast.3), channel_id=1, replica_groups=mesh['pts'=4,'ctr_0'=8,'ctr_1'=2,'ctr_2'=4] {'ctr_1','ctr_2'}, dimensions={0} | all-to-all | bytes 3145728 | tf_op jit(solution)/shard_map/all_to_all | solution.py:497
  79.9 12.9 %all_to_all.21.x_ref = bf16[8,96,128]{2,1,0:T(8,128)(2,1)S(1)} all-to-all(bf16[8,96,128]{2,1,0:T(8,128)(2,1)S(1)} %summed.1), channel_id=1, replica_groups=mesh['pts'=4,'ctr_0'=8,'ctr_1'=2,'ctr_2'=4] {'ctr_0'}, dimensions={0} | all-to-all | bytes 393216 | tf_op jit(solution)/shard_map/all_to_all | solution.py:497
  93.0 10.0 %all_to_all.22.x_ref = bf16[8,48,128]{2,1,0:T(8,128)(2,1)S(1)} all-to-all(bf16[8,48,128]{2,1,0:T(8,128)(2,1)S(1)} %owned.1), channel_id=1, replica_groups=mesh['pts'=4,'ctr_0'=8,'ctr_1'=2,'ctr_2'=4] {'ctr_0'}, dimensions={0} | all-to-all | bytes 196608 | tf_op jit(solution)/shard_map/all_to_all | solution.py:497
  103.9 4.9 %all-to-all-start.3 = ((bf16[8,272,128]{2,1,0:T(8,128)(2,1)}), bf16[8,272,128]{2,1,0:T(8,128)(2,1)S(1)}, u32[]{:S(2)}, u32[]{:S(2)}) async-start(bf16[8,272,128]{2,1,0:T(8,128)(2,1)} %relay.1), calls=%async_computation.3 | async-start | bytes 1114112 | tf_op jit(solution)/shard_map/all_to_all | solution.py:497
  108.9 11.5 %shard_map.79.refs_0_ = bf16[6,1024,2048]{2,1,0:T(8,128)(2,1)} custom-call(f32[32,1]{1,0:T(8,128)} %copy-done.11, bf16[8192,128]{1,0:T(8,128)(2,1)} %points_ref.7, bf16[2048,128]{1,0:T(8,128)(2,1)} %centers_ref.5), custom_call_target="tpu_custom_call" | custom-call | flops 5368709120 | bytes 20971520 | tf_op jit(solution)/shard_map/pallas_call | solution.py:107
  120.4 5.1 %shard_map.80.source_ref = bf16[6,1024,2048]{2,1,0:T(8,128)(2,1)} custom-call(bf16[6,1024,2048]{2,1,0:T(8,128)(2,1)} %shard_map.79.refs_0_, f32[32,1]{1,0:T(8,128)} %copy-done.11, bf16[8192,128]{1,0:T(8,128)(2,1)} %points_ref.7, bf16[2048,128]{1,0:T(8,128)(2,1)} %centers_ref.5), custom_call_target="tpu_custom_call", output_to_operand_aliasing={{}: (0, {})} | custom-call | flops 1073741824 | bytes 4194304 | tf_op jit(solution)/shard_map/pallas_call | solution.py:107
  125.6 10.3 %image.1 = (f32[16,2176]{1,0:T(8,128)S(1)}, f32[16,2176]{1,0:T(8,128)S(1)}) custom-call(s32[2]{0:T(128)S(1)} %copy-done.12, bf16[8,272,128]{2,1,0:T(8,128)(2,1)S(1)} %all-to-all-done.3.w_ref, bf16[2048,128]{1,0:T(8,128)(2,1)S(1)} %copy-done.4, bf16[8192,128]{1,0:T(8,128)(2,1)S(1)} %copy-done.1, bf16[6,1024,2048]{2,1,0:T(8,128)(2,1)} %shard_map.80.source_ref), custom_call_target="tpu_custom_call" | custom-call | flops 8589934592 | bytes 33554432 | tf_op jit(solution)/shard_map/image/pallas_call | solution.py:472
  135.9 3.4 %collective-permute-start.9 = (f32[16,2176]{1,0:T(8,128)S(1)}, f32[16,2176]{1,0:T(8,128)S(1)}, u32[]{:S(2)}, u32[]{:S(2)}) collective-permute-start(f32[16,2176]{1,0:T(8,128)S(1)} %get-tuple-element.15), channel_id=1, source_target_pairs={{0,64},{64,0},{128,192},{192,128},{1,65},{65,1},{129,193},{193,129... | collective-permute-start | bytes 417800 | tf_op jit(solution)/shard_map/ppermute | solution.py:521
  140.3 2.0 %collective-permute-start.10 = (f32[16,2176]{1,0:T(8,128)S(1)}, f32[16,2176]{1,0:T(8,128)S(1)}, u32[]{:S(2)}, u32[]{:S(2)}) collective-permute-start(f32[16,2176]{1,0:T(8,128)S(1)} %add.38), channel_id=1, source_target_pairs={{0,128},{64,192},{128,0},{192,64},{1,129},{65,193},{129,1},{193,65... | collective-permute-start | bytes 417800 | tf_op jit(solution)/shard_map/ppermute | solution.py:521
  142.3 4.4 %collective-permute-done.10 = f32[16,2176]{1,0:T(8,128)S(1)} collective-permute-done((f32[16,2176]{1,0:T(8,128)S(1)}, f32[16,2176]{1,0:T(8,128)S(1)}, u32[]{:S(2)}, u32[]{:S(2)}) %collective-permute-start.10) | collective-permute-done | bytes 139296 | tf_op jit(solution)/shard_map/ppermute | solution.py:521
  149.1 1.4 final.1
  (53 shorter events, 12.9 us)
Async XLA Ops:
  0.6 29.5 %copy-start.3 = (bf16[2048,128]{1,0:T(8,128)(2,1)S(1)}, bf16[2048,128]{1,0:T(8,128)(2,1)}, u32[]{:S(2)}) copy-start(bf16[2048,128]{1,0:T(8,128)(2,1)} %centers_ref.5) | copy-start | bytes 1572868
  0.6 25.4 %copy-start.7 = (bf16[128,512]{1,0:T(8,128)(2,1)S(1)}, bf16[128,512]{1,0:T(8,128)(2,1)}, u32[]{:S(2)}) copy-start(bf16[128,512]{1,0:T(8,128)(2,1)} %mine_ref.1) | copy-start | bytes 393220
  3.5 5.7 %collective-permute-start = (bf16[320,128]{1,0:T(8,128)(2,1)}, bf16[320,128]{1,0:T(8,128)(2,1)S(1)}, u32[]{:S(2)}, u32[]{:S(2)}) collective-permute-start(bf16[320,128]{1,0:T(8,128)(2,1)} %head.1), channel_id=1, source_target_pairs={{0,4},{64,68},{128,132},{192,196}} | collective-permute-start | bytes 245768 | tf_op jit(solution)/shard_map/ppermute | solution.py:516
  10.1 2.8 %collective-permute-start.1 = (bf16[320,128]{1,0:T(8,128)(2,1)S(1)}, bf16[320,128]{1,0:T(8,128)(2,1)S(1)}, u32[]{:S(2)}, u32[]{:S(2)}) collective-permute-start(bf16[320,128]{1,0:T(8,128)(2,1)S(1)} %add.32), channel_id=1, source_target_pairs={{0,2},{4,6},{64,66},{68,70},{128,130},{132,134},{192,194},{196,198}} | collective-permute-start | bytes 245768 | tf_op jit(solution)/shard_map/ppermute | solution.py:516
  12.9 3.5 %collective-permute-start.2 = (bf16[320,128]{1,0:T(8,128)(2,1)S(1)}, bf16[320,128]{1,0:T(8,128)(2,1)S(1)}, u32[]{:S(2)}, u32[]{:S(2)}) collective-permute-start(bf16[320,128]{1,0:T(8,128)(2,1)S(1)} %add.33), channel_id=1, source_target_pairs={{0,1},{4,5},{2,3},{6,7},{64,65},{68,69},{66,67},{70,71},{128,129},... | collective-permute-start | bytes 245768 | tf_op jit(solution)/shard_map/ppermute | solution.py:516
  14.2 11.8 %collective-permute-start.7 = (bf16[128,512]{1,0:T(8,128)(2,1)}, bf16[128,512]{1,0:T(8,128)(2,1)S(1)}, u32[]{:S(2)}, u32[]{:S(2)}) collective-permute-start(bf16[128,512]{1,0:T(8,128)(2,1)} %mine_ref.1), channel_id=1, source_target_pairs={{0,64},{64,0},{128,192},{192,128},{1,65},{65,1},{129,193},{193,129... | collective-permute-start | bytes 393224 | tf_op jit(solution)/shard_map/ppermute | solution.py:521
  16.5 8.2 %collective-permute-start.3 = (bf16[320,128]{1,0:T(8,128)(2,1)S(1)}, bf16[320,128]{1,0:T(8,128)(2,1)S(1)}, u32[]{:S(2)}, u32[]{:S(2)}) collective-permute-start(bf16[320,128]{1,0:T(8,128)(2,1)S(1)} %add.34), channel_id=1, source_target_pairs={{0,32},{4,36},{2,34},{6,38},{1,33},{5,37},{3,35},{7,39},{64,96},{6... | collective-permute-start | bytes 245768 | tf_op jit(solution)/shard_map/ppermute | solution.py:516
  24.7 3.9 %collective-permute-start.4 = (bf16[320,128]{1,0:T(8,128)(2,1)S(1)}, bf16[320,128]{1,0:T(8,128)(2,1)S(1)}, u32[]{:S(2)}, u32[]{:S(2)}) collective-permute-start(bf16[320,128]{1,0:T(8,128)(2,1)S(1)} %add.35), channel_id=1, source_target_pairs={{0,16},{4,20},{2,18},{6,22},{1,17},{5,21},{3,19},{7,23},{32,48},{3... | collective-permute-start | bytes 245768 | tf_op jit(solution)/shard_map/ppermute | solution.py:516
  26.1 13.9 %collective-permute-start.8 = (bf16[256,512]{1,0:T(8,128)(2,1)S(1)}, bf16[256,512]{1,0:T(8,128)(2,1)S(1)}, u32[]{:S(2)}, u32[]{:S(2)}) collective-permute-start(bf16[256,512]{1,0:T(8,128)(2,1)S(1)} %pad_maximum_fusion), channel_id=1, source_target_pairs={{0,128},{64,192},{128,0},{192,64},{1,129},{65,193},{129,1},{193,65... | collective-permute-start | bytes 786440 | tf_op jit(solution)/shard_map/ppermute | solution.py:521
  28.6 11.4 %copy-start.5 = (f32[32,2048]{1,0:T(8,128)S(1)}, f32[32,2048]{1,0:T(8,128)}, u32[]{:S(2)}) copy-start(f32[32,2048]{1,0:T(8,128)} %dir_ref.3) | copy-start | bytes 786436
  28.7 11.4 %copy-start.8 = (bf16[128,512]{1,0:T(8,128)(2,1)S(1)}, bf16[128,512]{1,0:T(8,128)(2,1)}, u32[]{:S(2)}) copy-start(bf16[128,512]{1,0:T(8,128)(2,1)} %mine_ref.1) | copy-start | bytes 393220
  28.7 11.4 %copy-start.12 = (s32[2]{0:T(128)S(1)}, s32[2]{0:T(128)}, u32[]{:S(2)}) copy-start(s32[2]{0:T(128)} %pad_add_fusion.flags_ref) | copy-start | bytes 28
  28.7 5.7 %collective-permute-start.5 = (bf16[320,128]{1,0:T(8,128)(2,1)S(1)}, bf16[320,128]{1,0:T(8,128)(2,1)S(1)}, u32[]{:S(2)}, u32[]{:S(2)}) collective-permute-start(bf16[320,128]{1,0:T(8,128)(2,1)S(1)} %add.36), channel_id=1, source_target_pairs={{0,8},{4,12},{2,10},{6,14},{1,9},{5,13},{3,11},{7,15},{32,40},{36,... | collective-permute-start | bytes 245768 | tf_op jit(solution)/shard_map/ppermute | solution.py:516
  34.5 5.6 %collective-permute-start.6 = (bf16[320,128]{1,0:T(8,128)(2,1)S(1)}, bf16[320,128]{1,0:T(8,128)(2,1)S(1)}, u32[]{:S(2)}, u32[]{:S(2)}) collective-permute-start(bf16[320,128]{1,0:T(8,128)(2,1)S(1)} %add.37.head_ref), channel_id=1, source_target_pairs={{0,64},{64,0},{128,192},{192,128},{1,65},{65,1},{129,193},{193,129... | collective-permute-start | bytes 245768 | tf_op jit(solution)/shard_map/ppermute | solution.py:521
  40.0 52.8 %copy-start.6 = (f32[32,2048]{1,0:T(8,128)S(1)}, f32[32,2048]{1,0:T(8,128)}, u32[]{:S(2)}) copy-start(f32[32,2048]{1,0:T(8,128)} %res_ref.3) | copy-start | bytes 786436
  52.3 50.7 %copy-start.9 = (f32[32,2048]{1,0:T(8,128)}, f32[32,2048]{1,0:T(8,128)S(1)}, u32[]{:S(2)}) copy-start(f32[32,2048]{1,0:T(8,128)S(1)} %get-tuple-element.16.z_ref) | copy-start | bytes 786436
  52.3 50.6 %copy-start.11 = (f32[32,1]{1,0:T(8,128)}, f32[32,1]{1,0:T(8,128)S(1)}, u32[]{:S(2)}) copy-start(f32[32,1]{1,0:T(8,128)S(1)} %get-tuple-element.13.z_squares_ref.refs_0_.refs_1_) | copy-start | bytes 388
  103.9 21.6 %all-to-all-start.3 = ((bf16[8,272,128]{2,1,0:T(8,128)(2,1)}), bf16[8,272,128]{2,1,0:T(8,128)(2,1)S(1)}, u32[]{:S(2)}, u32[]{:S(2)}) async-start(bf16[8,272,128]{2,1,0:T(8,128)(2,1)} %relay.1), calls=%async_computation.3 | async-start | bytes 1114112 | tf_op jit(solution)/shard_map/all_to_all | solution.py:497
  120.4 5.1 %copy-start.1 = (bf16[8192,128]{1,0:T(8,128)(2,1)S(1)}, bf16[8192,128]{1,0:T(8,128)(2,1)}, u32[]{:S(2)}) copy-start(bf16[8192,128]{1,0:T(8,128)(2,1)} %points_ref.7) | copy-start | bytes 6291460
  120.4 5.1 %copy-start.4 = (bf16[2048,128]{1,0:T(8,128)(2,1)S(1)}, bf16[2048,128]{1,0:T(8,128)(2,1)}, u32[]{:S(2)}) copy-start(bf16[2048,128]{1,0:T(8,128)(2,1)} %centers_ref.5) | copy-start | bytes 1572868
  125.6 23.5 %copy-start.10 = (f32[32,2048]{1,0:T(8,128)S(1)}, f32[32,2048]{1,0:T(8,128)}, u32[]{:S(2)}) copy-start(f32[32,2048]{1,0:T(8,128)} %copy-done.9) | copy-start | bytes 786436
  135.9 4.4 %collective-permute-start.9 = (f32[16,2176]{1,0:T(8,128)S(1)}, f32[16,2176]{1,0:T(8,128)S(1)}, u32[]{:S(2)}, u32[]{:S(2)}) collective-permute-start(f32[16,2176]{1,0:T(8,128)S(1)} %get-tuple-element.15), channel_id=1, source_target_pairs={{0,64},{64,0},{128,192},{192,128},{1,65},{65,1},{129,193},{193,129... | collective-permute-start | bytes 417800 | tf_op jit(solution)/shard_map/ppermute | solution.py:521
  140.3 6.5 %collective-permute-start.10 = (f32[16,2176]{1,0:T(8,128)S(1)}, f32[16,2176]{1,0:T(8,128)S(1)}, u32[]{:S(2)}, u32[]{:S(2)}) collective-permute-start(f32[16,2176]{1,0:T(8,128)S(1)} %add.38), channel_id=1, source_target_pairs={{0,128},{64,192},{128,0},{192,64},{1,129},{65,193},{129,1},{193,65... | collective-permute-start | bytes 417800 | tf_op jit(solution)/shard_map/ppermute | solution.py:521
  146.8 2.3 %collective-permute-start.11 = (f32[16,2176]{1,0:T(8,128)S(1)}, f32[16,2176]{1,0:T(8,128)S(1)}, u32[]{:S(2)}, u32[]{:S(2)}) collective-permute-start(f32[16,2176]{1,0:T(8,128)S(1)} %add.39.keep_ref), channel_id=1, source_target_pairs={{0,64},{64,0},{128,192},{192,128},{1,65},{65,1},{129,193},{193,129... | collective-permute-start | bytes 417800 | tf_op jit(solution)/shard_map/ppermute | solution.py:521
  (2 other events, 2.6 us)

commit v9 on v8

--- a/solution.py
+++ b/solution.py
@@ -256,12 +256,13 @@
     return jnp.concatenate([rows, jnp.zeros((EXTRA - 3, x.shape[1]), f32)], axis=0).astype(bf16)
 
 
-def owned_kernel(scale, image_scale, count, x_ref, z_squares_ref, res_ref, out_ref):
-    outputs = z_squares_ref.shape[0]
+def owned_kernel(scale, image_scale, count, x_ref, z_ref, res_ref, out_ref):
+    outputs = z_ref.shape[0]
     high, low = partial_sums(x_ref, outputs)
     w = (high * scale).astype(bf16)
     mine = jnp.sum(w.astype(f32) * (high + low), axis=1, keepdims=True) * image_scale
-    mine = mine + (RIDGE_TERM / count) * z_squares_ref[...]
+    z_squares = jnp.sum(z_ref[...] * z_ref[...], axis=1, keepdims=True)
+    mine = mine + (RIDGE_TERM / count) * z_squares
     squares = jnp.sum(res_ref[...] * res_ref[...], axis=1, keepdims=True) * (1.0 / count)
     lane = lax.broadcasted_iota(jnp.int32, w.shape, 1)
     row = lax.broadcasted_iota(jnp.int32, w.shape, 0)
@@ -272,8 +273,8 @@
         out_ref[i, outputs:] = scalars
 
 
-def owned_copies(x, z_squares, residual, scale, image_scale, count, ways):
-    outputs, lanes = z_squares.shape[0], x.shape[2]
+def owned_copies(x, z, residual, scale, image_scale, count, ways):
+    outputs, lanes = z.shape[0], x.shape[2]
     return pl.pallas_call(
         functools.partial(owned_kernel, scale, image_scale, count),
         out_shape=jax.ShapeDtypeStruct((ways, outputs + EXTRA, lanes), bf16),
@@ -281,7 +282,7 @@
         out_specs=VMEM,
         compiler_params=pltpu.CompilerParams(vmem_limit_bytes=LIMIT),
         name="owned",
-    )(x, z_squares, residual)
+    )(x, z, residual)
 
 
 def scalar_sum(ref, first):
@@ -322,8 +323,8 @@
     *refs
 ):
     blocks, refs = refs[:parts], refs[parts:]
-    z_ref, rows_ref, parts_out, zsq_ref = refs[:4]
-    head, pinv, zz, parts_buf, out_sems = refs[4:]
+    z_ref, rows_ref, parts_out = refs[:3]
+    head, pinv, zz, parts_buf, out_sems = refs[3:]
     share = mine_ref.shape[0]
     panel = pinv.shape[0]
     outputs = dir_ref.shape[0]
@@ -346,7 +347,6 @@
     q = jnp.dot(z1, pinv[...], preferred_element_type=f32).astype(bf16)
     heads = widened(head[:panel], 1)
     tile = panel
-    squares = jnp.zeros((outputs, 1), f32)
     for i in range(centers_ref.shape[0] // tile):
         rows = slice(i * tile, (i + 1) * tile)
         kp = similar(widened(centers_ref[rows], 0), heads, features)
@@ -357,11 +357,9 @@
         if i == 0:
             z = jnp.where(flags_ref[0] == 0, z1.astype(f32), z)
         z_ref[:, rows] = z
-        squares = squares + jnp.sum(z * z, axis=1, keepdims=True)
         high = z.astype(bf16)
         zz[:outputs, rows] = high
         zz[outputs:, rows] = (z - high.astype(f32)).astype(bf16)
-    zsq_ref[...] = squares
     puts = []
     done = 0
     for block in blocks:
@@ -397,10 +395,9 @@
             jax.ShapeDtypeStruct((outputs, m_dev), f32),
             jax.ShapeDtypeStruct((m_dev, share), bf16),
             values,
-            jax.ShapeDtypeStruct((outputs, 1), f32),
         ),
         in_specs=[SMEM] + [VMEM] * (7 + len(blocks)),
-        out_specs=(VMEM, VMEM, ANY, VMEM),
+        out_specs=(VMEM, VMEM, ANY),
         scratch_shapes=[
             pltpu.VMEM((2 * head_other.shape[0], features), bf16),
             pltpu.VMEM((panel, panel), bf16),
@@ -564,14 +561,14 @@
     head = head_payload(flags, centers, direction, panel)
     by_center = []
     first = 0
-    for count, limit in ((3, 12), (3, 12), (2, 12)):
-        by_center.append(resident_part(first, count, points, centers, limit))
+    for count in (2, 2, 2, 2):
+        by_center.append(resident_part(first, count, points, centers, 12))
         first += count
     for links in tree_pairs((n_far, n_near)):
         head = tree_stage(head, links)
     other = swap(panel_inverse, 1)
     pair = swap(jnp.concatenate([panel_inverse, other], axis=0), 2)
-    z, panel_rows, parts, z_squares = panel_step(
+    z, panel_rows, parts = panel_step(
         flags, centers, head, swap(head, 1),
         panel_inverse, other, pair, direction, by_center,
     )
@@ -581,8 +578,8 @@
     parts = exchange(summed(parts, rows), FAR)
     block = None
     for first, count in ((0, 5), (5, 1)):
-        block = block_part(1, CHUNK, 6, first, count, points, centers, block, z_squares)
-    w = owned_copies(parts, z_squares, residual, w_scale, image_scale, n_pts, n_far)
+        block = block_part(1, CHUNK, 6, first, count, points, centers, block)
+    w = owned_copies(parts, z, residual, w_scale, image_scale, n_pts, n_far)
     w = exchange(w, FAR)
     w = exchange(relay_copies(w, n_near), NEAR)
 

time: 151 us -> 153 us (1.013)
  blocking collectives: 50 us -> 52 us
  waiting for transfers between devices: 9.7 us -> 7.85 us
    all_to_all x3, blocking collectives: 50 us -> 52 us  [exchange(): return lax.all_to_all(x, axis, 0, 0, tiled=True)]
    pallas_call x3 -> x4, Pallas kernels: 11.6 us -> 12.2 us  [resident_part(): pl.pallas_call(kernel, out_shape=jax.ShapeDtypeStruct((m_dev, count * CHU...]
  transfers between devices with their start and end apart: 13 -> 13, of which waited for: 5 -> 4; matrix products, arithmetic and copies ran while one was open for 0% -> 0% of each run, Pallas kernels for 19% -> 19%
where the time goes in v9:
time: 153 us; the launch traced here: 152 us
  Pallas kernels  56.9 us (37%)
  blocking collectives  52 us (34%)
  starting transfers between devices  30 us (20%)
  waiting for transfers between devices  7.85 us (5%)
  local copies, waits for them, and re-layouts  2.67 us (2%)
  other arithmetic  1.68 us (1%)
    all_to_all x3, blocking collectives, exchange(): return lax.all_to_all(x, axis, 0, 0, tiled=True)  52 us
    pallas_call x2, Pallas kernels, block_part(): pl.pallas_call(functools.partial(block_kernel, side, size, first, count),...  16.6 us
    ppermute x6, starting transfers between devices, swap(): return lax.ppermute(x, 'pts', [(i, i ^ bit) for i in range(n)])  13.2 us
    pallas_call x4, Pallas kernels, resident_part(): pl.pallas_call(kernel, out_shape=jax.ShapeDtypeStruct((m_dev, count * CHU...  12.2 us
    pallas_call x1, Pallas kernels, panel_step(): pl.pallas_call(functools.partial(panel_kernel, len(blocks)), out_shape=(j...  12.1 us
    ppermute x6, starting transfers between devices, tree_stage(): return x + lax.ppermute(x, CTR, pairs)  11.9 us
    pallas_call x1, Pallas kernels, image(): pl.pallas_call(image_kernel, out_shape=(shape, shape), in_specs=[SMEM, VM...  10.8 us
    ppermute x6, waiting for transfers between devices, swap(): return lax.ppermute(x, 'pts', [(i, i ^ bit) for i in range(n)])  6.05 us
  transfers between devices with their start and end apart: 13, of which 4 were waited for; matrix products, arithmetic and copies ran while one was open for 0% of the time, Pallas kernels for 19%

profile of v9, /device:TPU:1, one launch (start us, length us, event | category | flops | bytes accessed | tf_op | source)
XLA Modules:
  0.0 152.1 jit_solution(10162003392146020708)
XLA Ops:
  1.2 2.2 %head.1 = bf16[320,128]{1,0:T(8,128)(2,1)} custom-call(s32[2]{0:T(128)} %pad_add_fusion.flags_ref, bf16[2048,128]{1,0:T(8,128)(2,1)} %centers_ref.5, f32[32,2048]{1,0:T(8,128)} %dir_ref.3), custom_call_target="tpu_custom_call" | custom-call | tf_op jit(solution)/shard_map/head/pallas_call | solution.py:198
  3.5 3.9 %collective-permute-start = (bf16[320,128]{1,0:T(8,128)(2,1)}, bf16[320,128]{1,0:T(8,128)(2,1)S(1)}, u32[]{:S(2)}, u32[]{:S(2)}) collective-permute-start(bf16[320,128]{1,0:T(8,128)(2,1)} %head.1), channel_id=1, source_target_pairs={{0,4},{64,68},{128,132},{192,196}} | collective-permute-start | bytes 245768 | tf_op jit(solution)/shard_map/ppermute | solution.py:513
  7.4 1.8 %collective-permute-done = bf16[320,128]{1,0:T(8,128)(2,1)S(1)} collective-permute-done((bf16[320,128]{1,0:T(8,128)(2,1)}, bf16[320,128]{1,0:T(8,128)(2,1)S(1)}, u32[]{:S(2)}, u32[]{:S(2)}) %collective-permute-start) | collective-permute-done | bytes 81952 | tf_op jit(solution)/shard_map/ppermute | solution.py:513
  11.4 1.6 %collective-permute-start.7 = (bf16[128,512]{1,0:T(8,128)(2,1)}, bf16[128,512]{1,0:T(8,128)(2,1)S(1)}, u32[]{:S(2)}, u32[]{:S(2)}) collective-permute-start(bf16[128,512]{1,0:T(8,128)(2,1)} %mine_ref.1), channel_id=1, source_target_pairs={{0,64},{64,0},{128,192},{192,128},{1,65},{65,1},{129,193},{193,129... | collective-permute-start | bytes 393224 | tf_op jit(solution)/shard_map/ppermute | solution.py:518
  14.4 1.6 %copy-done = bf16[8192,128]{1,0:T(8,128)(2,1)S(1)} copy-done((bf16[8192,128]{1,0:T(8,128)(2,1)S(1)}, bf16[8192,128]{1,0:T(8,128)(2,1)}, u32[]{:S(2)}) %copy-start) | copy-done | bytes 2097176
  17.0 3.1 %shard_map.79.refs_3_ = bf16[2048,2048]{1,0:T(8,128)(2,1)S(1)} custom-call(bf16[8192,128]{1,0:T(8,128)(2,1)S(1)} %copy-done, bf16[2048,128]{1,0:T(8,128)(2,1)S(1)} %copy-done.2), custom_call_target="tpu_custom_call" | custom-call | flops 2147483648 | bytes 8388608 | tf_op jit(solution)/shard_map/pallas_call | solution.py:151
  20.1 2.6 %collective-permute-start.3 = (bf16[320,128]{1,0:T(8,128)(2,1)S(1)}, bf16[320,128]{1,0:T(8,128)(2,1)S(1)}, u32[]{:S(2)}, u32[]{:S(2)}) collective-permute-start(bf16[320,128]{1,0:T(8,128)(2,1)S(1)} %add.34), channel_id=1, source_target_pairs={{0,32},{4,36},{2,34},{6,38},{1,33},{5,37},{3,35},{7,39},{64,96},{6... | collective-permute-start | bytes 245768 | tf_op jit(solution)/shard_map/ppermute | solution.py:513
  22.8 3.1 %shard_map.78.refs_2_ = bf16[2048,2048]{1,0:T(8,128)(2,1)S(1)} custom-call(bf16[8192,128]{1,0:T(8,128)(2,1)S(1)} %copy-done, bf16[2048,128]{1,0:T(8,128)(2,1)S(1)} %copy-done.2), custom_call_target="tpu_custom_call" | custom-call | flops 2147483648 | bytes 8388608 | tf_op jit(solution)/shard_map/pallas_call | solution.py:151
  27.2 2.8 %collective-permute-start.8 = (bf16[256,512]{1,0:T(8,128)(2,1)S(1)}, bf16[256,512]{1,0:T(8,128)(2,1)S(1)}, u32[]{:S(2)}, u32[]{:S(2)}) collective-permute-start(bf16[256,512]{1,0:T(8,128)(2,1)S(1)} %pad_maximum_fusion), channel_id=1, source_target_pairs={{0,128},{64,192},{128,0},{192,64},{1,129},{65,193},{129,1},{193,65... | collective-permute-start | bytes 786440 | tf_op jit(solution)/shard_map/ppermute | solution.py:518
  30.1 1.4 collective-permute-start.5
  31.6 3.1 %shard_map.77.refs_1_ = bf16[2048,2048]{1,0:T(8,128)(2,1)S(1)} custom-call(bf16[8192,128]{1,0:T(8,128)(2,1)S(1)} %copy-done, bf16[2048,128]{1,0:T(8,128)(2,1)S(1)} %copy-done.3), custom_call_target="tpu_custom_call" | custom-call | flops 2147483648 | bytes 8388608 | tf_op jit(solution)/shard_map/pallas_call | solution.py:151
  35.7 3.1 %shard_map.76.refs_0_ = bf16[2048,2048]{1,0:T(8,128)(2,1)S(1)} custom-call(bf16[8192,128]{1,0:T(8,128)(2,1)S(1)} %copy-done, bf16[2048,128]{1,0:T(8,128)(2,1)S(1)} %copy-done.3), custom_call_target="tpu_custom_call" | custom-call | flops 2147483648 | bytes 8388608 | tf_op jit(solution)/shard_map/pallas_call | solution.py:151
  38.8 12.1 %panel.1 = (f32[32,2048]{1,0:T(8,128)S(1)}, bf16[2048,128]{1,0:T(8,128)(2,1)}, bf16[64,96,128]{2,1,0:T(8,128)(2,1)S(1)}) custom-call(s32[2]{0:T(128)S(1)} %copy-done.8, bf16[2048,128]{1,0:T(8,128)(2,1)S(1)} %copy-done.3, bf16[320,128]{1,0:T(8,128)(2,1)S(1)} %add.37.head_ref, bf16[320,128]{1,0:T(8,128)(2,1)S(1)} %collective-permute-done.6.head_other_ref, ...), custom_call_target="tpu_custom_call" | custom-call | flops 8589934592 | bytes 33554432 | tf_op jit(solution)/shard_map/panel/pallas_call | solution.py:392
  50.9 25.9 %all_to_all.20.x_ref = bf16[8,768,128]{2,1,0:T(8,128)(2,1)S(1)} all-to-all(bf16[8,768,128]{2,1,0:T(8,128)(2,1)S(1)} %bitcast.3), channel_id=1, replica_groups=mesh['pts'=4,'ctr_0'=8,'ctr_1'=2,'ctr_2'=4] {'ctr_1','ctr_2'}, dimensions={0} | all-to-all | bytes 3145728 | tf_op jit(solution)/shard_map/all_to_all | solution.py:494
  77.3 16.2 %all_to_all.21.x_ref = bf16[8,96,128]{2,1,0:T(8,128)(2,1)S(1)} all-to-all(bf16[8,96,128]{2,1,0:T(8,128)(2,1)S(1)} %summed.1), channel_id=1, replica_groups=mesh['pts'=4,'ctr_0'=8,'ctr_1'=2,'ctr_2'=4] {'ctr_0'}, dimensions={0} | all-to-all | bytes 393216 | tf_op jit(solution)/shard_map/all_to_all | solution.py:494
  93.6 9.9 %all_to_all.22.x_ref = bf16[8,48,128]{2,1,0:T(8,128)(2,1)S(1)} all-to-all(bf16[8,48,128]{2,1,0:T(8,128)(2,1)S(1)} %owned.1), channel_id=1, replica_groups=mesh['pts'=4,'ctr_0'=8,'ctr_1'=2,'ctr_2'=4] {'ctr_0'}, dimensions={0} | all-to-all | bytes 196608 | tf_op jit(solution)/shard_map/all_to_all | solution.py:494
  104.4 4.9 %all-to-all-start.3 = ((bf16[8,272,128]{2,1,0:T(8,128)(2,1)}), bf16[8,272,128]{2,1,0:T(8,128)(2,1)}, u32[]{:S(2)}, u32[]{:S(2)}) async-start(bf16[8,272,128]{2,1,0:T(8,128)(2,1)} %relay.1), calls=%async_computation.3 | async-start | bytes 1114112 | tf_op jit(solution)/shard_map/all_to_all | solution.py:494
  109.4 11.5 %shard_map.80.refs_0_ = bf16[6,1024,2048]{2,1,0:T(8,128)(2,1)} custom-call(bf16[8192,128]{1,0:T(8,128)(2,1)} %points_ref.9, bf16[2048,128]{1,0:T(8,128)(2,1)} %centers_ref.5), custom_call_target="tpu_custom_call" | custom-call | flops 5368709120 | bytes 20971520 | tf_op jit(solution)/shard_map/pallas_call | solution.py:107
  120.9 5.1 %shard_map.81.source_ref = bf16[6,1024,2048]{2,1,0:T(8,128)(2,1)} custom-call(bf16[6,1024,2048]{2,1,0:T(8,128)(2,1)} %shard_map.80.refs_0_, bf16[8192,128]{1,0:T(8,128)(2,1)} %points_ref.9, bf16[2048,128]{1,0:T(8,128)(2,1)} %centers_ref.5), custom_call_target="tpu_custom_call", output_to_operand_aliasing={{}: (0, {})} | custom-call | flops 1073741824 | bytes 4194304 | tf_op jit(solution)/shard_map/pallas_call | solution.py:107
  126.0 10.8 %image.1 = (f32[16,2176]{1,0:T(8,128)S(1)}, f32[16,2176]{1,0:T(8,128)S(1)}) custom-call(s32[2]{0:T(128)S(1)} %copy-done.8, bf16[8,272,128]{2,1,0:T(8,128)(2,1)} %all-to-all-done.3.w_ref, bf16[2048,128]{1,0:T(8,128)(2,1)S(1)} %copy-done.4, bf16[8192,128]{1,0:T(8,128)(2,1)S(1)} %copy-done.1, bf16[6,1024,2048]{2,1,0:T(8,128)(2,1)} %shard_map.81.source_ref), custom_call_target="tpu_custom_call" | custom-call | flops 8589934592 | bytes 33554432 | tf_op jit(solution)/shard_map/image/pallas_call | solution.py:469
  136.8 4.0 %collective-permute-start.9 = (f32[16,2176]{1,0:T(8,128)S(1)}, f32[16,2176]{1,0:T(8,128)S(1)}, u32[]{:S(2)}, u32[]{:S(2)}) collective-permute-start(f32[16,2176]{1,0:T(8,128)S(1)} %get-tuple-element.14), channel_id=1, source_target_pairs={{0,64},{64,0},{128,192},{192,128},{1,65},{65,1},{129,193},{193,129... | collective-permute-start | bytes 417800 | tf_op jit(solution)/shard_map/ppermute | solution.py:518
  141.9 2.4 %collective-permute-start.10 = (f32[16,2176]{1,0:T(8,128)S(1)}, f32[16,2176]{1,0:T(8,128)S(1)}, u32[]{:S(2)}, u32[]{:S(2)}) collective-permute-start(f32[16,2176]{1,0:T(8,128)S(1)} %add.38), channel_id=1, source_target_pairs={{0,128},{64,192},{128,0},{192,64},{1,129},{65,193},{129,1},{193,65... | collective-permute-start | bytes 417800 | tf_op jit(solution)/shard_map/ppermute | solution.py:518
  144.3 4.0 %collective-permute-done.10 = f32[16,2176]{1,0:T(8,128)S(1)} collective-permute-done((f32[16,2176]{1,0:T(8,128)S(1)}, f32[16,2176]{1,0:T(8,128)S(1)}, u32[]{:S(2)}, u32[]{:S(2)}) %collective-permute-start.10) | collective-permute-done | bytes 139296 | tf_op jit(solution)/shard_map/ppermute | solution.py:518
  150.7 1.4 final.1
  (46 shorter events, 12.4 us)
Async XLA Ops:
  3.5 5.7 %collective-permute-start = (bf16[320,128]{1,0:T(8,128)(2,1)}, bf16[320,128]{1,0:T(8,128)(2,1)S(1)}, u32[]{:S(2)}, u32[]{:S(2)}) collective-permute-start(bf16[320,128]{1,0:T(8,128)(2,1)} %head.1), channel_id=1, source_target_pairs={{0,4},{64,68},{128,132},{192,196}} | collective-permute-start | bytes 245768 | tf_op jit(solution)/shard_map/ppermute | solution.py:513
  10.1 2.9 %collective-permute-start.1 = (bf16[320,128]{1,0:T(8,128)(2,1)S(1)}, bf16[320,128]{1,0:T(8,128)(2,1)S(1)}, u32[]{:S(2)}, u32[]{:S(2)}) collective-permute-start(bf16[320,128]{1,0:T(8,128)(2,1)S(1)} %add.32), channel_id=1, source_target_pairs={{0,2},{4,6},{64,66},{68,70},{128,130},{132,134},{192,194},{196,198}} | collective-permute-start | bytes 245768 | tf_op jit(solution)/shard_map/ppermute | solution.py:513
  11.4 15.8 %collective-permute-start.7 = (bf16[128,512]{1,0:T(8,128)(2,1)}, bf16[128,512]{1,0:T(8,128)(2,1)S(1)}, u32[]{:S(2)}, u32[]{:S(2)}) collective-permute-start(bf16[128,512]{1,0:T(8,128)(2,1)} %mine_ref.1), channel_id=1, source_target_pairs={{0,64},{64,0},{128,192},{192,128},{1,65},{65,1},{129,193},{193,129... | collective-permute-start | bytes 393224 | tf_op jit(solution)/shard_map/ppermute | solution.py:518
  13.1 7.0 %collective-permute-start.2 = (bf16[320,128]{1,0:T(8,128)(2,1)S(1)}, bf16[320,128]{1,0:T(8,128)(2,1)S(1)}, u32[]{:S(2)}, u32[]{:S(2)}) collective-permute-start(bf16[320,128]{1,0:T(8,128)(2,1)S(1)} %add.33), channel_id=1, source_target_pairs={{0,1},{4,5},{2,3},{6,7},{64,65},{68,69},{66,67},{70,71},{128,129},... | collective-permute-start | bytes 245768 | tf_op jit(solution)/shard_map/ppermute | solution.py:513
  14.4 1.6 %copy-start = (bf16[8192,128]{1,0:T(8,128)(2,1)S(1)}, bf16[8192,128]{1,0:T(8,128)(2,1)}, u32[]{:S(2)}) copy-start(bf16[8192,128]{1,0:T(8,128)(2,1)} %points_ref.9) | copy-start | bytes 6291460
  16.0 1.0 copy-start.2
  20.1 7.1 %copy-start.7 = (bf16[128,512]{1,0:T(8,128)(2,1)S(1)}, bf16[128,512]{1,0:T(8,128)(2,1)}, u32[]{:S(2)}) copy-start(bf16[128,512]{1,0:T(8,128)(2,1)} %mine_ref.1) | copy-start | bytes 393220
  20.1 11.5 %copy-start.3 = (bf16[2048,128]{1,0:T(8,128)(2,1)S(1)}, bf16[2048,128]{1,0:T(8,128)(2,1)}, u32[]{:S(2)}) copy-start(bf16[2048,128]{1,0:T(8,128)(2,1)} %centers_ref.5) | copy-start | bytes 1572868
  20.1 5.7 %collective-permute-start.3 = (bf16[320,128]{1,0:T(8,128)(2,1)S(1)}, bf16[320,128]{1,0:T(8,128)(2,1)S(1)}, u32[]{:S(2)}, u32[]{:S(2)}) collective-permute-start(bf16[320,128]{1,0:T(8,128)(2,1)S(1)} %add.34), channel_id=1, source_target_pairs={{0,32},{4,36},{2,34},{6,38},{1,33},{5,37},{3,35},{7,39},{64,96},{6... | collective-permute-start | bytes 245768 | tf_op jit(solution)/shard_map/ppermute | solution.py:513
  25.9 4.2 %collective-permute-start.4 = (bf16[320,128]{1,0:T(8,128)(2,1)S(1)}, bf16[320,128]{1,0:T(8,128)(2,1)S(1)}, u32[]{:S(2)}, u32[]{:S(2)}) collective-permute-start(bf16[320,128]{1,0:T(8,128)(2,1)S(1)} %add.35), channel_id=1, source_target_pairs={{0,16},{4,20},{2,18},{6,22},{1,17},{5,21},{3,19},{7,23},{32,48},{3... | collective-permute-start | bytes 245768 | tf_op jit(solution)/shard_map/ppermute | solution.py:513
  27.2 11.5 %collective-permute-start.8 = (bf16[256,512]{1,0:T(8,128)(2,1)S(1)}, bf16[256,512]{1,0:T(8,128)(2,1)S(1)}, u32[]{:S(2)}, u32[]{:S(2)}) collective-permute-start(bf16[256,512]{1,0:T(8,128)(2,1)S(1)} %pad_maximum_fusion), channel_id=1, source_target_pairs={{0,128},{64,192},{128,0},{192,64},{1,129},{65,193},{129,1},{193,65... | collective-permute-start | bytes 786440 | tf_op jit(solution)/shard_map/ppermute | solution.py:518
  30.1 8.7 %copy-start.5 = (f32[32,2048]{1,0:T(8,128)S(1)}, f32[32,2048]{1,0:T(8,128)}, u32[]{:S(2)}) copy-start(f32[32,2048]{1,0:T(8,128)} %dir_ref.3) | copy-start | bytes 786436
  30.1 8.7 %copy-start.8 = (s32[2]{0:T(128)S(1)}, s32[2]{0:T(128)}, u32[]{:S(2)}) copy-start(s32[2]{0:T(128)} %pad_add_fusion.flags_ref) | copy-start | bytes 28
  30.1 4.5 %collective-permute-start.5 = (bf16[320,128]{1,0:T(8,128)(2,1)S(1)}, bf16[320,128]{1,0:T(8,128)(2,1)S(1)}, u32[]{:S(2)}, u32[]{:S(2)}) collective-permute-start(bf16[320,128]{1,0:T(8,128)(2,1)S(1)} %add.36), channel_id=1, source_target_pairs={{0,8},{4,12},{2,10},{6,14},{1,9},{5,13},{3,11},{7,15},{32,40},{36,... | collective-permute-start | bytes 245768 | tf_op jit(solution)/shard_map/ppermute | solution.py:513
  34.7 4.1 %collective-permute-start.6 = (bf16[320,128]{1,0:T(8,128)(2,1)S(1)}, bf16[320,128]{1,0:T(8,128)(2,1)S(1)}, u32[]{:S(2)}, u32[]{:S(2)}) collective-permute-start(bf16[320,128]{1,0:T(8,128)(2,1)S(1)} %add.37.head_ref), channel_id=1, source_target_pairs={{0,64},{64,0},{128,192},{192,128},{1,65},{65,1},{129,193},{193,129... | collective-permute-start | bytes 245768 | tf_op jit(solution)/shard_map/ppermute | solution.py:518
  38.7 54.7 %copy-start.6 = (f32[32,2048]{1,0:T(8,128)S(1)}, f32[32,2048]{1,0:T(8,128)}, u32[]{:S(2)}) copy-start(f32[32,2048]{1,0:T(8,128)} %res_ref.3) | copy-start | bytes 786436
  104.4 21.5 %all-to-all-start.3 = ((bf16[8,272,128]{2,1,0:T(8,128)(2,1)}), bf16[8,272,128]{2,1,0:T(8,128)(2,1)}, u32[]{:S(2)}, u32[]{:S(2)}) async-start(bf16[8,272,128]{2,1,0:T(8,128)(2,1)} %relay.1), calls=%async_computation.3 | async-start | bytes 1114112 | tf_op jit(solution)/shard_map/all_to_all | solution.py:494
  120.9 5.1 %copy-start.1 = (bf16[8192,128]{1,0:T(8,128)(2,1)S(1)}, bf16[8192,128]{1,0:T(8,128)(2,1)}, u32[]{:S(2)}) copy-start(bf16[8192,128]{1,0:T(8,128)(2,1)} %points_ref.9) | copy-start | bytes 6291460
  120.9 5.1 %copy-start.4 = (bf16[2048,128]{1,0:T(8,128)(2,1)S(1)}, bf16[2048,128]{1,0:T(8,128)(2,1)}, u32[]{:S(2)}) copy-start(bf16[2048,128]{1,0:T(8,128)(2,1)} %centers_ref.5) | copy-start | bytes 1572868
  136.8 5.0 %collective-permute-start.9 = (f32[16,2176]{1,0:T(8,128)S(1)}, f32[16,2176]{1,0:T(8,128)S(1)}, u32[]{:S(2)}, u32[]{:S(2)}) collective-permute-start(f32[16,2176]{1,0:T(8,128)S(1)} %get-tuple-element.14), channel_id=1, source_target_pairs={{0,64},{64,0},{128,192},{192,128},{1,65},{65,1},{129,193},{193,129... | collective-permute-start | bytes 417800 | tf_op jit(solution)/shard_map/ppermute | solution.py:518
  141.9 6.5 %collective-permute-start.10 = (f32[16,2176]{1,0:T(8,128)S(1)}, f32[16,2176]{1,0:T(8,128)S(1)}, u32[]{:S(2)}, u32[]{:S(2)}) collective-permute-start(f32[16,2176]{1,0:T(8,128)S(1)} %add.38), channel_id=1, source_target_pairs={{0,128},{64,192},{128,0},{192,64},{1,129},{65,193},{129,1},{193,65... | collective-permute-start | bytes 417800 | tf_op jit(solution)/shard_map/ppermute | solution.py:518
  148.4 2.3 %collective-permute-start.11 = (f32[16,2176]{1,0:T(8,128)S(1)}, f32[16,2176]{1,0:T(8,128)S(1)}, u32[]{:S(2)}, u32[]{:S(2)}) collective-permute-start(f32[16,2176]{1,0:T(8,128)S(1)} %add.39.keep_ref), channel_id=1, source_target_pairs={{0,64},{64,0},{128,192},{192,128},{1,65},{65,1},{129,193},{193,129... | collective-permute-start | bytes 417800 | tf_op jit(solution)/shard_map/ppermute | solution.py:518

commit v10 on v9

--- a/solution.py
+++ b/solution.py
@@ -561,7 +561,7 @@
     head = head_payload(flags, centers, direction, panel)
     by_center = []
     first = 0
-    for count in (2, 2, 2, 2):
+    for count in (2, 3, 3):
         by_center.append(resident_part(first, count, points, centers, 12))
         first += count
     for links in tree_pairs((n_far, n_near)):
@@ -576,9 +576,7 @@
     rows = 3 * outputs
     parts = exchange(parts.reshape(n_near, n_far * rows, 128), NEAR)
     parts = exchange(summed(parts, rows), FAR)
-    block = None
-    for first, count in ((0, 5), (5, 1)):
-        block = block_part(1, CHUNK, 6, first, count, points, centers, block)
+    block = block_part(1, CHUNK, 6, 0, 6, points, centers)
     w = owned_copies(parts, z, residual, w_scale, image_scale, n_pts, n_far)
     w = exchange(w, FAR)
     w = exchange(relay_copies(w, n_near), NEAR)

time: 153 us -> 148 us (0.967)
  Pallas kernels: 56.9 us -> 52.9 us
  blocking collectives: 52 us -> 49.8 us
  waiting for transfers between devices: 7.85 us -> 9.56 us
    pallas_call x2 -> x1, Pallas kernels: 16.6 us -> 13.1 us  [block_part(): pl.pallas_call(functools.partial(block_kernel, side, size, first, count),...]
    all_to_all x3, blocking collectives: 52 us -> 49.8 us  [exchange(): return lax.all_to_all(x, axis, 0, 0, tiled=True)]
    pallas_call x4 -> x3, Pallas kernels: 12.2 us -> 11.6 us  [resident_part(): pl.pallas_call(kernel, out_shape=jax.ShapeDtypeStruct((m_dev, count * CHU...]
  transfers between devices with their start and end apart: 13 -> 13, of which waited for: 4 -> 5; matrix products, arithmetic and copies ran while one was open for 0% -> 0% of each run, Pallas kernels for 19% -> 17%
where the time goes in v10:
time: 148 us
  Pallas kernels  52.9 us (36%)
  blocking collectives  49.8 us (34%)
  starting transfers between devices  30 us (20%)
  waiting for transfers between devices  9.56 us (6%)
  local copies, waits for them, and re-layouts  2.66 us (2%)
  other arithmetic  1.74 us (1%)
    all_to_all x3, blocking collectives, exchange(): return lax.all_to_all(x, axis, 0, 0, tiled=True)  49.8 us
    ppermute x6, starting transfers between devices, swap(): return lax.ppermute(x, 'pts', [(i, i ^ bit) for i in range(n)])  14.7 us
    pallas_call x1, Pallas kernels, block_part(): pl.pallas_call(functools.partial(block_kernel, side, size, first, count),...  13.1 us
    pallas_call x1, Pallas kernels, panel_step(): pl.pallas_call(functools.partial(panel_kernel, len(blocks)), out_shape=(j...  12.1 us
    pallas_call x3, Pallas kernels, resident_part(): pl.pallas_call(kernel, out_shape=jax.ShapeDtypeStruct((m_dev, count * CHU...  11.6 us
    pallas_call x1, Pallas kernels, image(): pl.pallas_call(image_kernel, out_shape=(shape, shape), in_specs=[SMEM, VM...  10.8 us
    ppermute x6, starting transfers between devices, tree_stage(): return x + lax.ppermute(x, CTR, pairs)  10.4 us
    ppermute x6, waiting for transfers between devices, swap(): return lax.ppermute(x, 'pts', [(i, i ^ bit) for i in range(n)])  6.3 us
  transfers between devices with their start and end apart: 13, of which 5 were waited for; matrix products, arithmetic and copies ran while one was open for 0% of the time, Pallas kernels for 17%

profile of v10, /device:TPU:1, one launch (start us, length us, event | category | flops | bytes accessed | tf_op | source)
XLA Modules:
  0.0 147.7 jit_solution(11803386572203250930)
XLA Ops:
  1.2 2.4 %head.1 = bf16[320,128]{1,0:T(8,128)(2,1)} custom-call(s32[2]{0:T(128)} %pad_add_fusion.flags_ref, bf16[2048,128]{1,0:T(8,128)(2,1)} %centers_ref.5, f32[32,2048]{1,0:T(8,128)} %dir_ref.3), custom_call_target="tpu_custom_call" | custom-call | tf_op jit(solution)/shard_map/head/pallas_call | solution.py:198
  3.6 3.9 %collective-permute-start = (bf16[320,128]{1,0:T(8,128)(2,1)}, bf16[320,128]{1,0:T(8,128)(2,1)S(1)}, u32[]{:S(2)}, u32[]{:S(2)}) collective-permute-start(bf16[320,128]{1,0:T(8,128)(2,1)} %head.1), channel_id=1, source_target_pairs={{0,4},{64,68},{128,132},{192,196}} | collective-permute-start | bytes 245768 | tf_op jit(solution)/shard_map/ppermute | solution.py:513
  7.6 1.8 %collective-permute-done = bf16[320,128]{1,0:T(8,128)(2,1)S(1)} collective-permute-done((bf16[320,128]{1,0:T(8,128)(2,1)}, bf16[320,128]{1,0:T(8,128)(2,1)S(1)}, u32[]{:S(2)}, u32[]{:S(2)}) %collective-permute-start) | collective-permute-done | bytes 81952 | tf_op jit(solution)/shard_map/ppermute | solution.py:513
  10.3 1.3 collective-permute-start.1
  11.6 1.5 collective-permute-done.1
  14.4 2.2 %collective-permute-start.7 = (bf16[128,512]{1,0:T(8,128)(2,1)}, bf16[128,512]{1,0:T(8,128)(2,1)S(1)}, u32[]{:S(2)}, u32[]{:S(2)}) collective-permute-start(bf16[128,512]{1,0:T(8,128)(2,1)} %mine_ref.1), channel_id=1, source_target_pairs={{0,64},{64,0},{128,192},{192,128},{1,65},{65,1},{129,193},{193,129... | collective-permute-start | bytes 393224 | tf_op jit(solution)/shard_map/ppermute | solution.py:518
  17.9 1.6 %copy-done = bf16[8192,128]{1,0:T(8,128)(2,1)S(1)} copy-done((bf16[8192,128]{1,0:T(8,128)(2,1)S(1)}, bf16[8192,128]{1,0:T(8,128)(2,1)}, u32[]{:S(2)}) %copy-start) | copy-done | bytes 2097176
  20.6 4.3 %shard_map.78.refs_2_ = bf16[2048,3072]{1,0:T(8,128)(2,1)S(1)} custom-call(bf16[8192,128]{1,0:T(8,128)(2,1)S(1)} %copy-done, bf16[2048,128]{1,0:T(8,128)(2,1)S(1)} %copy-done.2), custom_call_target="tpu_custom_call" | custom-call | flops 3221225472 | bytes 12582912 | tf_op jit(solution)/shard_map/pallas_call | solution.py:151
  26.3 2.5 %collective-permute-start.8 = (bf16[256,512]{1,0:T(8,128)(2,1)S(1)}, bf16[256,512]{1,0:T(8,128)(2,1)S(1)}, u32[]{:S(2)}, u32[]{:S(2)}) collective-permute-start(bf16[256,512]{1,0:T(8,128)(2,1)S(1)} %pad_maximum_fusion), channel_id=1, source_target_pairs={{0,128},{64,192},{128,0},{192,64},{1,129},{65,193},{129,1},{193,65... | collective-permute-start | bytes 786440 | tf_op jit(solution)/shard_map/ppermute | solution.py:518
  30.1 4.3 %shard_map.77.refs_1_ = bf16[2048,3072]{1,0:T(8,128)(2,1)S(1)} custom-call(bf16[8192,128]{1,0:T(8,128)(2,1)S(1)} %copy-done, bf16[2048,128]{1,0:T(8,128)(2,1)S(1)} %copy-done.3), custom_call_target="tpu_custom_call" | custom-call | flops 3221225472 | bytes 12582912 | tf_op jit(solution)/shard_map/pallas_call | solution.py:151
  34.5 2.5 %collective-permute-start.6 = (bf16[320,128]{1,0:T(8,128)(2,1)S(1)}, bf16[320,128]{1,0:T(8,128)(2,1)S(1)}, u32[]{:S(2)}, u32[]{:S(2)}) collective-permute-start(bf16[320,128]{1,0:T(8,128)(2,1)S(1)} %add.37.head_ref), channel_id=1, source_target_pairs={{0,64},{64,0},{128,192},{192,128},{1,65},{65,1},{129,193},{193,129... | collective-permute-start | bytes 245768 | tf_op jit(solution)/shard_map/ppermute | solution.py:518
  37.0 3.1 %shard_map.76.refs_0_ = bf16[2048,2048]{1,0:T(8,128)(2,1)S(1)} custom-call(bf16[8192,128]{1,0:T(8,128)(2,1)S(1)} %copy-done, bf16[2048,128]{1,0:T(8,128)(2,1)S(1)} %copy-done.3), custom_call_target="tpu_custom_call" | custom-call | flops 2147483648 | bytes 8388608 | tf_op jit(solution)/shard_map/pallas_call | solution.py:151
  40.1 12.1 %panel.1 = (f32[32,2048]{1,0:T(8,128)S(1)}, bf16[2048,128]{1,0:T(8,128)(2,1)}, bf16[64,96,128]{2,1,0:T(8,128)(2,1)S(1)}) custom-call(s32[2]{0:T(128)S(1)} %copy-done.8, bf16[2048,128]{1,0:T(8,128)(2,1)S(1)} %copy-done.3, bf16[320,128]{1,0:T(8,128)(2,1)S(1)} %add.37.head_ref, bf16[320,128]{1,0:T(8,128)(2,1)S(1)} %collective-permute-done.6.head_other_ref, ...), custom_call_target="tpu_custom_call" | custom-call | flops 8589934592 | bytes 33554432 | tf_op jit(solution)/shard_map/panel/pallas_call | solution.py:392
  52.2 27.0 %all_to_all.20.x_ref = bf16[8,768,128]{2,1,0:T(8,128)(2,1)S(1)} all-to-all(bf16[8,768,128]{2,1,0:T(8,128)(2,1)S(1)} %bitcast.3), channel_id=1, replica_groups=mesh['pts'=4,'ctr_0'=8,'ctr_1'=2,'ctr_2'=4] {'ctr_1','ctr_2'}, dimensions={0} | all-to-all | bytes 3145728 | tf_op jit(solution)/shard_map/all_to_all | solution.py:494
  79.6 12.9 %all_to_all.21.x_ref = bf16[8,96,128]{2,1,0:T(8,128)(2,1)S(1)} all-to-all(bf16[8,96,128]{2,1,0:T(8,128)(2,1)S(1)} %summed.1), channel_id=1, replica_groups=mesh['pts'=4,'ctr_0'=8,'ctr_1'=2,'ctr_2'=4] {'ctr_0'}, dimensions={0} | all-to-all | bytes 393216 | tf_op jit(solution)/shard_map/all_to_all | solution.py:494
  92.7 9.9 %all_to_all.22.x_ref = bf16[8,48,128]{2,1,0:T(8,128)(2,1)S(1)} all-to-all(bf16[8,48,128]{2,1,0:T(8,128)(2,1)S(1)} %owned.1), channel_id=1, replica_groups=mesh['pts'=4,'ctr_0'=8,'ctr_1'=2,'ctr_2'=4] {'ctr_0'}, dimensions={0} | all-to-all | bytes 196608 | tf_op jit(solution)/shard_map/all_to_all | solution.py:494
  103.6 4.9 %all-to-all-start.3 = ((bf16[8,272,128]{2,1,0:T(8,128)(2,1)}), bf16[8,272,128]{2,1,0:T(8,128)(2,1)}, u32[]{:S(2)}, u32[]{:S(2)}) async-start(bf16[8,272,128]{2,1,0:T(8,128)(2,1)} %relay.1), calls=%async_computation.3 | async-start | bytes 1114112 | tf_op jit(solution)/shard_map/all_to_all | solution.py:494
  108.5 13.1 %shard_map.79.source_ref = bf16[6,1024,2048]{2,1,0:T(8,128)(2,1)} custom-call(bf16[8192,128]{1,0:T(8,128)(2,1)} %points_ref.7, bf16[2048,128]{1,0:T(8,128)(2,1)} %centers_ref.5), custom_call_target="tpu_custom_call" | custom-call | flops 6442450944 | bytes 25165824 | tf_op jit(solution)/shard_map/pallas_call | solution.py:107
  121.6 10.8 %image.1 = (f32[16,2176]{1,0:T(8,128)S(1)}, f32[16,2176]{1,0:T(8,128)S(1)}) custom-call(s32[2]{0:T(128)S(1)} %copy-done.8, bf16[8,272,128]{2,1,0:T(8,128)(2,1)} %all-to-all-done.3.w_ref, bf16[2048,128]{1,0:T(8,128)(2,1)S(1)} %copy-done.4, bf16[8192,128]{1,0:T(8,128)(2,1)S(1)} %copy-done.1, bf16[6,1024,2048]{2,1,0:T(8,128)(2,1)} %shard_map.79.source_ref), custom_call_target="tpu_custom_call" | custom-call | flops 8589934592 | bytes 33554432 | tf_op jit(solution)/shard_map/image/pallas_call | solution.py:469
  132.5 4.0 %collective-permute-start.9 = (f32[16,2176]{1,0:T(8,128)S(1)}, f32[16,2176]{1,0:T(8,128)S(1)}, u32[]{:S(2)}, u32[]{:S(2)}) collective-permute-start(f32[16,2176]{1,0:T(8,128)S(1)} %get-tuple-element.14), channel_id=1, source_target_pairs={{0,64},{64,0},{128,192},{192,128},{1,65},{65,1},{129,193},{193,129... | collective-permute-start | bytes 417800 | tf_op jit(solution)/shard_map/ppermute | solution.py:518
  137.5 2.2 %collective-permute-start.10 = (f32[16,2176]{1,0:T(8,128)S(1)}, f32[16,2176]{1,0:T(8,128)S(1)}, u32[]{:S(2)}, u32[]{:S(2)}) collective-permute-start(f32[16,2176]{1,0:T(8,128)S(1)} %add.38), channel_id=1, source_target_pairs={{0,128},{64,192},{128,0},{192,64},{1,129},{65,193},{129,1},{193,65... | collective-permute-start | bytes 417800 | tf_op jit(solution)/shard_map/ppermute | solution.py:518
  139.7 4.3 %collective-permute-done.10 = f32[16,2176]{1,0:T(8,128)S(1)} collective-permute-done((f32[16,2176]{1,0:T(8,128)S(1)}, f32[16,2176]{1,0:T(8,128)S(1)}, u32[]{:S(2)}, u32[]{:S(2)}) %collective-permute-start.10) | collective-permute-done | bytes 139296 | tf_op jit(solution)/shard_map/ppermute | solution.py:518
  144.0 1.3 collective-permute-start.11
  146.3 1.4 final.1
  (44 shorter events, 11.5 us)
Async XLA Ops:
  1.2 25.0 %copy-start.7 = (bf16[128,512]{1,0:T(8,128)(2,1)S(1)}, bf16[128,512]{1,0:T(8,128)(2,1)}, u32[]{:S(2)}) copy-start(bf16[128,512]{1,0:T(8,128)(2,1)} %mine_ref.1) | copy-start | bytes 393220
  3.6 5.7 %collective-permute-start = (bf16[320,128]{1,0:T(8,128)(2,1)}, bf16[320,128]{1,0:T(8,128)(2,1)S(1)}, u32[]{:S(2)}, u32[]{:S(2)}) collective-permute-start(bf16[320,128]{1,0:T(8,128)(2,1)} %head.1), channel_id=1, source_target_pairs={{0,4},{64,68},{128,132},{192,196}} | collective-permute-start | bytes 245768 | tf_op jit(solution)/shard_map/ppermute | solution.py:513
  9.3 20.8 %copy-start.3 = (bf16[2048,128]{1,0:T(8,128)(2,1)S(1)}, bf16[2048,128]{1,0:T(8,128)(2,1)}, u32[]{:S(2)}) copy-start(bf16[2048,128]{1,0:T(8,128)(2,1)} %centers_ref.5) | copy-start | bytes 1572868
  10.3 2.8 %collective-permute-start.1 = (bf16[320,128]{1,0:T(8,128)(2,1)S(1)}, bf16[320,128]{1,0:T(8,128)(2,1)S(1)}, u32[]{:S(2)}, u32[]{:S(2)}) collective-permute-start(bf16[320,128]{1,0:T(8,128)(2,1)S(1)} %add.32), channel_id=1, source_target_pairs={{0,2},{4,6},{64,66},{68,70},{128,130},{132,134},{192,194},{196,198}} | collective-permute-start | bytes 245768 | tf_op jit(solution)/shard_map/ppermute | solution.py:513
  13.1 3.5 %collective-permute-start.2 = (bf16[320,128]{1,0:T(8,128)(2,1)S(1)}, bf16[320,128]{1,0:T(8,128)(2,1)S(1)}, u32[]{:S(2)}, u32[]{:S(2)}) collective-permute-start(bf16[320,128]{1,0:T(8,128)(2,1)S(1)} %add.33), channel_id=1, source_target_pairs={{0,1},{4,5},{2,3},{6,7},{64,65},{68,69},{66,67},{70,71},{128,129},... | collective-permute-start | bytes 245768 | tf_op jit(solution)/shard_map/ppermute | solution.py:513
  14.4 11.8 %collective-permute-start.7 = (bf16[128,512]{1,0:T(8,128)(2,1)}, bf16[128,512]{1,0:T(8,128)(2,1)S(1)}, u32[]{:S(2)}, u32[]{:S(2)}) collective-permute-start(bf16[128,512]{1,0:T(8,128)(2,1)} %mine_ref.1), channel_id=1, source_target_pairs={{0,64},{64,0},{128,192},{192,128},{1,65},{65,1},{129,193},{193,129... | collective-permute-start | bytes 393224 | tf_op jit(solution)/shard_map/ppermute | solution.py:518
  16.6 8.2 %collective-permute-start.3 = (bf16[320,128]{1,0:T(8,128)(2,1)S(1)}, bf16[320,128]{1,0:T(8,128)(2,1)S(1)}, u32[]{:S(2)}, u32[]{:S(2)}) collective-permute-start(bf16[320,128]{1,0:T(8,128)(2,1)S(1)} %add.34), channel_id=1, source_target_pairs={{0,32},{4,36},{2,34},{6,38},{1,33},{5,37},{3,35},{7,39},{64,96},{6... | collective-permute-start | bytes 245768 | tf_op jit(solution)/shard_map/ppermute | solution.py:513
  17.9 1.6 %copy-start = (bf16[8192,128]{1,0:T(8,128)(2,1)S(1)}, bf16[8192,128]{1,0:T(8,128)(2,1)}, u32[]{:S(2)}) copy-start(bf16[8192,128]{1,0:T(8,128)(2,1)} %points_ref.7) | copy-start | bytes 6291460
  19.5 1.0 copy-start.2
  24.9 3.9 %collective-permute-start.4 = (bf16[320,128]{1,0:T(8,128)(2,1)S(1)}, bf16[320,128]{1,0:T(8,128)(2,1)S(1)}, u32[]{:S(2)}, u32[]{:S(2)}) collective-permute-start(bf16[320,128]{1,0:T(8,128)(2,1)S(1)} %add.35), channel_id=1, source_target_pairs={{0,16},{4,20},{2,18},{6,22},{1,17},{5,21},{3,19},{7,23},{32,48},{3... | collective-permute-start | bytes 245768 | tf_op jit(solution)/shard_map/ppermute | solution.py:513
  26.3 13.8 %collective-permute-start.8 = (bf16[256,512]{1,0:T(8,128)(2,1)S(1)}, bf16[256,512]{1,0:T(8,128)(2,1)S(1)}, u32[]{:S(2)}, u32[]{:S(2)}) collective-permute-start(bf16[256,512]{1,0:T(8,128)(2,1)S(1)} %pad_maximum_fusion), channel_id=1, source_target_pairs={{0,128},{64,192},{128,0},{192,64},{1,129},{65,193},{129,1},{193,65... | collective-permute-start | bytes 786440 | tf_op jit(solution)/shard_map/ppermute | solution.py:518
  28.8 5.6 %collective-permute-start.5 = (bf16[320,128]{1,0:T(8,128)(2,1)S(1)}, bf16[320,128]{1,0:T(8,128)(2,1)S(1)}, u32[]{:S(2)}, u32[]{:S(2)}) collective-permute-start(bf16[320,128]{1,0:T(8,128)(2,1)S(1)} %add.36), channel_id=1, source_target_pairs={{0,8},{4,12},{2,10},{6,14},{1,9},{5,13},{3,11},{7,15},{32,40},{36,... | collective-permute-start | bytes 245768 | tf_op jit(solution)/shard_map/ppermute | solution.py:513
  34.4 5.7 %copy-start.5 = (f32[32,2048]{1,0:T(8,128)S(1)}, f32[32,2048]{1,0:T(8,128)}, u32[]{:S(2)}) copy-start(f32[32,2048]{1,0:T(8,128)} %dir_ref.3) | copy-start | bytes 786436
  34.4 5.7 %copy-start.8 = (s32[2]{0:T(128)S(1)}, s32[2]{0:T(128)}, u32[]{:S(2)}) copy-start(s32[2]{0:T(128)} %pad_add_fusion.flags_ref) | copy-start | bytes 28
  34.5 5.6 %collective-permute-start.6 = (bf16[320,128]{1,0:T(8,128)(2,1)S(1)}, bf16[320,128]{1,0:T(8,128)(2,1)S(1)}, u32[]{:S(2)}, u32[]{:S(2)}) collective-permute-start(bf16[320,128]{1,0:T(8,128)(2,1)S(1)} %add.37.head_ref), channel_id=1, source_target_pairs={{0,64},{64,0},{128,192},{192,128},{1,65},{65,1},{129,193},{193,129... | collective-permute-start | bytes 245768 | tf_op jit(solution)/shard_map/ppermute | solution.py:518
  40.1 52.5 %copy-start.6 = (f32[32,2048]{1,0:T(8,128)S(1)}, f32[32,2048]{1,0:T(8,128)}, u32[]{:S(2)}) copy-start(f32[32,2048]{1,0:T(8,128)} %res_ref.3) | copy-start | bytes 786436
  103.6 18.0 %all-to-all-start.3 = ((bf16[8,272,128]{2,1,0:T(8,128)(2,1)}), bf16[8,272,128]{2,1,0:T(8,128)(2,1)}, u32[]{:S(2)}, u32[]{:S(2)}) async-start(bf16[8,272,128]{2,1,0:T(8,128)(2,1)} %relay.1), calls=%async_computation.3 | async-start | bytes 1114112 | tf_op jit(solution)/shard_map/all_to_all | solution.py:494
  108.5 13.1 %copy-start.1 = (bf16[8192,128]{1,0:T(8,128)(2,1)S(1)}, bf16[8192,128]{1,0:T(8,128)(2,1)}, u32[]{:S(2)}) copy-start(bf16[8192,128]{1,0:T(8,128)(2,1)} %points_ref.7) | copy-start | bytes 6291460
  108.5 13.1 %copy-start.4 = (bf16[2048,128]{1,0:T(8,128)(2,1)S(1)}, bf16[2048,128]{1,0:T(8,128)(2,1)}, u32[]{:S(2)}) copy-start(bf16[2048,128]{1,0:T(8,128)(2,1)} %centers_ref.5) | copy-start | bytes 1572868
  132.5 5.0 %collective-permute-start.9 = (f32[16,2176]{1,0:T(8,128)S(1)}, f32[16,2176]{1,0:T(8,128)S(1)}, u32[]{:S(2)}, u32[]{:S(2)}) collective-permute-start(f32[16,2176]{1,0:T(8,128)S(1)} %get-tuple-element.14), channel_id=1, source_target_pairs={{0,64},{64,0},{128,192},{192,128},{1,65},{65,1},{129,193},{193,129... | collective-permute-start | bytes 417800 | tf_op jit(solution)/shard_map/ppermute | solution.py:518
  137.5 6.5 %collective-permute-start.10 = (f32[16,2176]{1,0:T(8,128)S(1)}, f32[16,2176]{1,0:T(8,128)S(1)}, u32[]{:S(2)}, u32[]{:S(2)}) collective-permute-start(f32[16,2176]{1,0:T(8,128)S(1)} %add.38), channel_id=1, source_target_pairs={{0,128},{64,192},{128,0},{192,64},{1,129},{65,193},{129,1},{193,65... | collective-permute-start | bytes 417800 | tf_op jit(solution)/shard_map/ppermute | solution.py:518
  144.0 2.3 %collective-permute-start.11 = (f32[16,2176]{1,0:T(8,128)S(1)}, f32[16,2176]{1,0:T(8,128)S(1)}, u32[]{:S(2)}, u32[]{:S(2)}) collective-permute-start(f32[16,2176]{1,0:T(8,128)S(1)} %add.39.keep_ref), channel_id=1, source_target_pairs={{0,64},{64,0},{128,192},{192,128},{1,65},{65,1},{129,193},{193,129... | collective-permute-start | bytes 417800 | tf_op jit(solution)/shard_map/ppermute | solution.py:518

commit v11 on v10

--- a/solution.py
+++ b/solution.py
@@ -127,45 +127,42 @@
     )(*extra, points, centers)
 
 
-def resident_kernel(points_ref, centers_ref, out_ref, points_buf, centers_buf, wide, sems):
-    loads = [
-        pltpu.make_async_copy(centers_ref, centers_buf, sems.at[0]),
-        pltpu.make_async_copy(points_ref, points_buf, sems.at[1]),
-    ]
-    for copy in loads:
-        copy.start()
-    for copy in loads:
-        copy.wait()
-    wide[...] = widened(centers_buf[...], 0)
-    for i in range(points_buf.shape[0] // CHUNK):
-        rows = slice(i * CHUNK, (i + 1) * CHUNK)
-        fill(0, wide, points_buf[rows], out_ref.at[:, rows])
-
-
-def resident_part(first, count, points, centers, limit):
+def wide_kernel(points_ref, centers_ref, out_ref):
+    out_ref[...] = widened(centers_ref[...], 0)
+
+
+def wide_centers(points, centers):
     m_dev, features = centers.shape
-
-    def kernel(points_ref, *refs):
-        resident_kernel(points_ref.at[pl.ds(first * CHUNK, count * CHUNK)], *refs)
-
-    return pl.pallas_call(
-        kernel,
+    return pl.pallas_call(
+        wide_kernel,
+        out_shape=jax.ShapeDtypeStruct((m_dev, 2 * features), bf16),
+        in_specs=[VMEM, VMEM],
+        out_specs=VMEM,
+        compiler_params=pltpu.CompilerParams(vmem_limit_bytes=LIMIT),
+        name="wide",
+    )(points, centers)
+
+
+def resident_kernel(first, points_ref, wide_ref, out_ref):
+    for i in range(out_ref.shape[1] // CHUNK):
+        rows = slice((first + i) * CHUNK, (first + i + 1) * CHUNK)
+        fill(0, wide_ref, points_ref[rows], out_ref.at[:, i * CHUNK : (i + 1) * CHUNK])
+
+
+def resident_part(first, count, points, wide):
+    m_dev, features = wide.shape
+    return pl.pallas_call(
+        functools.partial(resident_kernel, first),
         out_shape=jax.ShapeDtypeStruct((m_dev, count * CHUNK), bf16),
-        in_specs=[ANY, ANY],
+        in_specs=[VMEM, VMEM],
         out_specs=VMEM,
-        scratch_shapes=[
-            pltpu.VMEM((count * CHUNK, features), bf16),
-            pltpu.VMEM((m_dev, features), bf16),
-            pltpu.VMEM((m_dev, 2 * features), bf16),
-            pltpu.SemaphoreType.DMA((2,)),
-        ],
-        compiler_params=pltpu.CompilerParams(vmem_limit_bytes=limit << 20),
+        compiler_params=pltpu.CompilerParams(vmem_limit_bytes=LIMIT),
         cost_estimate=pl.CostEstimate(
-            flops=4 * m_dev * count * CHUNK * features,
+            flops=2 * m_dev * count * CHUNK * features,
             bytes_accessed=2 * m_dev * count * CHUNK,
             transcendentals=m_dev * count * CHUNK,
         ),
-    )(points, centers)
+    )(points, wide)
 
 
 def head_kernel(flags_ref, centers_ref, dir_ref, out_ref, rows_ref, vals_ref, sems):
@@ -559,10 +556,11 @@
     image_scale = 1.0 / (2.0 * math.sqrt(npg * n_pts))
 
     head = head_payload(flags, centers, direction, panel)
+    wide = wide_centers(points, centers)
     by_center = []
     first = 0
     for count in (2, 3, 3):
-        by_center.append(resident_part(first, count, points, centers, 12))
+        by_center.append(resident_part(first, count, points, wide))
         first += count
     for links in tree_pairs((n_far, n_near)):
         head = tree_stage(head, links)

time: 148 us -> 147 us (level)
  local copies, waits for them, and re-layouts: 2.66 us -> 4.26 us
  Pallas kernels: 52.9 us -> 51.4 us
  starting transfers between devices: 30 us -> 28.5 us
    unnamed x18 -> x22, local copies, waits for them, and re-layouts: 2.66 us -> 4.26 us
    ppermute x6, starting transfers between devices: 14.7 us -> 13.1 us  [swap(): return lax.ppermute(x, 'pts', [(i, i ^ bit) for i in range(n)])]
    pallas_call x3 -> x4, Pallas kernels: 11.6 us -> 10.2 us  [the longest x3 9.81 us: resident_part(): pl.pallas_call(functools.partial(resident_kernel, first), out_shape=jax.S...]
  transfers between devices with their start and end apart: 13 -> 13, of which waited for: 5 -> 5; matrix products, arithmetic and copies ran while one was open for 0% -> 0% of each run, Pallas kernels for 17% -> 16%
where the time goes in v11:
time: 147 us; the launch traced here: 146 us
  Pallas kernels  51.4 us (35%)
  blocking collectives  50 us (34%)
  starting transfers between devices  28.5 us (19%)
  waiting for transfers between devices  9.17 us (6%)
  local copies, waits for them, and re-layouts  4.26 us (3%)
  other arithmetic  1.68 us (1%)
    all_to_all x3, blocking collectives, exchange(): return lax.all_to_all(x, axis, 0, 0, tiled=True)  50 us
    ppermute x6, starting transfers between devices, swap(): return lax.ppermute(x, 'pts', [(i, i ^ bit) for i in range(n)])  13.1 us
    pallas_call x1, Pallas kernels, block_part(): pl.pallas_call(functools.partial(block_kernel, side, size, first, count),...  13.1 us
    pallas_call x1, Pallas kernels, panel_step(): pl.pallas_call(functools.partial(panel_kernel, len(blocks)), out_shape=(j...  12.1 us
    pallas_call x1, Pallas kernels, image(): pl.pallas_call(image_kernel, out_shape=(shape, shape), in_specs=[SMEM, VM...  10.8 us
    ppermute x6, starting transfers between devices, tree_stage(): return x + lax.ppermute(x, CTR, pairs)  10.4 us
    pallas_call x3, Pallas kernels, resident_part(): pl.pallas_call(functools.partial(resident_kernel, first), out_shape=jax.S...  9.81 us
    ppermute x6, waiting for transfers between devices, swap(): return lax.ppermute(x, 'pts', [(i, i ^ bit) for i in range(n)])  5.91 us
  transfers between devices with their start and end apart: 13, of which 5 were waited for; matrix products, arithmetic and copies ran while one was open for 0% of the time, Pallas kernels for 16%

profile of v11, /device:TPU:1, one launch (start us, length us, event | category | flops | bytes accessed | tf_op | source)
XLA Modules:
  0.0 146.0 jit_solution(7764220350864391352)
XLA Ops:
  1.2 2.2 %head.1 = bf16[320,128]{1,0:T(8,128)(2,1)} custom-call(s32[2]{0:T(128)} %pad_add_fusion.flags_ref, bf16[2048,128]{1,0:T(8,128)(2,1)} %centers_ref.7, f32[32,2048]{1,0:T(8,128)} %dir_ref.3), custom_call_target="tpu_custom_call" | custom-call | tf_op jit(solution)/shard_map/head/pallas_call | solution.py:195
  3.5 3.9 %collective-permute-start = (bf16[320,128]{1,0:T(8,128)(2,1)}, bf16[320,128]{1,0:T(8,128)(2,1)S(1)}, u32[]{:S(2)}, u32[]{:S(2)}) collective-permute-start(bf16[320,128]{1,0:T(8,128)(2,1)} %head.1), channel_id=1, source_target_pairs={{0,4},{64,68},{128,132},{192,196}} | collective-permute-start | bytes 245768 | tf_op jit(solution)/shard_map/ppermute | solution.py:510
  7.4 1.8 %collective-permute-done = bf16[320,128]{1,0:T(8,128)(2,1)S(1)} collective-permute-done((bf16[320,128]{1,0:T(8,128)(2,1)}, bf16[320,128]{1,0:T(8,128)(2,1)S(1)}, u32[]{:S(2)}, u32[]{:S(2)}) %collective-permute-start) | collective-permute-done | bytes 81952 | tf_op jit(solution)/shard_map/ppermute | solution.py:510
  11.4 1.5 %collective-permute-done.1 = bf16[320,128]{1,0:T(8,128)(2,1)S(1)} collective-permute-done((bf16[320,128]{1,0:T(8,128)(2,1)S(1)}, bf16[320,128]{1,0:T(8,128)(2,1)S(1)}, u32[]{:S(2)}, u32[]{:S(2)}) %collective-permute-start.1) | collective-permute-done | bytes 81952 | tf_op jit(solution)/shard_map/ppermute | solution.py:510
  14.2 2.2 %collective-permute-start.7 = (bf16[128,512]{1,0:T(8,128)(2,1)}, bf16[128,512]{1,0:T(8,128)(2,1)S(1)}, u32[]{:S(2)}, u32[]{:S(2)}) collective-permute-start(bf16[128,512]{1,0:T(8,128)(2,1)} %mine_ref.1), channel_id=1, source_target_pairs={{0,64},{64,0},{128,192},{192,128},{1,65},{65,1},{129,193},{193,129... | collective-permute-start | bytes 393224 | tf_op jit(solution)/shard_map/ppermute | solution.py:515
  16.4 1.6 %copy-done = bf16[8192,128]{1,0:T(8,128)(2,1)S(1)} copy-done((bf16[8192,128]{1,0:T(8,128)(2,1)S(1)}, bf16[8192,128]{1,0:T(8,128)(2,1)}, u32[]{:S(2)}) %copy-start) | copy-done | bytes 2097176
  19.5 1.3 collective-permute-start.3
  20.9 1.6 %copy-done.1 = bf16[8192,128]{1,0:T(8,128)(2,1)S(1)} copy-done((bf16[8192,128]{1,0:T(8,128)(2,1)S(1)}, bf16[8192,128]{1,0:T(8,128)(2,1)}, u32[]{:S(2)}) %copy-start.1) | copy-done | bytes 2097176
  22.4 3.6 %shard_map.78.refs_2_ = bf16[2048,3072]{1,0:T(8,128)(2,1)S(1)} custom-call(bf16[8192,128]{1,0:T(8,128)(2,1)S(1)} %copy-done.1, bf16[2048,256]{1,0:T(8,128)(2,1)S(1)} %wide.1.wide_ref), custom_call_target="tpu_custom_call" | custom-call | flops 3221225472 | bytes 12582912 | tf_op jit(solution)/shard_map/pallas_call | solution.py:154
  27.5 2.5 %collective-permute-start.8 = (bf16[256,512]{1,0:T(8,128)(2,1)S(1)}, bf16[256,512]{1,0:T(8,128)(2,1)S(1)}, u32[]{:S(2)}, u32[]{:S(2)}) collective-permute-start(bf16[256,512]{1,0:T(8,128)(2,1)S(1)} %pad_maximum_fusion), channel_id=1, source_target_pairs={{0,128},{64,192},{128,0},{192,64},{1,129},{65,193},{129,1},{193,65... | collective-permute-start | bytes 786440 | tf_op jit(solution)/shard_map/ppermute | solution.py:515
  31.4 3.6 %shard_map.77.refs_1_ = bf16[2048,3072]{1,0:T(8,128)(2,1)S(1)} custom-call(bf16[8192,128]{1,0:T(8,128)(2,1)S(1)} %copy-done.2, bf16[2048,256]{1,0:T(8,128)(2,1)S(1)} %wide.1.wide_ref), custom_call_target="tpu_custom_call" | custom-call | flops 3221225472 | bytes 12582912 | tf_op jit(solution)/shard_map/pallas_call | solution.py:154
  35.7 2.5 %shard_map.76.refs_0_ = bf16[2048,2048]{1,0:T(8,128)(2,1)S(1)} custom-call(bf16[8192,128]{1,0:T(8,128)(2,1)S(1)} %copy-done.2, bf16[2048,256]{1,0:T(8,128)(2,1)S(1)} %wide.1.wide_ref), custom_call_target="tpu_custom_call" | custom-call | flops 2147483648 | bytes 8388608 | tf_op jit(solution)/shard_map/pallas_call | solution.py:154
  38.3 12.1 %panel.1 = (f32[32,2048]{1,0:T(8,128)S(1)}, bf16[2048,128]{1,0:T(8,128)(2,1)}, bf16[64,96,128]{2,1,0:T(8,128)(2,1)S(1)}) custom-call(s32[2]{0:T(128)S(1)} %copy-done.10, bf16[2048,128]{1,0:T(8,128)(2,1)S(1)} %copy-done.5, bf16[320,128]{1,0:T(8,128)(2,1)S(1)} %add.37.head_ref, bf16[320,128]{1,0:T(8,128)(2,1)S(1)} %collective-permute-done.6.head_other_ref, ...), custom_call_target="tpu_custom_call" | custom-call | flops 8589934592 | bytes 33554432 | tf_op jit(solution)/shard_map/panel/pallas_call | solution.py:389
  50.4 26.3 %all_to_all.20.x_ref = bf16[8,768,128]{2,1,0:T(8,128)(2,1)S(1)} all-to-all(bf16[8,768,128]{2,1,0:T(8,128)(2,1)S(1)} %bitcast.3), channel_id=1, replica_groups=mesh['pts'=4,'ctr_0'=8,'ctr_1'=2,'ctr_2'=4] {'ctr_1','ctr_2'}, dimensions={0} | all-to-all | bytes 3145728 | tf_op jit(solution)/shard_map/all_to_all | solution.py:491
  77.2 13.7 %all_to_all.21.x_ref = bf16[8,96,128]{2,1,0:T(8,128)(2,1)S(1)} all-to-all(bf16[8,96,128]{2,1,0:T(8,128)(2,1)S(1)} %summed.1), channel_id=1, replica_groups=mesh['pts'=4,'ctr_0'=8,'ctr_1'=2,'ctr_2'=4] {'ctr_0'}, dimensions={0} | all-to-all | bytes 393216 | tf_op jit(solution)/shard_map/all_to_all | solution.py:491
  91.1 9.9 %all_to_all.22.x_ref = bf16[8,48,128]{2,1,0:T(8,128)(2,1)S(1)} all-to-all(bf16[8,48,128]{2,1,0:T(8,128)(2,1)S(1)} %owned.1), channel_id=1, replica_groups=mesh['pts'=4,'ctr_0'=8,'ctr_1'=2,'ctr_2'=4] {'ctr_0'}, dimensions={0} | all-to-all | bytes 196608 | tf_op jit(solution)/shard_map/all_to_all | solution.py:491
  101.9 4.9 %all-to-all-start.3 = ((bf16[8,272,128]{2,1,0:T(8,128)(2,1)}), bf16[8,272,128]{2,1,0:T(8,128)(2,1)}, u32[]{:S(2)}, u32[]{:S(2)}) async-start(bf16[8,272,128]{2,1,0:T(8,128)(2,1)} %relay.1), calls=%async_computation.3 | async-start | bytes 1114112 | tf_op jit(solution)/shard_map/all_to_all | solution.py:491
  106.8 13.1 %shard_map.79.source_ref = bf16[6,1024,2048]{2,1,0:T(8,128)(2,1)} custom-call(bf16[8192,128]{1,0:T(8,128)(2,1)} %points_ref.9, bf16[2048,128]{1,0:T(8,128)(2,1)} %centers_ref.7), custom_call_target="tpu_custom_call" | custom-call | flops 6442450944 | bytes 25165824 | tf_op jit(solution)/shard_map/pallas_call | solution.py:107
  120.0 10.8 %image.1 = (f32[16,2176]{1,0:T(8,128)S(1)}, f32[16,2176]{1,0:T(8,128)S(1)}) custom-call(s32[2]{0:T(128)S(1)} %copy-done.10, bf16[8,272,128]{2,1,0:T(8,128)(2,1)} %all-to-all-done.3.w_ref, bf16[2048,128]{1,0:T(8,128)(2,1)S(1)} %copy-done.6, bf16[8192,128]{1,0:T(8,128)(2,1)S(1)} %copy-done.3, bf16[6,1024,2048]{2,1,0:T(8,128)(2,1)} %shard_map.79.source_ref), custom_call_target="tpu_custom_call" | custom-call | flops 8589934592 | bytes 33554432 | tf_op jit(solution)/shard_map/image/pallas_call | solution.py:466
  130.8 4.0 %collective-permute-start.9 = (f32[16,2176]{1,0:T(8,128)S(1)}, f32[16,2176]{1,0:T(8,128)S(1)}, u32[]{:S(2)}, u32[]{:S(2)}) collective-permute-start(f32[16,2176]{1,0:T(8,128)S(1)} %get-tuple-element.14), channel_id=1, source_target_pairs={{0,64},{64,0},{128,192},{192,128},{1,65},{65,1},{129,193},{193,129... | collective-permute-start | bytes 417800 | tf_op jit(solution)/shard_map/ppermute | solution.py:515
  135.8 2.5 %collective-permute-start.10 = (f32[16,2176]{1,0:T(8,128)S(1)}, f32[16,2176]{1,0:T(8,128)S(1)}, u32[]{:S(2)}, u32[]{:S(2)}) collective-permute-start(f32[16,2176]{1,0:T(8,128)S(1)} %add.38), channel_id=1, source_target_pairs={{0,128},{64,192},{128,0},{192,64},{1,129},{65,193},{129,1},{193,65... | collective-permute-start | bytes 417800 | tf_op jit(solution)/shard_map/ppermute | solution.py:515
  138.4 3.9 %collective-permute-done.10 = f32[16,2176]{1,0:T(8,128)S(1)} collective-permute-done((f32[16,2176]{1,0:T(8,128)S(1)}, f32[16,2176]{1,0:T(8,128)S(1)}, u32[]{:S(2)}, u32[]{:S(2)}) %collective-permute-start.10) | collective-permute-done | bytes 139296 | tf_op jit(solution)/shard_map/ppermute | solution.py:515
  142.3 1.3 collective-permute-start.11
  144.6 1.4 final.1
  (49 shorter events, 12.4 us)
Async XLA Ops:
  3.5 5.7 %collective-permute-start = (bf16[320,128]{1,0:T(8,128)(2,1)}, bf16[320,128]{1,0:T(8,128)(2,1)S(1)}, u32[]{:S(2)}, u32[]{:S(2)}) collective-permute-start(bf16[320,128]{1,0:T(8,128)(2,1)} %head.1), channel_id=1, source_target_pairs={{0,4},{64,68},{128,132},{192,196}} | collective-permute-start | bytes 245768 | tf_op jit(solution)/shard_map/ppermute | solution.py:510
  10.1 2.8 %collective-permute-start.1 = (bf16[320,128]{1,0:T(8,128)(2,1)S(1)}, bf16[320,128]{1,0:T(8,128)(2,1)S(1)}, u32[]{:S(2)}, u32[]{:S(2)}) collective-permute-start(bf16[320,128]{1,0:T(8,128)(2,1)S(1)} %add.32), channel_id=1, source_target_pairs={{0,2},{4,6},{64,66},{68,70},{128,130},{132,134},{192,194},{196,198}} | collective-permute-start | bytes 245768 | tf_op jit(solution)/shard_map/ppermute | solution.py:510
  12.9 6.6 %collective-permute-start.2 = (bf16[320,128]{1,0:T(8,128)(2,1)S(1)}, bf16[320,128]{1,0:T(8,128)(2,1)S(1)}, u32[]{:S(2)}, u32[]{:S(2)}) collective-permute-start(bf16[320,128]{1,0:T(8,128)(2,1)S(1)} %add.33), channel_id=1, source_target_pairs={{0,1},{4,5},{2,3},{6,7},{64,65},{68,69},{66,67},{70,71},{128,129},... | collective-permute-start | bytes 245768 | tf_op jit(solution)/shard_map/ppermute | solution.py:510
  14.2 13.2 %collective-permute-start.7 = (bf16[128,512]{1,0:T(8,128)(2,1)}, bf16[128,512]{1,0:T(8,128)(2,1)S(1)}, u32[]{:S(2)}, u32[]{:S(2)}) collective-permute-start(bf16[128,512]{1,0:T(8,128)(2,1)} %mine_ref.1), channel_id=1, source_target_pairs={{0,64},{64,0},{128,192},{192,128},{1,65},{65,1},{129,193},{193,129... | collective-permute-start | bytes 393224 | tf_op jit(solution)/shard_map/ppermute | solution.py:515
  16.4 1.6 %copy-start = (bf16[8192,128]{1,0:T(8,128)(2,1)S(1)}, bf16[8192,128]{1,0:T(8,128)(2,1)}, u32[]{:S(2)}) copy-start(bf16[8192,128]{1,0:T(8,128)(2,1)} %points_ref.9) | copy-start | bytes 6291460
  18.0 1.0 copy-start.4
  19.5 8.0 %copy-start.9 = (bf16[128,512]{1,0:T(8,128)(2,1)S(1)}, bf16[128,512]{1,0:T(8,128)(2,1)}, u32[]{:S(2)}) copy-start(bf16[128,512]{1,0:T(8,128)(2,1)} %mine_ref.1) | copy-start | bytes 393220
  19.5 6.5 %collective-permute-start.3 = (bf16[320,128]{1,0:T(8,128)(2,1)S(1)}, bf16[320,128]{1,0:T(8,128)(2,1)S(1)}, u32[]{:S(2)}, u32[]{:S(2)}) collective-permute-start(bf16[320,128]{1,0:T(8,128)(2,1)S(1)} %add.34), channel_id=1, source_target_pairs={{0,32},{4,36},{2,34},{6,38},{1,33},{5,37},{3,35},{7,39},{64,96},{6... | collective-permute-start | bytes 245768 | tf_op jit(solution)/shard_map/ppermute | solution.py:510
  20.8 1.6 %copy-start.1 = (bf16[8192,128]{1,0:T(8,128)(2,1)S(1)}, bf16[8192,128]{1,0:T(8,128)(2,1)}, u32[]{:S(2)}) copy-start(bf16[8192,128]{1,0:T(8,128)(2,1)} %points_ref.9) | copy-start | bytes 6291460
  22.4 8.9 %copy-start.2 = (bf16[8192,128]{1,0:T(8,128)(2,1)S(1)}, bf16[8192,128]{1,0:T(8,128)(2,1)}, u32[]{:S(2)}) copy-start(bf16[8192,128]{1,0:T(8,128)(2,1)} %points_ref.9) | copy-start | bytes 6291460
  26.1 3.9 %collective-permute-start.4 = (bf16[320,128]{1,0:T(8,128)(2,1)S(1)}, bf16[320,128]{1,0:T(8,128)(2,1)S(1)}, u32[]{:S(2)}, u32[]{:S(2)}) collective-permute-start(bf16[320,128]{1,0:T(8,128)(2,1)S(1)} %add.35), channel_id=1, source_target_pairs={{0,16},{4,20},{2,18},{6,22},{1,17},{5,21},{3,19},{7,23},{32,48},{3... | collective-permute-start | bytes 245768 | tf_op jit(solution)/shard_map/ppermute | solution.py:510
  27.5 10.7 %collective-permute-start.8 = (bf16[256,512]{1,0:T(8,128)(2,1)S(1)}, bf16[256,512]{1,0:T(8,128)(2,1)S(1)}, u32[]{:S(2)}, u32[]{:S(2)}) collective-permute-start(bf16[256,512]{1,0:T(8,128)(2,1)S(1)} %pad_maximum_fusion), channel_id=1, source_target_pairs={{0,128},{64,192},{128,0},{192,64},{1,129},{65,193},{129,1},{193,65... | collective-permute-start | bytes 786440 | tf_op jit(solution)/shard_map/ppermute | solution.py:515
  30.1 5.0 %collective-permute-start.5 = (bf16[320,128]{1,0:T(8,128)(2,1)S(1)}, bf16[320,128]{1,0:T(8,128)(2,1)S(1)}, u32[]{:S(2)}, u32[]{:S(2)}) collective-permute-start(bf16[320,128]{1,0:T(8,128)(2,1)S(1)} %add.36), channel_id=1, source_target_pairs={{0,8},{4,12},{2,10},{6,14},{1,9},{5,13},{3,11},{7,15},{32,40},{36,... | collective-permute-start | bytes 245768 | tf_op jit(solution)/shard_map/ppermute | solution.py:510
  35.0 3.2 %copy-start.5 = (bf16[2048,128]{1,0:T(8,128)(2,1)S(1)}, bf16[2048,128]{1,0:T(8,128)(2,1)}, u32[]{:S(2)}) copy-start(bf16[2048,128]{1,0:T(8,128)(2,1)} %centers_ref.7) | copy-start | bytes 1572868
  35.0 3.2 %copy-start.7 = (f32[32,2048]{1,0:T(8,128)S(1)}, f32[32,2048]{1,0:T(8,128)}, u32[]{:S(2)}) copy-start(f32[32,2048]{1,0:T(8,128)} %dir_ref.3) | copy-start | bytes 786436
  35.0 3.2 %copy-start.10 = (s32[2]{0:T(128)S(1)}, s32[2]{0:T(128)}, u32[]{:S(2)}) copy-start(s32[2]{0:T(128)} %pad_add_fusion.flags_ref) | copy-start | bytes 28
  35.1 3.1 %collective-permute-start.6 = (bf16[320,128]{1,0:T(8,128)(2,1)S(1)}, bf16[320,128]{1,0:T(8,128)(2,1)S(1)}, u32[]{:S(2)}, u32[]{:S(2)}) collective-permute-start(bf16[320,128]{1,0:T(8,128)(2,1)S(1)} %add.37.head_ref), channel_id=1, source_target_pairs={{0,64},{64,0},{128,192},{192,128},{1,65},{65,1},{129,193},{193,129... | collective-permute-start | bytes 245768 | tf_op jit(solution)/shard_map/ppermute | solution.py:515
  38.2 52.7 %copy-start.8 = (f32[32,2048]{1,0:T(8,128)S(1)}, f32[32,2048]{1,0:T(8,128)}, u32[]{:S(2)}) copy-start(f32[32,2048]{1,0:T(8,128)} %res_ref.3) | copy-start | bytes 786436
  101.9 18.1 %all-to-all-start.3 = ((bf16[8,272,128]{2,1,0:T(8,128)(2,1)}), bf16[8,272,128]{2,1,0:T(8,128)(2,1)}, u32[]{:S(2)}, u32[]{:S(2)}) async-start(bf16[8,272,128]{2,1,0:T(8,128)(2,1)} %relay.1), calls=%async_computation.3 | async-start | bytes 1114112 | tf_op jit(solution)/shard_map/all_to_all | solution.py:491
  106.8 13.2 %copy-start.3 = (bf16[8192,128]{1,0:T(8,128)(2,1)S(1)}, bf16[8192,128]{1,0:T(8,128)(2,1)}, u32[]{:S(2)}) copy-start(bf16[8192,128]{1,0:T(8,128)(2,1)} %points_ref.9) | copy-start | bytes 6291460
  106.8 13.2 %copy-start.6 = (bf16[2048,128]{1,0:T(8,128)(2,1)S(1)}, bf16[2048,128]{1,0:T(8,128)(2,1)}, u32[]{:S(2)}) copy-start(bf16[2048,128]{1,0:T(8,128)(2,1)} %centers_ref.7) | copy-start | bytes 1572868
  130.8 5.0 %collective-permute-start.9 = (f32[16,2176]{1,0:T(8,128)S(1)}, f32[16,2176]{1,0:T(8,128)S(1)}, u32[]{:S(2)}, u32[]{:S(2)}) collective-permute-start(f32[16,2176]{1,0:T(8,128)S(1)} %get-tuple-element.14), channel_id=1, source_target_pairs={{0,64},{64,0},{128,192},{192,128},{1,65},{65,1},{129,193},{193,129... | collective-permute-start | bytes 417800 | tf_op jit(solution)/shard_map/ppermute | solution.py:515
  135.8 6.5 %collective-permute-start.10 = (f32[16,2176]{1,0:T(8,128)S(1)}, f32[16,2176]{1,0:T(8,128)S(1)}, u32[]{:S(2)}, u32[]{:S(2)}) collective-permute-start(f32[16,2176]{1,0:T(8,128)S(1)} %add.38), channel_id=1, source_target_pairs={{0,128},{64,192},{128,0},{192,64},{1,129},{65,193},{129,1},{193,65... | collective-permute-start | bytes 417800 | tf_op jit(solution)/shard_map/ppermute | solution.py:515
  142.3 2.3 %collective-permute-start.11 = (f32[16,2176]{1,0:T(8,128)S(1)}, f32[16,2176]{1,0:T(8,128)S(1)}, u32[]{:S(2)}, u32[]{:S(2)}) collective-permute-start(f32[16,2176]{1,0:T(8,128)S(1)} %add.39.keep_ref), channel_id=1, source_target_pairs={{0,64},{64,0},{128,192},{192,128},{1,65},{65,1},{129,193},{193,129... | collective-permute-start | bytes 417800 | tf_op jit(solution)/shard_map/ppermute | solution.py:515
